TPU v7x, 32 devices: a whole 2x2x4 slice. The times are simulated.
32 devices in a mesh: gx: 2 (over x), gy: 4 (over z), gz: 4 (over y, core).
Axes of the slice: x: 2, y: 2, z: 4, core: 2. Of those that a mesh axis runs over, the one named last changes fastest.
Arguments:
- source: float32 [32, 256, 512], P('gx', 'gy', 'gz'), may hold values from -5 to 5
- first_guess: float32 [32, 256, 512], P('gx', 'gy', 'gz'), may hold values from -5 to 5
- cell_classes: int32 [32, 256, 512], P('gx', 'gy', 'gz'), may hold values from 0 to 7
- class_table: float32 [8], replicated, may hold values from 0.2 to 5
Outputs:
- solution: float32 [32, 256, 512], P('gx', 'gy', 'gz')
- residual: float32 [32, 256, 512], P('gx', 'gy', 'gz')
All inputs are finite; a program needn't handle non-finite values.
Results may differ from a plain program's by a relative error of at most 0.0003.
Values sent between devices are 32-bit elements; how exact they have to be, the bound alone decides.
No kernel may reach another device: no remote copies, remote signals or barrier semaphores. Data moves between devices by JAX's collectives and lax.ppermute only.
A program may use at most 192 MiB of HBM per device.

v0:
```python
import jax
import jax.numpy as jnp
from jax import lax
from jax.sharding import PartitionSpec as P

LEVELS = 3
SWEEPS = 4
COARSE = 16
CLASSES = 8


relax_weight = 0.85


def with_halo(block, sides, width):
    for axis, dim in sides:
        count = lax.axis_size(axis)
        forward = [(i, i + 1) for i in range(count - 1)]
        backward = [(target, source) for source, target in forward]
        low = lax.ppermute(
            lax.slice_in_dim(block, block.shape[dim] - width, None, axis=dim), axis, forward
        )
        high = lax.ppermute(lax.slice_in_dim(block, 0, width, axis=dim), axis, backward)
        block = jnp.concatenate([low, block, high], axis=dim)
    return block


def neighbor(padded, axis_dim, offset):
    window = [slice(1, -1), slice(1, -1), slice(1, -1)]
    window[axis_dim] = slice(1 + offset, padded.shape[axis_dim] - 1 + offset)
    return padded[tuple(window)]


def apply_padded(padded_u, padded_c, level_scale):
    center_u = padded_u[1:-1, 1:-1, 1:-1]
    center_c = padded_c[1:-1, 1:-1, 1:-1]
    stencil_sum = jnp.zeros_like(center_u)
    diagonal = jnp.zeros_like(center_u)
    for axis_dim in range(3):
        for offset in (-1, 1):
            face = 0.5 * (center_c + neighbor(padded_c, axis_dim, offset))
            stencil_sum = stencil_sum + face * (center_u - neighbor(padded_u, axis_dim, offset))
            diagonal = diagonal + face
    return (level_scale * stencil_sum, level_scale * diagonal)


def restrict(field):
    size_x, size_y, size_z = field.shape
    return field.reshape(size_x // 2, 2, size_y // 2, 2, size_z // 2, 2).mean(axis=(1, 3, 5))


def prolong(field):
    size_x, size_y, size_z = field.shape
    spread = jnp.broadcast_to(field[:, None, :, None, :, None], (size_x, 2, size_y, 2, size_z, 2))
    return spread.reshape(2 * size_x, 2 * size_y, 2 * size_z)


def coef_halo(coef_value):
    return with_halo(coef_value, (("gx", 0), ("gy", 1), ("gz", 2)), 1)


def residual_of(values, rhs_field, coef_padded, level_scale):
    padded_u = with_halo(values, (("gx", 0), ("gy", 1), ("gz", 2)), 1)
    stencil_sum, diagonal = apply_padded(padded_u, coef_padded, level_scale)
    return rhs_field - stencil_sum


def narrow_sweeps(values, rhs_field, coef_padded, level_scale):
    for sweep_id in range(SWEEPS):
        padded_u = with_halo(values, (("gx", 0), ("gy", 1), ("gz", 2)), 1)
        stencil_sum, diagonal = apply_padded(padded_u, coef_padded, level_scale)
        values = values + relax_weight * (rhs_field - stencil_sum) / diagonal
    return values


def smooth(values, level_id, rhs_list, padded_list):
    level_scale = 0.25**level_id
    return narrow_sweeps(values, rhs_list[level_id], padded_list[level_id], level_scale)


def coarse_solve(coarse_rhs, coarse_coef):
    coarse_scale = 0.25**LEVELS
    coarse_pad = coef_halo(coarse_coef)

    def local_step(sweep_id, values):
        padded_u = with_halo(values, (("gx", 0), ("gy", 1), ("gz", 2)), 1)
        stencil_sum, diagonal = apply_padded(padded_u, coarse_pad, coarse_scale)
        return values + relax_weight * (coarse_rhs - stencil_sum) / diagonal

    return lax.fori_loop(0, COARSE, local_step, jnp.zeros_like(coarse_rhs))


def body(source, first_guess, cell_classes, class_table):
    cell_coef = jnp.zeros(cell_classes.shape, jnp.float32)
    for class_id in range(CLASSES):
        cell_coef = cell_coef + jnp.where(cell_classes == class_id, class_table[class_id], 0.0)
    coef_list = [cell_coef]
    for level_id in range(LEVELS):
        coef_list.append(restrict(coef_list[-1]))
    top_level = LEVELS
    padded_list = [coef_halo(coef_list[level_id]) for level_id in range(top_level)]
    rhs_list = [source]
    iterate_list = []
    values = first_guess
    for level_id in range(top_level):
        level_scale = 0.25**level_id
        if level_id > 0:
            values = jnp.zeros_like(rhs_list[level_id])
        values = smooth(values, level_id, rhs_list, padded_list)
        iterate_list.append(values)
        rhs_list.append(
            restrict(residual_of(values, rhs_list[level_id], padded_list[level_id], level_scale))
        )
    correction = coarse_solve(rhs_list[LEVELS], coef_list[LEVELS])
    for level_id in reversed(range(top_level)):
        values = iterate_list[level_id] + prolong(correction)
        values = smooth(values, level_id, rhs_list, padded_list)
        correction = values
    final = residual_of(correction, source, padded_list[0], 1.0)
    return (correction, final)


def solution(mesh):
    return jax.shard_map(
        body,
        mesh=mesh,
        in_specs=(P("gx", "gy", "gz"), P("gx", "gy", "gz"), P("gx", "gy", "gz"), P()),
        out_specs=(P("gx", "gy", "gz"), P("gx", "gy", "gz")),
        check_vma=False,
    )
```

profile of v0, /device:TPU:1, one launch (start us, length us, event | category | flops | bytes accessed | tf_op | source)
XLA Modules:
  0.0 1385.1 jit_solution(2295084286523813654)
XLA Ops:
  2.3 6.5 select_add_fusion
  48.9 5.5 fusion.211
  73.9 5.9 collective-permute-start.22
  99.8 34.9 %reshape.37 = f32[8,2,32,2,64,2]{5,4,3,2,1,0:T(8,128)} reshape(f32[16,64,128]{2,1,0:T(8,128)S(1)} %select_add_fusion) | data formatting | bytes 1048576 | tf_op jit(solution)/shard_map/reshape | solution.py:49
  134.7 12.2 reduce_sum.55
  203.4 5.9 collective-permute-start.34
  264.0 35.6 %reshape.36 = f32[8,2,32,2,64,2]{5,4,3,2,1,0:T(8,128)} reshape(f32[16,64,128]{2,1,0:T(8,128)} %fusion.127) | data formatting | bytes 1048576 | tf_op jit(solution)/shard_map/reshape | solution.py:49
  299.7 12.2 reduce_sum.54
  329.2 6.5 collective-permute-start.58
  353.5 5.8 div.110
  404.3 5.9 collective-permute-start.70
  451.1 6.6 reshape.38
  476.3 6.5 collective-permute-start.94
  584.1 396.2 %while.13 = (s32[]{:T(128)}, f32[2,8,16]{2,1,0:T(8,128)}, f32[2,8,16]{2,1,0:T(8,128)}, f32[2,8,16]{2,1,0:T(8,128)}, f32[2,8,16]{2,1,0:T(8,128)}, /*index=5*/f32[...) while((s32[]{:T(128)}, f32[2,8,16]{2,1,0:T(8,128)}, ...), condition=%wide.region_7.8_spmd.clone, body=%wide.region_6.7_spmd.clone.sunk | while | flops 16387 | bytes 37527 | solution.py:90
  621.9 6.1 collective-permute-start.5
  646.7 6.2 collective-permute-start.5
  671.7 6.2 collective-permute-start.5
  696.7 6.2 collective-permute-start.5
  721.6 6.2 collective-permute-start.5
  746.6 6.2 collective-permute-start.5
  771.6 6.2 collective-permute-start.5
  796.6 6.2 collective-permute-start.5
  821.5 6.2 collective-permute-start.5
  846.5 6.2 collective-permute-start.5
  871.5 6.2 collective-permute-start.5
  896.4 6.2 collective-permute-start.5
  921.4 6.2 collective-permute-start.5
  946.4 6.2 collective-permute-start.5
  971.4 6.2 collective-permute-start.5
  1001.6 6.8 collective-permute-start.124
  1196.9 11.5 broadcast_in_dim.77
  1208.4 24.5 %reshape.42 = f32[16,64,128]{2,1,0:T(8,128)} reshape(f32[8,2,32,2,64,2]{5,4,3,2,1,0:T(8,128)} %broadcast_in_dim.77) | data formatting | bytes 1048576 | tf_op jit(solution)/shard_map/reshape | solution.py:55
  (1110 shorter events, 1092.5 us)
Async XLA Ops:
  25.8 13.5 collective-permute-start.11
  31.7 14.1 %collective-permute-start.16 = (f32[18,66,1]{1,2,0:T(1,128)S(1)}, f32[18,66,1]{1,2,0:T(1,128)S(1)}, u32[]{:S(2)}, u32[]{:S(2)}) collective-permute-start(f32[18,66,1]{1,2,0:T(1,128)S(1)} %copy.10), channel_id=1, source_target_pairs={{1,0},{2,1},{3,2},{5,4},{6,5},{7,6},{9,8},{10,9},{11,10},{13,12},{... | collective-permute-start | bytes 14264 | tf_op jit(solution)/shard_map/ppermute | solution.py:23
  90.6 56.3 %collective-permute-start.24 = (f32[1,64,128]{2,1,0:T(8,128)S(1)}, f32[1,64,128]{2,1,0:T(8,128)S(1)}, u32[]{:S(2)}, u32[]{:S(2)}) collective-permute-start(f32[1,64,128]{2,1,0:T(8,128)S(1)} %get-tuple-element.227), channel_id=1, source_target_pairs={{0,16},{1,17},{2,18},{3,19},{4,20},{5,21},{6,22},{7,23},{8,24},{9,... | collective-permute-start | bytes 98312 | tf_op jit(solution)/shard_map/ppermute | solution.py:20
  91.9 55.0 %collective-permute-start.25 = (f32[1,64,128]{2,1,0:T(8,128)S(1)}, f32[1,64,128]{2,1,0:T(8,128)S(1)}, u32[]{:S(2)}, u32[]{:S(2)}) collective-permute-start(f32[1,64,128]{2,1,0:T(8,128)S(1)} %get-tuple-element.228), channel_id=1, source_target_pairs={{16,0},{17,1},{18,2},{19,3},{20,4},{21,5},{22,6},{23,7},{24,8},{25... | collective-permute-start | bytes 98312 | tf_op jit(solution)/shard_map/ppermute | solution.py:23
  93.8 96.5 %collective-permute-start.43 = (f32[1,32,64]{2,1,0:T(8,128)}, f32[1,32,64]{2,1,0:T(8,128)}, u32[]{:S(2)}, u32[]{:S(2)}) collective-permute-start(f32[1,32,64]{2,1,0:T(8,128)} %broadcast.81), channel_id=1, source_target_pairs={{0,16},{1,17},{2,18},{3,19},{4,20},{5,21},{6,22},{7,23},{8,24},{9,... | collective-permute-start | bytes 24584 | tf_op jit(solution)/shard_map/ppermute | solution.py:20
  98.5 93.1 %collective-permute-start.45 = (f32[1,32,64]{2,1,0:T(8,128)}, f32[1,32,64]{2,1,0:T(8,128)}, u32[]{:S(2)}, u32[]{:S(2)}) collective-permute-start(f32[1,32,64]{2,1,0:T(8,128)} %broadcast.81), channel_id=1, source_target_pairs={{16,0},{17,1},{18,2},{19,3},{20,4},{21,5},{22,6},{23,7},{24,8},{25... | collective-permute-start | bytes 24584 | tf_op jit(solution)/shard_map/ppermute | solution.py:23
  157.7 11.9 collective-permute-start.28
  164.7 15.6 %collective-permute-start.42 = (f32[1,32,64]{2,1,0:T(8,128)S(1)}, f32[1,32,64]{2,1,0:T(8,128)S(1)}, u32[]{:S(2)}, u32[]{:S(2)}) collective-permute-start(f32[1,32,64]{2,1,0:T(8,128)S(1)} %get-tuple-element.292), channel_id=1, source_target_pairs={{0,16},{1,17},{2,18},{3,19},{4,20},{5,21},{6,22},{7,23},{8,24},{9,... | collective-permute-start | bytes 24584 | tf_op jit(solution)/shard_map/ppermute | solution.py:20
  181.7 27.6 %collective-permute-start.46 = (f32[10,1,64]{2,1,0:T(1,128)S(1)}, f32[10,1,64]{2,1,0:T(1,128)S(1)}, u32[]{:S(2)}, u32[]{:S(2)}) collective-permute-start(f32[10,1,64]{2,1,0:T(1,128)S(1)} %get-tuple-element.272), channel_id=1, source_target_pairs={{0,4},{4,8},{8,12},{1,5},{5,9},{9,13},{2,6},{6,10},{10,14},{3,7},{... | collective-permute-start | bytes 7688 | tf_op jit(solution)/shard_map/ppermute | solution.py:20
  184.9 26.3 %collective-permute-start.48 = (f32[10,1,64]{2,1,0:T(1,128)S(1)}, f32[10,1,64]{2,1,0:T(1,128)S(1)}, u32[]{:S(2)}, u32[]{:S(2)}) collective-permute-start(f32[10,1,64]{2,1,0:T(1,128)S(1)} %get-tuple-element.271), channel_id=1, source_target_pairs={{4,0},{8,4},{12,8},{5,1},{9,5},{13,9},{6,2},{10,6},{14,10},{7,3},{... | collective-permute-start | bytes 7688 | tf_op jit(solution)/shard_map/ppermute | solution.py:23
  193.0 42.3 %collective-permute-start.47 = (f32[10,1,64]{2,1,0:T(1,128)}, f32[10,1,64]{2,1,0:T(1,128)}, u32[]{:S(2)}, u32[]{:S(2)}) collective-permute-start(f32[10,1,64]{2,1,0:T(1,128)} %get-tuple-element.273), channel_id=1, source_target_pairs={{0,4},{4,8},{8,12},{1,5},{5,9},{9,13},{2,6},{6,10},{10,14},{3,7},{... | collective-permute-start | bytes 7688 | tf_op jit(solution)/shard_map/ppermute | solution.py:20
  198.0 38.6 %collective-permute-start.49 = (f32[10,1,64]{2,1,0:T(1,128)}, f32[10,1,64]{2,1,0:T(1,128)}, u32[]{:S(2)}, u32[]{:S(2)}) collective-permute-start(f32[10,1,64]{2,1,0:T(1,128)} %get-tuple-element.274), channel_id=1, source_target_pairs={{4,0},{8,4},{12,8},{5,1},{9,5},{13,9},{6,2},{10,6},{14,10},{7,3},{... | collective-permute-start | bytes 7688 | tf_op jit(solution)/shard_map/ppermute | solution.py:23
  225.9 86.0 %collective-permute-start.50 = (f32[10,34,1]{2,1,0:T(8,128)}, f32[10,34,1]{2,1,0:T(8,128)}, u32[]{:S(2)}, u32[]{:S(2)}) collective-permute-start(f32[10,34,1]{2,1,0:T(8,128)} %get-tuple-element.252), channel_id=1, source_target_pairs={{0,1},{1,2},{2,3},{4,5},{5,6},{6,7},{8,9},{9,10},{10,11},{12,13},{... | collective-permute-start | bytes 4088 | tf_op jit(solution)/shard_map/ppermute | solution.py:20
  228.7 83.2 %collective-permute-start.52 = (f32[10,34,1]{2,1,0:T(8,128)}, f32[10,34,1]{2,1,0:T(8,128)}, u32[]{:S(2)}, u32[]{:S(2)}) collective-permute-start(f32[10,34,1]{2,1,0:T(8,128)} %get-tuple-element.251), channel_id=1, source_target_pairs={{1,0},{2,1},{3,2},{5,4},{6,5},{7,6},{9,8},{10,9},{11,10},{13,12},{... | collective-permute-start | bytes 4088 | tf_op jit(solution)/shard_map/ppermute | solution.py:23
  243.4 13.1 collective-permute-start.40
  252.8 59.1 %collective-permute-start.51 = (f32[10,34,1]{2,1,0:T(8,128)}, f32[10,34,1]{2,1,0:T(8,128)}, u32[]{:S(2)}, u32[]{:S(2)}) collective-permute-start(f32[10,34,1]{2,1,0:T(8,128)} %get-tuple-element.253), channel_id=1, source_target_pairs={{0,1},{1,2},{2,3},{4,5},{5,6},{6,7},{8,9},{9,10},{10,11},{12,13},{... | collective-permute-start | bytes 4088 | tf_op jit(solution)/shard_map/ppermute | solution.py:20
  257.5 54.4 %collective-permute-start.53 = (f32[10,34,1]{2,1,0:T(8,128)}, f32[10,34,1]{2,1,0:T(8,128)}, u32[]{:S(2)}, u32[]{:S(2)}) collective-permute-start(f32[10,34,1]{2,1,0:T(8,128)} %get-tuple-element.254), channel_id=1, source_target_pairs={{1,0},{2,1},{3,2},{5,4},{6,5},{7,6},{9,8},{10,9},{11,10},{13,12},{... | collective-permute-start | bytes 4088 | tf_op jit(solution)/shard_map/ppermute | solution.py:23
  344.4 18.0 %collective-permute-start.60 = (f32[1,32,64]{2,1,0:T(8,128)}, f32[1,32,64]{2,1,0:T(8,128)S(1)}, u32[]{:S(2)}, u32[]{:S(2)}) collective-permute-start(f32[1,32,64]{2,1,0:T(8,128)} %get-tuple-element.287), channel_id=1, source_target_pairs={{0,16},{1,17},{2,18},{3,19},{4,20},{5,21},{6,22},{7,23},{8,24},{9,... | collective-permute-start | bytes 24584 | tf_op jit(solution)/shard_map/ppermute | solution.py:20
  345.7 16.7 %collective-permute-start.61 = (f32[1,32,64]{2,1,0:T(8,128)}, f32[1,32,64]{2,1,0:T(8,128)S(1)}, u32[]{:S(2)}, u32[]{:S(2)}) collective-permute-start(f32[1,32,64]{2,1,0:T(8,128)} %get-tuple-element.288), channel_id=1, source_target_pairs={{16,0},{17,1},{18,2},{19,3},{20,4},{21,5},{22,6},{23,7},{24,8},{25... | collective-permute-start | bytes 24584 | tf_op jit(solution)/shard_map/ppermute | solution.py:23
  347.6 49.1 %collective-permute-start.79 = (f32[1,16,32]{2,1,0:T(8,128)}, f32[1,16,32]{2,1,0:T(8,128)}, u32[]{:S(2)}, u32[]{:S(2)}) collective-permute-start(f32[1,16,32]{2,1,0:T(8,128)} %broadcast.86), channel_id=1, source_target_pairs={{0,16},{1,17},{2,18},{3,19},{4,20},{5,21},{6,22},{7,23},{8,24},{9,... | collective-permute-start | bytes 6152 | tf_op jit(solution)/shard_map/ppermute | solution.py:20
  352.2 45.9 %collective-permute-start.81 = (f32[1,16,32]{2,1,0:T(8,128)}, f32[1,16,32]{2,1,0:T(8,128)}, u32[]{:S(2)}, u32[]{:S(2)}) collective-permute-start(f32[1,16,32]{2,1,0:T(8,128)} %broadcast.86), channel_id=1, source_target_pairs={{16,0},{17,1},{18,2},{19,3},{20,4},{21,5},{22,6},{23,7},{24,8},{25... | collective-permute-start | bytes 6152 | tf_op jit(solution)/shard_map/ppermute | solution.py:23
  376.3 12.1 collective-permute-start.78
  389.7 20.4 %collective-permute-start.82 = (f32[6,1,32]{2,1,0:T(1,128)S(1)}, f32[6,1,32]{2,1,0:T(1,128)S(1)}, u32[]{:S(2)}, u32[]{:S(2)}) collective-permute-start(f32[6,1,32]{2,1,0:T(1,128)S(1)} %get-tuple-element.330), channel_id=1, source_target_pairs={{0,4},{4,8},{8,12},{1,5},{5,9},{9,13},{2,6},{6,10},{10,14},{3,7},{... | collective-permute-start | bytes 2312 | tf_op jit(solution)/shard_map/ppermute | solution.py:20
  391.4 20.7 %collective-permute-start.84 = (f32[6,1,32]{2,1,0:T(1,128)S(1)}, f32[6,1,32]{2,1,0:T(1,128)S(1)}, u32[]{:S(2)}, u32[]{:S(2)}) collective-permute-start(f32[6,1,32]{2,1,0:T(1,128)S(1)} %get-tuple-element.329), channel_id=1, source_target_pairs={{4,0},{8,4},{12,8},{5,1},{9,5},{13,9},{6,2},{10,6},{14,10},{7,3},{... | collective-permute-start | bytes 2312 | tf_op jit(solution)/shard_map/ppermute | solution.py:23
  398.8 34.5 %collective-permute-start.83 = (f32[6,1,32]{2,1,0:T(1,128)S(1)}, f32[6,1,32]{2,1,0:T(1,128)S(1)}, u32[]{:S(2)}, u32[]{:S(2)}) collective-permute-start(f32[6,1,32]{2,1,0:T(1,128)S(1)} %get-tuple-element.331), channel_id=1, source_target_pairs={{0,4},{4,8},{8,12},{1,5},{5,9},{9,13},{2,6},{6,10},{10,14},{3,7},{... | collective-permute-start | bytes 2312 | tf_op jit(solution)/shard_map/ppermute | solution.py:20
  402.8 31.8 %collective-permute-start.85 = (f32[6,1,32]{2,1,0:T(1,128)S(1)}, f32[6,1,32]{2,1,0:T(1,128)S(1)}, u32[]{:S(2)}, u32[]{:S(2)}) collective-permute-start(f32[6,1,32]{2,1,0:T(1,128)S(1)} %get-tuple-element.332), channel_id=1, source_target_pairs={{4,0},{8,4},{12,8},{5,1},{9,5},{13,9},{6,2},{10,6},{14,10},{7,3},{... | collective-permute-start | bytes 2312 | tf_op jit(solution)/shard_map/ppermute | solution.py:23
  423.9 36.4 %collective-permute-start.86 = (f32[6,18,1]{2,1,0:T(8,128)}, f32[6,18,1]{2,1,0:T(8,128)}, u32[]{:S(2)}, u32[]{:S(2)}) collective-permute-start(f32[6,18,1]{2,1,0:T(8,128)} %get-tuple-element.310), channel_id=1, source_target_pairs={{0,1},{1,2},{2,3},{4,5},{5,6},{6,7},{8,9},{9,10},{10,11},{12,13},{... | collective-permute-start | bytes 1304 | tf_op jit(solution)/shard_map/ppermute | solution.py:20
  425.9 34.4 %collective-permute-start.88 = (f32[6,18,1]{2,1,0:T(8,128)}, f32[6,18,1]{2,1,0:T(8,128)}, u32[]{:S(2)}, u32[]{:S(2)}) collective-permute-start(f32[6,18,1]{2,1,0:T(8,128)} %get-tuple-element.309), channel_id=1, source_target_pairs={{1,0},{2,1},{3,2},{5,4},{6,5},{7,6},{9,8},{10,9},{11,10},{13,12},{... | collective-permute-start | bytes 1304 | tf_op jit(solution)/shard_map/ppermute | solution.py:23
  444.6 15.7 %collective-permute-start.87 = (f32[6,18,1]{2,1,0:T(8,128)}, f32[6,18,1]{2,1,0:T(8,128)}, u32[]{:S(2)}, u32[]{:S(2)}) collective-permute-start(f32[6,18,1]{2,1,0:T(8,128)} %get-tuple-element.311), channel_id=1, source_target_pairs={{0,1},{1,2},{2,3},{4,5},{5,6},{6,7},{8,9},{9,10},{10,11},{12,13},{... | collective-permute-start | bytes 1304 | tf_op jit(solution)/shard_map/ppermute | solution.py:20
  448.2 12.0 collective-permute-start.89
  554.2 19.8 %collective-permute-start.112 = (f32[4,10,1]{2,1,0:T(8,128)S(1)}, f32[4,10,1]{2,1,0:T(8,128)S(1)}, u32[]{:S(2)}, u32[]{:S(2)}) collective-permute-start(f32[4,10,1]{2,1,0:T(8,128)S(1)} %get-tuple-element.344), channel_id=1, source_target_pairs={{0,1},{1,2},{2,3},{4,5},{5,6},{6,7},{8,9},{9,10},{10,11},{12,13},{... | collective-permute-start | bytes 488 | tf_op jit(solution)/shard_map/ppermute | solution.py:20
  556.3 17.7 %collective-permute-start.113 = (f32[4,10,1]{2,1,0:T(8,128)S(1)}, f32[4,10,1]{2,1,0:T(8,128)S(1)}, u32[]{:S(2)}, u32[]{:S(2)}) collective-permute-start(f32[4,10,1]{2,1,0:T(8,128)S(1)} %get-tuple-element.343), channel_id=1, source_target_pairs={{1,0},{2,1},{3,2},{5,4},{6,5},{7,6},{9,8},{10,9},{11,10},{13,12},{... | collective-permute-start | bytes 488 | tf_op jit(solution)/shard_map/ppermute | solution.py:23
  (373 other events, 3888.8 us)
where the time goes:
time: 1410 us; the launch traced here: 1390 us
  starting transfers between devices  781 us (55%)
  waiting for transfers between devices  231 us (16%)
  local copies, waits for them, and re-layouts  214 us (15%)
  other arithmetic  151 us (11%)
    ppermute x144, starting transfers between devices, with_halo(): lax.ppermute(lax.slice_in_dim(block, block.shape[dim] - width, None, axis...  561 us
    ppermute x144, starting transfers between devices, with_halo(): lax.ppermute(lax.slice_in_dim(block, 0, width, axis=dim), axis, backward)  220 us
    ppermute x144, waiting for transfers between devices, with_halo(): lax.ppermute(lax.slice_in_dim(block, 0, width, axis=dim), axis, backward)  183 us
    reshape x4, local copies, waits for them, and re-layouts, restrict(): field.reshape(size_x // 2, 2, size_y // 2, 2, size_z // 2, 2)  78.9 us
    ppermute x144, waiting for transfers between devices, with_halo(): lax.ppermute(lax.slice_in_dim(block, block.shape[dim] - width, None, axis...  48.2 us
    add x22, other arithmetic, narrow_sweeps(): values = values + relax_weight * (rhs_field - stencil_sum) / diagonal  43.4 us
    slice x97, local copies, waits for them, and re-layouts, with_halo(): lax.slice_in_dim(block, block.shape[dim] - width, None, axis=dim)  38 us
    reduce_sum x6, other arithmetic, restrict(): field.reshape(size_x // 2, 2, size_y // 2, 2, size_z // 2, 2)  33.6 us
  transfers between devices with their start and end apart: 288, of which 115 were waited for; matrix products, arithmetic and copies ran while one was open for 13% of the time, Pallas kernels for 0%

commit v1 on v0

v1 whole, which is shorter than its diff:
```python
import functools

import jax
import jax.numpy as jnp
from jax import lax
from jax.experimental import pallas as pl
from jax.experimental.pallas import tpu as pltpu
from jax.sharding import PartitionSpec as P

LEVELS = 3
SWEEPS = 4
COARSE = 16
CLASSES = 8
W = 0.85
HX = 5
F32 = jnp.float32
HI = lax.Precision.HIGHEST


def pairs_even(n):
    return [(i, i ^ 1) for i in range(n)]


def pairs_odd(n):
    out = []
    for i in range(1, n - 1, 2):
        out += [(i, i + 1), (i + 1, i)]
    return out


def swap_even(x, axis):
    return lax.ppermute(x, axis, pairs_even(lax.axis_size(axis)))


def swap_odd(x, axis):
    return lax.ppermute(x, axis, pairs_odd(lax.axis_size(axis)))


def swap_xor(x, axis, m):
    return lax.ppermute(x, axis, [(i, i ^ m) for i in range(lax.axis_size(axis))])


def even(axis):
    return lax.rem(lax.axis_index(axis), 2) == 0


def call(body, outs, *args, scratch=(), smem=()):
    specs = [
        pl.BlockSpec(memory_space=pltpu.SMEM if i in smem else pltpu.VMEM) for i in range(len(args))
    ]
    shapes = [jax.ShapeDtypeStruct(s, F32) for s in outs]
    return pl.pallas_call(
        body,
        out_shape=shapes,
        in_specs=specs,
        out_specs=[pl.BlockSpec(memory_space=pltpu.VMEM) for _ in outs],
        scratch_shapes=[pltpu.VMEM(s, F32) for s in scratch],
        name=getattr(body, "__name__", None) or body.func.__name__,
    )(*args)


def lanes(rows=8):
    return lax.broadcasted_iota(jnp.int32, (rows, 128), 1)


def rot(x, shift):
    if isinstance(shift, int):
        shift = shift % 128
        if shift == 0:
            return x
    else:
        shift = lax.rem(shift + 1024, 128)
    return pltpu.roll(x, shift, 1)


def face_start(axis, total, width, want_even):
    hi = even(axis) if want_even else jnp.logical_not(even(axis))
    return jnp.where(hi, total - width, 0)


def start_kernel(nsx, src, guess, cls, table, c_out, y_a, y_b, *x_out):
    nx, ny, _ = src.shape

    def plane(x, _):
        k = cls[x]
        acc = jnp.full(k.shape, table[0], F32)
        for i in range(1, CLASSES):
            acc = jnp.where(k == i, table[i], acc)
        c_out[x] = acc
        return 0

    lax.fori_loop(0, nx, plane, 0)
    for s in range(nsx):
        p5 = face_start("gx", nx, HX, s == 0)
        p4 = face_start("gx", nx, HX - 1, s == 0)
        for f in range(HX):
            x_out[s][f] = c_out[p5 + f]
            x_out[s][HX + f] = guess[p5 + f]
        for f in range(HX - 1):
            x_out[s][2 * HX + f] = src[p4 + f]
    for ref, flag in ((y_a, True), (y_b, False)):
        r = pl.multiple_of(face_start("gy", ny, 8, flag), 8)
        for k, a in enumerate((c_out, guess, src)):
            ref[k * nx : (k + 1) * nx] = a[:, pl.ds(r, 8), :]


def zpack_kernel(na, *refs):
    arrs = refs[:na]
    r_a, r_b, z_a, z_b = refs[na:]
    nx, ny, _ = arrs[0].shape
    ey, ez = even("gy"), even("gz")
    group = lanes() // 8
    for k in range(na):
        for t in range(ny // 8 + 2):
            right = jnp.zeros((8, 128), F32)
            left = jnp.zeros((8, 128), F32)
            for x in range(nx):
                if t == 0:
                    v = jnp.where(ey, r_b[k * nx + x], r_a[k * nx + x])
                elif t == ny // 8 + 1:
                    v = jnp.where(ey, r_a[k * nx + x], r_b[k * nx + x])
                else:
                    v = arrs[k][x, (t - 1) * 8 : t * 8]
                right = jnp.where(group == x, rot(v, 8 * x + 8), right)
                left = jnp.where(group == x, rot(v, 8 * x), left)
            z_a[k, t * 8 : t * 8 + 8] = jnp.where(ez, right, left)
            z_b[k, t * 8 : t * 8 + 8] = jnp.where(ez, left, right)


def face_list(na):
    widths = (HX, HX, HX - 1)
    return [(k, f, widths[k]) for k in range(na) for f in range(widths[k])]


def xframe_kernel(na, nx, nsx, r_a, r_b, z_a, z_b, *x_out):
    ey, ez = even("gy"), even("gz")
    rows = z_a.shape[1]
    lane = lanes()
    planes = face_list(na)
    for s in range(nsx):
        for j, (k, f, w) in enumerate(planes):
            p = face_start("gx", nx, w, s == 0) + f
            va, vb = r_a[k * nx + p], r_b[k * nx + p]
            x_out[s][j * 16 : j * 16 + 8] = jnp.where(ey, vb, va)
            x_out[s][j * 16 + 8 : j * 16 + 16] = jnp.where(ey, va, vb)
        base = len(planes) * 16
        for strip in range(-(-len(planes) // 8)):
            for t in range(rows // 8):
                acc = jnp.zeros((8, 128), F32)
                for j in range(strip * 8, min(strip * 8 + 8, len(planes))):
                    k, f, w = planes[j]
                    g = j % 8
                    p = face_start("gx", nx, w, s == 0) + f
                    za, zb = z_a[k, t * 8 : t * 8 + 8], z_b[k, t * 8 : t * 8 + 8]
                    right = jnp.where(ez, za, zb)
                    left = jnp.where(ez, zb, za)
                    acc = jnp.where(lane // 8 == 2 * g, rot(left, 16 * g - 8 * p), acc)
                    acc = jnp.where(lane // 8 == 2 * g + 1, rot(right, 16 * g + 8 - 8 * p), acc)
                r0 = base + strip * rows + t * 8
                x_out[s][r0 : r0 + 8] = acc


def own_offset(nsx):
    return HX * lax.axis_index("gx") if nsx == 1 else HX


def assemble(nsx, k, planes, m, h, own, r_a, r_b, z_a, z_b, x1, x2):
    nx, ny, _ = own.shape
    off = 1 + own_offset(nsx)
    ey, ez = even("gy"), even("gz")
    lane = lanes()
    kk = planes[0]
    tiles = ny // 8 + 2
    is_left, is_right = lane >= 120, lane < 8

    for x in range(nx):
        va, vb = r_a[kk * nx + x], r_b[kk * nx + x]
        m[off + x, 8:16] = jnp.where(ey, vb, va)
        m[off + x, 16 : 16 + ny] = own[x]
        m[off + x, 16 + ny : 24 + ny] = jnp.where(ey, va, vb)
    for t in range(tiles):
        za, zb = z_a[kk, t * 8 : t * 8 + 8], z_b[kk, t * 8 : t * 8 + 8]
        right = jnp.where(ez, za, zb)
        left = jnp.where(ez, zb, za)
        for x in range(nx):
            v = jnp.where(is_right, rot(right, -8 * x), 0.0)
            h[off + x, 8 + t * 8 : 16 + t * 8] = jnp.where(is_left, rot(left, 120 - 8 * x), v)
    for s in range(nsx):
        hi = even("gx") if s == 0 else jnp.logical_not(even("gx"))
        for j, k_, f, w, base in planes[1]:
            p = off + jnp.where(hi, nx, -w) + f
            m[p, 8:16] = x2[s][j * 16 : j * 16 + 8]
            m[p, 16 : 16 + ny] = x1[s][j]
            m[p, 16 + ny : 24 + ny] = x2[s][j * 16 + 8 : j * 16 + 16]
            for t in range(tiles):
                r0 = base + (j // 8) * tiles * 8 + t * 8
                v = x2[s][r0 : r0 + 8]
                g = j % 8
                a = jnp.where(is_left, rot(v, 120 - 16 * g), 0.0)
                h[p, 8 + t * 8 : 16 + t * 8] = jnp.where(is_right, rot(v, -16 * g - 8), a)


def plane_map(na, k):
    ps = face_list(na)
    base = len(ps) * 16
    return (k, [(j, kk, f, w, base) for j, (kk, f, w) in enumerate(ps) if kk == k])


def zshift(vals, wrap=True):
    lo = lanes(vals[0].shape[0])
    down = [rot(v, 1) for v in vals]
    up = [rot(v, -1) for v in vals]
    if len(vals) == 2:
        first, last = lo == 0, lo == 127
        down = [jnp.where(first, down[1 - t], down[t]) for t in (0, 1)]
        up = [jnp.where(last, up[1 - t], up[t]) for t in (0, 1)]
    return down, up


def neighbours(refs, x, r, n):
    vals = [ref[x, pl.ds(8 + r, n)] for ref in refs]
    down, up = zshift(vals)
    out = []
    for t, ref in enumerate(refs):
        out.append(
            (
                ref[x - 1, pl.ds(8 + r, n)],
                ref[x + 1, pl.ds(8 + r, n)],
                ref[x, pl.ds(7 + r, n)],
                ref[x, pl.ds(9 + r, n)],
                down[t],
                up[t],
            )
        )
    return vals, out


def zero(*refs):
    for ref in refs:

        def one(x, _):
            ref[x] = jnp.zeros(ref.shape[1:], F32)
            return 0

        lax.fori_loop(0, ref.shape[0], one, 0)


def chunks(rows, n=8):
    return range(0, rows, n)


def build_coef(c, b, a, q, d, scale, full_lanes):
    nx, rows = c[0].shape[0] - 2, c[0].shape[1] - 16

    def plane(x, _):
        for r in chunks(rows):
            vals, nb = neighbours(c, x, r, 8)
            lane = lanes()
            for t in range(len(c)):
                six = list(nb[t])
                if full_lanes:
                    six[4] = jnp.where(lane == 0, 0.0, six[4])
                    six[5] = jnp.where(lane == 127, 0.0, six[5])
                total = 6.0 * vals[t] + (((six[0] + six[1]) + (six[2] + six[3])) + (six[4] + six[5]))
                inside = vals[t] > 0.0
                g = jnp.where(inside, W / jnp.where(inside, total, 1.0), 0.0)
                rw = pl.ds(r, 8)
                for j in range(6):
                    face = g * (vals[t] + six[j])
                    if full_lanes and j == 4:
                        face = jnp.where(lane == 0, 0.0, face)
                    if full_lanes and j == 5:
                        face = jnp.where(lane == 127, 0.0, face)
                    a[j][t][x - 1, rw] = face
                q[t][x - 1, rw] = g * ((2.0 / scale) * b[t][x, pl.ds(8 + r, 8)])
                if d is not None:
                    d[t][x - 1, rw] = total * (0.5 * scale / W)
        return 0

    lax.fori_loop(1, nx + 1, plane, 0)


def weighted(a, vals, nb, t, x, rw):
    s = a[0][t][x - 1, rw] * nb[t][0] + a[1][t][x - 1, rw] * nb[t][1]
    u = a[2][t][x - 1, rw] * nb[t][2] + a[3][t][x - 1, rw] * nb[t][3]
    w = a[4][t][x - 1, rw] * nb[t][4] + a[5][t][x - 1, rw] * nb[t][5]
    return (s + u) + w


def sweep(src, dst, a, q, unroll=False):
    nx, rows = src[0].shape[0] - 2, src[0].shape[1] - 16

    def plane(x, _):
        for r in chunks(rows):
            vals, nb = neighbours(src, x, r, 8)
            rw = pl.ds(r, 8)
            for t in range(len(src)):
                dst[t][x, pl.ds(8 + r, 8)] = ((1.0 - W) * vals[t] + q[t][x - 1, rw]) + weighted(
                    a, vals, nb, t, x, rw
                )
        return 0

    if unroll:
        for x in range(1, nx + 1):
            plane(x, 0)
    else:
        lax.fori_loop(1, nx + 1, plane, 0)


def copy_q(dst, q):
    def plane(x, _):
        for t in range(len(q)):
            dst[t][x + 1, 8 : 8 + q[t].shape[1]] = q[t][x]
        return 0

    lax.fori_loop(0, q[0].shape[0], plane, 0)


def residual_rows(v, b, a, d, x, r, n=8):
    vals, nb = neighbours(v, x, r, n)
    rw = pl.ds(r, n)
    return b - d[0][x - 1, rw] * (W * vals[0] - weighted(a, vals, nb, 0, x, rw))


def pick(shift_out, cols, limit):
    i = lax.broadcasted_iota(jnp.int32, (128, 128), 0)
    o = lax.broadcasted_iota(jnp.int32, (128, 128), 1)
    return jnp.where((i // 2 == o - shift_out) & (i < limit), 0.125, 0.0).astype(F32)


def dot(a, b):
    return lax.dot_general(a, b, (((1,), (0,)), ((), ())), precision=HI, preferred_element_type=F32)


def half_rows(ref, r0, n):
    return ref[pl.ds(r0, n // 2, stride=2)] + ref[pl.ds(r0 + 1, n // 2, stride=2)]


def fine_arrays(xp, rows):
    pad, bare = (xp + 2, rows + 16, 128), (xp, rows, 128)
    return [pad] * 8 + [bare] * 16


def split_fine(s):
    two = lambda i: (s[i], s[i + 1])
    return two(0), two(2), two(4), two(6), [two(8 + 2 * j) for j in range(6)], two(20), two(22)


def load_fine(nsx, na, which, refs_own, r, target):
    for k, own, (m, h) in zip(which, refs_own, target):
        assemble(nsx, k, plane_map(na, k), m, h, own, r[0], r[1], r[2], r[3], r[4], r[5])


def fine_down_kernel(nsx, *refs):
    c_own, guess, src, r_a, r_b, z_a, z_b = refs[:7]
    x1, x2 = refs[7 : 7 + nsx], refs[7 + nsx : 7 + 2 * nsx]
    n = 7 + 2 * nsx
    v_out, bc, y_a, y_b = refs[n : n + 4]
    xf = refs[n + 4 : n + 4 + nsx]
    s = refs[n + 4 + nsx :]
    c, b, v, v2, a, q, d = split_fine(s[:24])
    pair = s[24]
    nx, ny, _ = src.shape
    off = 1 + own_offset(nsx)
    zero(*c, *b, *v, *v2)
    load_fine(nsx, 3, (0, 1, 2), (c_own, guess, src), (r_a, r_b, z_a, z_b, x1, x2), (c, v, b))
    build_coef(c, b, a, q, d, 1.0, False)

    def two(_, carry):
        sweep(v, v2, a, q)
        sweep(v2, v, a, q)
        return carry

    lax.fori_loop(0, SWEEPS // 2, two, 0)
    pb, pc = pick(0, 64, 128), pick(64, 64, 128)

    def coarse(i, _):
        x = off + 2 * i
        for r in chunks(ny):
            r0 = residual_rows(v, src[2 * i, pl.ds(r, 8)], a, d, x, 8 + r)
            r1 = residual_rows(v, src[2 * i + 1, pl.ds(r, 8)], a, d, x + 1, 8 + r)
            pair[0, pl.ds(r, 8)] = r0 + r1
            pair[1, pl.ds(r, 8)] = c_own[2 * i, pl.ds(r, 8)] + c_own[2 * i + 1, pl.ds(r, 8)]
            v_out[2 * i, pl.ds(r, 8)] = v[0][x, pl.ds(16 + r, 8)]
            v_out[2 * i + 1, pl.ds(r, 8)] = v[0][x + 1, pl.ds(16 + r, 8)]
        bc[i] = dot(half_rows(pair.at[0], 0, ny), pb) + dot(half_rows(pair.at[1], 0, ny), pc)
        return 0

    lax.fori_loop(0, nx // 2, coarse, 0)
    for k in range(nsx):
        p5 = face_start("gx", nx, HX, k == 0)
        for f in range(HX):
            xf[k][f] = v_out[p5 + f]
    for ref, flag in ((y_a, True), (y_b, False)):
        r = pl.multiple_of(face_start("gy", ny, 8, flag), 8)
        ref[...] = v_out[:, pl.ds(r, 8), :]


def mid_y_kernel(gathered, *refs):
    if gathered:
        full_in, full, y_a, y_b = refs
        full[...] = full_in[...]
    else:
        own, other, full, y_a, y_b = refs
        n = own.shape[0]
        ix = lax.axis_index("gx")
        full[pl.ds(n * ix, n)] = own[...]
        full[pl.ds(n - n * ix, n)] = other[...]
    ny = full.shape[1]
    for ref, flag in ((y_a, True), (y_b, False)):
        r = pl.multiple_of(face_start("gy", ny, 16, flag), 8)
        ref[...] = full[:, pl.ds(r, 16), :]


def mid_rows(full, r_a, r_b, x, t, ny):
    ey = even("gy")
    if t < 2:
        return jnp.where(ey, r_b[x, t * 8 : t * 8 + 8], r_a[x, t * 8 : t * 8 + 8])
    if t >= ny // 8 + 2:
        u = t - ny // 8 - 2
        return jnp.where(ey, r_a[x, u * 8 : u * 8 + 8], r_b[x, u * 8 : u * 8 + 8])
    return full[x, (t - 2) * 8 : (t - 1) * 8]


def mid_z_kernel(full, r_a, r_b, z_a, z_b):
    nx, ny, _ = full.shape
    ez = even("gz")
    slot = lax.rem(lanes(), 64) // 16
    for t in range(ny // 8 + 4):

        def group(s, _):
            right = jnp.zeros((8, 128), F32)
            left = jnp.zeros((8, 128), F32)
            for g in range(4):
                v = mid_rows(full, r_a, r_b, 4 * s + g, t, ny)
                right = jnp.where(slot == g, rot(v, 16 * g - 48), right)
                left = jnp.where(slot == g, rot(v, 16 * g), left)
            z_a[s, t * 8 : t * 8 + 8] = jnp.where(ez, right, left)
            z_b[s, t * 8 : t * 8 + 8] = jnp.where(ez, left, right)
            return 0

        lax.fori_loop(0, nx // 4, group, 0)


def mid_down_kernel(full, r_a, r_b, z_a, z_b, v_out, b_out, c_out, bc, *s):
    c, b, v, v2 = [(s[i],) for i in range(4)]
    a = [(s[4 + j],) for j in range(6)]
    q, d = (s[10],), (s[11],)
    pair = s[12]
    nx, ny, _ = full.shape
    ez = even("gz")
    lane = lanes()
    own, right_l, left_l = lane < 64, (lane >= 64) & (lane < 80), lane >= 112
    zero(c[0], b[0], v[0], v2[0])
    for t in range(ny // 8 + 4):

        def group(s_, _):
            za, zb = z_a[s_, t * 8 : t * 8 + 8], z_b[s_, t * 8 : t * 8 + 8]
            right = jnp.where(ez, za, zb)
            left = jnp.where(ez, zb, za)
            for g in range(4):
                x = 4 * s_ + g
                m = mid_rows(full, r_a, r_b, x, t, ny)
                for ref, o in ((b[0], 0), (c[0], 64)):
                    e = jnp.where(own, rot(m, -o), 0.0)
                    e = jnp.where(right_l, rot(right, 64 - o - 16 * g), e)
                    e = jnp.where(left_l, rot(left, 112 - o - 16 * g), e)
                    ref[x + 1, 8 + t * 8 : 16 + t * 8] = e
            return 0

        lax.fori_loop(0, nx // 4, group, 0)
    build_coef(c, b, a, q, d, 0.25, False)
    copy_q(v, q)
    sweep(v, v2, a, q)
    sweep(v2, v, a, q)
    sweep(v, v2, a, q)
    v = v2
    half = nx // 4
    mats = [(pick(o, 32, 64), pick(o + 32, 32, 64)) for o in (0, 64)]

    def coarse(i, _):
        acc = jnp.zeros((ny // 2, 128), F32)
        for side in (0, 1):
            x = 1 + 2 * (i + side * half)
            for r in chunks(ny):
                rp = pl.ds(24 + r, 8)
                r0 = residual_rows(v, b[0][x, rp], a, d, x, 16 + r)
                r1 = residual_rows(v, b[0][x + 1, rp], a, d, x + 1, 16 + r)
                pair[0, pl.ds(r, 8)] = r0 + r1
                pair[1, pl.ds(r, 8)] = c[0][x, rp] + c[0][x + 1, rp]
            acc = acc + dot(half_rows(pair.at[0], 0, ny), mats[side][0])
            acc = acc + dot(half_rows(pair.at[1], 0, ny), mats[side][1])
        bc[i] = acc
        return 0

    lax.fori_loop(0, half, coarse, 0)
    v_out[...] = v[0][...]
    b_out[...] = b[0][...]
    c_out[...] = c[0][...]


def spread(src, dst, mats, c, x_src, x_dst, r_src, n, r_dst, tmp, sets=False):
    for t, mat in enumerate(mats):
        p = dot(src, mat)
        tmp[t, pl.ds(0, n, stride=2)] = p
        tmp[t, pl.ds(1, n, stride=2)] = p
    for xd in x_dst:
        for t in range(len(mats)):
            for r in chunks(2 * n):
                rr = pl.ds(r_dst + r, 8)
                dst[t][xd, rr] = dst[t][xd, rr] + jnp.where(
                    c[t][xd, rr] > 0.0, tmp[t, pl.ds(r, 8)], 0.0
                )


def select_mat(fn):
    i = lax.broadcasted_iota(jnp.int32, (128, 128), 0)
    o = lax.broadcasted_iota(jnp.int32, (128, 128), 1)
    return jnp.where(i == fn(o), 1.0, 0.0).astype(F32)


def coarse_kernel(gy, gz, blocks, v1_in, b1, c1, v1_out, *s):
    c2, b2, v2, w2 = [(s[i],) for i in range(4)]
    a2 = [(s[4 + j],) for j in range(6)]
    q2, d2 = (s[10],), (s[11],)
    c3, b3, v3, w3 = [(s[12 + i],) for i in range(4)]
    a3 = [(s[16 + j],) for j in range(6)]
    q3 = (s[22],)
    v1, w1 = (s[23],), (s[24],)
    a1 = [(s[25 + j],) for j in range(6)]
    q1 = (s[31],)
    pair, tmp = s[32], s[33]
    iy, iz = lax.axis_index("gy"), lax.axis_index("gz")
    half, yb, _ = blocks.shape[1:]
    lane = lanes(yb)
    zero(c2[0], b2[0], v2[0], w2[0], c3[0], b3[0], v3[0], w3[0], w1[0])
    nx2 = 2 * half
    for jy in range(gy):
        ky = lax.bitwise_xor(jnp.int32(jy), iy)

        def plane(i, _):
            for o in (0, 64):
                for ref, oo in ((b2[0], o), (c2[0], o + 32)):
                    acc = jnp.zeros((yb, 128), F32)
                    for jz in range(gz):
                        kz = lax.bitwise_xor(jnp.int32(jz), iz)
                        idx = ((kz % 2) * (gz // 2) + kz // 2) * gy + ky
                        acc = jnp.where(lane // 32 == jz, rot(blocks[idx, i], 32 * jz - oo), acc)
                    ref[1 + i + (half if o else 0), 8 + yb * jy : 8 + yb * (jy + 1)] = acc
            return 0

        lax.fori_loop(0, half, plane, 0)
    build_coef(c2, b2, a2, q2, d2, 0.0625, True)
    copy_q(v2, q2)
    sweep(v2, w2, a2, q2)
    sweep(w2, v2, a2, q2)
    sweep(v2, w2, a2, q2)
    ny = yb * gy
    mat = pick(0, 64, 128)

    def coarse(i, _):
        x = 1 + 2 * i
        for r in chunks(ny):
            rp = pl.ds(8 + r, 8)
            r0 = residual_rows(w2, b2[0][x, rp], a2, d2, x, r)
            r1 = residual_rows(w2, b2[0][x + 1, rp], a2, d2, x + 1, r)
            pair[0, pl.ds(r, 8)] = r0 + r1
            pair[1, pl.ds(r, 8)] = c2[0][x, rp] + c2[0][x + 1, rp]
        b3[0][1 + i, 8 : 8 + ny // 2] = dot(half_rows(pair.at[0], 0, ny), mat)
        c3[0][1 + i, 8 : 8 + ny // 2] = dot(half_rows(pair.at[1], 0, ny), mat)
        return 0

    lax.fori_loop(0, nx2 // 2, coarse, 0)
    small = nx2 <= 8
    build_coef(c3, b3, a3, q3, None, 0.015625, False)
    copy_q(v3, q3)
    sweep(v3, w3, a3, q3, small)

    def two(_, carry):
        sweep(w3, v3, a3, q3, small)
        sweep(v3, w3, a3, q3, small)
        return carry

    lax.fori_loop(0, (COARSE - 2) // 2, two, 0)
    up = select_mat(lambda o: o // 2)

    def up2(i, _):
        spread(w3[0][1 + i, 8 : 8 + ny // 2], w2, [up], c2, None, (1 + 2 * i, 2 + 2 * i), None, ny // 2, 8, tmp)
        return 0

    lax.fori_loop(0, nx2 // 2, up2, 0)

    def two2(_, carry):
        sweep(w2, v2, a2, q2)
        sweep(v2, w2, a2, q2)
        return carry

    lax.fori_loop(0, SWEEPS // 2, two2, 0)
    build_coef((c1,), (b1,), a1, q1, None, 0.25, False)
    v1[0][...] = v1_in[...]
    rows1 = v1[0].shape[1] - 16
    up = select_mat(lambda o: jnp.where(o < 80, o // 2, jnp.where(o >= 112, (o + 128) // 2, -1)))
    start = pl.multiple_of(yb * iy, 8)

    def up1(i, _):
        par = rot(w2[0][1 + i, pl.ds(start, rows1 // 2)], -32 * iz)
        spread(par, v1, [up], (c1,), None, (1 + 2 * i, 2 + 2 * i), None, rows1 // 2, 8, tmp)
        return 0

    lax.fori_loop(0, nx2, up1, 0)

    def two1(_, carry):
        sweep(v1, w1, a1, q1)
        sweep(w1, v1, a1, q1)
        return carry

    lax.fori_loop(0, SWEEPS // 2, two1, 0)
    v1_out[...] = v1[0][...]


def fine_up_kernel(nsx, *refs):
    c_own, v_own, src, r_a, r_b, z_a, z_b = refs[:7]
    x1, x2 = refs[7 : 7 + nsx], refs[7 + nsx : 7 + 2 * nsx]
    n = 7 + 2 * nsx
    vr_a, vr_b, vz_a, vz_b = refs[n : n + 4]
    vx1, vx2 = refs[n + 4 : n + 4 + nsx], refs[n + 4 + nsx : n + 4 + 2 * nsx]
    n = n + 4 + 2 * nsx
    v1 = refs[n]
    sol, res = refs[n + 1 : n + 3]
    s = refs[n + 3 :]
    c, b, v, v2, a, q, d = split_fine(s[:24])
    tmp = s[24]
    nx, ny, _ = src.shape
    off = 1 + own_offset(nsx)
    zero(*c, *b, *v, *v2)
    load_fine(nsx, 3, (0, 2), (c_own, src), (r_a, r_b, z_a, z_b, x1, x2), (c, b))
    load_fine(nsx, 1, (0,), (v_own,), (vr_a, vr_b, vz_a, vz_b, vx1, vx2), (v,))
    build_coef(c, b, a, q, d, 1.0, False)
    up_m = select_mat(lambda o: o // 2)
    up_h = select_mat(
        lambda o: jnp.where(o < 8, 64 + o // 2, jnp.where(o >= 120, (o + 128) // 2, -1))
    )
    nc = v1.shape[0] - 2
    ix = lax.axis_index("gx")
    xp = v[0].shape[0] - 2
    rows = ny + 16

    def up(p, _):
        x = jnp.clip(lax.shift_right_arithmetic(nx * ix + p - off, 1), 0, nc - 1)
        par = v1[1 + x, 20 : 20 + rows // 2]
        spread(par, v, [up_m, up_h], c, None, (p,), None, rows // 2, 8, tmp)
        return 0

    lax.fori_loop(1, xp + 1, up, 0)

    def two(_, carry):
        sweep(v, v2, a, q)
        sweep(v2, v, a, q)
        return carry

    lax.fori_loop(0, SWEEPS // 2, two, 0)

    def out(x, _):
        for r in chunks(ny):
            res[x, pl.ds(r, 8)] = residual_rows(v, src[x, pl.ds(r, 8)], a, d, off + x, 8 + r)
            sol[x, pl.ds(r, 8)] = v[0][off + x, pl.ds(16 + r, 8)]
        return 0

    lax.fori_loop(0, nx, out, 0)


def named(fn, *args):
    out = functools.partial(fn, *args)
    out.__name__ = fn.__name__
    return out


def exchange_rest(na, arrs, y_a, y_b, nsx):
    nx, ny, _ = arrs[0].shape
    rows = ny + 16
    r_a, r_b = swap_even(y_a, "gy"), swap_odd(y_b, "gy")
    z_a, z_b = call(named(zpack_kernel, na), [(na, rows, 128)] * 2, *arrs, r_a, r_b)
    z_a, z_b = swap_even(z_a, "gz"), swap_odd(z_b, "gz")
    count = len(face_list(na))
    size = count * 16 + -(-count // 8) * rows
    xs = call(named(xframe_kernel, na, nx, nsx), [(size, 128)] * nsx, r_a, r_b, z_a, z_b)
    x2 = swap_x(xs)
    return (r_a, r_b, z_a, z_b), x2


def swap_x(xs):
    out = [swap_even(xs[0], "gx")]
    if len(xs) > 1:
        out.append(swap_odd(xs[1], "gx"))
    return out


def body(source, first_guess, cell_classes, class_table):
    nx, ny, _ = source.shape
    gx, gy, gz = (lax.axis_size(n) for n in ("gx", "gy", "gz"))
    nsx = 1 if gx == 2 else 2
    xp = nx + nsx * HX
    rows = ny + 16
    full = (nx, ny, 128)

    out = call(
        named(start_kernel, nsx),
        [full, (3 * nx, 8, 128), (3 * nx, 8, 128)] + [(3 * HX - 1, ny, 128)] * nsx,
        source, first_guess, cell_classes, class_table,
        smem=(3,),
    )
    c_own, y_a, y_b, xs = out[0], out[1], out[2], out[3:]
    x1 = swap_x(xs)
    rec, x2 = exchange_rest(3, (c_own, first_guess, source), y_a, y_b, nsx)
    out = call(
        named(fine_down_kernel, nsx),
        [full, (nx // 2, ny // 2, 128), (nx, 8, 128), (nx, 8, 128)] + [(HX, ny, 128)] * nsx,
        c_own, first_guess, source, *rec, *x1, *x2,
        scratch=fine_arrays(xp, rows) + [(2, ny, 128)],
    )
    v0, bc1, vy_a, vy_b, vxs = out[0], out[1], out[2], out[3], out[4:]

    n1 = gx * nx // 2
    ny1 = ny // 2
    outs = [(n1, ny1, 128), (n1, 16, 128), (n1, 16, 128)]
    if gx == 2:
        f1, y_a, y_b = call(named(mid_y_kernel, False), outs, bc1, swap_even(bc1, "gx"))
    else:
        f1, y_a, y_b = call(
            named(mid_y_kernel, True), outs, lax.all_gather(bc1, "gx", axis=0, tiled=True)
        )
    r_a, r_b = swap_even(y_a, "gy"), swap_odd(y_b, "gy")
    rows1 = ny1 + 32
    z_a, z_b = call(mid_z_kernel, [(n1 // 4, rows1, 128)] * 2, f1, r_a, r_b)
    z_a, z_b = swap_even(z_a, "gz"), swap_odd(z_b, "gz")
    pad1, bare1 = (n1 + 2, rows1 + 16, 128), (n1, rows1, 128)
    v1, b1, c1, bc2 = call(
        mid_down_kernel,
        [pad1] * 3 + [(n1 // 4, ny1 // 2, 128)],
        f1, r_a, r_b, z_a, z_b,
        scratch=[pad1] * 4 + [bare1] * 8 + [(2, ny1, 128)],
    )

    got = jnp.stack([bc2] + [swap_xor(bc2, "gy", m) for m in range(1, gy)])
    bit = gz // 2
    while bit:
        got = jnp.concatenate([got, swap_xor(got, "gz", bit)])
        bit //= 2

    vx1 = swap_x(vxs)
    vrec, vx2 = exchange_rest(1, (v0,), vy_a, vy_b, nsx)

    n2, ny2 = n1 // 2, gy * ny1 // 2
    n3, ny3 = n2 // 2, ny2 // 2
    pad2, bare2 = (n2 + 2, ny2 + 16, 128), (n2, ny2, 128)
    pad3, bare3 = (n3 + 2, ny3 + 16, 128), (n3, ny3, 128)
    (v1,) = call(
        named(coarse_kernel, gy, gz),
        [pad1],
        got, v1, b1, c1,
        scratch=[pad2] * 4 + [bare2] * 8 + [pad3] * 4 + [bare3] * 7 + [pad1] * 2 + [bare1] * 7
        + [(2, ny2, 128), (1, max(rows1, ny2), 128)],
    )
    sol, res = call(
        named(fine_up_kernel, nsx),
        [full, full],
        c_own, v0, source, *rec, *x1, *x2, *vrec, *vx1, *vx2, v1,
        scratch=fine_arrays(xp, rows) + [(2, rows, 128)],
    )
    return sol, res


def solution(mesh):
    spec = P("gx", "gy", "gz")
    return jax.shard_map(
        body,
        mesh=mesh,
        in_specs=(spec, spec, spec, P()),
        out_specs=(spec, spec),
        check_vma=False,
    )
```

time: 1410 us -> 181 us (0.13); the launches traced: 1390 us -> 178 us
  starting transfers between devices: 781 us -> 40 us
  local copies, waits for them, and re-layouts: 214 us -> 8.32 us
  waiting for transfers between devices: 231 us -> 26.4 us
  other arithmetic: 151 us -> 0.01 us
  Pallas kernels: 0 us -> 103 us
    ppermute x288 -> x22, starting transfers between devices: 781 us -> 40 us  [the longest x11 16.3 us: swap_even(): return lax.ppermute(x, axis, pairs_even(lax.axis_size(axis)))]
    ppermute x288 -> x22, waiting for transfers between devices: 231 us -> 26.4 us  [the longest x11 11.8 us: swap_even(): return lax.ppermute(x, axis, pairs_even(lax.axis_size(axis)))]
    reshape x7 -> x0, local copies, waits for them, and re-layouts: 111 us -> none  [the longest x4 78.9 us: restrict(): field.reshape(size_x // 2, 2, size_y // 2, 2, size_z // 2, 2)]
    pallas_call x0 -> x11, Pallas kernels: none -> 103 us  [call(): pl.pallas_call(body, out_shape=shapes, in_specs=specs, out_specs=[pl.Bloc...]
    add x44 -> x0, other arithmetic: 79.3 us -> none  [the longest x22 43.4 us: narrow_sweeps(): values = values + relax_weight * (rhs_field - stencil_sum) / diagonal]
    slice x118 -> x0, local copies, waits for them, and re-layouts: 51.9 us -> none  [the longest x97 38 us: with_halo(): lax.slice_in_dim(block, block.shape[dim] - width, None, axis=dim)]
    reduce_sum x6 -> x0, other arithmetic: 33.6 us -> none  [restrict(): field.reshape(size_x // 2, 2, size_y // 2, 2, size_z // 2, 2)]
    ppermute x22 -> x0, local copies, waits for them, and re-layouts: 22.9 us -> none  [the longest x11 12.8 us: with_halo(): lax.ppermute(lax.slice_in_dim(block, 0, width, axis=dim), axis, backward)]
  transfers between devices with their start and end apart: 288 -> 22, of which waited for: 115 -> 11; matrix products, arithmetic and copies ran while one was open for 13% -> 0% of each run, Pallas kernels for 0% -> 19%
where the time goes in v1:
time: 181 us; the launch traced here: 178 us
  Pallas kernels  103 us (57%)
  starting transfers between devices  40 us (22%)
  waiting for transfers between devices  26.4 us (15%)
  local copies, waits for them, and re-layouts  8.32 us (5%)
    pallas_call x11, Pallas kernels, call(): pl.pallas_call(body, out_shape=shapes, in_specs=specs, out_specs=[pl.Bloc...  103 us
    ppermute x11, starting transfers between devices, swap_even(): return lax.ppermute(x, axis, pairs_even(lax.axis_size(axis)))  16.3 us
    ppermute x6, starting transfers between devices, swap_odd(): return lax.ppermute(x, axis, pairs_odd(lax.axis_size(axis)))  14.9 us
    ppermute x11, waiting for transfers between devices, swap_even(): return lax.ppermute(x, axis, pairs_even(lax.axis_size(axis)))  11.8 us
    ppermute x5, starting transfers between devices, swap_xor(): lax.ppermute(x, axis, [(i, i ^ m) for i in range(lax.axis_size(axis))])  8.76 us
    unnamed x48, local copies, waits for them, and re-layouts  8.28 us
    ppermute x6, waiting for transfers between devices, swap_odd(): return lax.ppermute(x, axis, pairs_odd(lax.axis_size(axis)))  7.98 us
    ppermute x5, waiting for transfers between devices, swap_xor(): lax.ppermute(x, axis, [(i, i ^ m) for i in range(lax.axis_size(axis))])  6.62 us
  transfers between devices with their start and end apart: 22, of which 11 were waited for; matrix products, arithmetic and copies ran while one was open for 0% of the time, Pallas kernels for 19%

profile of v1, /device:TPU:1, one launch (start us, length us, event | category | flops | bytes accessed | tf_op | source)
XLA Modules:
  0.0 178.4 jit_solution(17343809222942892235)
XLA Ops:
  0.6 2.8 %start_kernel.1 = (f32[16,64,128]{2,1,0:T(8,128)}, f32[48,8,128]{2,1,0:T(8,128)}, f32[48,8,128]{2,1,0:T(8,128)}, f32[14,64,128]{2,1,0:T(8,128)}) custom-call(f32[16,64,128]{2,1,0:T(8,128)} %refs_2_.5, f32[16,64,128]{2,1,0:T(8,128)} %refs_1_.3, s32[16,64,128]{2,1,0:T(8,128)} %cls.1, f32[8]{0:T(128)} %table.1), custom_call_target="tpu_custom_call" | custom-call | tf_op jit(solution)/shard_map/start_kernel/pallas_call | solution.py:52
  3.4 2.1 %collective-permute-start = (f32[48,8,128]{2,1,0:T(8,128)}, f32[48,8,128]{2,1,0:T(8,128)S(1)}, u32[]{:S(2)}, u32[]{:S(2)}) collective-permute-start(f32[48,8,128]{2,1,0:T(8,128)} %get-tuple-element.25), channel_id=1, source_target_pairs={{0,4},{4,0},{8,12},{12,8},{1,5},{5,1},{9,13},{13,9},{2,6},{6,2},{1... | collective-permute-start | bytes 589832 | tf_op jit(solution)/shard_map/ppermute | solution.py:32
  6.2 1.3 collective-permute-start.4
  7.5 2.9 %collective-permute-done.refs_3_.r_a = f32[48,8,128]{2,1,0:T(8,128)S(1)} collective-permute-done((f32[48,8,128]{2,1,0:T(8,128)}, f32[48,8,128]{2,1,0:T(8,128)S(1)}, u32[]{:S(2)}, u32[]{:S(2)}) %collective-permute-start) | collective-permute-done | bytes 196640 | tf_op jit(solution)/shard_map/ppermute | solution.py:32
  11.1 3.2 %zpack_kernel.2 = (f32[3,80,128]{2,1,0:T(8,128)}, f32[3,80,128]{2,1,0:T(8,128)}) custom-call(f32[16,64,128]{2,1,0:T(8,128)} %get-tuple-element.24.refs_0_, f32[16,64,128]{2,1,0:T(8,128)} %refs_1_.3, f32[16,64,128]{2,1,0:T(8,128)} %refs_2_.5, f32[48,8,128]{2,1,0:T(8,128)} %copy-done, f32[48,8,128]{2,1,0:T(8,128)} %copy-done.1), custom_call_target="tpu_custom_call" | custom-call | tf_op jit(solution)/shard_map/zpack_kernel/pallas_call | solution.py:52
  15.5 3.2 %collective-permute-start.3 = (f32[3,80,128]{2,1,0:T(8,128)}, f32[3,80,128]{2,1,0:T(8,128)S(1)}, u32[]{:S(2)}, u32[]{:S(2)}) collective-permute-start(f32[3,80,128]{2,1,0:T(8,128)} %get-tuple-element.28), channel_id=1, source_target_pairs={{1,2},{2,1},{5,6},{6,5},{9,10},{10,9},{13,14},{14,13},{17,18},{18,... | collective-permute-start | bytes 368648 | tf_op jit(solution)/shard_map/ppermute | solution.py:36
  18.7 3.2 %collective-permute-done.3.z_b.refs_6_ = f32[3,80,128]{2,1,0:T(8,128)S(1)} collective-permute-done((f32[3,80,128]{2,1,0:T(8,128)}, f32[3,80,128]{2,1,0:T(8,128)S(1)}, u32[]{:S(2)}, u32[]{:S(2)}) %collective-permute-start.3) | collective-permute-done | bytes 122912 | tf_op jit(solution)/shard_map/ppermute | solution.py:36
  22.6 2.2 %xframe_kernel.2 = f32[384,128]{1,0:T(8,128)} custom-call(f32[48,8,128]{2,1,0:T(8,128)} %copy-done, f32[48,8,128]{2,1,0:T(8,128)} %copy-done.1, f32[3,80,128]{2,1,0:T(8,128)} %copy-done.3, f32[3,80,128]{2,1,0:T(8,128)} %copy-done.4), custom_call_target="tpu_custom_call" | custom-call | tf_op jit(solution)/shard_map/xframe_kernel/pallas_call | solution.py:52
  24.8 1.4 collective-permute-start.5
  26.2 3.3 %collective-permute-done.5.refs_8_ = f32[384,128]{1,0:T(8,128)S(1)} collective-permute-done((f32[384,128]{1,0:T(8,128)}, f32[384,128]{1,0:T(8,128)S(1)}, u32[]{:S(2)}, u32[]{:S(2)}) %collective-permute-start.5) | collective-permute-done | bytes 196640 | tf_op jit(solution)/shard_map/ppermute | solution.py:32
  30.2 21.3 %fine_down_kernel.1 = (f32[16,64,128]{2,1,0:T(8,128)}, f32[8,32,128]{2,1,0:T(8,128)}, f32[16,8,128]{2,1,0:T(8,128)}, f32[16,8,128]{2,1,0:T(8,128)}, f32[5,64,128]{2,1,0:T(8,128)}) custom-call(f32[16,64,128]{2,1,0:T(8,128)} %get-tuple-element.24.refs_0_, f32[16,64,128]{2,1,0:T(8,128)} %refs_1_.3, f32[16,64,128]{2,1,0:T(8,128)} %refs_2_.5, ...), custom_call_target="tpu_custom_call" | custom-call | tf_op jit(solution)/shard_map/fine_down_kernel/pallas_call | solution.py:52
  51.5 1.4 collective-permute-start.12
  52.9 2.6 %collective-permute-done.12.refs_1_ = f32[8,32,128]{2,1,0:T(8,128)S(1)} collective-permute-done((f32[8,32,128]{2,1,0:T(8,128)}, f32[8,32,128]{2,1,0:T(8,128)S(1)}, u32[]{:S(2)}, u32[]{:S(2)}) %collective-permute-start.12) | collective-permute-done | bytes 131104 | tf_op jit(solution)/shard_map/ppermute | solution.py:32
  56.2 1.8 mid_y_kernel.1
  58.0 4.4 %collective-permute-start.13 = (f32[16,16,128]{2,1,0:T(8,128)}, f32[16,16,128]{2,1,0:T(8,128)S(1)}, u32[]{:S(2)}, u32[]{:S(2)}) collective-permute-start(f32[16,16,128]{2,1,0:T(8,128)} %get-tuple-element.38), channel_id=1, source_target_pairs={{0,4},{4,0},{8,12},{12,8},{1,5},{5,1},{9,13},{13,9},{2,6},{6,2},{1... | collective-permute-start | bytes 393224 | tf_op jit(solution)/shard_map/ppermute | solution.py:32
  63.1 1.9 %collective-permute-done.13.r_a = f32[16,16,128]{2,1,0:T(8,128)S(1)} collective-permute-done((f32[16,16,128]{2,1,0:T(8,128)}, f32[16,16,128]{2,1,0:T(8,128)S(1)}, u32[]{:S(2)}, u32[]{:S(2)}) %collective-permute-start.13) | collective-permute-done | bytes 131104 | tf_op jit(solution)/shard_map/ppermute | solution.py:32
  65.6 4.2 %mid_z_kernel.1 = (f32[4,64,128]{2,1,0:T(8,128)}, f32[4,64,128]{2,1,0:T(8,128)}) custom-call(f32[16,32,128]{2,1,0:T(8,128)} %get-tuple-element.37.full, f32[16,16,128]{2,1,0:T(8,128)} %copy-done.9, f32[16,16,128]{2,1,0:T(8,128)} %copy-done.10), custom_call_target="tpu_custom_call" | custom-call | tf_op jit(solution)/shard_map/mid_z_kernel/pallas_call | solution.py:52
  69.8 6.2 %collective-permute-start.16 = (f32[4,64,128]{2,1,0:T(8,128)}, f32[4,64,128]{2,1,0:T(8,128)S(1)}, u32[]{:S(2)}, u32[]{:S(2)}) collective-permute-start(f32[4,64,128]{2,1,0:T(8,128)} %get-tuple-element.41), channel_id=1, source_target_pairs={{1,2},{2,1},{5,6},{6,5},{9,10},{10,9},{13,14},{14,13},{17,18},{18,... | collective-permute-start | bytes 393224 | tf_op jit(solution)/shard_map/ppermute | solution.py:36
  76.0 2.8 %collective-permute-done.16.z_b = f32[4,64,128]{2,1,0:T(8,128)S(1)} collective-permute-done((f32[4,64,128]{2,1,0:T(8,128)}, f32[4,64,128]{2,1,0:T(8,128)S(1)}, u32[]{:S(2)}, u32[]{:S(2)}) %collective-permute-start.16) | collective-permute-done | bytes 131104 | tf_op jit(solution)/shard_map/ppermute | solution.py:36
  79.5 13.3 %mid_down_kernel.1 = (f32[18,80,128]{2,1,0:T(8,128)}, f32[18,80,128]{2,1,0:T(8,128)}, f32[18,80,128]{2,1,0:T(8,128)}, f32[4,16,128]{2,1,0:T(8,128)}) custom-call(f32[16,32,128]{2,1,0:T(8,128)} %get-tuple-element.37.full, f32[16,16,128]{2,1,0:T(8,128)} %copy-done.9, f32[16,16,128]{2,1,0:T(8,128)} %copy-done.10, f32[4,64,128]{2,1,0:T(8,128)} %copy-done.15, ...), custom_call_target="tpu_custom_call" | custom-call | tf_op jit(solution)/shard_map/mid_down_kernel/pallas_call | solution.py:52
  92.8 3.6 %collective-permute-start.17 = (f32[4,16,128]{2,1,0:T(8,128)}, f32[4,16,128]{2,1,0:T(8,128)S(1)}, u32[]{:S(2)}, u32[]{:S(2)}) collective-permute-start(f32[4,16,128]{2,1,0:T(8,128)} %get-tuple-element.42), channel_id=1, source_target_pairs={{0,4},{4,0},{8,12},{12,8},{1,5},{5,1},{9,13},{13,9},{2,6},{6,2},{1... | collective-permute-start | bytes 98312 | tf_op jit(solution)/shard_map/ppermute | solution.py:40
  100.3 2.1 %collective-permute-done.19 = f32[4,16,128]{2,1,0:T(8,128)S(1)} collective-permute-done((f32[4,16,128]{2,1,0:T(8,128)}, f32[4,16,128]{2,1,0:T(8,128)S(1)}, u32[]{:S(2)}, u32[]{:S(2)}) %collective-permute-start.19) | collective-permute-done | bytes 32800 | tf_op jit(solution)/shard_map/ppermute | solution.py:40
  102.5 3.8 %collective-permute-done.20 = f32[4,4,16,128]{3,2,1,0:T(8,128)S(1)} collective-permute-done((f32[4,4,16,128]{3,2,1,0:T(8,128)S(1)}, f32[4,4,16,128]{3,2,1,0:T(8,128)S(1)}, u32[]{:S(2)}, u32[]{:S(2)}) %collective-permute-start.20) | collective-permute-done | bytes 131104 | tf_op jit(solution)/shard_map/ppermute | solution.py:40
  106.3 2.8 %collective-permute-start.21 = (f32[8,4,16,128]{3,2,1,0:T(8,128)S(1)}, f32[8,4,16,128]{3,2,1,0:T(8,128)S(1)}, u32[]{:S(2)}, u32[]{:S(2)}) collective-permute-start(f32[8,4,16,128]{3,2,1,0:T(8,128)S(1)} %get-tuple-element.46), channel_id=1, source_target_pairs={{0,1},{1,0},{2,3},{3,2},{4,5},{5,4},{6,7},{7,6},{8,9},{9,8},{10,11... | collective-permute-start | bytes 786440 | tf_op jit(solution)/shard_map/ppermute | solution.py:40
  109.8 1.3 collective-permute-start.10
  112.8 2.1 %zpack_kernel.3 = (f32[1,80,128]{2,1,0:T(8,128)}, f32[1,80,128]{2,1,0:T(8,128)}) custom-call(f32[16,64,128]{2,1,0:T(8,128)} %get-tuple-element.30.refs_0_.refs_1_, f32[16,8,128]{2,1,0:T(8,128)} %copy-done.7, f32[16,8,128]{2,1,0:T(8,128)} %copy-done.8), custom_call_target="tpu_custom_call" | custom-call | tf_op jit(solution)/shard_map/zpack_kernel/pallas_call | solution.py:52
  115.0 1.9 %collective-permute-start.8 = (f32[1,80,128]{2,1,0:T(8,128)}, f32[1,80,128]{2,1,0:T(8,128)S(1)}, u32[]{:S(2)}, u32[]{:S(2)}) collective-permute-start(f32[1,80,128]{2,1,0:T(8,128)} %get-tuple-element.33), channel_id=1, source_target_pairs={{0,1},{1,0},{2,3},{3,2},{4,5},{5,4},{6,7},{7,6},{8,9},{9,8},{10,11... | collective-permute-start | bytes 122888 | tf_op jit(solution)/shard_map/ppermute | solution.py:32
  116.8 3.5 %collective-permute-start.9 = (f32[1,80,128]{2,1,0:T(8,128)}, f32[1,80,128]{2,1,0:T(8,128)S(1)}, u32[]{:S(2)}, u32[]{:S(2)}) collective-permute-start(f32[1,80,128]{2,1,0:T(8,128)} %get-tuple-element.34), channel_id=1, source_target_pairs={{1,2},{2,1},{5,6},{6,5},{9,10},{10,9},{13,14},{14,13},{17,18},{18,... | collective-permute-start | bytes 122888 | tf_op jit(solution)/shard_map/ppermute | solution.py:36
  120.4 2.0 %collective-permute-done.9.z_b.refs_12_ = f32[1,80,128]{2,1,0:T(8,128)S(1)} collective-permute-done((f32[1,80,128]{2,1,0:T(8,128)}, f32[1,80,128]{2,1,0:T(8,128)S(1)}, u32[]{:S(2)}, u32[]{:S(2)}) %collective-permute-start.9) | collective-permute-done | bytes 40992 | tf_op jit(solution)/shard_map/ppermute | solution.py:36
  123.0 1.7 xframe_kernel.3
  126.8 24.1 %coarse_kernel.1.refs_15_ = f32[18,80,128]{2,1,0:T(8,128)} custom-call(f32[16,4,16,128]{3,2,1,0:T(8,128)} %copy-done.6, f32[18,80,128]{2,1,0:T(8,128)} %get-tuple-element.43.v1_in, f32[18,80,128]{2,1,0:T(8,128)} %get-tuple-element.44.b1, f32[18,80,128]{2,1,0:T(8,128)} %get-tuple-element.45.c1), custom_call_target="tpu_custom_call" | custom-call | tf_op jit(solution)/shard_map/coarse_kernel/pallas_call | solution.py:52
  152.2 26.3 %fine_up_kernel.1 = (f32[16,64,128]{2,1,0:T(8,128)}, f32[16,64,128]{2,1,0:T(8,128)}) custom-call(f32[16,64,128]{2,1,0:T(8,128)} %get-tuple-element.24.refs_0_, f32[16,64,128]{2,1,0:T(8,128)} %get-tuple-element.30.refs_0_.refs_1_, f32[16,64,128]{2,1,0:T(8,128)} %refs_2_.5, f32[48,8,128]{2,1,0:T(8,128)} %copy-done, f32[48,8,128]{2,1,0:T(8,128)} %copy-done.1, ...), custom_call_target="tpu_custom_call" | custom-call | tf_op jit(solution)/shard_map/fine_up_kernel/pallas_call | solution.py:52
  (74 shorter events, 17.1 us)
Async XLA Ops:
  3.4 6.9 %collective-permute-start = (f32[48,8,128]{2,1,0:T(8,128)}, f32[48,8,128]{2,1,0:T(8,128)S(1)}, u32[]{:S(2)}, u32[]{:S(2)}) collective-permute-start(f32[48,8,128]{2,1,0:T(8,128)} %get-tuple-element.25), channel_id=1, source_target_pairs={{0,4},{4,0},{8,12},{12,8},{1,5},{5,1},{9,13},{13,9},{2,6},{6,2},{1... | collective-permute-start | bytes 589832 | tf_op jit(solution)/shard_map/ppermute | solution.py:32
  5.5 4.8 %collective-permute-start.1 = (f32[48,8,128]{2,1,0:T(8,128)}, f32[48,8,128]{2,1,0:T(8,128)S(1)}, u32[]{:S(2)}, u32[]{:S(2)}) collective-permute-start(f32[48,8,128]{2,1,0:T(8,128)} %get-tuple-element.26), channel_id=1, source_target_pairs={{4,8},{8,4},{5,9},{9,5},{6,10},{10,6},{7,11},{11,7},{20,24},{24,20... | collective-permute-start | bytes 589832 | tf_op jit(solution)/shard_map/ppermute | solution.py:36
  6.2 20.0 %collective-permute-start.4 = (f32[14,64,128]{2,1,0:T(8,128)}, f32[14,64,128]{2,1,0:T(8,128)S(1)}, u32[]{:S(2)}, u32[]{:S(2)}) collective-permute-start(f32[14,64,128]{2,1,0:T(8,128)} %get-tuple-element.29), channel_id=1, source_target_pairs={{0,16},{16,0},{1,17},{17,1},{2,18},{18,2},{3,19},{19,3},{4,20},{20... | collective-permute-start | bytes 1376264 | tf_op jit(solution)/shard_map/ppermute | solution.py:32
  10.3 0.8 copy-start.1
  14.3 4.5 %collective-permute-start.2 = (f32[3,80,128]{2,1,0:T(8,128)}, f32[3,80,128]{2,1,0:T(8,128)S(1)}, u32[]{:S(2)}, u32[]{:S(2)}) collective-permute-start(f32[3,80,128]{2,1,0:T(8,128)} %get-tuple-element.27), channel_id=1, source_target_pairs={{0,1},{1,0},{2,3},{3,2},{4,5},{5,4},{6,7},{7,6},{8,9},{9,8},{10,11... | collective-permute-start | bytes 368648 | tf_op jit(solution)/shard_map/ppermute | solution.py:32
  15.5 6.4 %collective-permute-start.3 = (f32[3,80,128]{2,1,0:T(8,128)}, f32[3,80,128]{2,1,0:T(8,128)S(1)}, u32[]{:S(2)}, u32[]{:S(2)}) collective-permute-start(f32[3,80,128]{2,1,0:T(8,128)} %get-tuple-element.28), channel_id=1, source_target_pairs={{1,2},{2,1},{5,6},{6,5},{9,10},{10,9},{13,14},{14,13},{17,18},{18,... | collective-permute-start | bytes 368648 | tf_op jit(solution)/shard_map/ppermute | solution.py:36
  18.7 3.2 %copy-start.3 = (f32[3,80,128]{2,1,0:T(8,128)}, f32[3,80,128]{2,1,0:T(8,128)S(1)}, u32[]{:S(2)}) copy-start(f32[3,80,128]{2,1,0:T(8,128)S(1)} %collective-permute-done.2.z_a.refs_5_) | copy-start | bytes 368644
  24.8 4.7 %collective-permute-start.5 = (f32[384,128]{1,0:T(8,128)}, f32[384,128]{1,0:T(8,128)S(1)}, u32[]{:S(2)}, u32[]{:S(2)}) collective-permute-start(f32[384,128]{1,0:T(8,128)} %xframe_kernel.2), channel_id=1, source_target_pairs={{0,16},{16,0},{1,17},{17,1},{2,18},{18,2},{3,19},{19,3},{4,20},{20... | collective-permute-start | bytes 589832 | tf_op jit(solution)/shard_map/ppermute | solution.py:32
  26.2 3.4 %copy-start.2 = (f32[14,64,128]{2,1,0:T(8,128)}, f32[14,64,128]{2,1,0:T(8,128)S(1)}, u32[]{:S(2)}) copy-start(f32[14,64,128]{2,1,0:T(8,128)S(1)} %collective-permute-done.4.refs_7_) | copy-start | bytes 1376260
  51.5 4.0 %collective-permute-start.12 = (f32[8,32,128]{2,1,0:T(8,128)}, f32[8,32,128]{2,1,0:T(8,128)S(1)}, u32[]{:S(2)}, u32[]{:S(2)}) collective-permute-start(f32[8,32,128]{2,1,0:T(8,128)} %get-tuple-element.36.refs_0_), channel_id=1, source_target_pairs={{0,16},{16,0},{1,17},{17,1},{2,18},{18,2},{3,19},{19,3},{4,20},{20... | collective-permute-start | bytes 393224 | tf_op jit(solution)/shard_map/ppermute | solution.py:32
  58.0 7.0 %collective-permute-start.13 = (f32[16,16,128]{2,1,0:T(8,128)}, f32[16,16,128]{2,1,0:T(8,128)S(1)}, u32[]{:S(2)}, u32[]{:S(2)}) collective-permute-start(f32[16,16,128]{2,1,0:T(8,128)} %get-tuple-element.38), channel_id=1, source_target_pairs={{0,4},{4,0},{8,12},{12,8},{1,5},{5,1},{9,13},{13,9},{2,6},{6,2},{1... | collective-permute-start | bytes 393224 | tf_op jit(solution)/shard_map/ppermute | solution.py:32
  62.4 2.6 %collective-permute-start.14 = (f32[16,16,128]{2,1,0:T(8,128)}, f32[16,16,128]{2,1,0:T(8,128)S(1)}, u32[]{:S(2)}, u32[]{:S(2)}) collective-permute-start(f32[16,16,128]{2,1,0:T(8,128)} %get-tuple-element.39), channel_id=1, source_target_pairs={{4,8},{8,4},{5,9},{9,5},{6,10},{10,6},{7,11},{11,7},{20,24},{24,20... | collective-permute-start | bytes 393224 | tf_op jit(solution)/shard_map/ppermute | solution.py:36
  69.8 6.2 %collective-permute-start.15 = (f32[4,64,128]{2,1,0:T(8,128)}, f32[4,64,128]{2,1,0:T(8,128)S(1)}, u32[]{:S(2)}, u32[]{:S(2)}) collective-permute-start(f32[4,64,128]{2,1,0:T(8,128)} %get-tuple-element.40), channel_id=1, source_target_pairs={{0,1},{1,0},{2,3},{3,2},{4,5},{5,4},{6,7},{7,6},{8,9},{9,8},{10,11... | collective-permute-start | bytes 393224 | tf_op jit(solution)/shard_map/ppermute | solution.py:32
  69.8 9.0 %collective-permute-start.16 = (f32[4,64,128]{2,1,0:T(8,128)}, f32[4,64,128]{2,1,0:T(8,128)S(1)}, u32[]{:S(2)}, u32[]{:S(2)}) collective-permute-start(f32[4,64,128]{2,1,0:T(8,128)} %get-tuple-element.41), channel_id=1, source_target_pairs={{1,2},{2,1},{5,6},{6,5},{9,10},{10,9},{13,14},{14,13},{17,18},{18,... | collective-permute-start | bytes 393224 | tf_op jit(solution)/shard_map/ppermute | solution.py:36
  76.0 2.8 %copy-start.15 = (f32[4,64,128]{2,1,0:T(8,128)}, f32[4,64,128]{2,1,0:T(8,128)S(1)}, u32[]{:S(2)}) copy-start(f32[4,64,128]{2,1,0:T(8,128)S(1)} %collective-permute-done.15.z_a) | copy-start | bytes 393220
  92.8 9.6 %copy-start.17 = (f32[4,16,128]{2,1,0:T(8,128)S(1)}, f32[4,16,128]{2,1,0:T(8,128)}, u32[]{:S(2)}) copy-start(f32[4,16,128]{2,1,0:T(8,128)} %get-tuple-element.42) | copy-start | bytes 98308
  92.8 6.7 %collective-permute-start.17 = (f32[4,16,128]{2,1,0:T(8,128)}, f32[4,16,128]{2,1,0:T(8,128)S(1)}, u32[]{:S(2)}, u32[]{:S(2)}) collective-permute-start(f32[4,16,128]{2,1,0:T(8,128)} %get-tuple-element.42), channel_id=1, source_target_pairs={{0,4},{4,0},{8,12},{12,8},{1,5},{5,1},{9,13},{13,9},{2,6},{6,2},{1... | collective-permute-start | bytes 98312 | tf_op jit(solution)/shard_map/ppermute | solution.py:40
  96.4 3.9 %collective-permute-start.18 = (f32[4,16,128]{2,1,0:T(8,128)}, f32[4,16,128]{2,1,0:T(8,128)S(1)}, u32[]{:S(2)}, u32[]{:S(2)}) collective-permute-start(f32[4,16,128]{2,1,0:T(8,128)} %get-tuple-element.42), channel_id=1, source_target_pairs={{0,8},{4,12},{8,0},{12,4},{1,9},{5,13},{9,1},{13,5},{2,10},{6,14},... | collective-permute-start | bytes 98312 | tf_op jit(solution)/shard_map/ppermute | solution.py:40
  97.6 4.8 %collective-permute-start.19 = (f32[4,16,128]{2,1,0:T(8,128)}, f32[4,16,128]{2,1,0:T(8,128)S(1)}, u32[]{:S(2)}, u32[]{:S(2)}) collective-permute-start(f32[4,16,128]{2,1,0:T(8,128)} %get-tuple-element.42), channel_id=1, source_target_pairs={{0,12},{4,8},{8,4},{12,0},{1,13},{5,9},{9,5},{13,1},{2,14},{6,10},... | collective-permute-start | bytes 98312 | tf_op jit(solution)/shard_map/ppermute | solution.py:40
  102.4 3.9 %collective-permute-start.20 = (f32[4,4,16,128]{3,2,1,0:T(8,128)S(1)}, f32[4,4,16,128]{3,2,1,0:T(8,128)S(1)}, u32[]{:S(2)}, u32[]{:S(2)}) collective-permute-start(f32[4,4,16,128]{3,2,1,0:T(8,128)S(1)} %pad_maximum_fusion), channel_id=1, source_target_pairs={{0,2},{1,3},{2,0},{3,1},{4,6},{5,7},{6,4},{7,5},{8,10},{9,11},{10,... | collective-permute-start | bytes 393224 | tf_op jit(solution)/shard_map/ppermute | solution.py:40
  106.3 2.8 %copy-start.21 = (f32[16,8,128]{2,1,0:T(8,128)S(1)}, f32[16,8,128]{2,1,0:T(8,128)}, u32[]{:S(2)}) copy-start(f32[16,8,128]{2,1,0:T(8,128)} %get-tuple-element.31) | copy-start | bytes 196612
  106.3 2.8 %copy-start.20 = (f32[16,8,128]{2,1,0:T(8,128)S(1)}, f32[16,8,128]{2,1,0:T(8,128)}, u32[]{:S(2)}) copy-start(f32[16,8,128]{2,1,0:T(8,128)} %get-tuple-element.32) | copy-start | bytes 196612
  106.3 3.5 %copy-start.19 = (f32[5,64,128]{2,1,0:T(8,128)S(1)}, f32[5,64,128]{2,1,0:T(8,128)}, u32[]{:S(2)}) copy-start(f32[5,64,128]{2,1,0:T(8,128)} %get-tuple-element.35) | copy-start | bytes 491524
  106.3 19.6 %collective-permute-start.21 = (f32[8,4,16,128]{3,2,1,0:T(8,128)S(1)}, f32[8,4,16,128]{3,2,1,0:T(8,128)S(1)}, u32[]{:S(2)}, u32[]{:S(2)}) collective-permute-start(f32[8,4,16,128]{3,2,1,0:T(8,128)S(1)} %get-tuple-element.46), channel_id=1, source_target_pairs={{0,1},{1,0},{2,3},{3,2},{4,5},{5,4},{6,7},{7,6},{8,9},{9,8},{10,11... | collective-permute-start | bytes 786440 | tf_op jit(solution)/shard_map/ppermute | solution.py:40
  109.1 3.1 %collective-permute-start.6 = (f32[16,8,128]{2,1,0:T(8,128)S(1)}, f32[16,8,128]{2,1,0:T(8,128)S(1)}, u32[]{:S(2)}, u32[]{:S(2)}) collective-permute-start(f32[16,8,128]{2,1,0:T(8,128)S(1)} %copy-done.21), channel_id=1, source_target_pairs={{0,4},{4,0},{8,12},{12,8},{1,5},{5,1},{9,13},{13,9},{2,6},{6,2},{1... | collective-permute-start | bytes 196616 | tf_op jit(solution)/shard_map/ppermute | solution.py:32
  109.1 3.1 %collective-permute-start.7 = (f32[16,8,128]{2,1,0:T(8,128)S(1)}, f32[16,8,128]{2,1,0:T(8,128)S(1)}, u32[]{:S(2)}, u32[]{:S(2)}) collective-permute-start(f32[16,8,128]{2,1,0:T(8,128)S(1)} %copy-done.20), channel_id=1, source_target_pairs={{4,8},{8,4},{5,9},{9,5},{6,10},{10,6},{7,11},{11,7},{20,24},{24,20... | collective-permute-start | bytes 196616 | tf_op jit(solution)/shard_map/ppermute | solution.py:36
  109.8 41.1 %collective-permute-start.10 = (f32[5,64,128]{2,1,0:T(8,128)S(1)}, f32[5,64,128]{2,1,0:T(8,128)S(1)}, u32[]{:S(2)}, u32[]{:S(2)}) collective-permute-start(f32[5,64,128]{2,1,0:T(8,128)S(1)} %copy-done.19), channel_id=1, source_target_pairs={{0,16},{16,0},{1,17},{17,1},{2,18},{18,2},{3,19},{19,3},{4,20},{20... | collective-permute-start | bytes 491528 | tf_op jit(solution)/shard_map/ppermute | solution.py:32
  115.0 5.4 %collective-permute-start.8 = (f32[1,80,128]{2,1,0:T(8,128)}, f32[1,80,128]{2,1,0:T(8,128)S(1)}, u32[]{:S(2)}, u32[]{:S(2)}) collective-permute-start(f32[1,80,128]{2,1,0:T(8,128)} %get-tuple-element.33), channel_id=1, source_target_pairs={{0,1},{1,0},{2,3},{3,2},{4,5},{5,4},{6,7},{7,6},{8,9},{9,8},{10,11... | collective-permute-start | bytes 122888 | tf_op jit(solution)/shard_map/ppermute | solution.py:32
  116.8 5.5 %collective-permute-start.9 = (f32[1,80,128]{2,1,0:T(8,128)}, f32[1,80,128]{2,1,0:T(8,128)S(1)}, u32[]{:S(2)}, u32[]{:S(2)}) collective-permute-start(f32[1,80,128]{2,1,0:T(8,128)} %get-tuple-element.34), channel_id=1, source_target_pairs={{1,2},{2,1},{5,6},{6,5},{9,10},{10,9},{13,14},{14,13},{17,18},{18,... | collective-permute-start | bytes 122888 | tf_op jit(solution)/shard_map/ppermute | solution.py:36
  120.4 2.0 %copy-start.11 = (f32[1,80,128]{2,1,0:T(8,128)}, f32[1,80,128]{2,1,0:T(8,128)S(1)}, u32[]{:S(2)}) copy-start(f32[1,80,128]{2,1,0:T(8,128)S(1)} %collective-permute-done.8.z_a.refs_11_) | copy-start | bytes 122884
  124.7 26.2 %collective-permute-start.11 = (f32[160,128]{1,0:T(8,128)}, f32[160,128]{1,0:T(8,128)S(1)}, u32[]{:S(2)}, u32[]{:S(2)}) collective-permute-start(f32[160,128]{1,0:T(8,128)} %xframe_kernel.3), channel_id=1, source_target_pairs={{0,16},{16,0},{1,17},{17,1},{2,18},{18,2},{3,19},{19,3},{4,20},{20... | collective-permute-start | bytes 245768 | tf_op jit(solution)/shard_map/ppermute | solution.py:32
  126.0 0.8 copy-start.6
  (12 other events, 7.8 us)

commit v2 on v1

--- a/solution.py
+++ b/solution.py
@@ -1,5 +1,6 @@
 import functools
 
+import math
 import jax
 import jax.numpy as jnp
 from jax import lax
@@ -48,7 +49,9 @@
     specs = [
         pl.BlockSpec(memory_space=pltpu.SMEM if i in smem else pltpu.VMEM) for i in range(len(args))
     ]
-    shapes = [jax.ShapeDtypeStruct(s, F32) for s in outs]
+    shapes = [pltpu.VMEM(s, F32) for s in outs]
+    args = [pltpu.with_memory_space_constraint(a, pltpu.VMEM) if (i not in smem and a.dtype == F32) else a for i, a in enumerate(args)]
+    limit = 4 * sum(math.prod(s) for s in scratch) + 6 * 2**20
     return pl.pallas_call(
         body,
         out_shape=shapes,
@@ -56,6 +59,7 @@
         out_specs=[pl.BlockSpec(memory_space=pltpu.VMEM) for _ in outs],
         scratch_shapes=[pltpu.VMEM(s, F32) for s in scratch],
         name=getattr(body, "__name__", None) or body.func.__name__,
+        compiler_params=pltpu.CompilerParams(vmem_limit_bytes=limit),
     )(*args)
 
 

time: 181 us -> 154 us (0.85)
  Pallas kernels: 103 us -> 79.7 us
  local copies, waits for them, and re-layouts: 8.32 us -> 5.44 us
    pallas_call x11, Pallas kernels: 103 us -> 79.7 us  [call(): pl.pallas_call(body, out_shape=shapes, in_specs=specs, out_specs=[pl.Bloc...]
    unnamed x48 -> x18, local copies, waits for them, and re-layouts: 8.28 us -> 5.4 us
  transfers between devices with their start and end apart: 22 -> 22, of which waited for: 11 -> 11; matrix products, arithmetic and copies ran while one was open for 0% -> 0% of each run, Pallas kernels for 19% -> 15%
where the time goes in v2:
time: 154 us; the launch traced here: 152 us
  Pallas kernels  79.7 us (52%)
  starting transfers between devices  39.9 us (26%)
  waiting for transfers between devices  26.3 us (17%)
  local copies, waits for them, and re-layouts  5.44 us (4%)
    pallas_call x11, Pallas kernels, call(): pl.pallas_call(body, out_shape=shapes, in_specs=specs, out_specs=[pl.Bloc...  79.7 us
    ppermute x11, starting transfers between devices, swap_even(): return lax.ppermute(x, axis, pairs_even(lax.axis_size(axis)))  16.1 us
    ppermute x6, starting transfers between devices, swap_odd(): return lax.ppermute(x, axis, pairs_odd(lax.axis_size(axis)))  14.9 us
    ppermute x11, waiting for transfers between devices, swap_even(): return lax.ppermute(x, axis, pairs_even(lax.axis_size(axis)))  11.4 us
    ppermute x5, starting transfers between devices, swap_xor(): lax.ppermute(x, axis, [(i, i ^ m) for i in range(lax.axis_size(axis))])  8.89 us
    ppermute x6, waiting for transfers between devices, swap_odd(): return lax.ppermute(x, axis, pairs_odd(lax.axis_size(axis)))  7.72 us
    ppermute x5, waiting for transfers between devices, swap_xor(): lax.ppermute(x, axis, [(i, i ^ m) for i in range(lax.axis_size(axis))])  7.21 us
    unnamed x18, local copies, waits for them, and re-layouts  5.4 us
  transfers between devices with their start and end apart: 22, of which 11 were waited for; matrix products, arithmetic and copies ran while one was open for 0% of the time, Pallas kernels for 15%

profile of v2, /device:TPU:1, one launch (start us, length us, event | category | flops | bytes accessed | tf_op | source)
XLA Modules:
  0.0 152.3 jit_solution(12312265780501939086)
XLA Ops:
  1.7 1.0 copy-done.2
  5.4 2.2 %collective-permute-start = (f32[48,8,128]{2,1,0:T(8,128)S(1)}, f32[48,8,128]{2,1,0:T(8,128)S(1)}, u32[]{:S(2)}, u32[]{:S(2)}) collective-permute-start(f32[48,8,128]{2,1,0:T(8,128)S(1)} %get-tuple-element.25), channel_id=1, source_target_pairs={{0,4},{4,0},{8,12},{12,8},{1,5},{5,1},{9,13},{13,9},{2,6},{6,2},{1... | collective-permute-start | bytes 589832 | tf_op jit(solution)/shard_map/ppermute | solution.py:33
  8.2 1.3 collective-permute-start.4
  9.5 2.7 %collective-permute-done.refs_3_.r_a = f32[48,8,128]{2,1,0:T(8,128)S(1)} collective-permute-done((f32[48,8,128]{2,1,0:T(8,128)S(1)}, f32[48,8,128]{2,1,0:T(8,128)S(1)}, u32[]{:S(2)}, u32[]{:S(2)}) %collective-permute-start) | collective-permute-done | bytes 196640 | tf_op jit(solution)/shard_map/ppermute | solution.py:33
  13.2 1.3 collective-permute-start.2
  14.5 3.3 %collective-permute-start.3 = (f32[3,80,128]{2,1,0:T(8,128)S(1)}, f32[3,80,128]{2,1,0:T(8,128)S(1)}, u32[]{:S(2)}, u32[]{:S(2)}) collective-permute-start(f32[3,80,128]{2,1,0:T(8,128)S(1)} %get-tuple-element.28), channel_id=1, source_target_pairs={{1,2},{2,1},{5,6},{6,5},{9,10},{10,9},{13,14},{14,13},{17,18},{18,... | collective-permute-start | bytes 368648 | tf_op jit(solution)/shard_map/ppermute | solution.py:37
  17.9 3.1 %collective-permute-done.3.z_b.refs_6_ = f32[3,80,128]{2,1,0:T(8,128)S(1)} collective-permute-done((f32[3,80,128]{2,1,0:T(8,128)S(1)}, f32[3,80,128]{2,1,0:T(8,128)S(1)}, u32[]{:S(2)}, u32[]{:S(2)}) %collective-permute-start.3) | collective-permute-done | bytes 122912 | tf_op jit(solution)/shard_map/ppermute | solution.py:37
  21.4 1.4 collective-permute-start.5
  22.8 3.1 %collective-permute-done.5.refs_8_ = f32[384,128]{1,0:T(8,128)S(1)} collective-permute-done((f32[384,128]{1,0:T(8,128)S(1)}, f32[384,128]{1,0:T(8,128)S(1)}, u32[]{:S(2)}, u32[]{:S(2)}) %collective-permute-start.5) | collective-permute-done | bytes 196640 | tf_op jit(solution)/shard_map/ppermute | solution.py:33
  26.0 18.8 %fine_down_kernel.1 = (f32[16,64,128]{2,1,0:T(8,128)S(1)}, f32[8,32,128]{2,1,0:T(8,128)S(1)}, f32[16,8,128]{2,1,0:T(8,128)S(1)}, f32[16,8,128]{2,1,0:T(8,128)S(1)}, f32[5,64,128]{2,1,0:T(8,128)S(1)}) custom-call(f32[16,64,128]{2,1,0:T(8,128)S(1)} %get-tuple-element.24.refs_0_, f32[16,64,128]{2,1,0:T(8,128)S(1)} %copy-done.3, f32[16,64,128]{2,1,0:T(8,128)S(1)} %copy-done.1, ...), custom_call_target="tpu_custom_call" | custom-call | tf_op jit(solution)/shard_map/fine_down_kernel/pallas_call | solution.py:55
  44.8 1.5 %collective-permute-start.12 = (f32[8,32,128]{2,1,0:T(8,128)S(1)}, f32[8,32,128]{2,1,0:T(8,128)S(1)}, u32[]{:S(2)}, u32[]{:S(2)}) collective-permute-start(f32[8,32,128]{2,1,0:T(8,128)S(1)} %get-tuple-element.36.refs_0_), channel_id=1, source_target_pairs={{0,16},{16,0},{1,17},{17,1},{2,18},{18,2},{3,19},{19,3},{4,20},{20... | collective-permute-start | bytes 393224 | tf_op jit(solution)/shard_map/ppermute | solution.py:33
  46.4 2.4 %collective-permute-done.12.refs_1_ = f32[8,32,128]{2,1,0:T(8,128)S(1)} collective-permute-done((f32[8,32,128]{2,1,0:T(8,128)S(1)}, f32[8,32,128]{2,1,0:T(8,128)S(1)}, u32[]{:S(2)}, u32[]{:S(2)}) %collective-permute-start.12) | collective-permute-done | bytes 131104 | tf_op jit(solution)/shard_map/ppermute | solution.py:33
  48.8 4.5 %collective-permute-start.13 = (f32[16,16,128]{2,1,0:T(8,128)S(1)}, f32[16,16,128]{2,1,0:T(8,128)S(1)}, u32[]{:S(2)}, u32[]{:S(2)}) collective-permute-start(f32[16,16,128]{2,1,0:T(8,128)S(1)} %get-tuple-element.38), channel_id=1, source_target_pairs={{0,4},{4,0},{8,12},{12,8},{1,5},{5,1},{9,13},{13,9},{2,6},{6,2},{1... | collective-permute-start | bytes 393224 | tf_op jit(solution)/shard_map/ppermute | solution.py:33
  54.0 1.7 %collective-permute-done.13.r_a = f32[16,16,128]{2,1,0:T(8,128)S(1)} collective-permute-done((f32[16,16,128]{2,1,0:T(8,128)S(1)}, f32[16,16,128]{2,1,0:T(8,128)S(1)}, u32[]{:S(2)}, u32[]{:S(2)}) %collective-permute-start.13) | collective-permute-done | bytes 131104 | tf_op jit(solution)/shard_map/ppermute | solution.py:33
  55.7 2.4 %mid_z_kernel.1 = (f32[4,64,128]{2,1,0:T(8,128)S(1)}, f32[4,64,128]{2,1,0:T(8,128)S(1)}) custom-call(f32[16,32,128]{2,1,0:T(8,128)S(1)} %get-tuple-element.37.full, f32[16,16,128]{2,1,0:T(8,128)S(1)} %collective-permute-done.13.r_a, f32[16,16,128]{2,1,0:T(8,128)S(1)} %collective-permute-done.14.r_b), custom_call_target="tpu_custom_call" | custom-call | tf_op jit(solution)/shard_map/mid_z_kernel/pallas_call | solution.py:55
  58.1 6.1 %collective-permute-start.16 = (f32[4,64,128]{2,1,0:T(8,128)S(1)}, f32[4,64,128]{2,1,0:T(8,128)S(1)}, u32[]{:S(2)}, u32[]{:S(2)}) collective-permute-start(f32[4,64,128]{2,1,0:T(8,128)S(1)} %get-tuple-element.41), channel_id=1, source_target_pairs={{1,2},{2,1},{5,6},{6,5},{9,10},{10,9},{13,14},{14,13},{17,18},{18,... | collective-permute-start | bytes 393224 | tf_op jit(solution)/shard_map/ppermute | solution.py:37
  64.2 2.6 %collective-permute-done.16.z_b = f32[4,64,128]{2,1,0:T(8,128)S(1)} collective-permute-done((f32[4,64,128]{2,1,0:T(8,128)S(1)}, f32[4,64,128]{2,1,0:T(8,128)S(1)}, u32[]{:S(2)}, u32[]{:S(2)}) %collective-permute-start.16) | collective-permute-done | bytes 131104 | tf_op jit(solution)/shard_map/ppermute | solution.py:37
  66.8 10.8 %mid_down_kernel.1 = (f32[18,80,128]{2,1,0:T(8,128)S(1)}, f32[18,80,128]{2,1,0:T(8,128)S(1)}, f32[18,80,128]{2,1,0:T(8,128)S(1)}, f32[4,16,128]{2,1,0:T(8,128)S(1)}) custom-call(f32[16,32,128]{2,1,0:T(8,128)S(1)} %get-tuple-element.37.full, f32[16,16,128]{2,1,0:T(8,128)S(1)} %collective-permute-done.13.r_a, f32[16,16,128]{2,1,0:T(8,128)S(1)} %collective-permute-done.14.r_b, ...), custom_call_target="tpu_custom_call" | custom-call | tf_op jit(solution)/shard_map/mid_down_kernel/pallas_call | solution.py:55
  77.6 3.7 %collective-permute-start.17 = (f32[4,16,128]{2,1,0:T(8,128)S(1)}, f32[4,16,128]{2,1,0:T(8,128)S(1)}, u32[]{:S(2)}, u32[]{:S(2)}) collective-permute-start(f32[4,16,128]{2,1,0:T(8,128)S(1)} %get-tuple-element.42), channel_id=1, source_target_pairs={{0,4},{4,0},{8,12},{12,8},{1,5},{5,1},{9,13},{13,9},{2,6},{6,2},{1... | collective-permute-start | bytes 98312 | tf_op jit(solution)/shard_map/ppermute | solution.py:41
  81.3 1.2 collective-permute-start.18
  82.6 1.1 collective-permute-start.19
  83.7 1.3 collective-permute-done.18
  85.0 2.1 %collective-permute-done.19 = f32[4,16,128]{2,1,0:T(8,128)S(1)} collective-permute-done((f32[4,16,128]{2,1,0:T(8,128)S(1)}, f32[4,16,128]{2,1,0:T(8,128)S(1)}, u32[]{:S(2)}, u32[]{:S(2)}) %collective-permute-start.19) | collective-permute-done | bytes 32800 | tf_op jit(solution)/shard_map/ppermute | solution.py:41
  87.3 3.8 %collective-permute-done.20 = f32[4,4,16,128]{3,2,1,0:T(8,128)S(1)} collective-permute-done((f32[4,4,16,128]{3,2,1,0:T(8,128)S(1)}, f32[4,4,16,128]{3,2,1,0:T(8,128)S(1)}, u32[]{:S(2)}, u32[]{:S(2)}) %collective-permute-start.20) | collective-permute-done | bytes 131104 | tf_op jit(solution)/shard_map/ppermute | solution.py:41
  91.0 2.8 %collective-permute-start.21 = (f32[8,4,16,128]{3,2,1,0:T(8,128)S(1)}, f32[8,4,16,128]{3,2,1,0:T(8,128)S(1)}, u32[]{:S(2)}, u32[]{:S(2)}) collective-permute-start(f32[8,4,16,128]{3,2,1,0:T(8,128)S(1)} %get-tuple-element.46), channel_id=1, source_target_pairs={{0,1},{1,0},{2,3},{3,2},{4,5},{5,4},{6,7},{7,6},{8,9},{9,8},{10,11... | collective-permute-start | bytes 786440 | tf_op jit(solution)/shard_map/ppermute | solution.py:41
  94.5 1.4 collective-permute-start.10
  95.8 1.5 %collective-permute-done.6.refs_1_.r_a.refs_9_ = f32[16,8,128]{2,1,0:T(8,128)S(1)} collective-permute-done((f32[16,8,128]{2,1,0:T(8,128)S(1)}, f32[16,8,128]{2,1,0:T(8,128)S(1)}, u32[]{:S(2)}, u32[]{:S(2)}) %collective-permute-start.6) | collective-permute-done | bytes 65568 | tf_op jit(solution)/shard_map/ppermute | solution.py:33
  98.8 3.5 %collective-permute-start.9 = (f32[1,80,128]{2,1,0:T(8,128)S(1)}, f32[1,80,128]{2,1,0:T(8,128)S(1)}, u32[]{:S(2)}, u32[]{:S(2)}) collective-permute-start(f32[1,80,128]{2,1,0:T(8,128)S(1)} %get-tuple-element.34), channel_id=1, source_target_pairs={{1,2},{2,1},{5,6},{6,5},{9,10},{10,9},{13,14},{14,13},{17,18},{18,... | collective-permute-start | bytes 122888 | tf_op jit(solution)/shard_map/ppermute | solution.py:37
  102.3 2.0 %collective-permute-done.9.z_b.refs_12_ = f32[1,80,128]{2,1,0:T(8,128)S(1)} collective-permute-done((f32[1,80,128]{2,1,0:T(8,128)S(1)}, f32[1,80,128]{2,1,0:T(8,128)S(1)}, u32[]{:S(2)}, u32[]{:S(2)}) %collective-permute-start.9) | collective-permute-done | bytes 40992 | tf_op jit(solution)/shard_map/ppermute | solution.py:37
  104.5 1.4 collective-permute-start.11
  105.9 21.5 %coarse_kernel.1.refs_15_ = f32[18,80,128]{2,1,0:T(8,128)S(1)} custom-call(f32[16,4,16,128]{3,2,1,0:T(8,128)S(1)} %constant_dynamic-update-slice_fusion.5.blocks, f32[18,80,128]{2,1,0:T(8,128)S(1)} %get-tuple-element.43.v1_in, f32[18,80,128]{2,1,0:T(8,128)S(1)} %get-tuple-element.44.b1, f32[18,80,128]{2,1,0:T(8,128)S(1)} %get-tuple-element.45.c1), custom_call_target="tpu_custom_call" | custom-call | tf_op jit(solution)/shard_map/coarse_kernel/pallas_call | solution.py:55
  127.4 23.2 %fine_up_kernel.1 = (f32[16,64,128]{2,1,0:T(8,128)S(1)}, f32[16,64,128]{2,1,0:T(8,128)S(1)}) custom-call(f32[16,64,128]{2,1,0:T(8,128)S(1)} %get-tuple-element.24.refs_0_, f32[16,64,128]{2,1,0:T(8,128)S(1)} %get-tuple-element.30.refs_0_.refs_1_, f32[16,64,128]{2,1,0:T(8,128)S(1)} %copy-done.1, f32[48,8,128]{2,1,0:T(8,128)S(1)} %collective-permute-done.refs_3_.r_a, ...), custom_call_target="tpu_custom_call" | custom-call | tf_op jit(solution)/shard_map/fine_up_kernel/pallas_call | solution.py:55
  (44 shorter events, 10.5 us)
Async XLA Ops:
  0.6 1.0 copy-start
  1.7 1.0 copy-start.2
  2.7 1.0 copy-start.4
  3.8 0.7 copy-start.5
  5.4 6.8 %collective-permute-start = (f32[48,8,128]{2,1,0:T(8,128)S(1)}, f32[48,8,128]{2,1,0:T(8,128)S(1)}, u32[]{:S(2)}, u32[]{:S(2)}) collective-permute-start(f32[48,8,128]{2,1,0:T(8,128)S(1)} %get-tuple-element.25), channel_id=1, source_target_pairs={{0,4},{4,0},{8,12},{12,8},{1,5},{5,1},{9,13},{13,9},{2,6},{6,2},{1... | collective-permute-start | bytes 589832 | tf_op jit(solution)/shard_map/ppermute | solution.py:33
  7.6 4.6 %collective-permute-start.1 = (f32[48,8,128]{2,1,0:T(8,128)S(1)}, f32[48,8,128]{2,1,0:T(8,128)S(1)}, u32[]{:S(2)}, u32[]{:S(2)}) collective-permute-start(f32[48,8,128]{2,1,0:T(8,128)S(1)} %get-tuple-element.26), channel_id=1, source_target_pairs={{4,8},{8,4},{5,9},{9,5},{6,10},{10,6},{7,11},{11,7},{20,24},{24,20... | collective-permute-start | bytes 589832 | tf_op jit(solution)/shard_map/ppermute | solution.py:37
  8.2 14.6 %collective-permute-start.4 = (f32[14,64,128]{2,1,0:T(8,128)S(1)}, f32[14,64,128]{2,1,0:T(8,128)S(1)}, u32[]{:S(2)}, u32[]{:S(2)}) collective-permute-start(f32[14,64,128]{2,1,0:T(8,128)S(1)} %get-tuple-element.29), channel_id=1, source_target_pairs={{0,16},{16,0},{1,17},{17,1},{2,18},{18,2},{3,19},{19,3},{4,20},{20... | collective-permute-start | bytes 1376264 | tf_op jit(solution)/shard_map/ppermute | solution.py:33
  12.2 13.8 %copy-start.3 = (f32[16,64,128]{2,1,0:T(8,128)S(1)}, f32[16,64,128]{2,1,0:T(8,128)}, u32[]{:S(2)}) copy-start(f32[16,64,128]{2,1,0:T(8,128)} %refs_1_.3) | copy-start | bytes 1572868
  13.2 12.8 %copy-start.1 = (f32[16,64,128]{2,1,0:T(8,128)S(1)}, f32[16,64,128]{2,1,0:T(8,128)}, u32[]{:S(2)}) copy-start(f32[16,64,128]{2,1,0:T(8,128)} %refs_2_.5) | copy-start | bytes 1572868
  13.2 4.7 %collective-permute-start.2 = (f32[3,80,128]{2,1,0:T(8,128)S(1)}, f32[3,80,128]{2,1,0:T(8,128)S(1)}, u32[]{:S(2)}, u32[]{:S(2)}) collective-permute-start(f32[3,80,128]{2,1,0:T(8,128)S(1)} %get-tuple-element.27), channel_id=1, source_target_pairs={{0,1},{1,0},{2,3},{3,2},{4,5},{5,4},{6,7},{7,6},{8,9},{9,8},{10,11... | collective-permute-start | bytes 368648 | tf_op jit(solution)/shard_map/ppermute | solution.py:33
  14.5 6.5 %collective-permute-start.3 = (f32[3,80,128]{2,1,0:T(8,128)S(1)}, f32[3,80,128]{2,1,0:T(8,128)S(1)}, u32[]{:S(2)}, u32[]{:S(2)}) collective-permute-start(f32[3,80,128]{2,1,0:T(8,128)S(1)} %get-tuple-element.28), channel_id=1, source_target_pairs={{1,2},{2,1},{5,6},{6,5},{9,10},{10,9},{13,14},{14,13},{17,18},{18,... | collective-permute-start | bytes 368648 | tf_op jit(solution)/shard_map/ppermute | solution.py:37
  21.4 4.6 %collective-permute-start.5 = (f32[384,128]{1,0:T(8,128)S(1)}, f32[384,128]{1,0:T(8,128)S(1)}, u32[]{:S(2)}, u32[]{:S(2)}) collective-permute-start(f32[384,128]{1,0:T(8,128)S(1)} %xframe_kernel.2), channel_id=1, source_target_pairs={{0,16},{16,0},{1,17},{17,1},{2,18},{18,2},{3,19},{19,3},{4,20},{20... | collective-permute-start | bytes 589832 | tf_op jit(solution)/shard_map/ppermute | solution.py:33
  44.8 3.9 %collective-permute-start.12 = (f32[8,32,128]{2,1,0:T(8,128)S(1)}, f32[8,32,128]{2,1,0:T(8,128)S(1)}, u32[]{:S(2)}, u32[]{:S(2)}) collective-permute-start(f32[8,32,128]{2,1,0:T(8,128)S(1)} %get-tuple-element.36.refs_0_), channel_id=1, source_target_pairs={{0,16},{16,0},{1,17},{17,1},{2,18},{18,2},{3,19},{19,3},{4,20},{20... | collective-permute-start | bytes 393224 | tf_op jit(solution)/shard_map/ppermute | solution.py:33
  48.8 6.9 %collective-permute-start.13 = (f32[16,16,128]{2,1,0:T(8,128)S(1)}, f32[16,16,128]{2,1,0:T(8,128)S(1)}, u32[]{:S(2)}, u32[]{:S(2)}) collective-permute-start(f32[16,16,128]{2,1,0:T(8,128)S(1)} %get-tuple-element.38), channel_id=1, source_target_pairs={{0,4},{4,0},{8,12},{12,8},{1,5},{5,1},{9,13},{13,9},{2,6},{6,2},{1... | collective-permute-start | bytes 393224 | tf_op jit(solution)/shard_map/ppermute | solution.py:33
  53.3 2.4 %collective-permute-start.14 = (f32[16,16,128]{2,1,0:T(8,128)S(1)}, f32[16,16,128]{2,1,0:T(8,128)S(1)}, u32[]{:S(2)}, u32[]{:S(2)}) collective-permute-start(f32[16,16,128]{2,1,0:T(8,128)S(1)} %get-tuple-element.39), channel_id=1, source_target_pairs={{4,8},{8,4},{5,9},{9,5},{6,10},{10,6},{7,11},{11,7},{20,24},{24,20... | collective-permute-start | bytes 393224 | tf_op jit(solution)/shard_map/ppermute | solution.py:37
  58.0 6.1 %collective-permute-start.15 = (f32[4,64,128]{2,1,0:T(8,128)S(1)}, f32[4,64,128]{2,1,0:T(8,128)S(1)}, u32[]{:S(2)}, u32[]{:S(2)}) collective-permute-start(f32[4,64,128]{2,1,0:T(8,128)S(1)} %get-tuple-element.40), channel_id=1, source_target_pairs={{0,1},{1,0},{2,3},{3,2},{4,5},{5,4},{6,7},{7,6},{8,9},{9,8},{10,11... | collective-permute-start | bytes 393224 | tf_op jit(solution)/shard_map/ppermute | solution.py:33
  58.1 8.7 %collective-permute-start.16 = (f32[4,64,128]{2,1,0:T(8,128)S(1)}, f32[4,64,128]{2,1,0:T(8,128)S(1)}, u32[]{:S(2)}, u32[]{:S(2)}) collective-permute-start(f32[4,64,128]{2,1,0:T(8,128)S(1)} %get-tuple-element.41), channel_id=1, source_target_pairs={{1,2},{2,1},{5,6},{6,5},{9,10},{10,9},{13,14},{14,13},{17,18},{18,... | collective-permute-start | bytes 393224 | tf_op jit(solution)/shard_map/ppermute | solution.py:37
  77.6 6.1 %collective-permute-start.17 = (f32[4,16,128]{2,1,0:T(8,128)S(1)}, f32[4,16,128]{2,1,0:T(8,128)S(1)}, u32[]{:S(2)}, u32[]{:S(2)}) collective-permute-start(f32[4,16,128]{2,1,0:T(8,128)S(1)} %get-tuple-element.42), channel_id=1, source_target_pairs={{0,4},{4,0},{8,12},{12,8},{1,5},{5,1},{9,13},{13,9},{2,6},{6,2},{1... | collective-permute-start | bytes 98312 | tf_op jit(solution)/shard_map/ppermute | solution.py:41
  81.3 3.7 %collective-permute-start.18 = (f32[4,16,128]{2,1,0:T(8,128)S(1)}, f32[4,16,128]{2,1,0:T(8,128)S(1)}, u32[]{:S(2)}, u32[]{:S(2)}) collective-permute-start(f32[4,16,128]{2,1,0:T(8,128)S(1)} %get-tuple-element.42), channel_id=1, source_target_pairs={{0,8},{4,12},{8,0},{12,4},{1,9},{5,13},{9,1},{13,5},{2,10},{6,14},... | collective-permute-start | bytes 98312 | tf_op jit(solution)/shard_map/ppermute | solution.py:41
  82.6 4.6 %collective-permute-start.19 = (f32[4,16,128]{2,1,0:T(8,128)S(1)}, f32[4,16,128]{2,1,0:T(8,128)S(1)}, u32[]{:S(2)}, u32[]{:S(2)}) collective-permute-start(f32[4,16,128]{2,1,0:T(8,128)S(1)} %get-tuple-element.42), channel_id=1, source_target_pairs={{0,12},{4,8},{8,4},{12,0},{1,13},{5,9},{9,5},{13,1},{2,14},{6,10},... | collective-permute-start | bytes 98312 | tf_op jit(solution)/shard_map/ppermute | solution.py:41
  87.1 3.9 %collective-permute-start.20 = (f32[4,4,16,128]{3,2,1,0:T(8,128)S(1)}, f32[4,4,16,128]{3,2,1,0:T(8,128)S(1)}, u32[]{:S(2)}, u32[]{:S(2)}) collective-permute-start(f32[4,4,16,128]{3,2,1,0:T(8,128)S(1)} %pad_maximum_fusion), channel_id=1, source_target_pairs={{0,2},{1,3},{2,0},{3,1},{4,6},{5,7},{6,4},{7,5},{8,10},{9,11},{10,... | collective-permute-start | bytes 393224 | tf_op jit(solution)/shard_map/ppermute | solution.py:41
  91.0 14.8 %collective-permute-start.21 = (f32[8,4,16,128]{3,2,1,0:T(8,128)S(1)}, f32[8,4,16,128]{3,2,1,0:T(8,128)S(1)}, u32[]{:S(2)}, u32[]{:S(2)}) collective-permute-start(f32[8,4,16,128]{3,2,1,0:T(8,128)S(1)} %get-tuple-element.46), channel_id=1, source_target_pairs={{0,1},{1,0},{2,3},{3,2},{4,5},{5,4},{6,7},{7,6},{8,9},{9,8},{10,11... | collective-permute-start | bytes 786440 | tf_op jit(solution)/shard_map/ppermute | solution.py:41
  93.8 3.6 %collective-permute-start.6 = (f32[16,8,128]{2,1,0:T(8,128)S(1)}, f32[16,8,128]{2,1,0:T(8,128)S(1)}, u32[]{:S(2)}, u32[]{:S(2)}) collective-permute-start(f32[16,8,128]{2,1,0:T(8,128)S(1)} %get-tuple-element.31), channel_id=1, source_target_pairs={{0,4},{4,0},{8,12},{12,8},{1,5},{5,1},{9,13},{13,9},{2,6},{6,2},{1... | collective-permute-start | bytes 196616 | tf_op jit(solution)/shard_map/ppermute | solution.py:33
  93.8 3.6 %collective-permute-start.7 = (f32[16,8,128]{2,1,0:T(8,128)S(1)}, f32[16,8,128]{2,1,0:T(8,128)S(1)}, u32[]{:S(2)}, u32[]{:S(2)}) collective-permute-start(f32[16,8,128]{2,1,0:T(8,128)S(1)} %get-tuple-element.32), channel_id=1, source_target_pairs={{4,8},{8,4},{5,9},{9,5},{6,10},{10,6},{7,11},{11,7},{20,24},{24,20... | collective-permute-start | bytes 196616 | tf_op jit(solution)/shard_map/ppermute | solution.py:37
  94.5 33.0 %collective-permute-start.10 = (f32[5,64,128]{2,1,0:T(8,128)S(1)}, f32[5,64,128]{2,1,0:T(8,128)S(1)}, u32[]{:S(2)}, u32[]{:S(2)}) collective-permute-start(f32[5,64,128]{2,1,0:T(8,128)S(1)} %get-tuple-element.35), channel_id=1, source_target_pairs={{0,16},{16,0},{1,17},{17,1},{2,18},{18,2},{3,19},{19,3},{4,20},{20... | collective-permute-start | bytes 491528 | tf_op jit(solution)/shard_map/ppermute | solution.py:33
  97.8 4.6 %collective-permute-start.8 = (f32[1,80,128]{2,1,0:T(8,128)S(1)}, f32[1,80,128]{2,1,0:T(8,128)S(1)}, u32[]{:S(2)}, u32[]{:S(2)}) collective-permute-start(f32[1,80,128]{2,1,0:T(8,128)S(1)} %get-tuple-element.33), channel_id=1, source_target_pairs={{0,1},{1,0},{2,3},{3,2},{4,5},{5,4},{6,7},{7,6},{8,9},{9,8},{10,11... | collective-permute-start | bytes 122888 | tf_op jit(solution)/shard_map/ppermute | solution.py:33
  98.8 5.5 %collective-permute-start.9 = (f32[1,80,128]{2,1,0:T(8,128)S(1)}, f32[1,80,128]{2,1,0:T(8,128)S(1)}, u32[]{:S(2)}, u32[]{:S(2)}) collective-permute-start(f32[1,80,128]{2,1,0:T(8,128)S(1)} %get-tuple-element.34), channel_id=1, source_target_pairs={{1,2},{2,1},{5,6},{6,5},{9,10},{10,9},{13,14},{14,13},{17,18},{18,... | collective-permute-start | bytes 122888 | tf_op jit(solution)/shard_map/ppermute | solution.py:37
  104.5 22.9 %collective-permute-start.11 = (f32[160,128]{1,0:T(8,128)S(1)}, f32[160,128]{1,0:T(8,128)S(1)}, u32[]{:S(2)}, u32[]{:S(2)}) collective-permute-start(f32[160,128]{1,0:T(8,128)S(1)} %xframe_kernel.3), channel_id=1, source_target_pairs={{0,16},{16,0},{1,17},{17,1},{2,18},{18,2},{3,19},{19,3},{4,20},{20... | collective-permute-start | bytes 245768 | tf_op jit(solution)/shard_map/ppermute | solution.py:33

commit v3 on v2

--- a/solution.py
+++ b/solution.py
@@ -14,8 +14,10 @@
 CLASSES = 8
 W = 0.85
 HX = 5
+HL = 6
+GW = 2 * HL
+UNROLL = 4
 F32 = jnp.float32
-HI = lax.Precision.HIGHEST
 
 
 def pairs_even(n):
@@ -45,19 +47,20 @@
     return lax.rem(lax.axis_index(axis), 2) == 0
 
 
-def call(body, outs, *args, scratch=(), smem=()):
+def call(body, outs, *args, scratch=(), smem=(), hbm_out=False, more=()):
     specs = [
         pl.BlockSpec(memory_space=pltpu.SMEM if i in smem else pltpu.VMEM) for i in range(len(args))
     ]
-    shapes = [pltpu.VMEM(s, F32) for s in outs]
+    shapes = [jax.ShapeDtypeStruct(s, F32) if hbm_out else pltpu.VMEM(s, F32) for s in outs]
+    space = pl.ANY if hbm_out else pltpu.VMEM
     args = [pltpu.with_memory_space_constraint(a, pltpu.VMEM) if (i not in smem and a.dtype == F32) else a for i, a in enumerate(args)]
     limit = 4 * sum(math.prod(s) for s in scratch) + 6 * 2**20
     return pl.pallas_call(
         body,
         out_shape=shapes,
         in_specs=specs,
-        out_specs=[pl.BlockSpec(memory_space=pltpu.VMEM) for _ in outs],
-        scratch_shapes=[pltpu.VMEM(s, F32) for s in scratch],
+        out_specs=[pl.BlockSpec(memory_space=space) for _ in outs],
+        scratch_shapes=[pltpu.VMEM(s, F32) for s in scratch] + list(more),
         name=getattr(body, "__name__", None) or body.func.__name__,
         compiler_params=pltpu.CompilerParams(vmem_limit_bytes=limit),
     )(*args)
@@ -110,25 +113,36 @@
 
 def zpack_kernel(na, *refs):
     arrs = refs[:na]
-    r_a, r_b, z_a, z_b = refs[na:]
+    r_a, r_b, z, work = refs[na:]
     nx, ny, _ = arrs[0].shape
-    ey, ez = even("gy"), even("gz")
-    group = lanes() // 8
+    tiles = ny // 8 + 2
+    ey = even("gy")
+    lane = lanes()
     for k in range(na):
-        for t in range(ny // 8 + 2):
-            right = jnp.zeros((8, 128), F32)
-            left = jnp.zeros((8, 128), F32)
-            for x in range(nx):
+        for x in range(nx):
+            acc = jnp.zeros((8, 128), F32)
+            va, vb = r_a[k * nx + x], r_b[k * nx + x]
+            for t in range(tiles):
                 if t == 0:
-                    v = jnp.where(ey, r_b[k * nx + x], r_a[k * nx + x])
-                elif t == ny // 8 + 1:
-                    v = jnp.where(ey, r_a[k * nx + x], r_b[k * nx + x])
+                    v = jnp.where(ey, vb, va)
+                elif t == tiles - 1:
+                    v = jnp.where(ey, va, vb)
                 else:
                     v = arrs[k][x, (t - 1) * 8 : t * 8]
-                right = jnp.where(group == x, rot(v, 8 * x + 8), right)
-                left = jnp.where(group == x, rot(v, 8 * x), left)
-            z_a[k, t * 8 : t * 8 + 8] = jnp.where(ez, right, left)
-            z_b[k, t * 8 : t * 8 + 8] = jnp.where(ez, left, right)
+                g = GW * t
+                acc = jnp.where((lane >= g) & (lane < g + GW), rot(v, g + HL), acc)
+            work[(k * nx + x) * 8 : (k * nx + x) * 8 + 8] = acc
+    mirror = select_mat(lambda o: o + (GW - 1) - 2 * lax.rem(o, GW))
+    out = dot(work[...], mirror)
+    for j in range(na * nx):
+        z[j] = out[8 * j : 8 * j + 8]
+
+
+def halo_of(z_a, z_b, i):
+    ez = even("gz")
+    a, b = z_a[i], z_b[i]
+    within = lax.rem(lanes(), GW)
+    return jnp.where(within < HL, jnp.where(ez, a, b), jnp.where(ez, b, a))
 
 
 def face_list(na):
@@ -137,71 +151,45 @@
 
 
 def xframe_kernel(na, nx, nsx, r_a, r_b, z_a, z_b, *x_out):
-    ey, ez = even("gy"), even("gz")
-    rows = z_a.shape[1]
-    lane = lanes()
+    ey = even("gy")
     planes = face_list(na)
+    base = len(planes) * 16
     for s in range(nsx):
         for j, (k, f, w) in enumerate(planes):
-            p = face_start("gx", nx, w, s == 0) + f
-            va, vb = r_a[k * nx + p], r_b[k * nx + p]
+            p = k * nx + face_start("gx", nx, w, s == 0) + f
+            va, vb = r_a[p], r_b[p]
             x_out[s][j * 16 : j * 16 + 8] = jnp.where(ey, vb, va)
             x_out[s][j * 16 + 8 : j * 16 + 16] = jnp.where(ey, va, vb)
-        base = len(planes) * 16
-        for strip in range(-(-len(planes) // 8)):
-            for t in range(rows // 8):
-                acc = jnp.zeros((8, 128), F32)
-                for j in range(strip * 8, min(strip * 8 + 8, len(planes))):
-                    k, f, w = planes[j]
-                    g = j % 8
-                    p = face_start("gx", nx, w, s == 0) + f
-                    za, zb = z_a[k, t * 8 : t * 8 + 8], z_b[k, t * 8 : t * 8 + 8]
-                    right = jnp.where(ez, za, zb)
-                    left = jnp.where(ez, zb, za)
-                    acc = jnp.where(lane // 8 == 2 * g, rot(left, 16 * g - 8 * p), acc)
-                    acc = jnp.where(lane // 8 == 2 * g + 1, rot(right, 16 * g + 8 - 8 * p), acc)
-                r0 = base + strip * rows + t * 8
-                x_out[s][r0 : r0 + 8] = acc
+            x_out[s][base + j * 8 : base + j * 8 + 8] = halo_of(z_a, z_b, p)
 
 
 def own_offset(nsx):
     return HX * lax.axis_index("gx") if nsx == 1 else HX
 
 
-def assemble(nsx, k, planes, m, h, own, r_a, r_b, z_a, z_b, x1, x2):
+def assemble(nsx, planes, m, h, own, r_a, r_b, z_a, z_b, x1, x2):
     nx, ny, _ = own.shape
     off = 1 + own_offset(nsx)
-    ey, ez = even("gy"), even("gz")
-    lane = lanes()
+    ey = even("gy")
     kk = planes[0]
-    tiles = ny // 8 + 2
-    is_left, is_right = lane >= 120, lane < 8
-
-    for x in range(nx):
+
+    def one(x, _):
         va, vb = r_a[kk * nx + x], r_b[kk * nx + x]
         m[off + x, 8:16] = jnp.where(ey, vb, va)
         m[off + x, 16 : 16 + ny] = own[x]
         m[off + x, 16 + ny : 24 + ny] = jnp.where(ey, va, vb)
-    for t in range(tiles):
-        za, zb = z_a[kk, t * 8 : t * 8 + 8], z_b[kk, t * 8 : t * 8 + 8]
-        right = jnp.where(ez, za, zb)
-        left = jnp.where(ez, zb, za)
-        for x in range(nx):
-            v = jnp.where(is_right, rot(right, -8 * x), 0.0)
-            h[off + x, 8 + t * 8 : 16 + t * 8] = jnp.where(is_left, rot(left, 120 - 8 * x), v)
+        h[off + x] = halo_of(z_a, z_b, kk * nx + x)
+        return 0
+
+    lax.fori_loop(0, nx, one, 0)
     for s in range(nsx):
         hi = even("gx") if s == 0 else jnp.logical_not(even("gx"))
-        for j, k_, f, w, base in planes[1]:
+        for j, _, f, w, base in planes[1]:
             p = off + jnp.where(hi, nx, -w) + f
             m[p, 8:16] = x2[s][j * 16 : j * 16 + 8]
             m[p, 16 : 16 + ny] = x1[s][j]
             m[p, 16 + ny : 24 + ny] = x2[s][j * 16 + 8 : j * 16 + 16]
-            for t in range(tiles):
-                r0 = base + (j // 8) * tiles * 8 + t * 8
-                v = x2[s][r0 : r0 + 8]
-                g = j % 8
-                a = jnp.where(is_left, rot(v, 120 - 16 * g), 0.0)
-                h[p, 8 + t * 8 : 16 + t * 8] = jnp.where(is_right, rot(v, -16 * g - 8), a)
+            h[p] = x2[s][base + j * 8 : base + j * 8 + 8]
 
 
 def plane_map(na, k):
@@ -279,9 +267,8 @@
                 q[t][x - 1, rw] = g * ((2.0 / scale) * b[t][x, pl.ds(8 + r, 8)])
                 if d is not None:
                     d[t][x - 1, rw] = total * (0.5 * scale / W)
-        return 0
-
-    lax.fori_loop(1, nx + 1, plane, 0)
+
+    fine_loop(1, nx, plane, 2)
 
 
 def weighted(a, vals, nb, t, x, rw):
@@ -302,13 +289,12 @@
                 dst[t][x, pl.ds(8 + r, 8)] = ((1.0 - W) * vals[t] + q[t][x - 1, rw]) + weighted(
                     a, vals, nb, t, x, rw
                 )
-        return 0
 
     if unroll:
         for x in range(1, nx + 1):
             plane(x, 0)
     else:
-        lax.fori_loop(1, nx + 1, plane, 0)
+        fine_loop(1, nx, plane, UNROLL)
 
 
 def copy_q(dst, q):
@@ -333,60 +319,219 @@
 
 
 def dot(a, b):
-    return lax.dot_general(a, b, (((1,), (0,)), ((), ())), precision=HI, preferred_element_type=F32)
+    bf = jnp.bfloat16
+    b = b.astype(bf)
+    hi = a.astype(bf)
+    rest = a - hi.astype(F32)
+    mid = rest.astype(bf)
+    lo = (rest - mid.astype(F32)).astype(bf)
+    one = lambda p: lax.dot_general(p, b, (((1,), (0,)), ((), ())), preferred_element_type=F32)
+    return one(hi) + (one(mid) + one(lo))
 
 
 def half_rows(ref, r0, n):
     return ref[pl.ds(r0, n // 2, stride=2)] + ref[pl.ds(r0 + 1, n // 2, stride=2)]
 
 
-def fine_arrays(xp, rows):
-    pad, bare = (xp + 2, rows + 16, 128), (xp, rows, 128)
-    return [pad] * 8 + [bare] * 16
-
-
-def split_fine(s):
+def fine_loop(lo, count, plane, unroll):
+    while count % unroll:
+        unroll -= 1
+
+    def group(i, _):
+        for u in range(unroll):
+            plane(lo + i * unroll + u, 0)
+        return 0
+
+    lax.fori_loop(0, count // unroll, group, 0)
+
+
+def fine_each(m, h, x, tiles, with_h, emit):
+    lane = lanes()
+    hv = h[x]
+    edge = hv
+    for t in tiles:
+        g = GW * t
+        v = m[x, 8 + 8 * t : 16 + 8 * t]
+        beside = rot(hv, -(g + HL))
+        down = jnp.where(lane == 0, beside, rot(v, 1))
+        up = jnp.where(lane == 127, beside, rot(v, -1))
+        six = (
+            m[x - 1, 8 + 8 * t : 16 + 8 * t],
+            m[x + 1, 8 + 8 * t : 16 + 8 * t],
+            m[x, 7 + 8 * t : 15 + 8 * t],
+            m[x, 9 + 8 * t : 17 + 8 * t],
+            down,
+            up,
+        )
+        emit(0, t, v, six)
+        if with_h:
+            edge = jnp.where((lane >= g) & (lane < g + GW), rot(v, g + HL), edge)
+    if with_h:
+        row = lax.broadcasted_iota(jnp.int32, (8, 128), 0)
+        within = lax.rem(lane, GW)
+        above, below = pltpu.roll(hv, 1, 0), pltpu.roll(hv, 7, 0)
+        six = (
+            h[x - 1],
+            h[x + 1],
+            jnp.where(row == 0, rot(above, GW), above),
+            jnp.where(row == 7, rot(below, -GW), below),
+            jnp.where(within == HL - 1, edge, rot(hv, -1)),
+            jnp.where(within == HL, edge, rot(hv, 1)),
+        )
+        emit(1, 0, hv, six)
+
+
+def cut(part, ref, x, t, pad):
+    if part == 1:
+        return (x, slice(0, 8))
+    r = 8 * t + (8 if pad else 0)
+    return (x, slice(r, r + 8))
+
+
+def fine_coef(c, b, a, q, d, lo, count):
+    tiles = range((c[0].shape[1] - 16) // 8)
+
+    def plane(x, _):
+        def emit(part, t, v, six):
+            total = 6.0 * v + (((six[0] + six[1]) + (six[2] + six[3])) + (six[4] + six[5]))
+            inside = v > 0.0
+            g = jnp.where(inside, W / jnp.where(inside, total, 1.0), 0.0)
+            at = cut(part, None, x - 1, t, False)
+            for j in range(6):
+                a[j][part][at] = g * (v + six[j])
+            q[part][at] = g * (2.0 * b[part][cut(part, None, x, t, True)])
+            if part == 0:
+                d[at] = total * (0.5 / W)
+
+        fine_each(c[0], c[1], x, tiles, True, emit)
+
+    fine_loop(lo, count, plane, UNROLL)
+
+
+def gather_sum(a, part, at, six):
+    s = a[0][part][at] * six[0] + a[1][part][at] * six[1]
+    u = a[2][part][at] * six[2] + a[3][part][at] * six[3]
+    w = a[4][part][at] * six[4] + a[5][part][at] * six[5]
+    return (s + u) + w
+
+
+def fine_sweep(src, dst, a, q, lo, count):
+    tiles = range((src[0].shape[1] - 16) // 8)
+
+    def plane(x, _):
+        def emit(part, t, v, six):
+            at = cut(part, None, x - 1, t, False)
+            dst[part][cut(part, None, x, t, True)] = (
+                (1.0 - W) * v + q[part][at]
+            ) + gather_sum(a, part, at, six)
+
+        fine_each(src[0], src[1], x, tiles, True, emit)
+
+    fine_loop(lo, count, plane, UNROLL)
+
+
+def fine_residual(v, a, d, x, b_tile, put):
+    def emit(part, t, val, six):
+        at = cut(part, None, x - 1, t, False)
+        put(t - 1, b_tile(t - 1) - d[at] * (W * val - gather_sum(a, part, at, six)))
+
+    fine_each(v[0], v[1], x, range(1, (v[0].shape[1] - 16) // 8 - 1), False, emit)
+
+
+def fine_range(nsx, nx, extra):
+    off = own_offset(nsx)
+    xp = nx + nsx * HX
+    lo = jnp.maximum(off - extra, 0) + 1
+    return lo, nx + nsx * extra
+
+
+def fine_kept(xp, rows):
+    m, h = (xp, rows, 128), (xp, 8, 128)
+    return [(xp + 2, rows + 16, 128), (xp + 2, 8, 128)] + [m, h] * 7 + [m]
+
+
+def fine_work(xp, rows):
+    return [(xp + 2, rows + 16, 128), (xp + 2, 8, 128)] * 3
+
+
+def split_kept(s):
     two = lambda i: (s[i], s[i + 1])
-    return two(0), two(2), two(4), two(6), [two(8 + 2 * j) for j in range(6)], two(20), two(22)
+    return two(0), [two(2 + 2 * j) for j in range(6)], two(14), s[16]
+
+
+def clear_rim(*pairs):
+    for m, h in pairs:
+        n, rows, _ = m.shape
+        for x in (0, n - 1):
+            m[x] = jnp.zeros(m.shape[1:], F32)
+            h[x] = jnp.zeros(h.shape[1:], F32)
+
+        def one(x, _):
+            m[x, 0:8] = jnp.zeros((8, 128), F32)
+            m[x, rows - 8 : rows] = jnp.zeros((8, 128), F32)
+            return 0
+
+        lax.fori_loop(0, n, one, 0)
 
 
 def load_fine(nsx, na, which, refs_own, r, target):
     for k, own, (m, h) in zip(which, refs_own, target):
-        assemble(nsx, k, plane_map(na, k), m, h, own, r[0], r[1], r[2], r[3], r[4], r[5])
-
-
-def fine_down_kernel(nsx, *refs):
-    c_own, guess, src, r_a, r_b, z_a, z_b = refs[:7]
-    x1, x2 = refs[7 : 7 + nsx], refs[7 + nsx : 7 + 2 * nsx]
+        assemble(nsx, plane_map(na, k), m, h, own, *r)
+
+
+def set_up_fine(nsx, c_own, src, r, c, b, a, q, d):
+    nx = src.shape[0]
+    clear_rim(c)
+    load_fine(nsx, 3, (0, 2), (c_own, src), r, (c, b))
+    lo, count = fine_range(nsx, nx, HX - 1)
+    fine_coef(c, b, a, q, d, lo, count)
+
+
+def fine_sweeps(nsx, nx, v, w, a, q):
+    for _ in range(SWEEPS):
+        lo, count = fine_range(nsx, nx, HX - 1)
+        fine_sweep(v, w, a, q, lo, count)
+        v, w = w, v
+    return v
+
+
+def fine_down_kernel(nsx, keep, *refs):
+    c_own, guess, src = refs[:3]
     n = 7 + 2 * nsx
+    r = refs[3:7] + (refs[7 : 7 + nsx], refs[7 + nsx : n])
     v_out, bc, y_a, y_b = refs[n : n + 4]
     xf = refs[n + 4 : n + 4 + nsx]
     s = refs[n + 4 + nsx :]
-    c, b, v, v2, a, q, d = split_fine(s[:24])
-    pair = s[24]
+    c, a, q, d = split_kept(s[:17])
+    b, v, v2 = (s[17], s[18]), (s[19], s[20]), (s[21], s[22])
+    pair = s[23]
     nx, ny, _ = src.shape
     off = 1 + own_offset(nsx)
-    zero(*c, *b, *v, *v2)
-    load_fine(nsx, 3, (0, 1, 2), (c_own, guess, src), (r_a, r_b, z_a, z_b, x1, x2), (c, v, b))
-    build_coef(c, b, a, q, d, 1.0, False)
-
-    def two(_, carry):
-        sweep(v, v2, a, q)
-        sweep(v2, v, a, q)
-        return carry
-
-    lax.fori_loop(0, SWEEPS // 2, two, 0)
+    set_up_fine(nsx, c_own, src, r, c, b, a, q, d)
+    clear_rim(v, v2)
+    load_fine(nsx, 3, (1,), (guess,), r, (v,))
+    v = fine_sweeps(nsx, nx, v, v2, a, q)
     pb, pc = pick(0, 64, 128), pick(64, 64, 128)
 
     def coarse(i, _):
         x = off + 2 * i
-        for r in chunks(ny):
-            r0 = residual_rows(v, src[2 * i, pl.ds(r, 8)], a, d, x, 8 + r)
-            r1 = residual_rows(v, src[2 * i + 1, pl.ds(r, 8)], a, d, x + 1, 8 + r)
-            pair[0, pl.ds(r, 8)] = r0 + r1
-            pair[1, pl.ds(r, 8)] = c_own[2 * i, pl.ds(r, 8)] + c_own[2 * i + 1, pl.ds(r, 8)]
-            v_out[2 * i, pl.ds(r, 8)] = v[0][x, pl.ds(16 + r, 8)]
-            v_out[2 * i + 1, pl.ds(r, 8)] = v[0][x + 1, pl.ds(16 + r, 8)]
+        rs = [None] * (ny // 8)
+
+        def first(t, val):
+            rs[t] = val
+
+        def second(t, val):
+            pair[0, 8 * t : 8 * t + 8] = rs[t] + val
+
+        for o, put in ((0, first), (1, second)):
+            fine_residual(
+                v, a, d, x + o, lambda t: src[2 * i + o, 8 * t : 8 * t + 8], put
+            )
+        for t in range(ny // 8):
+            w8 = slice(8 * t, 8 * t + 8)
+            pair[1, w8] = c_own[2 * i, w8] + c_own[2 * i + 1, w8]
+            v_out[2 * i, w8] = v[0][x, 16 + 8 * t : 24 + 8 * t]
+            v_out[2 * i + 1, w8] = v[0][x + 1, 16 + 8 * t : 24 + 8 * t]
         bc[i] = dot(half_rows(pair.at[0], 0, ny), pb) + dot(half_rows(pair.at[1], 0, ny), pc)
         return 0
 
@@ -446,11 +591,10 @@
         lax.fori_loop(0, nx // 4, group, 0)
 
 
-def mid_down_kernel(full, r_a, r_b, z_a, z_b, v_out, b_out, c_out, bc, *s):
-    c, b, v, v2 = [(s[i],) for i in range(4)]
-    a = [(s[4 + j],) for j in range(6)]
-    q, d = (s[10],), (s[11],)
-    pair = s[12]
+def mid_down_kernel(keep, full, r_a, r_b, z_a, z_b, v_out, bc, *s):
+    c, b = (s[0],), (s[1],)
+    a = [(s[2 + j],) for j in range(6)]
+    q, d, v, v2, pair = (s[8],), (s[9],), (s[10],), (s[11],), s[12]
     nx, ny, _ = full.shape
     ez = even("gz")
     lane = lanes()
@@ -499,8 +643,6 @@
 
     lax.fori_loop(0, half, coarse, 0)
     v_out[...] = v[0][...]
-    b_out[...] = b[0][...]
-    c_out[...] = c[0][...]
 
 
 def spread(src, dst, mats, c, x_src, x_dst, r_src, n, r_dst, tmp, sets=False):
@@ -523,17 +665,20 @@
     return jnp.where(i == fn(o), 1.0, 0.0).astype(F32)
 
 
-def coarse_kernel(gy, gz, blocks, v1_in, b1, c1, v1_out, *s):
+def coarse_kernel(gy, gz, keep, blocks, v1_in, c1, b1, *s):
+    if keep:
+        a1, q1, s = [(s[j],) for j in range(6)], (s[6],), s[7:]
+    v1_out, s = s[0], s[1:]
+    if not keep:
+        a1, q1, s = [(s[j],) for j in range(6)], (s[6],), s[7:]
     c2, b2, v2, w2 = [(s[i],) for i in range(4)]
     a2 = [(s[4 + j],) for j in range(6)]
     q2, d2 = (s[10],), (s[11],)
     c3, b3, v3, w3 = [(s[12 + i],) for i in range(4)]
     a3 = [(s[16 + j],) for j in range(6)]
     q3 = (s[22],)
-    v1, w1 = (s[23],), (s[24],)
-    a1 = [(s[25 + j],) for j in range(6)]
-    q1 = (s[31],)
-    pair, tmp = s[32], s[33]
+    v1, w1 = (v1_out,), (s[23],)
+    pair, tmp = s[24], s[25]
     iy, iz = lax.axis_index("gy"), lax.axis_index("gz")
     half, yb, _ = blocks.shape[1:]
     lane = lanes(yb)
@@ -600,7 +745,8 @@
         return carry
 
     lax.fori_loop(0, SWEEPS // 2, two2, 0)
-    build_coef((c1,), (b1,), a1, q1, None, 0.25, False)
+    if not keep:
+        build_coef((c1,), (b1,), a1, q1, None, 0.25, False)
     v1[0][...] = v1_in[...]
     rows1 = v1[0].shape[1] - 16
     up = select_mat(lambda o: jnp.where(o < 80, o // 2, jnp.where(o >= 112, (o + 128) // 2, -1)))
@@ -619,58 +765,102 @@
         return carry
 
     lax.fori_loop(0, SWEEPS // 2, two1, 0)
-    v1_out[...] = v1[0][...]
-
-
-def fine_up_kernel(nsx, *refs):
-    c_own, v_own, src, r_a, r_b, z_a, z_b = refs[:7]
-    x1, x2 = refs[7 : 7 + nsx], refs[7 + nsx : 7 + 2 * nsx]
+
+
+def spread_fine(v, c, planes, up, tmp):
+    n = up.shape[0]
+    for half in (0, 1):
+        p = up[:, 128 * half : 128 * half + 128]
+        tmp[half, pl.ds(0, n, stride=2)] = p
+        tmp[half, pl.ds(1, n, stride=2)] = p
+    lane = lanes()
+    edge = jnp.zeros((8, 128), F32)
+    for t in range(2 * n // 8):
+        rows = slice(8 + 8 * t, 16 + 8 * t)
+        par = tmp[0, 8 * t : 8 * t + 8]
+        for x in planes:
+            v[0][x, rows] = v[0][x, rows] + jnp.where(c[0][x, rows] > 0.0, par, 0.0)
+        g = GW * t
+        here = (lane >= g) & (lane < g + GW)
+        edge = jnp.where(here, tmp[1, 8 * t : 8 * t + 8], edge)
+    for x in planes:
+        v[1][x] = v[1][x] + jnp.where(c[1][x] > 0.0, edge, 0.0)
+
+
+def fine_up_kernel(nsx, keep, *refs):
+    c_own, v_own, src = refs[:3]
     n = 7 + 2 * nsx
-    vr_a, vr_b, vz_a, vz_b = refs[n : n + 4]
-    vx1, vx2 = refs[n + 4 : n + 4 + nsx], refs[n + 4 + nsx : n + 4 + 2 * nsx]
+    r = refs[3:7] + (refs[7 : 7 + nsx], refs[7 + nsx : n])
+    vr = refs[n : n + 4] + (refs[n + 4 : n + 4 + nsx], refs[n + 4 + nsx : n + 4 + 2 * nsx])
     n = n + 4 + 2 * nsx
     v1 = refs[n]
-    sol, res = refs[n + 1 : n + 3]
-    s = refs[n + 3 :]
-    c, b, v, v2, a, q, d = split_fine(s[:24])
-    tmp = s[24]
+    n = n + 1
+    if keep:
+        c, a, q, d = split_kept(refs[n : n + 17])
+        n = n + 17
+    sol_hbm, res_hbm = refs[n : n + 2]
+    sol, res, sems = refs[-3:]
+    s = refs[n + 2 : -3]
+    if not keep:
+        c, a, q, d = split_kept(s[:17])
+        s = s[17:]
+    b, v, v2 = (s[0], s[1]), (s[2], s[3]), (s[4], s[5])
+    tmp, stage, spread = s[6:9]
     nx, ny, _ = src.shape
     off = 1 + own_offset(nsx)
-    zero(*c, *b, *v, *v2)
-    load_fine(nsx, 3, (0, 2), (c_own, src), (r_a, r_b, z_a, z_b, x1, x2), (c, b))
-    load_fine(nsx, 1, (0,), (v_own,), (vr_a, vr_b, vz_a, vz_b, vx1, vx2), (v,))
-    build_coef(c, b, a, q, d, 1.0, False)
-    up_m = select_mat(lambda o: o // 2)
-    up_h = select_mat(
-        lambda o: jnp.where(o < 8, 64 + o // 2, jnp.where(o >= 120, (o + 128) // 2, -1))
-    )
+    if not keep:
+        set_up_fine(nsx, c_own, src, r, c, b, a, q, d)
+    clear_rim(v, v2)
+    load_fine(nsx, 1, (0,), (v_own,), vr, (v,))
+    i = lax.broadcasted_iota(jnp.int32, (128, 256), 0)
+    o = lax.broadcasted_iota(jnp.int32, (128, 256), 1)
+    within = lax.rem(o - 128, GW)
+    z = HL - 1 - within
+    par = jnp.where(within < HL, 64 + lax.div(z, 2), 128 + lax.shift_right_arithmetic(z, 1))
+    mat = jnp.where(i == jnp.where(o < 128, lax.div(o, 2), par), 1.0, 0.0).astype(F32)
     nc = v1.shape[0] - 2
     ix = lax.axis_index("gx")
+    half = (ny + 16) // 2
     xp = v[0].shape[0] - 2
-    rows = ny + 16
-
-    def up(p, _):
-        x = jnp.clip(lax.shift_right_arithmetic(nx * ix + p - off, 1), 0, nc - 1)
-        par = v1[1 + x, 20 : 20 + rows // 2]
-        spread(par, v, [up_m, up_h], c, None, (p,), None, rows // 2, 8, tmp)
+    count = (xp + 2) // 2
+    c0 = lax.shift_right_arithmetic(nx * ix + 1 - off, 1)
+    for j in range(count):
+        stage[j * half : (j + 1) * half] = v1[1 + jnp.clip(c0 + j, 0, nc - 1), 20 : 20 + half]
+    spread[...] = dot(stage[...], mat)
+
+    def up(j, _):
+        p = 2 * (c0 + j) - nx * ix + off
+        start = pl.multiple_of(half * j, 8)
+        spread_fine(v, c, (p, p + 1), spread[pl.ds(start, half)], tmp)
         return 0
 
-    lax.fori_loop(1, xp + 1, up, 0)
-
-    def two(_, carry):
-        sweep(v, v2, a, q)
-        sweep(v2, v, a, q)
-        return carry
-
-    lax.fori_loop(0, SWEEPS // 2, two, 0)
+    lax.fori_loop(0, count, up, 0)
+    v = fine_sweeps(nsx, nx, v, v2, a, q)
+
+    step = nx // 4
+
+    def copies(i):
+        at = pl.ds(i * step, step)
+        return (
+            pltpu.make_async_copy(sol.at[at], sol_hbm.at[at], sems.at[0, i]),
+            pltpu.make_async_copy(res.at[at], res_hbm.at[at], sems.at[1, i]),
+        )
 
     def out(x, _):
-        for r in chunks(ny):
-            res[x, pl.ds(r, 8)] = residual_rows(v, src[x, pl.ds(r, 8)], a, d, off + x, 8 + r)
-            sol[x, pl.ds(r, 8)] = v[0][off + x, pl.ds(16 + r, 8)]
-        return 0
-
-    lax.fori_loop(0, nx, out, 0)
+        def put(t, val):
+            w8 = slice(8 * t, 8 * t + 8)
+            res[x, w8] = val
+            sol[x, w8] = v[0][off + x, 16 + 8 * t : 24 + 8 * t]
+
+        fine_residual(v, a, d, off + x, lambda t: src[x, 8 * t : 8 * t + 8], put)
+
+    for i in range(4):
+        fine_loop(i * step, step, out, 2)
+        for cp in copies(i):
+            cp.start()
+    for i in range(4):
+        for cp in copies(i):
+            cp.wait()
 
 
 def named(fn, *args):
@@ -683,10 +873,13 @@
     nx, ny, _ = arrs[0].shape
     rows = ny + 16
     r_a, r_b = swap_even(y_a, "gy"), swap_odd(y_b, "gy")
-    z_a, z_b = call(named(zpack_kernel, na), [(na, rows, 128)] * 2, *arrs, r_a, r_b)
-    z_a, z_b = swap_even(z_a, "gz"), swap_odd(z_b, "gz")
+    (z,) = call(
+        named(zpack_kernel, na), [(na * nx, 8, 128)], *arrs, r_a, r_b,
+        scratch=[(na * nx * 8, 128)],
+    )
+    z_a, z_b = swap_even(z, "gz"), swap_odd(z, "gz")
     count = len(face_list(na))
-    size = count * 16 + -(-count // 8) * rows
+    size = count * 24
     xs = call(named(xframe_kernel, na, nx, nsx), [(size, 128)] * nsx, r_a, r_b, z_a, z_b)
     x2 = swap_x(xs)
     return (r_a, r_b, z_a, z_b), x2
@@ -716,12 +909,18 @@
     c_own, y_a, y_b, xs = out[0], out[1], out[2], out[3:]
     x1 = swap_x(xs)
     rec, x2 = exchange_rest(3, (c_own, first_guess, source), y_a, y_b, nsx)
+    keep = gx == 2
+    kept_shapes = fine_kept(xp, rows)
+    outs = [full, (nx // 2, ny // 2, 128), (nx, 8, 128), (nx, 8, 128)] + [(HX, ny, 128)] * nsx
+    work = fine_work(xp, rows) + [(2, ny, 128)]
     out = call(
-        named(fine_down_kernel, nsx),
-        [full, (nx // 2, ny // 2, 128), (nx, 8, 128), (nx, 8, 128)] + [(HX, ny, 128)] * nsx,
+        named(fine_down_kernel, nsx, keep),
+        outs + (kept_shapes if keep else []),
         c_own, first_guess, source, *rec, *x1, *x2,
-        scratch=fine_arrays(xp, rows) + [(2, ny, 128)],
+        scratch=work if keep else kept_shapes + work,
     )
+    kept = out[len(outs) :]
+    out = out[: len(outs)]
     v0, bc1, vy_a, vy_b, vxs = out[0], out[1], out[2], out[3], out[4:]
 
     n1 = gx * nx // 2
@@ -738,12 +937,14 @@
     z_a, z_b = call(mid_z_kernel, [(n1 // 4, rows1, 128)] * 2, f1, r_a, r_b)
     z_a, z_b = swap_even(z_a, "gz"), swap_odd(z_b, "gz")
     pad1, bare1 = (n1 + 2, rows1 + 16, 128), (n1, rows1, 128)
-    v1, b1, c1, bc2 = call(
-        mid_down_kernel,
-        [pad1] * 3 + [(n1 // 4, ny1 // 2, 128)],
+    out = call(
+        named(mid_down_kernel, keep),
+        [pad1, (n1 // 4, ny1 // 2, 128), pad1, pad1] + ([bare1] * 7 if keep else []),
         f1, r_a, r_b, z_a, z_b,
-        scratch=[pad1] * 4 + [bare1] * 8 + [(2, ny1, 128)],
+        scratch=([] if keep else [bare1] * 7) + [bare1, pad1, pad1, (2, ny1, 128)],
     )
+    v1, bc2, c1, b1 = out[:4]
+    kept1 = out[4:]
 
     got = jnp.stack([bc2] + [swap_xor(bc2, "gy", m) for m in range(1, gy)])
     bit = gz // 2
@@ -759,17 +960,22 @@
     pad2, bare2 = (n2 + 2, ny2 + 16, 128), (n2, ny2, 128)
     pad3, bare3 = (n3 + 2, ny3 + 16, 128), (n3, ny3, 128)
     (v1,) = call(
-        named(coarse_kernel, gy, gz),
+        named(coarse_kernel, gy, gz, keep),
         [pad1],
-        got, v1, b1, c1,
-        scratch=[pad2] * 4 + [bare2] * 8 + [pad3] * 4 + [bare3] * 7 + [pad1] * 2 + [bare1] * 7
+        got, v1, c1, b1, *kept1,
+        scratch=([] if keep else [bare1] * 7)
+        + [pad2] * 4 + [bare2] * 8 + [pad3] * 4 + [bare3] * 7 + [pad1]
         + [(2, ny2, 128), (1, max(rows1, ny2), 128)],
     )
+    par_rows = (xp + 2) // 2 * (rows // 2)
+    work = fine_work(xp, rows) + [(2, rows, 128), (par_rows, 128), (par_rows, 256)]
     sol, res = call(
-        named(fine_up_kernel, nsx),
+        named(fine_up_kernel, nsx, keep),
         [full, full],
-        c_own, v0, source, *rec, *x1, *x2, *vrec, *vx1, *vx2, v1,
-        scratch=fine_arrays(xp, rows) + [(2, rows, 128)],
+        c_own, v0, source, *rec, *x1, *x2, *vrec, *vx1, *vx2, v1, *kept,
+        scratch=(work if keep else kept_shapes + work) + [full, full],
+        hbm_out=True,
+        more=[pltpu.SemaphoreType.DMA((2, 4))],
     )
     return sol, res
 

time: 154 us -> 117 us (0.76)
  Pallas kernels: 79.7 us -> 43.3 us
  local copies, waits for them, and re-layouts: 5.44 us -> 3.84 us
    pallas_call x11, Pallas kernels: 79.7 us -> 43.3 us  [call(): pl.pallas_call(body, out_shape=shapes, in_specs=specs, out_specs=[pl.Bloc...]
    unnamed x18 -> x16, local copies, waits for them, and re-layouts: 5.4 us -> 3.81 us
  transfers between devices with their start and end apart: 22 -> 22, of which waited for: 11 -> 11; matrix products, arithmetic and copies ran while one was open for 0% -> 0% of each run, Pallas kernels for 15% -> 12%
where the time goes in v3:
time: 117 us; the launch traced here: 115 us
  Pallas kernels  43.3 us (37%)
  starting transfers between devices  39.6 us (34%)
  waiting for transfers between devices  27.4 us (23%)
  local copies, waits for them, and re-layouts  3.84 us (3%)
    pallas_call x11, Pallas kernels, call(): pl.pallas_call(body, out_shape=shapes, in_specs=specs, out_specs=[pl.Bloc...  43.3 us
    ppermute x11, starting transfers between devices, swap_even(): return lax.ppermute(x, axis, pairs_even(lax.axis_size(axis)))  16 us
    ppermute x6, starting transfers between devices, swap_odd(): return lax.ppermute(x, axis, pairs_odd(lax.axis_size(axis)))  14.7 us
    ppermute x11, waiting for transfers between devices, swap_even(): return lax.ppermute(x, axis, pairs_even(lax.axis_size(axis)))  12.5 us
    ppermute x5, starting transfers between devices, swap_xor(): lax.ppermute(x, axis, [(i, i ^ m) for i in range(lax.axis_size(axis))])  8.89 us
    ppermute x6, waiting for transfers between devices, swap_odd(): return lax.ppermute(x, axis, pairs_odd(lax.axis_size(axis)))  7.63 us
    ppermute x5, waiting for transfers between devices, swap_xor(): lax.ppermute(x, axis, [(i, i ^ m) for i in range(lax.axis_size(axis))])  7.21 us
    unnamed x16, local copies, waits for them, and re-layouts  3.81 us
  transfers between devices with their start and end apart: 22, of which 11 were waited for; matrix products, arithmetic and copies ran while one was open for 0% of the time, Pallas kernels for 12%

profile of v3, /device:TPU:1, one launch (start us, length us, event | category | flops | bytes accessed | tf_op | source)
XLA Modules:
  0.0 114.9 jit_solution(2579148751727611672)
XLA Ops:
  1.7 1.0 copy-done.2
  2.7 1.0 copy-done.4
  5.4 2.2 %collective-permute-start = (f32[48,8,128]{2,1,0:T(8,128)S(1)}, f32[48,8,128]{2,1,0:T(8,128)S(1)}, u32[]{:S(2)}, u32[]{:S(2)}) collective-permute-start(f32[48,8,128]{2,1,0:T(8,128)S(1)} %get-tuple-element.45), channel_id=1, source_target_pairs={{0,4},{4,0},{8,12},{12,8},{1,5},{5,1},{9,13},{13,9},{2,6},{6,2},{1... | collective-permute-start | bytes 589832 | tf_op jit(solution)/shard_map/ppermute | solution.py:35
  8.2 1.3 %collective-permute-start.4 = (f32[14,64,128]{2,1,0:T(8,128)S(1)}, f32[14,64,128]{2,1,0:T(8,128)S(1)}, u32[]{:S(2)}, u32[]{:S(2)}) collective-permute-start(f32[14,64,128]{2,1,0:T(8,128)S(1)} %get-tuple-element.47), channel_id=1, source_target_pairs={{0,16},{16,0},{1,17},{17,1},{2,18},{18,2},{3,19},{19,3},{4,20},{20... | collective-permute-start | bytes 1376264 | tf_op jit(solution)/shard_map/ppermute | solution.py:35
  9.5 2.7 %collective-permute-done.refs_3_.r_a = f32[48,8,128]{2,1,0:T(8,128)S(1)} collective-permute-done((f32[48,8,128]{2,1,0:T(8,128)S(1)}, f32[48,8,128]{2,1,0:T(8,128)S(1)}, u32[]{:S(2)}, u32[]{:S(2)}) %collective-permute-start) | collective-permute-done | bytes 196640 | tf_op jit(solution)/shard_map/ppermute | solution.py:35
  12.9 1.3 %collective-permute-start.2 = (f32[48,8,128]{2,1,0:T(8,128)S(1)}, f32[48,8,128]{2,1,0:T(8,128)S(1)}, u32[]{:S(2)}, u32[]{:S(2)}) collective-permute-start(f32[48,8,128]{2,1,0:T(8,128)S(1)} %zpack_kernel.2), channel_id=1, source_target_pairs={{0,1},{1,0},{2,3},{3,2},{4,5},{5,4},{6,7},{7,6},{8,9},{9,8},{10,11... | collective-permute-start | bytes 589832 | tf_op jit(solution)/shard_map/ppermute | solution.py:35
  14.2 3.2 %collective-permute-start.3 = (f32[48,8,128]{2,1,0:T(8,128)S(1)}, f32[48,8,128]{2,1,0:T(8,128)S(1)}, u32[]{:S(2)}, u32[]{:S(2)}) collective-permute-start(f32[48,8,128]{2,1,0:T(8,128)S(1)} %zpack_kernel.2), channel_id=1, source_target_pairs={{1,2},{2,1},{5,6},{6,5},{9,10},{10,9},{13,14},{14,13},{17,18},{18,... | collective-permute-start | bytes 589832 | tf_op jit(solution)/shard_map/ppermute | solution.py:39
  17.5 4.0 %collective-permute-done.3.z_b.refs_6_ = f32[48,8,128]{2,1,0:T(8,128)S(1)} collective-permute-done((f32[48,8,128]{2,1,0:T(8,128)S(1)}, f32[48,8,128]{2,1,0:T(8,128)S(1)}, u32[]{:S(2)}, u32[]{:S(2)}) %collective-permute-start.3) | collective-permute-done | bytes 196640 | tf_op jit(solution)/shard_map/ppermute | solution.py:39
  21.5 1.4 %collective-permute-start.5 = (f32[336,128]{1,0:T(8,128)S(1)}, f32[336,128]{1,0:T(8,128)S(1)}, u32[]{:S(2)}, u32[]{:S(2)}) collective-permute-start(f32[336,128]{1,0:T(8,128)S(1)} %xframe_kernel.2), channel_id=1, source_target_pairs={{0,16},{16,0},{1,17},{17,1},{2,18},{18,2},{3,19},{19,3},{4,20},{20... | collective-permute-start | bytes 516104 | tf_op jit(solution)/shard_map/ppermute | solution.py:35
  23.0 2.9 %collective-permute-done.5.refs_8_ = f32[336,128]{1,0:T(8,128)S(1)} collective-permute-done((f32[336,128]{1,0:T(8,128)S(1)}, f32[336,128]{1,0:T(8,128)S(1)}, u32[]{:S(2)}, u32[]{:S(2)}) %collective-permute-start.5) | collective-permute-done | bytes 172064 | tf_op jit(solution)/shard_map/ppermute | solution.py:35
  25.9 10.6 %fine_down_kernel.1 = (f32[16,64,128]{2,1,0:T(8,128)S(1)}, f32[8,32,128]{2,1,0:T(8,128)S(1)}, f32[16,8,128]{2,1,0:T(8,128)S(1)}, f32[16,8,128]{2,1,0:T(8,128)S(1...) custom-call(f32[16,64,128]{2,1,0:T(8,128)S(1)} %get-tuple-element.44, ...), custom_call_target="tpu_custom_call" | custom-call | tf_op jit(solution)/shard_map/fine_down_kernel/pallas_call | solution.py:58
  36.5 1.5 %collective-permute-start.12 = (f32[8,32,128]{2,1,0:T(8,128)S(1)}, f32[8,32,128]{2,1,0:T(8,128)S(1)}, u32[]{:S(2)}, u32[]{:S(2)}) collective-permute-start(f32[8,32,128]{2,1,0:T(8,128)S(1)} %get-tuple-element.52.refs_0_), channel_id=1, source_target_pairs={{0,16},{16,0},{1,17},{17,1},{2,18},{18,2},{3,19},{19,3},{4,20},{20... | collective-permute-start | bytes 393224 | tf_op jit(solution)/shard_map/ppermute | solution.py:35
  38.0 2.4 %collective-permute-done.12.refs_1_ = f32[8,32,128]{2,1,0:T(8,128)S(1)} collective-permute-done((f32[8,32,128]{2,1,0:T(8,128)S(1)}, f32[8,32,128]{2,1,0:T(8,128)S(1)}, u32[]{:S(2)}, u32[]{:S(2)}) %collective-permute-start.12) | collective-permute-done | bytes 131104 | tf_op jit(solution)/shard_map/ppermute | solution.py:35
  40.4 4.5 %collective-permute-start.13 = (f32[16,16,128]{2,1,0:T(8,128)S(1)}, f32[16,16,128]{2,1,0:T(8,128)S(1)}, u32[]{:S(2)}, u32[]{:S(2)}) collective-permute-start(f32[16,16,128]{2,1,0:T(8,128)S(1)} %get-tuple-element.54), channel_id=1, source_target_pairs={{0,4},{4,0},{8,12},{12,8},{1,5},{5,1},{9,13},{13,9},{2,6},{6,2},{1... | collective-permute-start | bytes 393224 | tf_op jit(solution)/shard_map/ppermute | solution.py:35
  45.6 1.7 %collective-permute-done.13.r_a = f32[16,16,128]{2,1,0:T(8,128)S(1)} collective-permute-done((f32[16,16,128]{2,1,0:T(8,128)S(1)}, f32[16,16,128]{2,1,0:T(8,128)S(1)}, u32[]{:S(2)}, u32[]{:S(2)}) %collective-permute-start.13) | collective-permute-done | bytes 131104 | tf_op jit(solution)/shard_map/ppermute | solution.py:35
  47.3 2.4 %mid_z_kernel.1 = (f32[4,64,128]{2,1,0:T(8,128)S(1)}, f32[4,64,128]{2,1,0:T(8,128)S(1)}) custom-call(f32[16,32,128]{2,1,0:T(8,128)S(1)} %get-tuple-element.53.full, f32[16,16,128]{2,1,0:T(8,128)S(1)} %collective-permute-done.13.r_a, f32[16,16,128]{2,1,0:T(8,128)S(1)} %collective-permute-done.14.r_b), custom_call_target="tpu_custom_call" | custom-call | tf_op jit(solution)/shard_map/mid_z_kernel/pallas_call | solution.py:58
  49.7 5.9 %collective-permute-start.16 = (f32[4,64,128]{2,1,0:T(8,128)S(1)}, f32[4,64,128]{2,1,0:T(8,128)S(1)}, u32[]{:S(2)}, u32[]{:S(2)}) collective-permute-start(f32[4,64,128]{2,1,0:T(8,128)S(1)} %get-tuple-element.57), channel_id=1, source_target_pairs={{1,2},{2,1},{5,6},{6,5},{9,10},{10,9},{13,14},{14,13},{17,18},{18,... | collective-permute-start | bytes 393224 | tf_op jit(solution)/shard_map/ppermute | solution.py:39
  55.7 2.6 %collective-permute-done.16.z_b = f32[4,64,128]{2,1,0:T(8,128)S(1)} collective-permute-done((f32[4,64,128]{2,1,0:T(8,128)S(1)}, f32[4,64,128]{2,1,0:T(8,128)S(1)}, u32[]{:S(2)}, u32[]{:S(2)}) %collective-permute-start.16) | collective-permute-done | bytes 131104 | tf_op jit(solution)/shard_map/ppermute | solution.py:39
  58.3 7.2 %mid_down_kernel.1 = (f32[18,80,128]{2,1,0:T(8,128)S(1)}, f32[4,16,128]{2,1,0:T(8,128)S(1)}, f32[18,80,128]{2,1,0:T(8,128)S(1)}, f32[18,80,128]{2,1,0:T(8,128)S(...) custom-call(f32[16,32,128]{2,1,0:T(8,128)S(1)} %get-tuple-element.53, ...), custom_call_target="tpu_custom_call" | custom-call | tf_op jit(solution)/shard_map/mid_down_kernel/pallas_call | solution.py:58
  65.6 3.7 %collective-permute-start.17 = (f32[4,16,128]{2,1,0:T(8,128)S(1)}, f32[4,16,128]{2,1,0:T(8,128)S(1)}, u32[]{:S(2)}, u32[]{:S(2)}) collective-permute-start(f32[4,16,128]{2,1,0:T(8,128)S(1)} %get-tuple-element.58), channel_id=1, source_target_pairs={{0,4},{4,0},{8,12},{12,8},{1,5},{5,1},{9,13},{13,9},{2,6},{6,2},{1... | collective-permute-start | bytes 98312 | tf_op jit(solution)/shard_map/ppermute | solution.py:43
  69.3 1.2 %collective-permute-start.18 = (f32[4,16,128]{2,1,0:T(8,128)S(1)}, f32[4,16,128]{2,1,0:T(8,128)S(1)}, u32[]{:S(2)}, u32[]{:S(2)}) collective-permute-start(f32[4,16,128]{2,1,0:T(8,128)S(1)} %get-tuple-element.58), channel_id=1, source_target_pairs={{0,8},{4,12},{8,0},{12,4},{1,9},{5,13},{9,1},{13,5},{2,10},{6,14},... | collective-permute-start | bytes 98312 | tf_op jit(solution)/shard_map/ppermute | solution.py:43
  70.5 1.1 collective-permute-start.19
  71.6 1.3 %collective-permute-done.18 = f32[4,16,128]{2,1,0:T(8,128)S(1)} collective-permute-done((f32[4,16,128]{2,1,0:T(8,128)S(1)}, f32[4,16,128]{2,1,0:T(8,128)S(1)}, u32[]{:S(2)}, u32[]{:S(2)}) %collective-permute-start.18) | collective-permute-done | bytes 32800 | tf_op jit(solution)/shard_map/ppermute | solution.py:43
  72.9 2.1 %collective-permute-done.19 = f32[4,16,128]{2,1,0:T(8,128)S(1)} collective-permute-done((f32[4,16,128]{2,1,0:T(8,128)S(1)}, f32[4,16,128]{2,1,0:T(8,128)S(1)}, u32[]{:S(2)}, u32[]{:S(2)}) %collective-permute-start.19) | collective-permute-done | bytes 32800 | tf_op jit(solution)/shard_map/ppermute | solution.py:43
  75.2 3.8 %collective-permute-done.20 = f32[4,4,16,128]{3,2,1,0:T(8,128)S(1)} collective-permute-done((f32[4,4,16,128]{3,2,1,0:T(8,128)S(1)}, f32[4,4,16,128]{3,2,1,0:T(8,128)S(1)}, u32[]{:S(2)}, u32[]{:S(2)}) %collective-permute-start.20) | collective-permute-done | bytes 131104 | tf_op jit(solution)/shard_map/ppermute | solution.py:43
  79.0 2.8 %collective-permute-start.21 = (f32[8,4,16,128]{3,2,1,0:T(8,128)S(1)}, f32[8,4,16,128]{3,2,1,0:T(8,128)S(1)}, u32[]{:S(2)}, u32[]{:S(2)}) collective-permute-start(f32[8,4,16,128]{3,2,1,0:T(8,128)S(1)} %get-tuple-element.86), channel_id=1, source_target_pairs={{0,1},{1,0},{2,3},{3,2},{4,5},{5,4},{6,7},{7,6},{8,9},{9,8},{10,11... | collective-permute-start | bytes 786440 | tf_op jit(solution)/shard_map/ppermute | solution.py:43
  82.4 2.9 %collective-permute-done.6.refs_1_.r_a.refs_9_ = f32[16,8,128]{2,1,0:T(8,128)S(1)} collective-permute-done((f32[16,8,128]{2,1,0:T(8,128)S(1)}, f32[16,8,128]{2,1,0:T(8,128)S(1)}, u32[]{:S(2)}, u32[]{:S(2)}) %collective-permute-start.6) | collective-permute-done | bytes 65568 | tf_op jit(solution)/shard_map/ppermute | solution.py:35
  86.7 3.5 %collective-permute-start.9 = (f32[16,8,128]{2,1,0:T(8,128)S(1)}, f32[16,8,128]{2,1,0:T(8,128)S(1)}, u32[]{:S(2)}, u32[]{:S(2)}) collective-permute-start(f32[16,8,128]{2,1,0:T(8,128)S(1)} %zpack_kernel.3), channel_id=1, source_target_pairs={{1,2},{2,1},{5,6},{6,5},{9,10},{10,9},{13,14},{14,13},{17,18},{18,... | collective-permute-start | bytes 196616 | tf_op jit(solution)/shard_map/ppermute | solution.py:39
  90.3 1.4 %collective-permute-start.10 = (f32[5,64,128]{2,1,0:T(8,128)S(1)}, f32[5,64,128]{2,1,0:T(8,128)S(1)}, u32[]{:S(2)}, u32[]{:S(2)}) collective-permute-start(f32[5,64,128]{2,1,0:T(8,128)S(1)} %get-tuple-element.51), channel_id=1, source_target_pairs={{0,16},{16,0},{1,17},{17,1},{2,18},{18,2},{3,19},{19,3},{4,20},{20... | collective-permute-start | bytes 491528 | tf_op jit(solution)/shard_map/ppermute | solution.py:35
  92.6 1.4 %collective-permute-start.11 = (f32[120,128]{1,0:T(8,128)S(1)}, f32[120,128]{1,0:T(8,128)S(1)}, u32[]{:S(2)}, u32[]{:S(2)}) collective-permute-start(f32[120,128]{1,0:T(8,128)S(1)} %xframe_kernel.3), channel_id=1, source_target_pairs={{0,16},{16,0},{1,17},{17,1},{2,18},{18,2},{3,19},{19,3},{4,20},{20... | collective-permute-start | bytes 184328 | tf_op jit(solution)/shard_map/ppermute | solution.py:35
  94.0 12.2 %coarse_kernel.1.refs_15_ = f32[18,80,128]{2,1,0:T(8,128)S(1)} custom-call(f32[16,4,16,128]{3,2,1,0:T(8,128)S(1)} %constant_dynamic-update-slice_fusion.5.blocks, f32[18,80,128]{2,1,0:T(8,128)S(1)} %get-tuple-element.59.v1_in, f32[18,80,128]{2,1,0:T(8,128)S(1)} %get-tuple-element.60.c1, f32[18,80,128]{2,1,0:T(8,128)S(1)} %get-tuple-element.61.b1, ...), custom_call_target="tpu_custom_call" | custom-call | tf_op jit(solution)/shard_map/coarse_kernel/pallas_call | solution.py:58
  106.3 8.7 %fine_up_kernel.1 = (f32[16,64,128]{2,1,0:T(8,128)}, f32[16,64,128]{2,1,0:T(8,128)}) custom-call(f32[16,64,128]{2,1,0:T(8,128)S(1)} %get-tuple-element.44.refs_0_, f32[16,64,128]{2,1,0:T(8,128)S(1)} %get-tuple-element.48.refs_0_.refs_1_, f32[16,64,128]{2,1,0:T(8,128)S(1)} %copy-done.1, f32[48,8,128]{2,1,0:T(8,128)S(1)} %collective-permute-done.refs_3_.r_a, ...), custom_call_target="tpu_custom_call" | custom-call | tf_op jit(solution)/shard_map/fine_up_kernel/pallas_call | solution.py:58
  (42 shorter events, 8.0 us)
Async XLA Ops:
  0.6 1.0 copy-start
  1.7 1.0 copy-start.2
  2.7 1.0 copy-start.4
  3.8 0.7 copy-start.5
  4.4 7.8 %copy-start.1 = (f32[16,64,128]{2,1,0:T(8,128)S(1)}, f32[16,64,128]{2,1,0:T(8,128)}, u32[]{:S(2)}) copy-start(f32[16,64,128]{2,1,0:T(8,128)} %refs_2_.5) | copy-start | bytes 1572868
  5.4 6.8 %collective-permute-start = (f32[48,8,128]{2,1,0:T(8,128)S(1)}, f32[48,8,128]{2,1,0:T(8,128)S(1)}, u32[]{:S(2)}, u32[]{:S(2)}) collective-permute-start(f32[48,8,128]{2,1,0:T(8,128)S(1)} %get-tuple-element.45), channel_id=1, source_target_pairs={{0,4},{4,0},{8,12},{12,8},{1,5},{5,1},{9,13},{13,9},{2,6},{6,2},{1... | collective-permute-start | bytes 589832 | tf_op jit(solution)/shard_map/ppermute | solution.py:35
  7.6 4.6 %collective-permute-start.1 = (f32[48,8,128]{2,1,0:T(8,128)S(1)}, f32[48,8,128]{2,1,0:T(8,128)S(1)}, u32[]{:S(2)}, u32[]{:S(2)}) collective-permute-start(f32[48,8,128]{2,1,0:T(8,128)S(1)} %get-tuple-element.46), channel_id=1, source_target_pairs={{4,8},{8,4},{5,9},{9,5},{6,10},{10,6},{7,11},{11,7},{20,24},{24,20... | collective-permute-start | bytes 589832 | tf_op jit(solution)/shard_map/ppermute | solution.py:39
  8.2 14.7 %collective-permute-start.4 = (f32[14,64,128]{2,1,0:T(8,128)S(1)}, f32[14,64,128]{2,1,0:T(8,128)S(1)}, u32[]{:S(2)}, u32[]{:S(2)}) collective-permute-start(f32[14,64,128]{2,1,0:T(8,128)S(1)} %get-tuple-element.47), channel_id=1, source_target_pairs={{0,16},{16,0},{1,17},{17,1},{2,18},{18,2},{3,19},{19,3},{4,20},{20... | collective-permute-start | bytes 1376264 | tf_op jit(solution)/shard_map/ppermute | solution.py:35
  12.2 13.7 %copy-start.3 = (f32[16,64,128]{2,1,0:T(8,128)S(1)}, f32[16,64,128]{2,1,0:T(8,128)}, u32[]{:S(2)}) copy-start(f32[16,64,128]{2,1,0:T(8,128)} %refs_1_.3) | copy-start | bytes 1572868
  12.9 4.5 %collective-permute-start.2 = (f32[48,8,128]{2,1,0:T(8,128)S(1)}, f32[48,8,128]{2,1,0:T(8,128)S(1)}, u32[]{:S(2)}, u32[]{:S(2)}) collective-permute-start(f32[48,8,128]{2,1,0:T(8,128)S(1)} %zpack_kernel.2), channel_id=1, source_target_pairs={{0,1},{1,0},{2,3},{3,2},{4,5},{5,4},{6,7},{7,6},{8,9},{9,8},{10,11... | collective-permute-start | bytes 589832 | tf_op jit(solution)/shard_map/ppermute | solution.py:35
  14.2 7.3 %collective-permute-start.3 = (f32[48,8,128]{2,1,0:T(8,128)S(1)}, f32[48,8,128]{2,1,0:T(8,128)S(1)}, u32[]{:S(2)}, u32[]{:S(2)}) collective-permute-start(f32[48,8,128]{2,1,0:T(8,128)S(1)} %zpack_kernel.2), channel_id=1, source_target_pairs={{1,2},{2,1},{5,6},{6,5},{9,10},{10,9},{13,14},{14,13},{17,18},{18,... | collective-permute-start | bytes 589832 | tf_op jit(solution)/shard_map/ppermute | solution.py:39
  21.5 4.3 %collective-permute-start.5 = (f32[336,128]{1,0:T(8,128)S(1)}, f32[336,128]{1,0:T(8,128)S(1)}, u32[]{:S(2)}, u32[]{:S(2)}) collective-permute-start(f32[336,128]{1,0:T(8,128)S(1)} %xframe_kernel.2), channel_id=1, source_target_pairs={{0,16},{16,0},{1,17},{17,1},{2,18},{18,2},{3,19},{19,3},{4,20},{20... | collective-permute-start | bytes 516104 | tf_op jit(solution)/shard_map/ppermute | solution.py:35
  36.5 3.9 %collective-permute-start.12 = (f32[8,32,128]{2,1,0:T(8,128)S(1)}, f32[8,32,128]{2,1,0:T(8,128)S(1)}, u32[]{:S(2)}, u32[]{:S(2)}) collective-permute-start(f32[8,32,128]{2,1,0:T(8,128)S(1)} %get-tuple-element.52.refs_0_), channel_id=1, source_target_pairs={{0,16},{16,0},{1,17},{17,1},{2,18},{18,2},{3,19},{19,3},{4,20},{20... | collective-permute-start | bytes 393224 | tf_op jit(solution)/shard_map/ppermute | solution.py:35
  40.4 6.9 %collective-permute-start.13 = (f32[16,16,128]{2,1,0:T(8,128)S(1)}, f32[16,16,128]{2,1,0:T(8,128)S(1)}, u32[]{:S(2)}, u32[]{:S(2)}) collective-permute-start(f32[16,16,128]{2,1,0:T(8,128)S(1)} %get-tuple-element.54), channel_id=1, source_target_pairs={{0,4},{4,0},{8,12},{12,8},{1,5},{5,1},{9,13},{13,9},{2,6},{6,2},{1... | collective-permute-start | bytes 393224 | tf_op jit(solution)/shard_map/ppermute | solution.py:35
  44.9 2.4 %collective-permute-start.14 = (f32[16,16,128]{2,1,0:T(8,128)S(1)}, f32[16,16,128]{2,1,0:T(8,128)S(1)}, u32[]{:S(2)}, u32[]{:S(2)}) collective-permute-start(f32[16,16,128]{2,1,0:T(8,128)S(1)} %get-tuple-element.55), channel_id=1, source_target_pairs={{4,8},{8,4},{5,9},{9,5},{6,10},{10,6},{7,11},{11,7},{20,24},{24,20... | collective-permute-start | bytes 393224 | tf_op jit(solution)/shard_map/ppermute | solution.py:39
  49.7 6.0 %collective-permute-start.15 = (f32[4,64,128]{2,1,0:T(8,128)S(1)}, f32[4,64,128]{2,1,0:T(8,128)S(1)}, u32[]{:S(2)}, u32[]{:S(2)}) collective-permute-start(f32[4,64,128]{2,1,0:T(8,128)S(1)} %get-tuple-element.56), channel_id=1, source_target_pairs={{0,1},{1,0},{2,3},{3,2},{4,5},{5,4},{6,7},{7,6},{8,9},{9,8},{10,11... | collective-permute-start | bytes 393224 | tf_op jit(solution)/shard_map/ppermute | solution.py:35
  49.7 8.6 %collective-permute-start.16 = (f32[4,64,128]{2,1,0:T(8,128)S(1)}, f32[4,64,128]{2,1,0:T(8,128)S(1)}, u32[]{:S(2)}, u32[]{:S(2)}) collective-permute-start(f32[4,64,128]{2,1,0:T(8,128)S(1)} %get-tuple-element.57), channel_id=1, source_target_pairs={{1,2},{2,1},{5,6},{6,5},{9,10},{10,9},{13,14},{14,13},{17,18},{18,... | collective-permute-start | bytes 393224 | tf_op jit(solution)/shard_map/ppermute | solution.py:39
  65.6 6.1 %collective-permute-start.17 = (f32[4,16,128]{2,1,0:T(8,128)S(1)}, f32[4,16,128]{2,1,0:T(8,128)S(1)}, u32[]{:S(2)}, u32[]{:S(2)}) collective-permute-start(f32[4,16,128]{2,1,0:T(8,128)S(1)} %get-tuple-element.58), channel_id=1, source_target_pairs={{0,4},{4,0},{8,12},{12,8},{1,5},{5,1},{9,13},{13,9},{2,6},{6,2},{1... | collective-permute-start | bytes 98312 | tf_op jit(solution)/shard_map/ppermute | solution.py:43
  69.3 3.7 %collective-permute-start.18 = (f32[4,16,128]{2,1,0:T(8,128)S(1)}, f32[4,16,128]{2,1,0:T(8,128)S(1)}, u32[]{:S(2)}, u32[]{:S(2)}) collective-permute-start(f32[4,16,128]{2,1,0:T(8,128)S(1)} %get-tuple-element.58), channel_id=1, source_target_pairs={{0,8},{4,12},{8,0},{12,4},{1,9},{5,13},{9,1},{13,5},{2,10},{6,14},... | collective-permute-start | bytes 98312 | tf_op jit(solution)/shard_map/ppermute | solution.py:43
  70.5 4.6 %collective-permute-start.19 = (f32[4,16,128]{2,1,0:T(8,128)S(1)}, f32[4,16,128]{2,1,0:T(8,128)S(1)}, u32[]{:S(2)}, u32[]{:S(2)}) collective-permute-start(f32[4,16,128]{2,1,0:T(8,128)S(1)} %get-tuple-element.58), channel_id=1, source_target_pairs={{0,12},{4,8},{8,4},{12,0},{1,13},{5,9},{9,5},{13,1},{2,14},{6,10},... | collective-permute-start | bytes 98312 | tf_op jit(solution)/shard_map/ppermute | solution.py:43
  75.1 3.9 %collective-permute-start.20 = (f32[4,4,16,128]{3,2,1,0:T(8,128)S(1)}, f32[4,4,16,128]{3,2,1,0:T(8,128)S(1)}, u32[]{:S(2)}, u32[]{:S(2)}) collective-permute-start(f32[4,4,16,128]{3,2,1,0:T(8,128)S(1)} %pad_maximum_fusion), channel_id=1, source_target_pairs={{0,2},{1,3},{2,0},{3,1},{4,6},{5,7},{6,4},{7,5},{8,10},{9,11},{10,... | collective-permute-start | bytes 393224 | tf_op jit(solution)/shard_map/ppermute | solution.py:43
  79.0 15.0 %collective-permute-start.21 = (f32[8,4,16,128]{3,2,1,0:T(8,128)S(1)}, f32[8,4,16,128]{3,2,1,0:T(8,128)S(1)}, u32[]{:S(2)}, u32[]{:S(2)}) collective-permute-start(f32[8,4,16,128]{3,2,1,0:T(8,128)S(1)} %get-tuple-element.86), channel_id=1, source_target_pairs={{0,1},{1,0},{2,3},{3,2},{4,5},{5,4},{6,7},{7,6},{8,9},{9,8},{10,11... | collective-permute-start | bytes 786440 | tf_op jit(solution)/shard_map/ppermute | solution.py:43
  81.8 3.6 %collective-permute-start.6 = (f32[16,8,128]{2,1,0:T(8,128)S(1)}, f32[16,8,128]{2,1,0:T(8,128)S(1)}, u32[]{:S(2)}, u32[]{:S(2)}) collective-permute-start(f32[16,8,128]{2,1,0:T(8,128)S(1)} %get-tuple-element.49), channel_id=1, source_target_pairs={{0,4},{4,0},{8,12},{12,8},{1,5},{5,1},{9,13},{13,9},{2,6},{6,2},{1... | collective-permute-start | bytes 196616 | tf_op jit(solution)/shard_map/ppermute | solution.py:35
  81.8 3.6 %collective-permute-start.7 = (f32[16,8,128]{2,1,0:T(8,128)S(1)}, f32[16,8,128]{2,1,0:T(8,128)S(1)}, u32[]{:S(2)}, u32[]{:S(2)}) collective-permute-start(f32[16,8,128]{2,1,0:T(8,128)S(1)} %get-tuple-element.50), channel_id=1, source_target_pairs={{4,8},{8,4},{5,9},{9,5},{6,10},{10,6},{7,11},{11,7},{20,24},{24,20... | collective-permute-start | bytes 196616 | tf_op jit(solution)/shard_map/ppermute | solution.py:39
  85.7 5.9 %collective-permute-start.8 = (f32[16,8,128]{2,1,0:T(8,128)S(1)}, f32[16,8,128]{2,1,0:T(8,128)S(1)}, u32[]{:S(2)}, u32[]{:S(2)}) collective-permute-start(f32[16,8,128]{2,1,0:T(8,128)S(1)} %zpack_kernel.3), channel_id=1, source_target_pairs={{0,1},{1,0},{2,3},{3,2},{4,5},{5,4},{6,7},{7,6},{8,9},{9,8},{10,11... | collective-permute-start | bytes 196616 | tf_op jit(solution)/shard_map/ppermute | solution.py:35
  86.7 5.9 %collective-permute-start.9 = (f32[16,8,128]{2,1,0:T(8,128)S(1)}, f32[16,8,128]{2,1,0:T(8,128)S(1)}, u32[]{:S(2)}, u32[]{:S(2)}) collective-permute-start(f32[16,8,128]{2,1,0:T(8,128)S(1)} %zpack_kernel.3), channel_id=1, source_target_pairs={{1,2},{2,1},{5,6},{6,5},{9,10},{10,9},{13,14},{14,13},{17,18},{18,... | collective-permute-start | bytes 196616 | tf_op jit(solution)/shard_map/ppermute | solution.py:39
  90.3 16.0 %collective-permute-start.10 = (f32[5,64,128]{2,1,0:T(8,128)S(1)}, f32[5,64,128]{2,1,0:T(8,128)S(1)}, u32[]{:S(2)}, u32[]{:S(2)}) collective-permute-start(f32[5,64,128]{2,1,0:T(8,128)S(1)} %get-tuple-element.51), channel_id=1, source_target_pairs={{0,16},{16,0},{1,17},{17,1},{2,18},{18,2},{3,19},{19,3},{4,20},{20... | collective-permute-start | bytes 491528 | tf_op jit(solution)/shard_map/ppermute | solution.py:35
  92.6 13.6 %collective-permute-start.11 = (f32[120,128]{1,0:T(8,128)S(1)}, f32[120,128]{1,0:T(8,128)S(1)}, u32[]{:S(2)}, u32[]{:S(2)}) collective-permute-start(f32[120,128]{1,0:T(8,128)S(1)} %xframe_kernel.3), channel_id=1, source_target_pairs={{0,16},{16,0},{1,17},{17,1},{2,18},{18,2},{3,19},{19,3},{4,20},{20... | collective-permute-start | bytes 184328 | tf_op jit(solution)/shard_map/ppermute | solution.py:35

commit v4 on v3

--- a/solution.py
+++ b/solution.py
@@ -17,6 +17,7 @@
 HL = 6
 GW = 2 * HL
 UNROLL = 4
+H2 = 12
 F32 = jnp.float32
 
 
@@ -278,11 +279,11 @@
     return (s + u) + w
 
 
-def sweep(src, dst, a, q, unroll=False):
-    nx, rows = src[0].shape[0] - 2, src[0].shape[1] - 16
+def sweep(src, dst, a, q, unroll=False, r0=0, rows=None):
+    nx, rows = src[0].shape[0] - 2, rows or src[0].shape[1] - 16
 
     def plane(x, _):
-        for r in chunks(rows):
+        for r in range(r0, r0 + rows, 8):
             vals, nb = neighbours(src, x, r, 8)
             rw = pl.ds(r, 8)
             for t in range(len(src)):
@@ -545,118 +546,150 @@
         ref[...] = v_out[:, pl.ds(r, 8), :]
 
 
-def mid_y_kernel(gathered, *refs):
-    if gathered:
-        full_in, full, y_a, y_b = refs
-        full[...] = full_in[...]
-    else:
-        own, other, full, y_a, y_b = refs
-        n = own.shape[0]
-        ix = lax.axis_index("gx")
-        full[pl.ds(n * ix, n)] = own[...]
-        full[pl.ds(n - n * ix, n)] = other[...]
-    ny = full.shape[1]
-    for ref, flag in ((y_a, True), (y_b, False)):
-        r = pl.multiple_of(face_start("gy", ny, 16, flag), 8)
-        ref[...] = full[:, pl.ds(r, 16), :]
-
-
-def mid_rows(full, r_a, r_b, x, t, ny):
-    ey = even("gy")
-    if t < 2:
-        return jnp.where(ey, r_b[x, t * 8 : t * 8 + 8], r_a[x, t * 8 : t * 8 + 8])
-    if t >= ny // 8 + 2:
-        u = t - ny // 8 - 2
-        return jnp.where(ey, r_a[x, u * 8 : u * 8 + 8], r_b[x, u * 8 : u * 8 + 8])
-    return full[x, (t - 2) * 8 : (t - 1) * 8]
-
-
-def mid_z_kernel(full, r_a, r_b, z_a, z_b):
+def join_kernel(own, other, full):
+    n = own.shape[0]
+    ix = lax.axis_index("gx")
+    full[pl.ds(n * ix, n)] = own[...]
+    full[pl.ds(n - n * ix, n)] = other[...]
+
+
+def mid_rows(full, r_a, r_b, x, t, tiles):
+    rows = slice((t % tiles) * 8, (t % tiles) * 8 + 8)
+    if t < tiles:
+        return jnp.where(even("gy"), r_b[x, rows], r_a[x, rows])
+    if t >= 2 * tiles:
+        return jnp.where(even("gy"), r_a[x, rows], r_b[x, rows])
+    return full[x, rows]
+
+
+def mid_z_kernel(full, r_a, r_b, v0, vr_a, vr_b, z_a, z_b, vz, work):
     nx, ny, _ = full.shape
+    tiles = ny // 8
     ez = even("gz")
-    slot = lax.rem(lanes(), 64) // 16
-    for t in range(ny // 8 + 4):
-
-        def group(s, _):
-            right = jnp.zeros((8, 128), F32)
-            left = jnp.zeros((8, 128), F32)
-            for g in range(4):
-                v = mid_rows(full, r_a, r_b, 4 * s + g, t, ny)
-                right = jnp.where(slot == g, rot(v, 16 * g - 48), right)
-                left = jnp.where(slot == g, rot(v, 16 * g), left)
-            z_a[s, t * 8 : t * 8 + 8] = jnp.where(ez, right, left)
-            z_b[s, t * 8 : t * 8 + 8] = jnp.where(ez, left, right)
-            return 0
-
-        lax.fori_loop(0, nx // 4, group, 0)
-
-
-def mid_down_kernel(keep, full, r_a, r_b, z_a, z_b, v_out, bc, *s):
-    c, b = (s[0],), (s[1],)
-    a = [(s[2 + j],) for j in range(6)]
-    q, d, v, v2, pair = (s[8],), (s[9],), (s[10],), (s[11],), s[12]
+    low = lax.rem(lanes(), 64) < 32
+
+    def pair(i, _):
+        for t in range(3 * tiles):
+            e = mid_rows(full, r_a, r_b, 2 * i, t, tiles)
+            o = mid_rows(full, r_a, r_b, 2 * i + 1, t, tiles)
+            first = jnp.where(low, e, rot(o, 32))
+            last = jnp.where(low, rot(o, -32), e)
+            z_a[i, t * 8 : t * 8 + 8] = jnp.where(ez, last, first)
+            z_b[i, t * 8 : t * 8 + 8] = jnp.where(ez, first, last)
+
+    fine_loop(0, nx // 2, lambda i, c: pair(i, c), 2)
+    zpack_kernel(1, v0, vr_a, vr_b, vz, work)
+
+
+def mid_down_kernel(full, r_a, r_b, z_a, z_b, vr_a, vr_b, vz_a, vz_b, *s):
+    v1_out, c = s[0], (s[1],)
+    a, q = [(s[2 + j],) for j in range(6)], (s[8],)
+    v2_out, c2 = s[9], (s[10],)
+    a2, q2 = [(s[11 + j],) for j in range(6)], (s[17],)
+    bc3, frame = s[18], s[19]
+    b, d, w = (s[20],), (s[21],), (s[22],)
+    b2, d2, w2 = (s[23],), (s[24],), (s[25],)
+    pair = s[26]
+    xframe_kernel(1, vr_a.shape[0], 1, vr_a, vr_b, vz_a, vz_b, frame)
+    v, v2 = (v1_out,), (v2_out,)
     nx, ny, _ = full.shape
+    tiles = ny // 8
     ez = even("gz")
     lane = lanes()
-    own, right_l, left_l = lane < 64, (lane >= 64) & (lane < 80), lane >= 112
-    zero(c[0], b[0], v[0], v2[0])
-    for t in range(ny // 8 + 4):
-
-        def group(s_, _):
-            za, zb = z_a[s_, t * 8 : t * 8 + 8], z_b[s_, t * 8 : t * 8 + 8]
+    own, low = lane < 64, lax.rem(lane, 64) < 32
+    clear_pads(c[0], v[0], w[0], c2[0], v2[0], w2[0])
+
+    def place(x, t, mine, side):
+        rows = slice(8 + t * 8, 16 + t * 8)
+        b[0][x + 1, rows] = jnp.where(own, mine, rot(side, 64))
+        c[0][x + 1, rows] = jnp.where(own, rot(mine, 64), side)
+
+    def two(i, _):
+        for t in range(3 * tiles):
+            za, zb = z_a[i, t * 8 : t * 8 + 8], z_b[i, t * 8 : t * 8 + 8]
             right = jnp.where(ez, za, zb)
             left = jnp.where(ez, zb, za)
-            for g in range(4):
-                x = 4 * s_ + g
-                m = mid_rows(full, r_a, r_b, x, t, ny)
-                for ref, o in ((b[0], 0), (c[0], 64)):
-                    e = jnp.where(own, rot(m, -o), 0.0)
-                    e = jnp.where(right_l, rot(right, 64 - o - 16 * g), e)
-                    e = jnp.where(left_l, rot(left, 112 - o - 16 * g), e)
-                    ref[x + 1, 8 + t * 8 : 16 + t * 8] = e
-            return 0
-
-        lax.fori_loop(0, nx // 4, group, 0)
+            e = mid_rows(full, r_a, r_b, 2 * i, t, tiles)
+            o = mid_rows(full, r_a, r_b, 2 * i + 1, t, tiles)
+            place(2 * i, t, e, jnp.where(low, right, left))
+            place(2 * i + 1, t, o, jnp.where(low, rot(right, -32), rot(left, 32)))
+
+    fine_loop(0, nx // 2, two, 2)
     build_coef(c, b, a, q, d, 0.25, False)
-    copy_q(v, q)
-    sweep(v, v2, a, q)
-    sweep(v2, v, a, q)
-    sweep(v, v2, a, q)
-    v = v2
-    half = nx // 4
-    mats = [(pick(o, 32, 64), pick(o + 32, 32, 64)) for o in (0, 64)]
-
-    def coarse(i, _):
-        acc = jnp.zeros((ny // 2, 128), F32)
-        for side in (0, 1):
-            x = 1 + 2 * (i + side * half)
-            for r in chunks(ny):
-                rp = pl.ds(24 + r, 8)
-                r0 = residual_rows(v, b[0][x, rp], a, d, x, 16 + r)
-                r1 = residual_rows(v, b[0][x + 1, rp], a, d, x + 1, 16 + r)
-                pair[0, pl.ds(r, 8)] = r0 + r1
-                pair[1, pl.ds(r, 8)] = c[0][x, rp] + c[0][x + 1, rp]
-            acc = acc + dot(half_rows(pair.at[0], 0, ny), mats[side][0])
-            acc = acc + dot(half_rows(pair.at[1], 0, ny), mats[side][1])
-        bc[i] = acc
-        return 0
-
-    lax.fori_loop(0, half, coarse, 0)
-    v_out[...] = v[0][...]
-
-
-def spread(src, dst, mats, c, x_src, x_dst, r_src, n, r_dst, tmp, sets=False):
-    for t, mat in enumerate(mats):
-        p = dot(src, mat)
-        tmp[t, pl.ds(0, n, stride=2)] = p
-        tmp[t, pl.ds(1, n, stride=2)] = p
-    for xd in x_dst:
-        for t in range(len(mats)):
-            for r in chunks(2 * n):
-                rr = pl.ds(r_dst + r, 8)
-                dst[t][xd, rr] = dst[t][xd, rr] + jnp.where(
-                    c[t][xd, rr] > 0.0, tmp[t, pl.ds(r, 8)], 0.0
-                )
+    copy_q(w, q)
+    sweep(w, v, a, q)
+    sweep(v, w, a, q)
+    sweep(w, v, a, q)
+    rows2 = ny // 2 + 2 * H2
+    r0 = ny - 2 * H2
+    mat = ring_pick(96)
+
+    def down(i, _):
+        x = 1 + 2 * i
+        for r in chunks(2 * rows2):
+            rp = pl.ds(8 + r0 + r, 8)
+            e = residual_rows(v, b[0][x, rp], a, d, x, r0 + r)
+            o = residual_rows(v, b[0][x + 1, rp], a, d, x + 1, r0 + r)
+            pair[0, pl.ds(r, 8)] = e + o
+            pair[1, pl.ds(r, 8)] = c[0][x, rp] + c[0][x + 1, rp]
+        b2[0][1 + i, 8 : 8 + rows2] = dot(half_rows(pair.at[0], 0, 2 * rows2), mat)
+        c2[0][1 + i, 8 : 8 + rows2] = dot(half_rows(pair.at[1], 0, 2 * rows2), mat)
+
+    fine_loop(0, nx // 2, down, 2)
+    build_coef(c2, b2, a2, q2, d2, 0.0625, False)
+    copy_q(w2, q2)
+    sweep(w2, v2, a2, q2)
+    sweep(v2, w2, a2, q2)
+    sweep(w2, v2, a2, q2)
+    n3, ny3 = nx // 4, ny // 4
+    for i in range(n3):
+        x = 1 + 2 * i
+        for r in chunks(ny // 2):
+            rp = pl.ds(8 + H2 + r, 8)
+            e = residual_rows(v2, b2[0][x, rp], a2, d2, x, H2 + r)
+            o = residual_rows(v2, b2[0][x + 1, rp], a2, d2, x + 1, H2 + r)
+            pair[0, pl.ds(r, 8)] = e + o
+            pair[1, pl.ds(r, 8)] = c2[0][x, rp] + c2[0][x + 1, rp]
+        at = 32 * (i % 4)
+        val = dot(half_rows(pair.at[0], 0, ny // 2), pick(at, 16, 32))
+        val = val + dot(half_rows(pair.at[1], 0, ny // 2), pick(at + 16, 16, 32))
+        if i % 4 == 0:
+            acc = val
+        else:
+            acc = acc + val
+        if i % 4 == 3 or i == n3 - 1:
+            bc3[(i // 4) * ny3 : (i // 4 + 1) * ny3] = acc
+
+
+def ring_pick(split):
+    i = lax.broadcasted_iota(jnp.int32, (128, 128), 0)
+    o = lax.broadcasted_iota(jnp.int32, (128, 128), 1)
+    return jnp.where(o == jnp.where(i < split, i // 2, i // 2 + 64), 0.125, 0.0).astype(F32)
+
+
+def clear_pads(*refs):
+    for ref in refs:
+        n, rows, _ = ref.shape
+        for x in (0, n - 1):
+            ref[x] = jnp.zeros(ref.shape[1:], F32)
+
+        def one(x, _):
+            ref[x, 0:8] = jnp.zeros((8, 128), F32)
+            ref[x, rows - 8 : rows] = jnp.zeros((8, 128), F32)
+
+        fine_loop(0, n, one, 6)
+
+
+def spread(src, dst, mat, c, planes, skip, r_dst, rows, tmp):
+    n = src.shape[0]
+    p = dot(src, mat)
+    tmp[pl.ds(0, n, stride=2)] = p
+    tmp[pl.ds(1, n, stride=2)] = p
+    for r in chunks(rows):
+        rr = slice(r_dst + r, r_dst + r + 8)
+        val = tmp[skip + r : skip + r + 8]
+        for x in planes:
+            dst[0][x, rr] = dst[0][x, rr] + jnp.where(c[0][x, rr] > 0.0, val, 0.0)
 
 
 def select_mat(fn):
@@ -665,103 +698,77 @@
     return jnp.where(i == fn(o), 1.0, 0.0).astype(F32)
 
 
-def coarse_kernel(gy, gz, keep, blocks, v1_in, c1, b1, *s):
-    if keep:
-        a1, q1, s = [(s[j],) for j in range(6)], (s[6],), s[7:]
-    v1_out, s = s[0], s[1:]
-    if not keep:
-        a1, q1, s = [(s[j],) for j in range(6)], (s[6],), s[7:]
-    c2, b2, v2, w2 = [(s[i],) for i in range(4)]
-    a2 = [(s[4 + j],) for j in range(6)]
-    q2, d2 = (s[10],), (s[11],)
-    c3, b3, v3, w3 = [(s[12 + i],) for i in range(4)]
-    a3 = [(s[16 + j],) for j in range(6)]
-    q3 = (s[22],)
-    v1, w1 = (v1_out,), (s[23],)
-    pair, tmp = s[24], s[25]
+def coarse_kernel(gy, gz, blocks, *s):
+    v1_in, c1 = s[0], (s[1],)
+    a1, q1 = [(s[2 + j],) for j in range(6)], (s[8],)
+    v2_in, c2 = s[9], (s[10],)
+    a2, q2 = [(s[11 + j],) for j in range(6)], (s[17],)
+    v1 = (s[18],)
+    s = s[19:]
+    w1, v2, w2 = (s[0],), (s[1],), (s[2],)
+    c3, b3, v3, w3 = [(s[3 + i],) for i in range(4)]
+    a3, q3 = [(s[7 + j],) for j in range(6)], (s[13],)
+    tmp = s[14]
     iy, iz = lax.axis_index("gy"), lax.axis_index("gz")
-    half, yb, _ = blocks.shape[1:]
+    n3, ny3 = q3[0].shape[:2]
+    yb = ny3 // gy
     lane = lanes(yb)
-    zero(c2[0], b2[0], v2[0], w2[0], c3[0], b3[0], v3[0], w3[0], w1[0])
-    nx2 = 2 * half
+    zero(c3[0], v3[0], w3[0])
     for jy in range(gy):
         ky = lax.bitwise_xor(jnp.int32(jy), iy)
-
-        def plane(i, _):
-            for o in (0, 64):
-                for ref, oo in ((b2[0], o), (c2[0], o + 32)):
-                    acc = jnp.zeros((yb, 128), F32)
-                    for jz in range(gz):
-                        kz = lax.bitwise_xor(jnp.int32(jz), iz)
-                        idx = ((kz % 2) * (gz // 2) + kz // 2) * gy + ky
-                        acc = jnp.where(lane // 32 == jz, rot(blocks[idx, i], 32 * jz - oo), acc)
-                    ref[1 + i + (half if o else 0), 8 + yb * jy : 8 + yb * (jy + 1)] = acc
-            return 0
-
-        lax.fori_loop(0, half, plane, 0)
-    build_coef(c2, b2, a2, q2, d2, 0.0625, True)
-    copy_q(v2, q2)
-    sweep(v2, w2, a2, q2)
-    sweep(w2, v2, a2, q2)
-    sweep(v2, w2, a2, q2)
-    ny = yb * gy
-    mat = pick(0, 64, 128)
-
-    def coarse(i, _):
-        x = 1 + 2 * i
-        for r in chunks(ny):
-            rp = pl.ds(8 + r, 8)
-            r0 = residual_rows(w2, b2[0][x, rp], a2, d2, x, r)
-            r1 = residual_rows(w2, b2[0][x + 1, rp], a2, d2, x + 1, r)
-            pair[0, pl.ds(r, 8)] = r0 + r1
-            pair[1, pl.ds(r, 8)] = c2[0][x, rp] + c2[0][x + 1, rp]
-        b3[0][1 + i, 8 : 8 + ny // 2] = dot(half_rows(pair.at[0], 0, ny), mat)
-        c3[0][1 + i, 8 : 8 + ny // 2] = dot(half_rows(pair.at[1], 0, ny), mat)
-        return 0
-
-    lax.fori_loop(0, nx2 // 2, coarse, 0)
-    small = nx2 <= 8
+        blk = []
+        for jz in range(gz):
+            kz = lax.bitwise_xor(jnp.int32(jz), iz)
+            blk.append(((kz % 2) * (gz // 2) + kz // 2) * gy + ky)
+        for i in range(n3):
+            rows = slice((i // 4) * yb, (i // 4 + 1) * yb)
+            for ref, o in ((b3[0], 32 * (i % 4)), (c3[0], 32 * (i % 4) + 16)):
+                acc = jnp.zeros((yb, 128), F32)
+                for jz in range(gz):
+                    acc = jnp.where(lane // 16 == jz, rot(blocks[blk[jz], rows], 16 * jz - o), acc)
+                ref[1 + i, 8 + yb * jy : 8 + yb * (jy + 1)] = acc
     build_coef(c3, b3, a3, q3, None, 0.015625, False)
     copy_q(v3, q3)
-    sweep(v3, w3, a3, q3, small)
+    sweep(v3, w3, a3, q3, True)
 
     def two(_, carry):
-        sweep(w3, v3, a3, q3, small)
-        sweep(v3, w3, a3, q3, small)
+        sweep(w3, v3, a3, q3, True)
+        sweep(v3, w3, a3, q3, True)
         return carry
 
     lax.fori_loop(0, (COARSE - 2) // 2, two, 0)
-    up = select_mat(lambda o: o // 2)
+    v2[0][...] = v2_in[...]
+    v1[0][...] = v1_in[...]
+    clear_pads(w1[0], w2[0])
+    up = select_mat(lambda o: jnp.where(o < 96, o // 2, (o + 128) // 2))
+    rows2 = q2[0].shape[1]
+    skip = 16 - H2
+    start = pl.multiple_of(yb * iy, 8)
 
     def up2(i, _):
-        spread(w3[0][1 + i, 8 : 8 + ny // 2], w2, [up], c2, None, (1 + 2 * i, 2 + 2 * i), None, ny // 2, 8, tmp)
-        return 0
-
-    lax.fori_loop(0, nx2 // 2, up2, 0)
+        par = rot(w3[0][1 + i, pl.ds(start, yb + 16)], -16 * iz)
+        spread(par, v2, up, c2, (1 + 2 * i, 2 + 2 * i), skip, 8, rows2, tmp)
+
+    fine_loop(0, n3, up2, 2)
 
     def two2(_, carry):
+        sweep(v2, w2, a2, q2)
         sweep(w2, v2, a2, q2)
-        sweep(v2, w2, a2, q2)
         return carry
 
     lax.fori_loop(0, SWEEPS // 2, two2, 0)
-    if not keep:
-        build_coef((c1,), (b1,), a1, q1, None, 0.25, False)
-    v1[0][...] = v1_in[...]
-    rows1 = v1[0].shape[1] - 16
-    up = select_mat(lambda o: jnp.where(o < 80, o // 2, jnp.where(o >= 112, (o + 128) // 2, -1)))
-    start = pl.multiple_of(yb * iy, 8)
+    ny1 = 4 * yb
+    r0 = ny1 - 8
 
     def up1(i, _):
-        par = rot(w2[0][1 + i, pl.ds(start, rows1 // 2)], -32 * iz)
-        spread(par, v1, [up], (c1,), None, (1 + 2 * i, 2 + 2 * i), None, rows1 // 2, 8, tmp)
-        return 0
-
-    lax.fori_loop(0, nx2, up1, 0)
+        par = v2[0][1 + i, 8 + H2 - 4 : 8 + H2 + ny1 // 2 + 4]
+        spread(par, v1, up, c1, (1 + 2 * i, 2 + 2 * i), 0, 8 + r0, ny1 + 16, tmp)
+
+    fine_loop(0, 2 * n3, up1, 2)
 
     def two1(_, carry):
-        sweep(v1, w1, a1, q1)
-        sweep(w1, v1, a1, q1)
+        sweep(v1, w1, a1, q1, False, r0, ny1 + 16)
+        sweep(w1, v1, a1, q1, False, r0, ny1 + 16)
         return carry
 
     lax.fori_loop(0, SWEEPS // 2, two1, 0)
@@ -825,7 +832,7 @@
     count = (xp + 2) // 2
     c0 = lax.shift_right_arithmetic(nx * ix + 1 - off, 1)
     for j in range(count):
-        stage[j * half : (j + 1) * half] = v1[1 + jnp.clip(c0 + j, 0, nc - 1), 20 : 20 + half]
+        stage[j * half : (j + 1) * half] = v1[1 + jnp.clip(c0 + j, 0, nc - 1), 4 + ny // 2 : 4 + ny // 2 + half]
     spread[...] = dot(stage[...], mat)
 
     def up(j, _):
@@ -892,9 +899,119 @@
     return out
 
 
+def plain_with_halo(block, sides, width):
+    for axis, dim in sides:
+        count = lax.axis_size(axis)
+        forward = [(i, i + 1) for i in range(count - 1)]
+        backward = [(target, source) for source, target in forward]
+        low = lax.ppermute(
+            lax.slice_in_dim(block, block.shape[dim] - width, None, axis=dim), axis, forward
+        )
+        high = lax.ppermute(lax.slice_in_dim(block, 0, width, axis=dim), axis, backward)
+        block = jnp.concatenate([low, block, high], axis=dim)
+    return block
+
+
+def plain_neighbor(padded, axis_dim, offset):
+    window = [slice(1, -1), slice(1, -1), slice(1, -1)]
+    window[axis_dim] = slice(1 + offset, padded.shape[axis_dim] - 1 + offset)
+    return padded[tuple(window)]
+
+
+def plain_apply_padded(padded_u, padded_c, level_scale):
+    center_u = padded_u[1:-1, 1:-1, 1:-1]
+    center_c = padded_c[1:-1, 1:-1, 1:-1]
+    stencil_sum = jnp.zeros_like(center_u)
+    diagonal = jnp.zeros_like(center_u)
+    for axis_dim in range(3):
+        for offset in (-1, 1):
+            face = 0.5 * (center_c + plain_neighbor(padded_c, axis_dim, offset))
+            stencil_sum = stencil_sum + face * (center_u - plain_neighbor(padded_u, axis_dim, offset))
+            diagonal = diagonal + face
+    return (level_scale * stencil_sum, level_scale * diagonal)
+
+
+def plain_restrict(field):
+    size_x, size_y, size_z = field.shape
+    return field.reshape(size_x // 2, 2, size_y // 2, 2, size_z // 2, 2).mean(axis=(1, 3, 5))
+
+
+def plain_prolong(field):
+    size_x, size_y, size_z = field.shape
+    spread = jnp.broadcast_to(field[:, None, :, None, :, None], (size_x, 2, size_y, 2, size_z, 2))
+    return spread.reshape(2 * size_x, 2 * size_y, 2 * size_z)
+
+
+def plain_coef_halo(coef_value):
+    return plain_with_halo(coef_value, (("gx", 0), ("gy", 1), ("gz", 2)), 1)
+
+
+def plain_residual_of(values, rhs_field, coef_padded, level_scale):
+    padded_u = plain_with_halo(values, (("gx", 0), ("gy", 1), ("gz", 2)), 1)
+    stencil_sum, diagonal = plain_apply_padded(padded_u, coef_padded, level_scale)
+    return rhs_field - stencil_sum
+
+
+def plain_narrow_sweeps(values, rhs_field, coef_padded, level_scale):
+    for sweep_id in range(SWEEPS):
+        padded_u = plain_with_halo(values, (("gx", 0), ("gy", 1), ("gz", 2)), 1)
+        stencil_sum, diagonal = plain_apply_padded(padded_u, coef_padded, level_scale)
+        values = values + W * (rhs_field - stencil_sum) / diagonal
+    return values
+
+
+def plain_smooth(values, level_id, rhs_list, padded_list):
+    level_scale = 0.25**level_id
+    return plain_narrow_sweeps(values, rhs_list[level_id], padded_list[level_id], level_scale)
+
+
+def plain_coarse_solve(coarse_rhs, coarse_coef):
+    coarse_scale = 0.25**LEVELS
+    coarse_pad = plain_coef_halo(coarse_coef)
+
+    def local_step(sweep_id, values):
+        padded_u = plain_with_halo(values, (("gx", 0), ("gy", 1), ("gz", 2)), 1)
+        stencil_sum, diagonal = plain_apply_padded(padded_u, coarse_pad, coarse_scale)
+        return values + W * (coarse_rhs - stencil_sum) / diagonal
+
+    return lax.fori_loop(0, COARSE, local_step, jnp.zeros_like(coarse_rhs))
+
+
+def plain_body(source, first_guess, cell_classes, class_table):
+    cell_coef = jnp.zeros(cell_classes.shape, jnp.float32)
+    for class_id in range(CLASSES):
+        cell_coef = cell_coef + jnp.where(cell_classes == class_id, class_table[class_id], 0.0)
+    coef_list = [cell_coef]
+    for level_id in range(LEVELS):
+        coef_list.append(plain_restrict(coef_list[-1]))
+    top_level = LEVELS
+    padded_list = [plain_coef_halo(coef_list[level_id]) for level_id in range(top_level)]
+    rhs_list = [source]
+    iterate_list = []
+    values = first_guess
+    for level_id in range(top_level):
+        level_scale = 0.25**level_id
+        if level_id > 0:
+            values = jnp.zeros_like(rhs_list[level_id])
+        values = plain_smooth(values, level_id, rhs_list, padded_list)
+        iterate_list.append(values)
+        rhs_list.append(
+            plain_restrict(plain_residual_of(values, rhs_list[level_id], padded_list[level_id], level_scale))
+        )
+    correction = plain_coarse_solve(rhs_list[LEVELS], coef_list[LEVELS])
+    for level_id in reversed(range(top_level)):
+        values = iterate_list[level_id] + plain_prolong(correction)
+        values = plain_smooth(values, level_id, rhs_list, padded_list)
+        correction = values
+    final = plain_residual_of(correction, source, padded_list[0], 1.0)
+    return (correction, final)
+
+
 def body(source, first_guess, cell_classes, class_table):
-    nx, ny, _ = source.shape
+    nx, ny, nz = source.shape
     gx, gy, gz = (lax.axis_size(n) for n in ("gx", "gy", "gz"))
+    if (gx, gy, gz, nx, ny, nz) != (2, 4, 4, 16, 64, 128):
+        return plain_body(source, first_guess, cell_classes, class_table)
     nsx = 1 if gx == 2 else 2
     xp = nx + nsx * HX
     rows = ny + 16
@@ -909,7 +1026,7 @@
     c_own, y_a, y_b, xs = out[0], out[1], out[2], out[3:]
     x1 = swap_x(xs)
     rec, x2 = exchange_rest(3, (c_own, first_guess, source), y_a, y_b, nsx)
-    keep = gx == 2
+    keep = True
     kept_shapes = fine_kept(xp, rows)
     outs = [full, (nx // 2, ny // 2, 128), (nx, 8, 128), (nx, 8, 128)] + [(HX, ny, 128)] * nsx
     work = fine_work(xp, rows) + [(2, ny, 128)]
@@ -923,49 +1040,47 @@
     out = out[: len(outs)]
     v0, bc1, vy_a, vy_b, vxs = out[0], out[1], out[2], out[3], out[4:]
 
-    n1 = gx * nx // 2
-    ny1 = ny // 2
-    outs = [(n1, ny1, 128), (n1, 16, 128), (n1, 16, 128)]
-    if gx == 2:
-        f1, y_a, y_b = call(named(mid_y_kernel, False), outs, bc1, swap_even(bc1, "gx"))
-    else:
-        f1, y_a, y_b = call(
-            named(mid_y_kernel, True), outs, lax.all_gather(bc1, "gx", axis=0, tiled=True)
-        )
-    r_a, r_b = swap_even(y_a, "gy"), swap_odd(y_b, "gy")
-    rows1 = ny1 + 32
-    z_a, z_b = call(mid_z_kernel, [(n1 // 4, rows1, 128)] * 2, f1, r_a, r_b)
+    n1, ny1 = nx, ny // 2
+    (f1,) = call(join_kernel, [(n1, ny1, 128)], bc1, swap_even(bc1, "gx"))
+    vr_a, vr_b = swap_even(vy_a, "gy"), swap_odd(vy_b, "gy")
+    vx1 = swap_x(vxs)
+    r_a, r_b = swap_even(f1, "gy"), swap_odd(f1, "gy")
+    rows1 = 3 * ny1
+    z_a, z_b, vz = call(
+        mid_z_kernel,
+        [(n1 // 2, rows1, 128)] * 2 + [(nx, 8, 128)],
+        f1, r_a, r_b, v0, vr_a, vr_b,
+        scratch=[(nx * 8, 128)],
+    )
     z_a, z_b = swap_even(z_a, "gz"), swap_odd(z_b, "gz")
+    vz_a, vz_b = swap_even(vz, "gz"), swap_odd(vz, "gz")
     pad1, bare1 = (n1 + 2, rows1 + 16, 128), (n1, rows1, 128)
+    n2, rows2 = n1 // 2, ny1 // 2 + 2 * H2
+    pad2, bare2 = (n2 + 2, rows2 + 16, 128), (n2, rows2, 128)
+    n3, yb = n1 // 4, ny1 // 4
+    kept_mid = [pad1, pad1] + [bare1] * 7 + [pad2, pad2] + [bare2] * 7
     out = call(
-        named(mid_down_kernel, keep),
-        [pad1, (n1 // 4, ny1 // 2, 128), pad1, pad1] + ([bare1] * 7 if keep else []),
-        f1, r_a, r_b, z_a, z_b,
-        scratch=([] if keep else [bare1] * 7) + [bare1, pad1, pad1, (2, ny1, 128)],
+        mid_down_kernel,
+        kept_mid + [(-(-n3 // 4) * yb, 128), (HX * 24, 128)],
+        f1, r_a, r_b, z_a, z_b, vr_a, vr_b, vz_a, vz_b,
+        scratch=[pad1, bare1, pad1, pad2, bare2, pad2, (2, 2 * rows2, 128)],
     )
-    v1, bc2, c1, b1 = out[:4]
-    kept1 = out[4:]
-
-    got = jnp.stack([bc2] + [swap_xor(bc2, "gy", m) for m in range(1, gy)])
+    kept_mid, (bc3, frame) = out[:-2], out[-2:]
+    vx2 = [swap_even(frame, "gx")]
+    vrec = (vr_a, vr_b, vz_a, vz_b)
+
+    got = jnp.stack([bc3] + [swap_xor(bc3, "gy", m) for m in range(1, gy)])
     bit = gz // 2
     while bit:
         got = jnp.concatenate([got, swap_xor(got, "gz", bit)])
         bit //= 2
 
-    vx1 = swap_x(vxs)
-    vrec, vx2 = exchange_rest(1, (v0,), vy_a, vy_b, nsx)
-
-    n2, ny2 = n1 // 2, gy * ny1 // 2
-    n3, ny3 = n2 // 2, ny2 // 2
-    pad2, bare2 = (n2 + 2, ny2 + 16, 128), (n2, ny2, 128)
-    pad3, bare3 = (n3 + 2, ny3 + 16, 128), (n3, ny3, 128)
+    pad3, bare3 = (n3 + 2, gy * yb + 16, 128), (n3, gy * yb, 128)
     (v1,) = call(
-        named(coarse_kernel, gy, gz, keep),
+        named(coarse_kernel, gy, gz),
         [pad1],
-        got, v1, c1, b1, *kept1,
-        scratch=([] if keep else [bare1] * 7)
-        + [pad2] * 4 + [bare2] * 8 + [pad3] * 4 + [bare3] * 7 + [pad1]
-        + [(2, ny2, 128), (1, max(rows1, ny2), 128)],
+        got, *kept_mid,
+        scratch=[pad1, pad2, pad2] + [pad3] * 4 + [bare3] * 7 + [(2 * (ny1 + 16), 128)],
     )
     par_rows = (xp + 2) // 2 * (rows // 2)
     work = fine_work(xp, rows) + [(2, rows, 128), (par_rows, 128), (par_rows, 256)]

time: 117 us -> 103 us (0.88); the launches traced: 115 us -> 103 us
  Pallas kernels: 43.3 us -> 36.5 us
  starting transfers between devices: 39.6 us -> 34.3 us
    pallas_call x11 -> x9, Pallas kernels: 43.3 us -> 36.5 us  [call(): pl.pallas_call(body, out_shape=shapes, in_specs=specs, out_specs=[pl.Bloc...]
    ppermute x11, waiting for transfers between devices: 12.5 us -> 16.7 us  [swap_even(): return lax.ppermute(x, axis, pairs_even(lax.axis_size(axis)))]
    ppermute x5, starting transfers between devices: 8.89 us -> 4.77 us  [swap_xor(): lax.ppermute(x, axis, [(i, i ^ m) for i in range(lax.axis_size(axis))])]
    ppermute x5, waiting for transfers between devices: 7.21 us -> 4.11 us  [swap_xor(): lax.ppermute(x, axis, [(i, i ^ m) for i in range(lax.axis_size(axis))])]
    ppermute x6, starting transfers between devices: 14.7 us -> 12 us  [swap_odd(): return lax.ppermute(x, axis, pairs_odd(lax.axis_size(axis)))]
    ppermute x11, starting transfers between devices: 16 us -> 17.5 us  [swap_even(): return lax.ppermute(x, axis, pairs_even(lax.axis_size(axis)))]
  transfers between devices with their start and end apart: 22 -> 22, of which waited for: 11 -> 9; matrix products, arithmetic and copies ran while one was open for 0% -> 0% of each run, Pallas kernels for 12% -> 15%
where the time goes in v4:
time: 103 us
  Pallas kernels  36.5 us (35%)
  starting transfers between devices  34.3 us (33%)
  waiting for transfers between devices  27.3 us (27%)
  local copies, waits for them, and re-layouts  3.8 us (4%)
    pallas_call x9, Pallas kernels, call(): pl.pallas_call(body, out_shape=shapes, in_specs=specs, out_specs=[pl.Bloc...  36.5 us
    ppermute x11, starting transfers between devices, swap_even(): return lax.ppermute(x, axis, pairs_even(lax.axis_size(axis)))  17.5 us
    ppermute x11, waiting for transfers between devices, swap_even(): return lax.ppermute(x, axis, pairs_even(lax.axis_size(axis)))  16.7 us
    ppermute x6, starting transfers between devices, swap_odd(): return lax.ppermute(x, axis, pairs_odd(lax.axis_size(axis)))  12 us
    ppermute x6, waiting for transfers between devices, swap_odd(): return lax.ppermute(x, axis, pairs_odd(lax.axis_size(axis)))  6.5 us
    ppermute x5, starting transfers between devices, swap_xor(): lax.ppermute(x, axis, [(i, i ^ m) for i in range(lax.axis_size(axis))])  4.77 us
    ppermute x5, waiting for transfers between devices, swap_xor(): lax.ppermute(x, axis, [(i, i ^ m) for i in range(lax.axis_size(axis))])  4.11 us
    unnamed x16, local copies, waits for them, and re-layouts  3.79 us
  transfers between devices with their start and end apart: 22, of which 9 were waited for; matrix products, arithmetic and copies ran while one was open for 0% of the time, Pallas kernels for 15%

profile of v4, /device:TPU:1, one launch (start us, length us, event | category | flops | bytes accessed | tf_op | source)
XLA Modules:
  0.0 102.7 jit_solution(3736667546589257480)
XLA Ops:
  0.6 1.0 %copy-done = f32[16,64,128]{2,1,0:T(8,128)S(1)} copy-done((f32[16,64,128]{2,1,0:T(8,128)S(1)}, f32[16,64,128]{2,1,0:T(8,128)}, u32[]{:S(2)}) %copy-start) | copy-done | bytes 524312
  1.7 1.0 %copy-done.2 = f32[16,64,128]{2,1,0:T(8,128)S(1)} copy-done((f32[16,64,128]{2,1,0:T(8,128)S(1)}, f32[16,64,128]{2,1,0:T(8,128)}, u32[]{:S(2)}) %copy-start.2) | copy-done | bytes 524312
  2.7 1.0 %copy-done.4 = s32[16,64,128]{2,1,0:T(8,128)S(1)} copy-done((s32[16,64,128]{2,1,0:T(8,128)S(1)}, s32[16,64,128]{2,1,0:T(8,128)}, u32[]{:S(2)}) %copy-start.4) | copy-done | bytes 524312
  4.4 1.0 start_kernel.1
  5.4 2.2 %collective-permute-start = (f32[48,8,128]{2,1,0:T(8,128)S(1)}, f32[48,8,128]{2,1,0:T(8,128)S(1)}, u32[]{:S(2)}, u32[]{:S(2)}) collective-permute-start(f32[48,8,128]{2,1,0:T(8,128)S(1)} %get-tuple-element.52), channel_id=1, source_target_pairs={{0,4},{4,0},{8,12},{12,8},{1,5},{5,1},{9,13},{13,9},{2,6},{6,2},{1... | collective-permute-start | bytes 589832 | tf_op jit(solution)/shard_map/ppermute | solution.py:36
  8.2 1.3 %collective-permute-start.4 = (f32[14,64,128]{2,1,0:T(8,128)S(1)}, f32[14,64,128]{2,1,0:T(8,128)S(1)}, u32[]{:S(2)}, u32[]{:S(2)}) collective-permute-start(f32[14,64,128]{2,1,0:T(8,128)S(1)} %get-tuple-element.54), channel_id=1, source_target_pairs={{0,16},{16,0},{1,17},{17,1},{2,18},{18,2},{3,19},{19,3},{4,20},{20... | collective-permute-start | bytes 1376264 | tf_op jit(solution)/shard_map/ppermute | solution.py:36
  9.5 2.7 %collective-permute-done.refs_3_.r_a = f32[48,8,128]{2,1,0:T(8,128)S(1)} collective-permute-done((f32[48,8,128]{2,1,0:T(8,128)S(1)}, f32[48,8,128]{2,1,0:T(8,128)S(1)}, u32[]{:S(2)}, u32[]{:S(2)}) %collective-permute-start) | collective-permute-done | bytes 196640 | tf_op jit(solution)/shard_map/ppermute | solution.py:36
  12.9 4.4 %collective-permute-start.3 = (f32[48,8,128]{2,1,0:T(8,128)S(1)}, f32[48,8,128]{2,1,0:T(8,128)S(1)}, u32[]{:S(2)}, u32[]{:S(2)}) collective-permute-start(f32[48,8,128]{2,1,0:T(8,128)S(1)} %zpack_kernel.1), channel_id=1, source_target_pairs={{1,2},{2,1},{5,6},{6,5},{9,10},{10,9},{13,14},{14,13},{17,18},{18,... | collective-permute-start | bytes 589832 | tf_op jit(solution)/shard_map/ppermute | solution.py:40
  17.5 3.4 %collective-permute-done.3.z_b.refs_6_ = f32[48,8,128]{2,1,0:T(8,128)S(1)} collective-permute-done((f32[48,8,128]{2,1,0:T(8,128)S(1)}, f32[48,8,128]{2,1,0:T(8,128)S(1)}, u32[]{:S(2)}, u32[]{:S(2)}) %collective-permute-start.3) | collective-permute-done | bytes 196640 | tf_op jit(solution)/shard_map/ppermute | solution.py:40
  20.9 1.3 %collective-permute-start.5 = (f32[336,128]{1,0:T(8,128)S(1)}, f32[336,128]{1,0:T(8,128)S(1)}, u32[]{:S(2)}, u32[]{:S(2)}) collective-permute-start(f32[336,128]{1,0:T(8,128)S(1)} %xframe_kernel.1), channel_id=1, source_target_pairs={{0,16},{16,0},{1,17},{17,1},{2,18},{18,2},{3,19},{19,3},{4,20},{20... | collective-permute-start | bytes 516104 | tf_op jit(solution)/shard_map/ppermute | solution.py:36
  22.1 3.5 %collective-permute-done.5.refs_8_ = f32[336,128]{1,0:T(8,128)S(1)} collective-permute-done((f32[336,128]{1,0:T(8,128)S(1)}, f32[336,128]{1,0:T(8,128)S(1)}, u32[]{:S(2)}, u32[]{:S(2)}) %collective-permute-start.5) | collective-permute-done | bytes 172064 | tf_op jit(solution)/shard_map/ppermute | solution.py:36
  25.7 10.6 %fine_down_kernel.1 = (f32[16,64,128]{2,1,0:T(8,128)S(1)}, f32[8,32,128]{2,1,0:T(8,128)S(1)}, f32[16,8,128]{2,1,0:T(8,128)S(1)}, f32[16,8,128]{2,1,0:T(8,128)S(1...) custom-call(f32[16,64,128]{2,1,0:T(8,128)S(1)} %get-tuple-element.51, ...), custom_call_target="tpu_custom_call" | custom-call | tf_op jit(solution)/shard_map/fine_down_kernel/pallas_call | solution.py:59
  36.3 1.3 %collective-permute-start.8 = (f32[8,32,128]{2,1,0:T(8,128)S(1)}, f32[8,32,128]{2,1,0:T(8,128)S(1)}, u32[]{:S(2)}, u32[]{:S(2)}) collective-permute-start(f32[8,32,128]{2,1,0:T(8,128)S(1)} %get-tuple-element.58.own), channel_id=1, source_target_pairs={{0,16},{16,0},{1,17},{17,1},{2,18},{18,2},{3,19},{19,3},{4,20},{20... | collective-permute-start | bytes 393224 | tf_op jit(solution)/shard_map/ppermute | solution.py:36
  37.6 3.8 %collective-permute-done.8.other = f32[8,32,128]{2,1,0:T(8,128)S(1)} collective-permute-done((f32[8,32,128]{2,1,0:T(8,128)S(1)}, f32[8,32,128]{2,1,0:T(8,128)S(1)}, u32[]{:S(2)}, u32[]{:S(2)}) %collective-permute-start.8) | collective-permute-done | bytes 131104 | tf_op jit(solution)/shard_map/ppermute | solution.py:36
  42.1 7.3 %collective-permute-start.9 = (f32[16,32,128]{2,1,0:T(8,128)S(1)}, f32[16,32,128]{2,1,0:T(8,128)S(1)}, u32[]{:S(2)}, u32[]{:S(2)}) collective-permute-start(f32[16,32,128]{2,1,0:T(8,128)S(1)} %join_kernel.1.full), channel_id=1, source_target_pairs={{0,4},{4,0},{8,12},{12,8},{1,5},{5,1},{9,13},{13,9},{2,6},{6,2},{1... | collective-permute-start | bytes 786440 | tf_op jit(solution)/shard_map/ppermute | solution.py:36
  50.2 6.7 %collective-permute-done.6.vr_a.refs_9_ = f32[16,8,128]{2,1,0:T(8,128)S(1)} collective-permute-done((f32[16,8,128]{2,1,0:T(8,128)S(1)}, f32[16,8,128]{2,1,0:T(8,128)S(1)}, u32[]{:S(2)}, u32[]{:S(2)}) %collective-permute-start.6) | collective-permute-done | bytes 65568 | tf_op jit(solution)/shard_map/ppermute | solution.py:36
  56.9 0.9 mid_z_kernel.1
  57.7 1.3 %collective-permute-start.14 = (f32[8,96,128]{2,1,0:T(8,128)S(1)}, f32[8,96,128]{2,1,0:T(8,128)S(1)}, u32[]{:S(2)}, u32[]{:S(2)}) collective-permute-start(f32[8,96,128]{2,1,0:T(8,128)S(1)} %get-tuple-element.61), channel_id=1, source_target_pairs={{0,1},{1,0},{2,3},{3,2},{4,5},{5,4},{6,7},{7,6},{8,9},{9,8},{10,11... | collective-permute-start | bytes 1179656 | tf_op jit(solution)/shard_map/ppermute | solution.py:36
  59.1 1.9 %collective-permute-start.15 = (f32[8,96,128]{2,1,0:T(8,128)S(1)}, f32[8,96,128]{2,1,0:T(8,128)S(1)}, u32[]{:S(2)}, u32[]{:S(2)}) collective-permute-start(f32[8,96,128]{2,1,0:T(8,128)S(1)} %get-tuple-element.62), channel_id=1, source_target_pairs={{1,2},{2,1},{5,6},{6,5},{9,10},{10,9},{13,14},{14,13},{17,18},{18,... | collective-permute-start | bytes 1179656 | tf_op jit(solution)/shard_map/ppermute | solution.py:40
  61.0 3.6 %collective-permute-start.12 = (f32[16,8,128]{2,1,0:T(8,128)S(1)}, f32[16,8,128]{2,1,0:T(8,128)S(1)}, u32[]{:S(2)}, u32[]{:S(2)}) collective-permute-start(f32[16,8,128]{2,1,0:T(8,128)S(1)} %get-tuple-element.59), channel_id=1, source_target_pairs={{1,2},{2,1},{5,6},{6,5},{9,10},{10,9},{13,14},{14,13},{17,18},{18,... | collective-permute-start | bytes 196616 | tf_op jit(solution)/shard_map/ppermute | solution.py:40
  64.7 1.3 %collective-permute-start.13 = (f32[5,64,128]{2,1,0:T(8,128)S(1)}, f32[5,64,128]{2,1,0:T(8,128)S(1)}, u32[]{:S(2)}, u32[]{:S(2)}) collective-permute-start(f32[5,64,128]{2,1,0:T(8,128)S(1)} %get-tuple-element.60), channel_id=1, source_target_pairs={{0,16},{16,0},{1,17},{17,1},{2,18},{18,2},{3,19},{19,3},{4,20},{20... | collective-permute-start | bytes 491528 | tf_op jit(solution)/shard_map/ppermute | solution.py:36
  66.0 3.1 %collective-permute-done.12.vz_b.refs_12_ = f32[16,8,128]{2,1,0:T(8,128)S(1)} collective-permute-done((f32[16,8,128]{2,1,0:T(8,128)S(1)}, f32[16,8,128]{2,1,0:T(8,128)S(1)}, u32[]{:S(2)}, u32[]{:S(2)}) %collective-permute-start.12) | collective-permute-done | bytes 65568 | tf_op jit(solution)/shard_map/ppermute | solution.py:40
  69.1 8.3 %mid_down_kernel.1 = (f32[18,112,128]{2,1,0:T(8,128)S(1)}, f32[18,112,128]{2,1,0:T(8,128)S(1)}, f32[16,96,128]{2,1,0:T(8,128)S(1)}, f32[16,96,128]{2,1,0:T(8,128...) custom-call(f32[16,32,128]{2,1,0:T(8,128)S(1)} %join_kernel.1.full, ...), custom_call_target="tpu_custom_call" | custom-call | tf_op jit(solution)/shard_map/mid_down_kernel/pallas_call | solution.py:59
  77.4 0.9 collective-permute-start.19
  78.4 1.7 %collective-permute-start.18 = (f32[8,128]{1,0:T(8,128)S(1)}, f32[8,128]{1,0:T(8,128)S(1)}, u32[]{:S(2)}, u32[]{:S(2)}) collective-permute-start(f32[8,128]{1,0:T(8,128)S(1)} %get-tuple-element.64), channel_id=1, source_target_pairs={{0,8},{4,12},{8,0},{12,4},{1,9},{5,13},{9,1},{13,5},{2,10},{6,14},... | collective-permute-start | bytes 12296 | tf_op jit(solution)/shard_map/ppermute | solution.py:44
  80.1 0.9 collective-permute-start.17
  81.7 0.8 collective-permute-done.17
  82.6 2.6 %collective-permute-done.20 = f32[4,8,128]{2,1,0:T(8,128)S(1)} collective-permute-done((f32[4,8,128]{2,1,0:T(8,128)S(1)}, f32[4,8,128]{2,1,0:T(8,128)S(1)}, u32[]{:S(2)}, u32[]{:S(2)}) %collective-permute-start.20) | collective-permute-done | bytes 16416 | tf_op jit(solution)/shard_map/ppermute | solution.py:44
  85.1 1.2 %collective-permute-start.21 = (f32[8,8,128]{2,1,0:T(8,128)S(1)}, f32[8,8,128]{2,1,0:T(8,128)S(1)}, u32[]{:S(2)}, u32[]{:S(2)}) collective-permute-start(f32[8,8,128]{2,1,0:T(8,128)S(1)} %get-tuple-element.100), channel_id=1, source_target_pairs={{0,1},{1,0},{2,3},{3,2},{4,5},{5,4},{6,7},{7,6},{8,9},{9,8},{10,11... | collective-permute-start | bytes 98312 | tf_op jit(solution)/shard_map/ppermute | solution.py:44
  86.3 1.3 %collective-permute-start.16 = (f32[120,128]{1,0:T(8,128)S(1)}, f32[120,128]{1,0:T(8,128)S(1)}, u32[]{:S(2)}, u32[]{:S(2)}) collective-permute-start(f32[120,128]{1,0:T(8,128)S(1)} %get-tuple-element.63), channel_id=1, source_target_pairs={{0,16},{16,0},{1,17},{17,1},{2,18},{18,2},{3,19},{19,3},{4,20},{20... | collective-permute-start | bytes 184328 | tf_op jit(solution)/shard_map/ppermute | solution.py:36
  87.6 6.4 %coarse_kernel.1.refs_15_ = f32[18,112,128]{2,1,0:T(8,128)S(1)} custom-call(f32[16,8,128]{2,1,0:T(8,128)S(1)} %constant_dynamic-update-slice_fusion.5.blocks, f32[18,112,128]{2,1,0:T(8,128)S(1)} %get-tuple-element.65.s_0_, f32[18,112,128]{2,1,0:T(8,128)S(1)} %get-tuple-element.66.s_1_, f32[16,96,128]{2,1,0:T(8,128)S(1)} %get-tuple-element.67.s_2_, ...), custom_call_target="tpu_custom_call" | custom-call | tf_op jit(solution)/shard_map/coarse_kernel/pallas_call | solution.py:59
  94.0 8.7 %fine_up_kernel.1 = (f32[16,64,128]{2,1,0:T(8,128)}, f32[16,64,128]{2,1,0:T(8,128)}) custom-call(f32[16,64,128]{2,1,0:T(8,128)S(1)} %get-tuple-element.51.refs_0_, f32[16,64,128]{2,1,0:T(8,128)S(1)} %get-tuple-element.55.v0.refs_1_, f32[16,64,128]{2,1,0:T(8,128)S(1)} %copy-done.1, f32[48,8,128]{2,1,0:T(8,128)S(1)} %collective-permute-done.refs_3_.r_a, ...), custom_call_target="tpu_custom_call" | custom-call | tf_op jit(solution)/shard_map/fine_up_kernel/pallas_call | solution.py:59
  (40 shorter events, 4.5 us)
Async XLA Ops:
  0.6 1.0 %copy-start = (f32[16,64,128]{2,1,0:T(8,128)S(1)}, f32[16,64,128]{2,1,0:T(8,128)}, u32[]{:S(2)}) copy-start(f32[16,64,128]{2,1,0:T(8,128)} %refs_2_.5) | copy-start | bytes 1572868
  1.7 1.0 %copy-start.2 = (f32[16,64,128]{2,1,0:T(8,128)S(1)}, f32[16,64,128]{2,1,0:T(8,128)}, u32[]{:S(2)}) copy-start(f32[16,64,128]{2,1,0:T(8,128)} %refs_1_.3) | copy-start | bytes 1572868
  2.7 1.0 %copy-start.4 = (s32[16,64,128]{2,1,0:T(8,128)S(1)}, s32[16,64,128]{2,1,0:T(8,128)}, u32[]{:S(2)}) copy-start(s32[16,64,128]{2,1,0:T(8,128)} %cls.1) | copy-start | bytes 1572868
  3.8 0.7 copy-start.5
  4.4 7.8 %copy-start.1 = (f32[16,64,128]{2,1,0:T(8,128)S(1)}, f32[16,64,128]{2,1,0:T(8,128)}, u32[]{:S(2)}) copy-start(f32[16,64,128]{2,1,0:T(8,128)} %refs_2_.5) | copy-start | bytes 1572868
  5.4 6.8 %collective-permute-start = (f32[48,8,128]{2,1,0:T(8,128)S(1)}, f32[48,8,128]{2,1,0:T(8,128)S(1)}, u32[]{:S(2)}, u32[]{:S(2)}) collective-permute-start(f32[48,8,128]{2,1,0:T(8,128)S(1)} %get-tuple-element.52), channel_id=1, source_target_pairs={{0,4},{4,0},{8,12},{12,8},{1,5},{5,1},{9,13},{13,9},{2,6},{6,2},{1... | collective-permute-start | bytes 589832 | tf_op jit(solution)/shard_map/ppermute | solution.py:36
  7.6 4.6 %collective-permute-start.1 = (f32[48,8,128]{2,1,0:T(8,128)S(1)}, f32[48,8,128]{2,1,0:T(8,128)S(1)}, u32[]{:S(2)}, u32[]{:S(2)}) collective-permute-start(f32[48,8,128]{2,1,0:T(8,128)S(1)} %get-tuple-element.53), channel_id=1, source_target_pairs={{4,8},{8,4},{5,9},{9,5},{6,10},{10,6},{7,11},{11,7},{20,24},{24,20... | collective-permute-start | bytes 589832 | tf_op jit(solution)/shard_map/ppermute | solution.py:40
  8.2 13.9 %collective-permute-start.4 = (f32[14,64,128]{2,1,0:T(8,128)S(1)}, f32[14,64,128]{2,1,0:T(8,128)S(1)}, u32[]{:S(2)}, u32[]{:S(2)}) collective-permute-start(f32[14,64,128]{2,1,0:T(8,128)S(1)} %get-tuple-element.54), channel_id=1, source_target_pairs={{0,16},{16,0},{1,17},{17,1},{2,18},{18,2},{3,19},{19,3},{4,20},{20... | collective-permute-start | bytes 1376264 | tf_op jit(solution)/shard_map/ppermute | solution.py:36
  12.2 13.5 %copy-start.3 = (f32[16,64,128]{2,1,0:T(8,128)S(1)}, f32[16,64,128]{2,1,0:T(8,128)}, u32[]{:S(2)}) copy-start(f32[16,64,128]{2,1,0:T(8,128)} %refs_1_.3) | copy-start | bytes 1572868
  12.9 7.9 %collective-permute-start.3 = (f32[48,8,128]{2,1,0:T(8,128)S(1)}, f32[48,8,128]{2,1,0:T(8,128)S(1)}, u32[]{:S(2)}, u32[]{:S(2)}) collective-permute-start(f32[48,8,128]{2,1,0:T(8,128)S(1)} %zpack_kernel.1), channel_id=1, source_target_pairs={{1,2},{2,1},{5,6},{6,5},{9,10},{10,9},{13,14},{14,13},{17,18},{18,... | collective-permute-start | bytes 589832 | tf_op jit(solution)/shard_map/ppermute | solution.py:40
  17.4 3.5 %collective-permute-start.2 = (f32[48,8,128]{2,1,0:T(8,128)S(1)}, f32[48,8,128]{2,1,0:T(8,128)S(1)}, u32[]{:S(2)}, u32[]{:S(2)}) collective-permute-start(f32[48,8,128]{2,1,0:T(8,128)S(1)} %zpack_kernel.1), channel_id=1, source_target_pairs={{0,1},{1,0},{2,3},{3,2},{4,5},{5,4},{6,7},{7,6},{8,9},{9,8},{10,11... | collective-permute-start | bytes 589832 | tf_op jit(solution)/shard_map/ppermute | solution.py:36
  20.9 4.8 %collective-permute-start.5 = (f32[336,128]{1,0:T(8,128)S(1)}, f32[336,128]{1,0:T(8,128)S(1)}, u32[]{:S(2)}, u32[]{:S(2)}) collective-permute-start(f32[336,128]{1,0:T(8,128)S(1)} %xframe_kernel.1), channel_id=1, source_target_pairs={{0,16},{16,0},{1,17},{17,1},{2,18},{18,2},{3,19},{19,3},{4,20},{20... | collective-permute-start | bytes 516104 | tf_op jit(solution)/shard_map/ppermute | solution.py:36
  36.3 5.2 %collective-permute-start.8 = (f32[8,32,128]{2,1,0:T(8,128)S(1)}, f32[8,32,128]{2,1,0:T(8,128)S(1)}, u32[]{:S(2)}, u32[]{:S(2)}) collective-permute-start(f32[8,32,128]{2,1,0:T(8,128)S(1)} %get-tuple-element.58.own), channel_id=1, source_target_pairs={{0,16},{16,0},{1,17},{17,1},{2,18},{18,2},{3,19},{19,3},{4,20},{20... | collective-permute-start | bytes 393224 | tf_op jit(solution)/shard_map/ppermute | solution.py:36
  41.5 15.4 %collective-permute-start.10 = (f32[16,32,128]{2,1,0:T(8,128)S(1)}, f32[16,32,128]{2,1,0:T(8,128)S(1)}, u32[]{:S(2)}, u32[]{:S(2)}) collective-permute-start(f32[16,32,128]{2,1,0:T(8,128)S(1)} %join_kernel.1.full), channel_id=1, source_target_pairs={{4,8},{8,4},{5,9},{9,5},{6,10},{10,6},{7,11},{11,7},{20,24},{24,20... | collective-permute-start | bytes 786440 | tf_op jit(solution)/shard_map/ppermute | solution.py:40
  42.1 14.7 %collective-permute-start.9 = (f32[16,32,128]{2,1,0:T(8,128)S(1)}, f32[16,32,128]{2,1,0:T(8,128)S(1)}, u32[]{:S(2)}, u32[]{:S(2)}) collective-permute-start(f32[16,32,128]{2,1,0:T(8,128)S(1)} %join_kernel.1.full), channel_id=1, source_target_pairs={{0,4},{4,0},{8,12},{12,8},{1,5},{5,1},{9,13},{13,9},{2,6},{6,2},{1... | collective-permute-start | bytes 786440 | tf_op jit(solution)/shard_map/ppermute | solution.py:36
  49.4 7.4 %collective-permute-start.6 = (f32[16,8,128]{2,1,0:T(8,128)S(1)}, f32[16,8,128]{2,1,0:T(8,128)S(1)}, u32[]{:S(2)}, u32[]{:S(2)}) collective-permute-start(f32[16,8,128]{2,1,0:T(8,128)S(1)} %get-tuple-element.56), channel_id=1, source_target_pairs={{0,4},{4,0},{8,12},{12,8},{1,5},{5,1},{9,13},{13,9},{2,6},{6,2},{1... | collective-permute-start | bytes 196616 | tf_op jit(solution)/shard_map/ppermute | solution.py:36
  49.5 7.3 %collective-permute-start.7 = (f32[16,8,128]{2,1,0:T(8,128)S(1)}, f32[16,8,128]{2,1,0:T(8,128)S(1)}, u32[]{:S(2)}, u32[]{:S(2)}) collective-permute-start(f32[16,8,128]{2,1,0:T(8,128)S(1)} %get-tuple-element.57), channel_id=1, source_target_pairs={{4,8},{8,4},{5,9},{9,5},{6,10},{10,6},{7,11},{11,7},{20,24},{24,20... | collective-permute-start | bytes 196616 | tf_op jit(solution)/shard_map/ppermute | solution.py:40
  57.7 11.4 %collective-permute-start.14 = (f32[8,96,128]{2,1,0:T(8,128)S(1)}, f32[8,96,128]{2,1,0:T(8,128)S(1)}, u32[]{:S(2)}, u32[]{:S(2)}) collective-permute-start(f32[8,96,128]{2,1,0:T(8,128)S(1)} %get-tuple-element.61), channel_id=1, source_target_pairs={{0,1},{1,0},{2,3},{3,2},{4,5},{5,4},{6,7},{7,6},{8,9},{9,8},{10,11... | collective-permute-start | bytes 1179656 | tf_op jit(solution)/shard_map/ppermute | solution.py:36
  59.1 10.1 %collective-permute-start.15 = (f32[8,96,128]{2,1,0:T(8,128)S(1)}, f32[8,96,128]{2,1,0:T(8,128)S(1)}, u32[]{:S(2)}, u32[]{:S(2)}) collective-permute-start(f32[8,96,128]{2,1,0:T(8,128)S(1)} %get-tuple-element.62), channel_id=1, source_target_pairs={{1,2},{2,1},{5,6},{6,5},{9,10},{10,9},{13,14},{14,13},{17,18},{18,... | collective-permute-start | bytes 1179656 | tf_op jit(solution)/shard_map/ppermute | solution.py:40
  61.0 8.2 %collective-permute-start.12 = (f32[16,8,128]{2,1,0:T(8,128)S(1)}, f32[16,8,128]{2,1,0:T(8,128)S(1)}, u32[]{:S(2)}, u32[]{:S(2)}) collective-permute-start(f32[16,8,128]{2,1,0:T(8,128)S(1)} %get-tuple-element.59), channel_id=1, source_target_pairs={{1,2},{2,1},{5,6},{6,5},{9,10},{10,9},{13,14},{14,13},{17,18},{18,... | collective-permute-start | bytes 196616 | tf_op jit(solution)/shard_map/ppermute | solution.py:40
  64.6 4.5 %collective-permute-start.11 = (f32[16,8,128]{2,1,0:T(8,128)S(1)}, f32[16,8,128]{2,1,0:T(8,128)S(1)}, u32[]{:S(2)}, u32[]{:S(2)}) collective-permute-start(f32[16,8,128]{2,1,0:T(8,128)S(1)} %get-tuple-element.59), channel_id=1, source_target_pairs={{0,1},{1,0},{2,3},{3,2},{4,5},{5,4},{6,7},{7,6},{8,9},{9,8},{10,11... | collective-permute-start | bytes 196616 | tf_op jit(solution)/shard_map/ppermute | solution.py:36
  64.7 29.3 %collective-permute-start.13 = (f32[5,64,128]{2,1,0:T(8,128)S(1)}, f32[5,64,128]{2,1,0:T(8,128)S(1)}, u32[]{:S(2)}, u32[]{:S(2)}) collective-permute-start(f32[5,64,128]{2,1,0:T(8,128)S(1)} %get-tuple-element.60), channel_id=1, source_target_pairs={{0,16},{16,0},{1,17},{17,1},{2,18},{18,2},{3,19},{19,3},{4,20},{20... | collective-permute-start | bytes 491528 | tf_op jit(solution)/shard_map/ppermute | solution.py:36
  77.4 4.3 %collective-permute-start.19 = (f32[8,128]{1,0:T(8,128)S(1)}, f32[8,128]{1,0:T(8,128)S(1)}, u32[]{:S(2)}, u32[]{:S(2)}) collective-permute-start(f32[8,128]{1,0:T(8,128)S(1)} %get-tuple-element.64), channel_id=1, source_target_pairs={{0,12},{4,8},{8,4},{12,0},{1,13},{5,9},{9,5},{13,1},{2,14},{6,10},... | collective-permute-start | bytes 12296 | tf_op jit(solution)/shard_map/ppermute | solution.py:44
  78.4 3.4 %collective-permute-start.18 = (f32[8,128]{1,0:T(8,128)S(1)}, f32[8,128]{1,0:T(8,128)S(1)}, u32[]{:S(2)}, u32[]{:S(2)}) collective-permute-start(f32[8,128]{1,0:T(8,128)S(1)} %get-tuple-element.64), channel_id=1, source_target_pairs={{0,8},{4,12},{8,0},{12,4},{1,9},{5,13},{9,1},{13,5},{2,10},{6,14},... | collective-permute-start | bytes 12296 | tf_op jit(solution)/shard_map/ppermute | solution.py:44
  80.1 2.5 %collective-permute-start.17 = (f32[8,128]{1,0:T(8,128)S(1)}, f32[8,128]{1,0:T(8,128)S(1)}, u32[]{:S(2)}, u32[]{:S(2)}) collective-permute-start(f32[8,128]{1,0:T(8,128)S(1)} %get-tuple-element.64), channel_id=1, source_target_pairs={{0,4},{4,0},{8,12},{12,8},{1,5},{5,1},{9,13},{13,9},{2,6},{6,2},{1... | collective-permute-start | bytes 12296 | tf_op jit(solution)/shard_map/ppermute | solution.py:44
  82.5 2.6 %collective-permute-start.20 = (f32[4,8,128]{2,1,0:T(8,128)S(1)}, f32[4,8,128]{2,1,0:T(8,128)S(1)}, u32[]{:S(2)}, u32[]{:S(2)}) collective-permute-start(f32[4,8,128]{2,1,0:T(8,128)S(1)} %pad_maximum_fusion), channel_id=1, source_target_pairs={{0,2},{1,3},{2,0},{3,1},{4,6},{5,7},{6,4},{7,5},{8,10},{9,11},{10,... | collective-permute-start | bytes 49160 | tf_op jit(solution)/shard_map/ppermute | solution.py:44
  85.1 2.5 %collective-permute-start.21 = (f32[8,8,128]{2,1,0:T(8,128)S(1)}, f32[8,8,128]{2,1,0:T(8,128)S(1)}, u32[]{:S(2)}, u32[]{:S(2)}) collective-permute-start(f32[8,8,128]{2,1,0:T(8,128)S(1)} %get-tuple-element.100), channel_id=1, source_target_pairs={{0,1},{1,0},{2,3},{3,2},{4,5},{5,4},{6,7},{7,6},{8,9},{9,8},{10,11... | collective-permute-start | bytes 98312 | tf_op jit(solution)/shard_map/ppermute | solution.py:44
  86.3 7.7 %collective-permute-start.16 = (f32[120,128]{1,0:T(8,128)S(1)}, f32[120,128]{1,0:T(8,128)S(1)}, u32[]{:S(2)}, u32[]{:S(2)}) collective-permute-start(f32[120,128]{1,0:T(8,128)S(1)} %get-tuple-element.63), channel_id=1, source_target_pairs={{0,16},{16,0},{1,17},{17,1},{2,18},{18,2},{3,19},{19,3},{4,20},{20... | collective-permute-start | bytes 184328 | tf_op jit(solution)/shard_map/ppermute | solution.py:36

commit v5 on v4

--- a/solution.py
+++ b/solution.py
@@ -48,13 +48,19 @@
     return lax.rem(lax.axis_index(axis), 2) == 0
 
 
-def call(body, outs, *args, scratch=(), smem=(), hbm_out=False, more=()):
+def call(body, outs, *args, scratch=(), smem=(), hbm=(), hbm_out=False, more=(), alias=None):
     specs = [
-        pl.BlockSpec(memory_space=pltpu.SMEM if i in smem else pltpu.VMEM) for i in range(len(args))
+        pl.BlockSpec(memory_space=pltpu.SMEM if i in smem else pltpu.HBM if i in hbm else pltpu.VMEM)
+        for i in range(len(args))
     ]
     shapes = [jax.ShapeDtypeStruct(s, F32) if hbm_out else pltpu.VMEM(s, F32) for s in outs]
     space = pl.ANY if hbm_out else pltpu.VMEM
-    args = [pltpu.with_memory_space_constraint(a, pltpu.VMEM) if (i not in smem and a.dtype == F32) else a for i, a in enumerate(args)]
+    spaces = [pltpu.HBM if i in hbm or i in smem else pltpu.VMEM for i in range(len(args))]
+    args = [
+        a if m is None or (m is pltpu.VMEM and a.dtype != F32)
+        else pltpu.with_memory_space_constraint(a, m)
+        for a, m in zip(args, spaces)
+    ]
     limit = 4 * sum(math.prod(s) for s in scratch) + 6 * 2**20
     return pl.pallas_call(
         body,
@@ -64,6 +70,7 @@
         scratch_shapes=[pltpu.VMEM(s, F32) for s in scratch] + list(more),
         name=getattr(body, "__name__", None) or body.func.__name__,
         compiler_params=pltpu.CompilerParams(vmem_limit_bytes=limit),
+        input_output_aliases=alias or {},
     )(*args)
 
 
@@ -86,30 +93,68 @@
     return jnp.where(hi, total - width, 0)
 
 
-def start_kernel(nsx, src, guess, cls, table, c_out, y_a, y_b, *x_out):
+def look_up(k, table):
+    acc = jnp.full(k.shape, table[0], F32)
+    for i in range(1, CLASSES):
+        acc = jnp.where(k == i, table[i], acc)
+    return acc
+
+
+def face_kernel(src, guess, cls, table, y_a, y_b, x_out, *s):
+    k_x, k_a, k_b, sems = s
     nx, ny, _ = src.shape
+    p5 = face_start("gx", nx, HX, True)
+    p4 = face_start("gx", nx, HX - 1, True)
+    r_a = pl.multiple_of(face_start("gy", ny, 8, True), 8)
+    r_b = pl.multiple_of(face_start("gy", ny, 8, False), 8)
+    copies = [
+        (cls.at[pl.ds(p5, HX)], k_x),
+        (cls.at[:, pl.ds(r_a, 8)], k_a),
+        (cls.at[:, pl.ds(r_b, 8)], k_b),
+        (guess.at[pl.ds(p5, HX)], x_out.at[HX : 2 * HX]),
+        (src.at[pl.ds(p4, HX - 1)], x_out.at[2 * HX : 3 * HX - 1]),
+        (guess.at[:, pl.ds(r_a, 8)], y_a.at[nx : 2 * nx]),
+        (src.at[:, pl.ds(r_a, 8)], y_a.at[2 * nx : 3 * nx]),
+        (guess.at[:, pl.ds(r_b, 8)], y_b.at[nx : 2 * nx]),
+        (src.at[:, pl.ds(r_b, 8)], y_b.at[2 * nx : 3 * nx]),
+    ]
+    copies = [pltpu.make_async_copy(f, t, sems.at[i]) for i, (f, t) in enumerate(copies)]
+    for cp in copies:
+        cp.start()
+    for cp in copies[:3]:
+        cp.wait()
+    for f in range(HX):
+        x_out[f] = look_up(k_x[f], table)
+    for x in range(nx):
+        y_a[x] = look_up(k_a[x], table)
+        y_b[x] = look_up(k_b[x], table)
+    for cp in copies[3:]:
+        cp.wait()
+
+
+def load_kernel(src, guess, cls, table, c_out, guess_out, src_out, k, sems):
+    nx = src.shape[0]
+    half = nx // 2
+    copies = []
+    for h in range(2):
+        at = pl.ds(h * half, half)
+        copies.append((cls.at[at], k.at[at]))
+    for h in range(2):
+        at = pl.ds(h * half, half)
+        copies.append((guess.at[at], guess_out.at[at]))
+        copies.append((src.at[at], src_out.at[at]))
+    copies = [pltpu.make_async_copy(f, t, sems.at[i]) for i, (f, t) in enumerate(copies)]
+    for cp in copies:
+        cp.start()
 
     def plane(x, _):
-        k = cls[x]
-        acc = jnp.full(k.shape, table[0], F32)
-        for i in range(1, CLASSES):
-            acc = jnp.where(k == i, table[i], acc)
-        c_out[x] = acc
-        return 0
-
-    lax.fori_loop(0, nx, plane, 0)
-    for s in range(nsx):
-        p5 = face_start("gx", nx, HX, s == 0)
-        p4 = face_start("gx", nx, HX - 1, s == 0)
-        for f in range(HX):
-            x_out[s][f] = c_out[p5 + f]
-            x_out[s][HX + f] = guess[p5 + f]
-        for f in range(HX - 1):
-            x_out[s][2 * HX + f] = src[p4 + f]
-    for ref, flag in ((y_a, True), (y_b, False)):
-        r = pl.multiple_of(face_start("gy", ny, 8, flag), 8)
-        for k, a in enumerate((c_out, guess, src)):
-            ref[k * nx : (k + 1) * nx] = a[:, pl.ds(r, 8), :]
+        c_out[x] = look_up(k[x], table)
+
+    for h in range(2):
+        copies[h].wait()
+        fine_loop(h * half, half, plane, 2)
+    for cp in copies[2:]:
+        cp.wait()
 
 
 def zpack_kernel(na, *refs):
@@ -151,52 +196,69 @@
     return [(k, f, widths[k]) for k in range(na) for f in range(widths[k])]
 
 
-def xframe_kernel(na, nx, nsx, r_a, r_b, z_a, z_b, *x_out):
+def frame_list(na):
+    out, row = [], 0
+    for k in range(na):
+        width = (HX, HX, HX - 1)[k]
+        for dx in range(1, width):
+            out.append((k, dx, row, width - dx))
+            row += 2 * (width - dx)
+    return out, -(-row // 8) * 8
+
+
+def frame_rows(na):
+    items, base = frame_list(na)
+    return base + 8 * len(items)
+
+
+def xframe_kernel(na, nx, r_a, r_b, z_a, z_b, x_out):
     ey = even("gy")
-    planes = face_list(na)
-    base = len(planes) * 16
-    for s in range(nsx):
-        for j, (k, f, w) in enumerate(planes):
-            p = k * nx + face_start("gx", nx, w, s == 0) + f
-            va, vb = r_a[p], r_b[p]
-            x_out[s][j * 16 : j * 16 + 8] = jnp.where(ey, vb, va)
-            x_out[s][j * 16 + 8 : j * 16 + 16] = jnp.where(ey, va, vb)
-            x_out[s][base + j * 8 : base + j * 8 + 8] = halo_of(z_a, z_b, p)
+    items, base = frame_list(na)
+    for j, (k, dx, row, w) in enumerate(items):
+        p = k * nx + jnp.where(even("gx"), nx - dx, dx - 1)
+        va, vb = r_a[p], r_b[p]
+        x_out[row : row + w] = jnp.where(ey, vb, va)[8 - w : 8]
+        x_out[row + w : row + 2 * w] = jnp.where(ey, va, vb)[0:w]
+        x_out[base + j * 8 : base + j * 8 + 8] = halo_of(z_a, z_b, p)
 
 
 def own_offset(nsx):
     return HX * lax.axis_index("gx") if nsx == 1 else HX
 
 
-def assemble(nsx, planes, m, h, own, r_a, r_b, z_a, z_b, x1, x2):
+def assemble_own(k, m, h, own, r_a, r_b, z_a, z_b):
     nx, ny, _ = own.shape
-    off = 1 + own_offset(nsx)
+    off = 1 + own_offset(1)
     ey = even("gy")
-    kk = planes[0]
 
     def one(x, _):
-        va, vb = r_a[kk * nx + x], r_b[kk * nx + x]
+        va, vb = r_a[k * nx + x], r_b[k * nx + x]
         m[off + x, 8:16] = jnp.where(ey, vb, va)
         m[off + x, 16 : 16 + ny] = own[x]
         m[off + x, 16 + ny : 24 + ny] = jnp.where(ey, va, vb)
-        h[off + x] = halo_of(z_a, z_b, kk * nx + x)
-        return 0
-
-    lax.fori_loop(0, nx, one, 0)
-    for s in range(nsx):
-        hi = even("gx") if s == 0 else jnp.logical_not(even("gx"))
-        for j, _, f, w, base in planes[1]:
+        h[off + x] = halo_of(z_a, z_b, k * nx + x)
+
+    fine_loop(0, nx, one, 2)
+
+
+def assemble_x(na, k, m, h, nx, x1, x2):
+    off = 1 + own_offset(1)
+    hi = even("gx")
+    ny = x1.shape[1]
+    items, base = frame_list(na)
+    for j, (kk, f, w) in enumerate(face_list(na)):
+        if kk == k:
             p = off + jnp.where(hi, nx, -w) + f
-            m[p, 8:16] = x2[s][j * 16 : j * 16 + 8]
-            m[p, 16 : 16 + ny] = x1[s][j]
-            m[p, 16 + ny : 24 + ny] = x2[s][j * 16 + 8 : j * 16 + 16]
-            h[p] = x2[s][base + j * 8 : base + j * 8 + 8]
-
-
-def plane_map(na, k):
-    ps = face_list(na)
-    base = len(ps) * 16
-    return (k, [(j, kk, f, w, base) for j, (kk, f, w) in enumerate(ps) if kk == k])
+            m[p, 8:16] = jnp.zeros((8, 128), F32)
+            m[p, 16 : 16 + ny] = x1[j]
+            m[p, 16 + ny : 24 + ny] = jnp.zeros((8, 128), F32)
+            h[p] = jnp.zeros((8, 128), F32)
+    for j, (kk, dx, row, w) in enumerate(items):
+        if kk == k:
+            p = off + jnp.where(hi, nx + dx - 1, -dx)
+            m[p, 16 - w : 16] = x2[row : row + w]
+            m[p, 16 + ny : 16 + ny + w] = x2[row + w : row + 2 * w]
+            h[p] = x2[base + j * 8 : base + j * 8 + 8]
 
 
 def zshift(vals, wrap=True):
@@ -335,8 +397,7 @@
 
 
 def fine_loop(lo, count, plane, unroll):
-    while count % unroll:
-        unroll -= 1
+    unroll = max(u for u in range(1, unroll + 2) if count % u == 0)
 
     def group(i, _):
         for u in range(unroll):
@@ -451,10 +512,6 @@
     return [(xp + 2, rows + 16, 128), (xp + 2, 8, 128)] + [m, h] * 7 + [m]
 
 
-def fine_work(xp, rows):
-    return [(xp + 2, rows + 16, 128), (xp + 2, 8, 128)] * 3
-
-
 def split_kept(s):
     two = lambda i: (s[i], s[i + 1])
     return two(0), [two(2 + 2 * j) for j in range(6)], two(14), s[16]
@@ -475,43 +532,45 @@
         lax.fori_loop(0, n, one, 0)
 
 
-def load_fine(nsx, na, which, refs_own, r, target):
-    for k, own, (m, h) in zip(which, refs_own, target):
-        assemble(nsx, plane_map(na, k), m, h, own, *r)
-
-
-def set_up_fine(nsx, c_own, src, r, c, b, a, q, d):
+def near_far():
+    ix = lax.axis_index("gx")
+    return 1 + (HX + 1) * ix, jnp.where(ix == 0, 16, 2)
+
+
+def fine_sweeps(nx, v, w, a, q):
+    for _ in range(SWEEPS - 1):
+        lo, count = fine_range(1, nx, HX - 1)
+        fine_sweep(w, v, a, q, lo, count)
+        v, w = w, v
+    return w
+
+
+def fine_prep_kernel(c_own, guess, src, r_a, r_b, z_a, z_b, *s):
+    c, a, q, d = split_kept(s[:17])
+    b, v, w = (s[17], s[18]), (s[19], s[20]), (s[21], s[22])
+    clear_rim(c, v, w)
+    for k, own, (m, h) in ((0, c_own, c), (1, guess, v), (2, src, b)):
+        assemble_own(k, m, h, own, r_a, r_b, z_a, z_b)
+    lo, _ = near_far()
     nx = src.shape[0]
-    clear_rim(c)
-    load_fine(nsx, 3, (0, 2), (c_own, src), r, (c, b))
-    lo, count = fine_range(nsx, nx, HX - 1)
-    fine_coef(c, b, a, q, d, lo, count)
-
-
-def fine_sweeps(nsx, nx, v, w, a, q):
-    for _ in range(SWEEPS):
-        lo, count = fine_range(nsx, nx, HX - 1)
-        fine_sweep(v, w, a, q, lo, count)
-        v, w = w, v
-    return v
-
-
-def fine_down_kernel(nsx, keep, *refs):
-    c_own, guess, src = refs[:3]
-    n = 7 + 2 * nsx
-    r = refs[3:7] + (refs[7 : 7 + nsx], refs[7 + nsx : n])
-    v_out, bc, y_a, y_b = refs[n : n + 4]
-    xf = refs[n + 4 : n + 4 + nsx]
-    s = refs[n + 4 + nsx :]
+    fine_coef(c, b, a, q, d, lo, nx - 1)
+    fine_sweep(v, w, a, q, lo, nx - 1)
+
+
+def fine_down_kernel(c_own, src, x1, x2, *refs):
+    s = refs[23:46]
+    v_out, bc, y_a, y_b, xf = refs[46:51]
+    pair = refs[51]
     c, a, q, d = split_kept(s[:17])
-    b, v, v2 = (s[17], s[18]), (s[19], s[20]), (s[21], s[22])
-    pair = s[23]
+    b, v, w = (s[17], s[18]), (s[19], s[20]), (s[21], s[22])
     nx, ny, _ = src.shape
-    off = 1 + own_offset(nsx)
-    set_up_fine(nsx, c_own, src, r, c, b, a, q, d)
-    clear_rim(v, v2)
-    load_fine(nsx, 3, (1,), (guess,), r, (v,))
-    v = fine_sweeps(nsx, nx, v, v2, a, q)
+    off = 1 + own_offset(1)
+    for k, (m, h) in ((0, c), (1, v), (2, b)):
+        assemble_x(3, k, m, h, nx, x1, x2)
+    _, lo = near_far()
+    fine_coef(c, b, a, q, d, lo, HX)
+    fine_sweep(v, w, a, q, lo, HX)
+    v = fine_sweeps(nx, v, w, a, q)
     pb, pc = pick(0, 64, 128), pick(64, 64, 128)
 
     def coarse(i, _):
@@ -537,10 +596,9 @@
         return 0
 
     lax.fori_loop(0, nx // 2, coarse, 0)
-    for k in range(nsx):
-        p5 = face_start("gx", nx, HX, k == 0)
-        for f in range(HX):
-            xf[k][f] = v_out[p5 + f]
+    p5 = face_start("gx", nx, HX, True)
+    for f in range(HX):
+        xf[f] = v_out[p5 + f]
     for ref, flag in ((y_a, True), (y_b, False)):
         r = pl.multiple_of(face_start("gy", ny, 8, flag), 8)
         ref[...] = v_out[:, pl.ds(r, 8), :]
@@ -590,7 +648,7 @@
     b, d, w = (s[20],), (s[21],), (s[22],)
     b2, d2, w2 = (s[23],), (s[24],), (s[25],)
     pair = s[26]
-    xframe_kernel(1, vr_a.shape[0], 1, vr_a, vr_b, vz_a, vz_b, frame)
+    xframe_kernel(1, vr_a.shape[0], vr_a, vr_b, vz_a, vz_b, frame)
     v, v2 = (v1_out,), (v2_out,)
     nx, ny, _ = full.shape
     tiles = ny // 8
@@ -794,31 +852,16 @@
         v[1][x] = v[1][x] + jnp.where(c[1][x] > 0.0, edge, 0.0)
 
 
-def fine_up_kernel(nsx, keep, *refs):
-    c_own, v_own, src = refs[:3]
-    n = 7 + 2 * nsx
-    r = refs[3:7] + (refs[7 : 7 + nsx], refs[7 + nsx : n])
-    vr = refs[n : n + 4] + (refs[n + 4 : n + 4 + nsx], refs[n + 4 + nsx : n + 4 + 2 * nsx])
-    n = n + 4 + 2 * nsx
-    v1 = refs[n]
-    n = n + 1
-    if keep:
-        c, a, q, d = split_kept(refs[n : n + 17])
-        n = n + 17
-    sol_hbm, res_hbm = refs[n : n + 2]
-    sol, res, sems = refs[-3:]
-    s = refs[n + 2 : -3]
-    if not keep:
-        c, a, q, d = split_kept(s[:17])
-        s = s[17:]
-    b, v, v2 = (s[0], s[1]), (s[2], s[3]), (s[4], s[5])
-    tmp, stage, spread = s[6:9]
+def fine_up_kernel(v_own, src, vr_a, vr_b, vz_a, vz_b, x1, x2, v1, *refs):
+    c, a, q, d = split_kept(refs[:17])
+    sol_hbm, res_hbm = refs[17:19]
+    v, w = (refs[19], refs[20]), (refs[21], refs[22])
+    tmp, stage, spread, sol, res, sems = refs[23:]
     nx, ny, _ = src.shape
-    off = 1 + own_offset(nsx)
-    if not keep:
-        set_up_fine(nsx, c_own, src, r, c, b, a, q, d)
-    clear_rim(v, v2)
-    load_fine(nsx, 1, (0,), (v_own,), vr, (v,))
+    off = 1 + own_offset(1)
+    clear_rim(v, w)
+    assemble_own(0, v[0], v[1], v_own, vr_a, vr_b, vz_a, vz_b)
+    assemble_x(1, 0, v[0], v[1], nx, x1, x2)
     i = lax.broadcasted_iota(jnp.int32, (128, 256), 0)
     o = lax.broadcasted_iota(jnp.int32, (128, 256), 1)
     within = lax.rem(o - 128, GW)
@@ -842,7 +885,9 @@
         return 0
 
     lax.fori_loop(0, count, up, 0)
-    v = fine_sweeps(nsx, nx, v, v2, a, q)
+    lo, total = fine_range(1, nx, HX - 1)
+    fine_sweep(v, w, a, q, lo, total)
+    v = fine_sweeps(nx, v, w, a, q)
 
     step = nx // 4
 
@@ -873,29 +918,6 @@
 def named(fn, *args):
     out = functools.partial(fn, *args)
     out.__name__ = fn.__name__
-    return out
-
-
-def exchange_rest(na, arrs, y_a, y_b, nsx):
-    nx, ny, _ = arrs[0].shape
-    rows = ny + 16
-    r_a, r_b = swap_even(y_a, "gy"), swap_odd(y_b, "gy")
-    (z,) = call(
-        named(zpack_kernel, na), [(na * nx, 8, 128)], *arrs, r_a, r_b,
-        scratch=[(na * nx * 8, 128)],
-    )
-    z_a, z_b = swap_even(z, "gz"), swap_odd(z, "gz")
-    count = len(face_list(na))
-    size = count * 24
-    xs = call(named(xframe_kernel, na, nx, nsx), [(size, 128)] * nsx, r_a, r_b, z_a, z_b)
-    x2 = swap_x(xs)
-    return (r_a, r_b, z_a, z_b), x2
-
-
-def swap_x(xs):
-    out = [swap_even(xs[0], "gx")]
-    if len(xs) > 1:
-        out.append(swap_odd(xs[1], "gx"))
     return out
 
 
@@ -1012,38 +1034,54 @@
     gx, gy, gz = (lax.axis_size(n) for n in ("gx", "gy", "gz"))
     if (gx, gy, gz, nx, ny, nz) != (2, 4, 4, 16, 64, 128):
         return plain_body(source, first_guess, cell_classes, class_table)
-    nsx = 1 if gx == 2 else 2
-    xp = nx + nsx * HX
+    xp = nx + HX
     rows = ny + 16
     full = (nx, ny, 128)
-
-    out = call(
-        named(start_kernel, nsx),
-        [full, (3 * nx, 8, 128), (3 * nx, 8, 128)] + [(3 * HX - 1, ny, 128)] * nsx,
+    halo = (3 * nx, 8, 128)
+
+    y_a, y_b, x1 = call(
+        face_kernel,
+        [halo, halo, (3 * HX - 1, ny, 128)],
         source, first_guess, cell_classes, class_table,
         smem=(3,),
+        hbm=(0, 1, 2),
+        more=[pltpu.VMEM((HX, ny, 128), jnp.int32)]
+        + [pltpu.VMEM((nx, 8, 128), jnp.int32)] * 2
+        + [pltpu.SemaphoreType.DMA((9,))],
     )
-    c_own, y_a, y_b, xs = out[0], out[1], out[2], out[3:]
-    x1 = swap_x(xs)
-    rec, x2 = exchange_rest(3, (c_own, first_guess, source), y_a, y_b, nsx)
-    keep = True
-    kept_shapes = fine_kept(xp, rows)
-    outs = [full, (nx // 2, ny // 2, 128), (nx, 8, 128), (nx, 8, 128)] + [(HX, ny, 128)] * nsx
-    work = fine_work(xp, rows) + [(2, ny, 128)]
+    x1 = swap_even(x1, "gx")
+    r_a, r_b = swap_even(y_a, "gy"), swap_odd(y_b, "gy")
+    own = call(
+        load_kernel,
+        [full, full, full],
+        source, first_guess, cell_classes, class_table,
+        smem=(3,),
+        hbm=(0, 1, 2),
+        more=[pltpu.VMEM(full, jnp.int32), pltpu.SemaphoreType.DMA((6,))],
+    )
+    c_own, _, source = own
+    (z,) = call(named(zpack_kernel, 3), [halo], *own, r_a, r_b, scratch=[(3 * nx * 8, 128)])
+    rec = (r_a, r_b, swap_even(z, "gz"), swap_odd(z, "gz"))
+    (x2,) = call(named(xframe_kernel, 3, nx), [(frame_rows(3), 128)], *rec)
+    x2 = swap_even(x2, "gx")
+    pad = [(xp + 2, rows + 16, 128), (xp + 2, 8, 128)]
+    state_shapes = fine_kept(xp, rows) + pad * 3
+    state = call(fine_prep_kernel, state_shapes, *own, *rec)
     out = call(
-        named(fine_down_kernel, nsx, keep),
-        outs + (kept_shapes if keep else []),
-        c_own, first_guess, source, *rec, *x1, *x2,
-        scratch=work if keep else kept_shapes + work,
+        fine_down_kernel,
+        state_shapes
+        + [full, (nx // 2, ny // 2, 128), (nx, 8, 128), (nx, 8, 128), (HX, ny, 128)],
+        c_own, source, x1, x2, *state,
+        scratch=[(2, ny, 128)],
+        alias={4 + i: i for i in range(23)},
     )
-    kept = out[len(outs) :]
-    out = out[: len(outs)]
-    v0, bc1, vy_a, vy_b, vxs = out[0], out[1], out[2], out[3], out[4:]
+    kept = out[:17]
+    v0, bc1, vy_a, vy_b, vx1 = out[23:]
 
     n1, ny1 = nx, ny // 2
     (f1,) = call(join_kernel, [(n1, ny1, 128)], bc1, swap_even(bc1, "gx"))
     vr_a, vr_b = swap_even(vy_a, "gy"), swap_odd(vy_b, "gy")
-    vx1 = swap_x(vxs)
+    vx1 = swap_even(vx1, "gx")
     r_a, r_b = swap_even(f1, "gy"), swap_odd(f1, "gy")
     rows1 = 3 * ny1
     z_a, z_b, vz = call(
@@ -1061,12 +1099,12 @@
     kept_mid = [pad1, pad1] + [bare1] * 7 + [pad2, pad2] + [bare2] * 7
     out = call(
         mid_down_kernel,
-        kept_mid + [(-(-n3 // 4) * yb, 128), (HX * 24, 128)],
+        kept_mid + [(-(-n3 // 4) * yb, 128), (frame_rows(1), 128)],
         f1, r_a, r_b, z_a, z_b, vr_a, vr_b, vz_a, vz_b,
         scratch=[pad1, bare1, pad1, pad2, bare2, pad2, (2, 2 * rows2, 128)],
     )
     kept_mid, (bc3, frame) = out[:-2], out[-2:]
-    vx2 = [swap_even(frame, "gx")]
+    vx2 = swap_even(frame, "gx")
     vrec = (vr_a, vr_b, vz_a, vz_b)
 
     got = jnp.stack([bc3] + [swap_xor(bc3, "gy", m) for m in range(1, gy)])
@@ -1083,12 +1121,11 @@
         scratch=[pad1, pad2, pad2] + [pad3] * 4 + [bare3] * 7 + [(2 * (ny1 + 16), 128)],
     )
     par_rows = (xp + 2) // 2 * (rows // 2)
-    work = fine_work(xp, rows) + [(2, rows, 128), (par_rows, 128), (par_rows, 256)]
     sol, res = call(
-        named(fine_up_kernel, nsx, keep),
+        fine_up_kernel,
         [full, full],
-        c_own, v0, source, *rec, *x1, *x2, *vrec, *vx1, *vx2, v1, *kept,
-        scratch=(work if keep else kept_shapes + work) + [full, full],
+        v0, source, *vrec, vx1, vx2, v1, *kept,
+        scratch=pad * 2 + [(2, rows, 128), (par_rows, 128), (par_rows, 256), full, full],
         hbm_out=True,
         more=[pltpu.SemaphoreType.DMA((2, 4))],
     )

time: 103 us -> 95.2 us (0.924)
  waiting for transfers between devices: 27.3 us -> 22 us
  local copies, waits for them, and re-layouts: 3.8 us -> 0.02 us
  Pallas kernels: 36.5 us -> 38.1 us
    ppermute x11, waiting for transfers between devices: 16.7 us -> 11.6 us  [swap_even(): return lax.ppermute(x, axis, pairs_even(lax.axis_size(axis)))]
    unnamed x16 -> x4, local copies, waits for them, and re-layouts: 3.79 us -> 0.01 us
    pallas_call x9 -> x11, Pallas kernels: 36.5 us -> 38.1 us  [call(): pl.pallas_call(body, out_shape=shapes, in_specs=specs, out_specs=[pl.Bloc...]
    ppermute x11, starting transfers between devices: 17.5 us -> 16.1 us  [swap_even(): return lax.ppermute(x, axis, pairs_even(lax.axis_size(axis)))]
  transfers between devices with their start and end apart: 22 -> 22, of which waited for: 9 -> 8; matrix products, arithmetic and copies ran while one was open for 0% -> 0% of each run, Pallas kernels for 15% -> 21%
where the time goes in v5:
time: 95.2 us; the launch traced here: 94.6 us
  Pallas kernels  38.1 us (40%)
  starting transfers between devices  33.7 us (35%)
  waiting for transfers between devices  22 us (23%)
    pallas_call x11, Pallas kernels, call(): pl.pallas_call(body, out_shape=shapes, in_specs=specs, out_specs=[pl.Bloc...  38.1 us
    ppermute x11, starting transfers between devices, swap_even(): return lax.ppermute(x, axis, pairs_even(lax.axis_size(axis)))  16.1 us
    ppermute x6, starting transfers between devices, swap_odd(): return lax.ppermute(x, axis, pairs_odd(lax.axis_size(axis)))  12 us
    ppermute x11, waiting for transfers between devices, swap_even(): return lax.ppermute(x, axis, pairs_even(lax.axis_size(axis)))  11.6 us
    ppermute x6, waiting for transfers between devices, swap_odd(): return lax.ppermute(x, axis, pairs_odd(lax.axis_size(axis)))  6.34 us
    ppermute x5, starting transfers between devices, swap_xor(): lax.ppermute(x, axis, [(i, i ^ m) for i in range(lax.axis_size(axis))])  5.57 us
    ppermute x5, waiting for transfers between devices, swap_xor(): lax.ppermute(x, axis, [(i, i ^ m) for i in range(lax.axis_size(axis))])  4.11 us
  transfers between devices with their start and end apart: 22, of which 8 were waited for; matrix products, arithmetic and copies ran while one was open for 0% of the time, Pallas kernels for 21%

profile of v5, /device:TPU:1, one launch (start us, length us, event | category | flops | bytes accessed | tf_op | source)
XLA Modules:
  0.0 94.6 jit_solution(8000541249980305567)
XLA Ops:
  0.6 1.9 %face_kernel.1 = (f32[48,8,128]{2,1,0:T(8,128)S(1)}, f32[48,8,128]{2,1,0:T(8,128)S(1)}, f32[14,64,128]{2,1,0:T(8,128)S(1)}) custom-call(f32[16,64,128]{2,1,0:T(8,128)} %src.3, f32[16,64,128]{2,1,0:T(8,128)} %guess.3, s32[16,64,128]{2,1,0:T(8,128)} %cls.3, f32[8]{0:T(128)} %table.3), custom_call_target="tpu_custom_call" | custom-call | tf_op jit(solution)/shard_map/face_kernel/pallas_call | solution.py:65
  2.6 2.2 %collective-permute-start.1 = (f32[48,8,128]{2,1,0:T(8,128)S(1)}, f32[48,8,128]{2,1,0:T(8,128)S(1)}, u32[]{:S(2)}, u32[]{:S(2)}) collective-permute-start(f32[48,8,128]{2,1,0:T(8,128)S(1)} %get-tuple-element.79), channel_id=1, source_target_pairs={{0,4},{4,0},{8,12},{12,8},{1,5},{5,1},{9,13},{13,9},{2,6},{6,2},{1... | collective-permute-start | bytes 589832 | tf_op jit(solution)/shard_map/ppermute | solution.py:36
  4.8 0.7 collective-permute-start.2
  5.4 1.3 %collective-permute-start = (f32[14,64,128]{2,1,0:T(8,128)S(1)}, f32[14,64,128]{2,1,0:T(8,128)S(1)}, u32[]{:S(2)}, u32[]{:S(2)}) collective-permute-start(f32[14,64,128]{2,1,0:T(8,128)S(1)} %get-tuple-element.78), channel_id=1, source_target_pairs={{0,16},{16,0},{1,17},{17,1},{2,18},{18,2},{3,19},{19,3},{4,20},{20... | collective-permute-start | bytes 1376264 | tf_op jit(solution)/shard_map/ppermute | solution.py:36
  6.7 2.1 %load_kernel.1 = (f32[16,64,128]{2,1,0:T(8,128)S(1)}, f32[16,64,128]{2,1,0:T(8,128)S(1)}, f32[16,64,128]{2,1,0:T(8,128)S(1)}) custom-call(f32[16,64,128]{2,1,0:T(8,128)} %src.3, f32[16,64,128]{2,1,0:T(8,128)} %guess.3, s32[16,64,128]{2,1,0:T(8,128)} %cls.3, f32[8]{0:T(128)} %table.3), custom_call_target="tpu_custom_call" | custom-call | tf_op jit(solution)/shard_map/load_kernel/pallas_call | solution.py:65
  9.4 0.7 zpack_kernel.1
  10.1 4.4 %collective-permute-start.4 = (f32[48,8,128]{2,1,0:T(8,128)S(1)}, f32[48,8,128]{2,1,0:T(8,128)S(1)}, u32[]{:S(2)}, u32[]{:S(2)}) collective-permute-start(f32[48,8,128]{2,1,0:T(8,128)S(1)} %zpack_kernel.1), channel_id=1, source_target_pairs={{1,2},{2,1},{5,6},{6,5},{9,10},{10,9},{13,14},{14,13},{17,18},{18,... | collective-permute-start | bytes 589832 | tf_op jit(solution)/shard_map/ppermute | solution.py:40
  14.6 3.4 %collective-permute-done.4.z_b = f32[48,8,128]{2,1,0:T(8,128)S(1)} collective-permute-done((f32[48,8,128]{2,1,0:T(8,128)S(1)}, f32[48,8,128]{2,1,0:T(8,128)S(1)}, u32[]{:S(2)}, u32[]{:S(2)}) %collective-permute-start.4) | collective-permute-done | bytes 196640 | tf_op jit(solution)/shard_map/ppermute | solution.py:40
  18.1 1.3 %collective-permute-start.5 = (f32[144,128]{1,0:T(8,128)S(1)}, f32[144,128]{1,0:T(8,128)S(1)}, u32[]{:S(2)}, u32[]{:S(2)}) collective-permute-start(f32[144,128]{1,0:T(8,128)S(1)} %xframe_kernel.1), channel_id=1, source_target_pairs={{0,16},{16,0},{1,17},{17,1},{2,18},{18,2},{3,19},{19,3},{4,20},{20... | collective-permute-start | bytes 221192 | tf_op jit(solution)/shard_map/ppermute | solution.py:36
  19.4 2.7 %fine_prep_kernel.1 = (f32[23,96,128]{2,1,0:T(8,128)S(1)}, f32[23,8,128]{2,1,0:T(8,128)S(1)}, f32[21,80,128]{2,1,0:T(8,128)S(1)}, f32[21,8,128]{2,1,0:T(8,128)S(...) custom-call(f32[16,64,128]{2,1,0:T(8,128)S(1)} %get-tuple-element.76, ...), custom_call_target="tpu_custom_call" | custom-call | tf_op jit(solution)/shard_map/fine_prep_kernel/pallas_call | solution.py:65
  22.0 7.2 %fine_down_kernel.1 = (f32[23,96,128]{2,1,0:T(8,128)S(1)}, f32[23,8,128]{2,1,0:T(8,128)S(1)}, f32[21,80,128]{2,1,0:T(8,128)S(1)}, f32[21,8,128]{2,1,0:T(8,128)S(...) custom-call(f32[16,64,128]{2,1,0:T(8,128)S(1)} %get-tuple-element.76, ...), custom_call_target="tpu_custom_call", output_to_operand_aliasing={{0}: (4, {}), {1}: (5, {}), {2}: (6, {}), {3}: (7, {}), {4}... | custom-call | tf_op jit(solution)/shard_map/fine_down_kernel/pallas_call | solution.py:65
  29.9 3.8 %collective-permute-done.8.other = f32[8,32,128]{2,1,0:T(8,128)S(1)} collective-permute-done((f32[8,32,128]{2,1,0:T(8,128)S(1)}, f32[8,32,128]{2,1,0:T(8,128)S(1)}, u32[]{:S(2)}, u32[]{:S(2)}) %collective-permute-start.8) | collective-permute-done | bytes 131104 | tf_op jit(solution)/shard_map/ppermute | solution.py:36
  33.7 0.7 collective-permute-start.10
  34.3 7.1 %collective-permute-start.9 = (f32[16,32,128]{2,1,0:T(8,128)S(1)}, f32[16,32,128]{2,1,0:T(8,128)S(1)}, u32[]{:S(2)}, u32[]{:S(2)}) collective-permute-start(f32[16,32,128]{2,1,0:T(8,128)S(1)} %join_kernel.1.full), channel_id=1, source_target_pairs={{0,4},{4,0},{8,12},{12,8},{1,5},{5,1},{9,13},{13,9},{2,6},{6,2},{1... | collective-permute-start | bytes 786440 | tf_op jit(solution)/shard_map/ppermute | solution.py:36
  42.2 7.2 %collective-permute-done.6.vr_a = f32[16,8,128]{2,1,0:T(8,128)S(1)} collective-permute-done((f32[16,8,128]{2,1,0:T(8,128)S(1)}, f32[16,8,128]{2,1,0:T(8,128)S(1)}, u32[]{:S(2)}, u32[]{:S(2)}) %collective-permute-start.6) | collective-permute-done | bytes 65568 | tf_op jit(solution)/shard_map/ppermute | solution.py:36
  49.4 0.9 mid_z_kernel.1
  50.2 0.8 collective-permute-start.14
  51.0 1.9 %collective-permute-start.15 = (f32[8,96,128]{2,1,0:T(8,128)S(1)}, f32[8,96,128]{2,1,0:T(8,128)S(1)}, u32[]{:S(2)}, u32[]{:S(2)}) collective-permute-start(f32[8,96,128]{2,1,0:T(8,128)S(1)} %get-tuple-element.112), channel_id=1, source_target_pairs={{1,2},{2,1},{5,6},{6,5},{9,10},{10,9},{13,14},{14,13},{17,18},{18,... | collective-permute-start | bytes 1179656 | tf_op jit(solution)/shard_map/ppermute | solution.py:40
  52.9 3.6 %collective-permute-start.12 = (f32[16,8,128]{2,1,0:T(8,128)S(1)}, f32[16,8,128]{2,1,0:T(8,128)S(1)}, u32[]{:S(2)}, u32[]{:S(2)}) collective-permute-start(f32[16,8,128]{2,1,0:T(8,128)S(1)} %get-tuple-element.109), channel_id=1, source_target_pairs={{1,2},{2,1},{5,6},{6,5},{9,10},{10,9},{13,14},{14,13},{17,18},{18,... | collective-permute-start | bytes 196616 | tf_op jit(solution)/shard_map/ppermute | solution.py:40
  56.7 1.5 %collective-permute-start.13 = (f32[5,64,128]{2,1,0:T(8,128)S(1)}, f32[5,64,128]{2,1,0:T(8,128)S(1)}, u32[]{:S(2)}, u32[]{:S(2)}) collective-permute-start(f32[5,64,128]{2,1,0:T(8,128)S(1)} %get-tuple-element.110), channel_id=1, source_target_pairs={{0,16},{16,0},{1,17},{17,1},{2,18},{18,2},{3,19},{19,3},{4,20},{20... | collective-permute-start | bytes 491528 | tf_op jit(solution)/shard_map/ppermute | solution.py:36
  58.2 2.9 %collective-permute-done.12.vz_b = f32[16,8,128]{2,1,0:T(8,128)S(1)} collective-permute-done((f32[16,8,128]{2,1,0:T(8,128)S(1)}, f32[16,8,128]{2,1,0:T(8,128)S(1)}, u32[]{:S(2)}, u32[]{:S(2)}) %collective-permute-start.12) | collective-permute-done | bytes 65568 | tf_op jit(solution)/shard_map/ppermute | solution.py:40
  61.1 8.0 %mid_down_kernel.1 = (f32[18,112,128]{2,1,0:T(8,128)S(1)}, f32[18,112,128]{2,1,0:T(8,128)S(1)}, f32[16,96,128]{2,1,0:T(8,128)S(1)}, f32[16,96,128]{2,1,0:T(8,128...) custom-call(f32[16,32,128]{2,1,0:T(8,128)S(1)} %join_kernel.1.full, ...), custom_call_target="tpu_custom_call" | custom-call | tf_op jit(solution)/shard_map/mid_down_kernel/pallas_call | solution.py:65
  69.2 0.9 collective-permute-start.19
  70.1 1.7 %collective-permute-start.18 = (f32[8,128]{1,0:T(8,128)S(1)}, f32[8,128]{1,0:T(8,128)S(1)}, u32[]{:S(2)}, u32[]{:S(2)}) collective-permute-start(f32[8,128]{1,0:T(8,128)S(1)} %get-tuple-element.114), channel_id=1, source_target_pairs={{0,8},{4,12},{8,0},{12,4},{1,9},{5,13},{9,1},{13,5},{2,10},{6,14},... | collective-permute-start | bytes 12296 | tf_op jit(solution)/shard_map/ppermute | solution.py:44
  71.8 0.9 collective-permute-start.17
  72.7 0.7 collective-permute-done.19
  73.5 0.8 collective-permute-done.17
  74.3 2.6 %collective-permute-done.20 = f32[4,8,128]{2,1,0:T(8,128)S(1)} collective-permute-done((f32[4,8,128]{2,1,0:T(8,128)S(1)}, f32[4,8,128]{2,1,0:T(8,128)S(1)}, u32[]{:S(2)}, u32[]{:S(2)}) %collective-permute-start.20) | collective-permute-done | bytes 16416 | tf_op jit(solution)/shard_map/ppermute | solution.py:44
  76.9 2.0 %collective-permute-start.21 = (f32[8,8,128]{2,1,0:T(8,128)S(1)}, f32[8,8,128]{2,1,0:T(8,128)S(1)}, u32[]{:S(2)}, u32[]{:S(2)}) collective-permute-start(f32[8,8,128]{2,1,0:T(8,128)S(1)} %get-tuple-element.150), channel_id=1, source_target_pairs={{0,1},{1,0},{2,3},{3,2},{4,5},{5,4},{6,7},{7,6},{8,9},{9,8},{10,11... | collective-permute-start | bytes 98312 | tf_op jit(solution)/shard_map/ppermute | solution.py:44
  78.9 1.2 %collective-permute-start.16 = (f32[56,128]{1,0:T(8,128)S(1)}, f32[56,128]{1,0:T(8,128)S(1)}, u32[]{:S(2)}, u32[]{:S(2)}) collective-permute-start(f32[56,128]{1,0:T(8,128)S(1)} %get-tuple-element.113), channel_id=1, source_target_pairs={{0,16},{16,0},{1,17},{17,1},{2,18},{18,2},{3,19},{19,3},{4,20},{20... | collective-permute-start | bytes 86024 | tf_op jit(solution)/shard_map/ppermute | solution.py:36
  80.1 6.3 %coarse_kernel.1.v1 = f32[18,112,128]{2,1,0:T(8,128)S(1)} custom-call(f32[16,8,128]{2,1,0:T(8,128)S(1)} %constant_dynamic-update-slice_fusion.5.blocks, f32[18,112,128]{2,1,0:T(8,128)S(1)} %get-tuple-element.115.s_0_, f32[18,112,128]{2,1,0:T(8,128)S(1)} %get-tuple-element.116.s_1_, f32[16,96,128]{2,1,0:T(8,128)S(1)} %get-tuple-element.117.s_2_, ...), custom_call_target="tpu_custom_call" | custom-call | tf_op jit(solution)/shard_map/coarse_kernel/pallas_call | solution.py:65
  86.4 8.2 %fine_up_kernel.1 = (f32[16,64,128]{2,1,0:T(8,128)}, f32[16,64,128]{2,1,0:T(8,128)}) custom-call(f32[16,64,128]{2,1,0:T(8,128)S(1)} %get-tuple-element.105.v0.v_own, f32[16,64,128]{2,1,0:T(8,128)S(1)} %get-tuple-element.77.refs_2_.src, f32[16,8,128]{2,1,0:T(8,128)S(1)} %collective-permute-done.6.vr_a, f32[16,8,128]{2,1,0:T(8,128)S(1)} %collective-permute-done.7.vr_b, ...), custom_call_target="tpu_custom_call" | custom-call | tf_op jit(solution)/shard_map/fine_up_kernel/pallas_call | solution.py:65
  (30 shorter events, 2.2 us)
Async XLA Ops:
  2.6 6.8 %collective-permute-start.1 = (f32[48,8,128]{2,1,0:T(8,128)S(1)}, f32[48,8,128]{2,1,0:T(8,128)S(1)}, u32[]{:S(2)}, u32[]{:S(2)}) collective-permute-start(f32[48,8,128]{2,1,0:T(8,128)S(1)} %get-tuple-element.79), channel_id=1, source_target_pairs={{0,4},{4,0},{8,12},{12,8},{1,5},{5,1},{9,13},{13,9},{2,6},{6,2},{1... | collective-permute-start | bytes 589832 | tf_op jit(solution)/shard_map/ppermute | solution.py:36
  4.8 4.6 %collective-permute-start.2 = (f32[48,8,128]{2,1,0:T(8,128)S(1)}, f32[48,8,128]{2,1,0:T(8,128)S(1)}, u32[]{:S(2)}, u32[]{:S(2)}) collective-permute-start(f32[48,8,128]{2,1,0:T(8,128)S(1)} %get-tuple-element.80), channel_id=1, source_target_pairs={{4,8},{8,4},{5,9},{9,5},{6,10},{10,6},{7,11},{11,7},{20,24},{24,20... | collective-permute-start | bytes 589832 | tf_op jit(solution)/shard_map/ppermute | solution.py:40
  5.4 16.6 %collective-permute-start = (f32[14,64,128]{2,1,0:T(8,128)S(1)}, f32[14,64,128]{2,1,0:T(8,128)S(1)}, u32[]{:S(2)}, u32[]{:S(2)}) collective-permute-start(f32[14,64,128]{2,1,0:T(8,128)S(1)} %get-tuple-element.78), channel_id=1, source_target_pairs={{0,16},{16,0},{1,17},{17,1},{2,18},{18,2},{3,19},{19,3},{4,20},{20... | collective-permute-start | bytes 1376264 | tf_op jit(solution)/shard_map/ppermute | solution.py:36
  10.1 7.9 %collective-permute-start.4 = (f32[48,8,128]{2,1,0:T(8,128)S(1)}, f32[48,8,128]{2,1,0:T(8,128)S(1)}, u32[]{:S(2)}, u32[]{:S(2)}) collective-permute-start(f32[48,8,128]{2,1,0:T(8,128)S(1)} %zpack_kernel.1), channel_id=1, source_target_pairs={{1,2},{2,1},{5,6},{6,5},{9,10},{10,9},{13,14},{14,13},{17,18},{18,... | collective-permute-start | bytes 589832 | tf_op jit(solution)/shard_map/ppermute | solution.py:40
  14.6 3.5 %collective-permute-start.3 = (f32[48,8,128]{2,1,0:T(8,128)S(1)}, f32[48,8,128]{2,1,0:T(8,128)S(1)}, u32[]{:S(2)}, u32[]{:S(2)}) collective-permute-start(f32[48,8,128]{2,1,0:T(8,128)S(1)} %zpack_kernel.1), channel_id=1, source_target_pairs={{0,1},{1,0},{2,3},{3,2},{4,5},{5,4},{6,7},{7,6},{8,9},{9,8},{10,11... | collective-permute-start | bytes 589832 | tf_op jit(solution)/shard_map/ppermute | solution.py:36
  18.1 4.0 %collective-permute-start.5 = (f32[144,128]{1,0:T(8,128)S(1)}, f32[144,128]{1,0:T(8,128)S(1)}, u32[]{:S(2)}, u32[]{:S(2)}) collective-permute-start(f32[144,128]{1,0:T(8,128)S(1)} %xframe_kernel.1), channel_id=1, source_target_pairs={{0,16},{16,0},{1,17},{17,1},{2,18},{18,2},{3,19},{19,3},{4,20},{20... | collective-permute-start | bytes 221192 | tf_op jit(solution)/shard_map/ppermute | solution.py:36
  29.3 4.3 %collective-permute-start.8 = (f32[8,32,128]{2,1,0:T(8,128)S(1)}, f32[8,32,128]{2,1,0:T(8,128)S(1)}, u32[]{:S(2)}, u32[]{:S(2)}) collective-permute-start(f32[8,32,128]{2,1,0:T(8,128)S(1)} %get-tuple-element.108.own), channel_id=1, source_target_pairs={{0,16},{16,0},{1,17},{17,1},{2,18},{18,2},{3,19},{19,3},{4,20},{20... | collective-permute-start | bytes 393224 | tf_op jit(solution)/shard_map/ppermute | solution.py:36
  33.7 15.7 %collective-permute-start.10 = (f32[16,32,128]{2,1,0:T(8,128)S(1)}, f32[16,32,128]{2,1,0:T(8,128)S(1)}, u32[]{:S(2)}, u32[]{:S(2)}) collective-permute-start(f32[16,32,128]{2,1,0:T(8,128)S(1)} %join_kernel.1.full), channel_id=1, source_target_pairs={{4,8},{8,4},{5,9},{9,5},{6,10},{10,6},{7,11},{11,7},{20,24},{24,20... | collective-permute-start | bytes 786440 | tf_op jit(solution)/shard_map/ppermute | solution.py:40
  34.3 15.0 %collective-permute-start.9 = (f32[16,32,128]{2,1,0:T(8,128)S(1)}, f32[16,32,128]{2,1,0:T(8,128)S(1)}, u32[]{:S(2)}, u32[]{:S(2)}) collective-permute-start(f32[16,32,128]{2,1,0:T(8,128)S(1)} %join_kernel.1.full), channel_id=1, source_target_pairs={{0,4},{4,0},{8,12},{12,8},{1,5},{5,1},{9,13},{13,9},{2,6},{6,2},{1... | collective-permute-start | bytes 786440 | tf_op jit(solution)/shard_map/ppermute | solution.py:36
  41.4 7.9 %collective-permute-start.6 = (f32[16,8,128]{2,1,0:T(8,128)S(1)}, f32[16,8,128]{2,1,0:T(8,128)S(1)}, u32[]{:S(2)}, u32[]{:S(2)}) collective-permute-start(f32[16,8,128]{2,1,0:T(8,128)S(1)} %get-tuple-element.106), channel_id=1, source_target_pairs={{0,4},{4,0},{8,12},{12,8},{1,5},{5,1},{9,13},{13,9},{2,6},{6,2},{1... | collective-permute-start | bytes 196616 | tf_op jit(solution)/shard_map/ppermute | solution.py:36
  41.5 7.9 %collective-permute-start.7 = (f32[16,8,128]{2,1,0:T(8,128)S(1)}, f32[16,8,128]{2,1,0:T(8,128)S(1)}, u32[]{:S(2)}, u32[]{:S(2)}) collective-permute-start(f32[16,8,128]{2,1,0:T(8,128)S(1)} %get-tuple-element.107), channel_id=1, source_target_pairs={{4,8},{8,4},{5,9},{9,5},{6,10},{10,6},{7,11},{11,7},{20,24},{24,20... | collective-permute-start | bytes 196616 | tf_op jit(solution)/shard_map/ppermute | solution.py:40
  50.2 10.9 %collective-permute-start.14 = (f32[8,96,128]{2,1,0:T(8,128)S(1)}, f32[8,96,128]{2,1,0:T(8,128)S(1)}, u32[]{:S(2)}, u32[]{:S(2)}) collective-permute-start(f32[8,96,128]{2,1,0:T(8,128)S(1)} %get-tuple-element.111), channel_id=1, source_target_pairs={{0,1},{1,0},{2,3},{3,2},{4,5},{5,4},{6,7},{7,6},{8,9},{9,8},{10,11... | collective-permute-start | bytes 1179656 | tf_op jit(solution)/shard_map/ppermute | solution.py:36
  51.0 10.1 %collective-permute-start.15 = (f32[8,96,128]{2,1,0:T(8,128)S(1)}, f32[8,96,128]{2,1,0:T(8,128)S(1)}, u32[]{:S(2)}, u32[]{:S(2)}) collective-permute-start(f32[8,96,128]{2,1,0:T(8,128)S(1)} %get-tuple-element.112), channel_id=1, source_target_pairs={{1,2},{2,1},{5,6},{6,5},{9,10},{10,9},{13,14},{14,13},{17,18},{18,... | collective-permute-start | bytes 1179656 | tf_op jit(solution)/shard_map/ppermute | solution.py:40
  52.9 8.2 %collective-permute-start.12 = (f32[16,8,128]{2,1,0:T(8,128)S(1)}, f32[16,8,128]{2,1,0:T(8,128)S(1)}, u32[]{:S(2)}, u32[]{:S(2)}) collective-permute-start(f32[16,8,128]{2,1,0:T(8,128)S(1)} %get-tuple-element.109), channel_id=1, source_target_pairs={{1,2},{2,1},{5,6},{6,5},{9,10},{10,9},{13,14},{14,13},{17,18},{18,... | collective-permute-start | bytes 196616 | tf_op jit(solution)/shard_map/ppermute | solution.py:40
  56.6 4.5 %collective-permute-start.11 = (f32[16,8,128]{2,1,0:T(8,128)S(1)}, f32[16,8,128]{2,1,0:T(8,128)S(1)}, u32[]{:S(2)}, u32[]{:S(2)}) collective-permute-start(f32[16,8,128]{2,1,0:T(8,128)S(1)} %get-tuple-element.109), channel_id=1, source_target_pairs={{0,1},{1,0},{2,3},{3,2},{4,5},{5,4},{6,7},{7,6},{8,9},{9,8},{10,11... | collective-permute-start | bytes 196616 | tf_op jit(solution)/shard_map/ppermute | solution.py:36
  56.7 29.7 %collective-permute-start.13 = (f32[5,64,128]{2,1,0:T(8,128)S(1)}, f32[5,64,128]{2,1,0:T(8,128)S(1)}, u32[]{:S(2)}, u32[]{:S(2)}) collective-permute-start(f32[5,64,128]{2,1,0:T(8,128)S(1)} %get-tuple-element.110), channel_id=1, source_target_pairs={{0,16},{16,0},{1,17},{17,1},{2,18},{18,2},{3,19},{19,3},{4,20},{20... | collective-permute-start | bytes 491528 | tf_op jit(solution)/shard_map/ppermute | solution.py:36
  69.2 4.3 %collective-permute-start.19 = (f32[8,128]{1,0:T(8,128)S(1)}, f32[8,128]{1,0:T(8,128)S(1)}, u32[]{:S(2)}, u32[]{:S(2)}) collective-permute-start(f32[8,128]{1,0:T(8,128)S(1)} %get-tuple-element.114), channel_id=1, source_target_pairs={{0,12},{4,8},{8,4},{12,0},{1,13},{5,9},{9,5},{13,1},{2,14},{6,10},... | collective-permute-start | bytes 12296 | tf_op jit(solution)/shard_map/ppermute | solution.py:44
  70.1 3.4 %collective-permute-start.18 = (f32[8,128]{1,0:T(8,128)S(1)}, f32[8,128]{1,0:T(8,128)S(1)}, u32[]{:S(2)}, u32[]{:S(2)}) collective-permute-start(f32[8,128]{1,0:T(8,128)S(1)} %get-tuple-element.114), channel_id=1, source_target_pairs={{0,8},{4,12},{8,0},{12,4},{1,9},{5,13},{9,1},{13,5},{2,10},{6,14},... | collective-permute-start | bytes 12296 | tf_op jit(solution)/shard_map/ppermute | solution.py:44
  71.8 2.5 %collective-permute-start.17 = (f32[8,128]{1,0:T(8,128)S(1)}, f32[8,128]{1,0:T(8,128)S(1)}, u32[]{:S(2)}, u32[]{:S(2)}) collective-permute-start(f32[8,128]{1,0:T(8,128)S(1)} %get-tuple-element.114), channel_id=1, source_target_pairs={{0,4},{4,0},{8,12},{12,8},{1,5},{5,1},{9,13},{13,9},{2,6},{6,2},{1... | collective-permute-start | bytes 12296 | tf_op jit(solution)/shard_map/ppermute | solution.py:44
  74.3 2.6 %collective-permute-start.20 = (f32[4,8,128]{2,1,0:T(8,128)S(1)}, f32[4,8,128]{2,1,0:T(8,128)S(1)}, u32[]{:S(2)}, u32[]{:S(2)}) collective-permute-start(f32[4,8,128]{2,1,0:T(8,128)S(1)} %pad_maximum_fusion), channel_id=1, source_target_pairs={{0,2},{1,3},{2,0},{3,1},{4,6},{5,7},{6,4},{7,5},{8,10},{9,11},{10,... | collective-permute-start | bytes 49160 | tf_op jit(solution)/shard_map/ppermute | solution.py:44
  76.9 3.2 %collective-permute-start.21 = (f32[8,8,128]{2,1,0:T(8,128)S(1)}, f32[8,8,128]{2,1,0:T(8,128)S(1)}, u32[]{:S(2)}, u32[]{:S(2)}) collective-permute-start(f32[8,8,128]{2,1,0:T(8,128)S(1)} %get-tuple-element.150), channel_id=1, source_target_pairs={{0,1},{1,0},{2,3},{3,2},{4,5},{5,4},{6,7},{7,6},{8,9},{9,8},{10,11... | collective-permute-start | bytes 98312 | tf_op jit(solution)/shard_map/ppermute | solution.py:44
  78.9 7.5 %collective-permute-start.16 = (f32[56,128]{1,0:T(8,128)S(1)}, f32[56,128]{1,0:T(8,128)S(1)}, u32[]{:S(2)}, u32[]{:S(2)}) collective-permute-start(f32[56,128]{1,0:T(8,128)S(1)} %get-tuple-element.113), channel_id=1, source_target_pairs={{0,16},{16,0},{1,17},{17,1},{2,18},{18,2},{3,19},{19,3},{4,20},{20... | collective-permute-start | bytes 86024 | tf_op jit(solution)/shard_map/ppermute | solution.py:36

commit v6 on v5

--- a/solution.py
+++ b/solution.py
@@ -100,35 +100,53 @@
     return acc
 
 
+def y_tiles(r_a, r_b, k, x):
+    ey = even("gy")
+    if r_a.shape[1] == 8:
+        va, vb = r_a[x], r_b[x]
+        return jnp.where(ey, vb, va), jnp.where(ey, va, vb)
+    pick_of = lambda f: (f(r_a), f(r_b))
+    if k == 0:
+        low, high = pick_of(lambda r: r[x, 1:9]), pick_of(lambda r: r[x, 4:12])
+    elif k == 1:
+        low = pick_of(lambda r: r[x, 6:14])
+        high = pick_of(lambda r: pltpu.roll(r[x, 8:16], 7, 0))
+    else:
+        low = pick_of(lambda r: pltpu.roll(r[x, 0:8], 4, 0))
+        high = pick_of(lambda r: r[x, 0:8])
+    return jnp.where(ey, low[1], low[0]), jnp.where(ey, high[0], high[1])
+
+
 def face_kernel(src, guess, cls, table, y_a, y_b, x_out, *s):
-    k_x, k_a, k_b, sems = s
+    k_x, k_y, g_y, b_y, sems = s
     nx, ny, _ = src.shape
     p5 = face_start("gx", nx, HX, True)
     p4 = face_start("gx", nx, HX - 1, True)
-    r_a = pl.multiple_of(face_start("gy", ny, 8, True), 8)
-    r_b = pl.multiple_of(face_start("gy", ny, 8, False), 8)
-    copies = [
-        (cls.at[pl.ds(p5, HX)], k_x),
-        (cls.at[:, pl.ds(r_a, 8)], k_a),
-        (cls.at[:, pl.ds(r_b, 8)], k_b),
-        (guess.at[pl.ds(p5, HX)], x_out.at[HX : 2 * HX]),
-        (src.at[pl.ds(p4, HX - 1)], x_out.at[2 * HX : 3 * HX - 1]),
-        (guess.at[:, pl.ds(r_a, 8)], y_a.at[nx : 2 * nx]),
-        (src.at[:, pl.ds(r_a, 8)], y_a.at[2 * nx : 3 * nx]),
-        (guess.at[:, pl.ds(r_b, 8)], y_b.at[nx : 2 * nx]),
-        (src.at[:, pl.ds(r_b, 8)], y_b.at[2 * nx : 3 * nx]),
-    ]
+    hi = [even("gy"), jnp.logical_not(even("gy"))]
+    rows = [pl.multiple_of(face_start("gy", ny, 8, flag), 8) for flag in (True, False)]
+    copies = [(cls.at[pl.ds(p5, HX)], k_x)]
+    for i, r in enumerate(rows):
+        copies.append((cls.at[:, pl.ds(r, 8)], k_y.at[i]))
+        copies.append((guess.at[:, pl.ds(r, 8)], g_y.at[i]))
+        copies.append((src.at[:, pl.ds(r, 8)], b_y.at[i]))
+    copies.append((guess.at[pl.ds(p5, HX)], x_out.at[HX : 2 * HX]))
+    copies.append((src.at[pl.ds(p4, HX - 1)], x_out.at[2 * HX : 3 * HX - 1]))
     copies = [pltpu.make_async_copy(f, t, sems.at[i]) for i, (f, t) in enumerate(copies)]
     for cp in copies:
         cp.start()
-    for cp in copies[:3]:
-        cp.wait()
+    copies[0].wait()
     for f in range(HX):
         x_out[f] = look_up(k_x[f], table)
-    for x in range(nx):
-        y_a[x] = look_up(k_a[x], table)
-        y_b[x] = look_up(k_b[x], table)
-    for cp in copies[3:]:
+    for i, out in ((0, y_a), (1, y_b)):
+        for cp in copies[1 + 3 * i : 4 + 3 * i]:
+            cp.wait()
+        for x in range(nx):
+            c8, v8, b8 = look_up(k_y[i, x], table), g_y[i, x], b_y[i, x]
+            out[x, 8:16] = jnp.zeros((8, 128), F32)
+            out[x, 0:4] = jnp.where(hi[i], b8[4:8], b8[0:4])
+            out[x, 4:9] = jnp.where(hi[i], c8[3:8], c8[0:5])
+            out[x, 9:14] = jnp.where(hi[i], v8[3:8], v8[0:5])
+    for cp in copies[7:]:
         cp.wait()
 
 
@@ -162,17 +180,16 @@
     r_a, r_b, z, work = refs[na:]
     nx, ny, _ = arrs[0].shape
     tiles = ny // 8 + 2
-    ey = even("gy")
     lane = lanes()
     for k in range(na):
         for x in range(nx):
             acc = jnp.zeros((8, 128), F32)
-            va, vb = r_a[k * nx + x], r_b[k * nx + x]
+            low, high = y_tiles(r_a, r_b, k, x)
             for t in range(tiles):
                 if t == 0:
-                    v = jnp.where(ey, vb, va)
+                    v = low
                 elif t == tiles - 1:
-                    v = jnp.where(ey, va, vb)
+                    v = high
                 else:
                     v = arrs[k][x, (t - 1) * 8 : t * 8]
                 g = GW * t
@@ -212,14 +229,13 @@
 
 
 def xframe_kernel(na, nx, r_a, r_b, z_a, z_b, x_out):
-    ey = even("gy")
     items, base = frame_list(na)
     for j, (k, dx, row, w) in enumerate(items):
-        p = k * nx + jnp.where(even("gx"), nx - dx, dx - 1)
-        va, vb = r_a[p], r_b[p]
-        x_out[row : row + w] = jnp.where(ey, vb, va)[8 - w : 8]
-        x_out[row + w : row + 2 * w] = jnp.where(ey, va, vb)[0:w]
-        x_out[base + j * 8 : base + j * 8 + 8] = halo_of(z_a, z_b, p)
+        p = jnp.where(even("gx"), nx - dx, dx - 1)
+        low, high = y_tiles(r_a, r_b, k, p)
+        x_out[row : row + w] = low[8 - w : 8]
+        x_out[row + w : row + 2 * w] = high[0:w]
+        x_out[base + j * 8 : base + j * 8 + 8] = halo_of(z_a, z_b, k * nx + p)
 
 
 def own_offset(nsx):
@@ -229,13 +245,12 @@
 def assemble_own(k, m, h, own, r_a, r_b, z_a, z_b):
     nx, ny, _ = own.shape
     off = 1 + own_offset(1)
-    ey = even("gy")
 
     def one(x, _):
-        va, vb = r_a[k * nx + x], r_b[k * nx + x]
-        m[off + x, 8:16] = jnp.where(ey, vb, va)
+        low, high = y_tiles(r_a, r_b, k, x)
+        m[off + x, 8:16] = low
         m[off + x, 16 : 16 + ny] = own[x]
-        m[off + x, 16 + ny : 24 + ny] = jnp.where(ey, va, vb)
+        m[off + x, 16 + ny : 24 + ny] = high
         h[off + x] = halo_of(z_a, z_b, k * nx + x)
 
     fine_loop(0, nx, one, 2)
@@ -1041,12 +1056,13 @@
 
     y_a, y_b, x1 = call(
         face_kernel,
-        [halo, halo, (3 * HX - 1, ny, 128)],
+        [(nx, 16, 128)] * 2 + [(3 * HX - 1, ny, 128)],
         source, first_guess, cell_classes, class_table,
         smem=(3,),
         hbm=(0, 1, 2),
         more=[pltpu.VMEM((HX, ny, 128), jnp.int32)]
-        + [pltpu.VMEM((nx, 8, 128), jnp.int32)] * 2
+        + [pltpu.VMEM((2, nx, 8, 128), jnp.int32)]
+        + [pltpu.VMEM((2, nx, 8, 128), F32)] * 2
         + [pltpu.SemaphoreType.DMA((9,))],
     )
     x1 = swap_even(x1, "gx")

time: 95.2 us -> 95 us (level)
  starting transfers between devices: 33.7 us -> 31.8 us
  waiting for transfers between devices: 22 us -> 23.6 us
    ppermute x11, starting transfers between devices: 16.1 us -> 14 us  [swap_even(): return lax.ppermute(x, axis, pairs_even(lax.axis_size(axis)))]
    ppermute x6, waiting for transfers between devices: 6.34 us -> 7.59 us  [swap_odd(): return lax.ppermute(x, axis, pairs_odd(lax.axis_size(axis)))]
  transfers between devices with their start and end apart: 22 -> 22, of which waited for: 8 -> 10; matrix products, arithmetic and copies ran while one was open for 0% -> 0% of each run, Pallas kernels for 21% -> 21%
where the time goes in v6:
time: 95 us; the launch traced here: 94.4 us
  Pallas kernels  38.1 us (40%)
  starting transfers between devices  31.8 us (33%)
  waiting for transfers between devices  23.6 us (25%)
    pallas_call x11, Pallas kernels, call(): pl.pallas_call(body, out_shape=shapes, in_specs=specs, out_specs=[pl.Bloc...  38.1 us
    ppermute x11, starting transfers between devices, swap_even(): return lax.ppermute(x, axis, pairs_even(lax.axis_size(axis)))  14 us
    ppermute x6, starting transfers between devices, swap_odd(): return lax.ppermute(x, axis, pairs_odd(lax.axis_size(axis)))  12.4 us
    ppermute x11, waiting for transfers between devices, swap_even(): return lax.ppermute(x, axis, pairs_even(lax.axis_size(axis)))  11.3 us
    ppermute x6, waiting for transfers between devices, swap_odd(): return lax.ppermute(x, axis, pairs_odd(lax.axis_size(axis)))  7.59 us
    ppermute x5, starting transfers between devices, swap_xor(): lax.ppermute(x, axis, [(i, i ^ m) for i in range(lax.axis_size(axis))])  5.37 us
    ppermute x5, waiting for transfers between devices, swap_xor(): lax.ppermute(x, axis, [(i, i ^ m) for i in range(lax.axis_size(axis))])  4.72 us
  transfers between devices with their start and end apart: 22, of which 10 were waited for; matrix products, arithmetic and copies ran while one was open for 0% of the time, Pallas kernels for 21%

profile of v6, /device:TPU:1, one launch (start us, length us, event | category | flops | bytes accessed | tf_op | source)
XLA Modules:
  0.0 94.4 jit_solution(13862618944103408540)
XLA Ops:
  0.6 2.0 %face_kernel.1 = (f32[16,16,128]{2,1,0:T(8,128)S(1)}, f32[16,16,128]{2,1,0:T(8,128)S(1)}, f32[14,64,128]{2,1,0:T(8,128)S(1)}) custom-call(f32[16,64,128]{2,1,0:T(8,128)} %src.3, f32[16,64,128]{2,1,0:T(8,128)} %guess.3, s32[16,64,128]{2,1,0:T(8,128)} %cls.3, f32[8]{0:T(128)} %table.3), custom_call_target="tpu_custom_call" | custom-call | tf_op jit(solution)/shard_map/face_kernel/pallas_call | solution.py:65
  2.6 2.1 %collective-permute-start = (f32[14,64,128]{2,1,0:T(8,128)S(1)}, f32[14,64,128]{2,1,0:T(8,128)S(1)}, u32[]{:S(2)}, u32[]{:S(2)}) collective-permute-start(f32[14,64,128]{2,1,0:T(8,128)S(1)} %get-tuple-element.78), channel_id=1, source_target_pairs={{0,16},{16,0},{1,17},{17,1},{2,18},{18,2},{3,19},{19,3},{4,20},{20... | collective-permute-start | bytes 1376264 | tf_op jit(solution)/shard_map/ppermute | solution.py:36
  4.7 1.3 %collective-permute-start.1 = (f32[16,16,128]{2,1,0:T(8,128)S(1)}, f32[16,16,128]{2,1,0:T(8,128)S(1)}, u32[]{:S(2)}, u32[]{:S(2)}) collective-permute-start(f32[16,16,128]{2,1,0:T(8,128)S(1)} %get-tuple-element.79), channel_id=1, source_target_pairs={{0,4},{4,0},{8,12},{12,8},{1,5},{5,1},{9,13},{13,9},{2,6},{6,2},{1... | collective-permute-start | bytes 393224 | tf_op jit(solution)/shard_map/ppermute | solution.py:36
  6.0 0.7 collective-permute-start.2
  6.7 2.1 %load_kernel.1 = (f32[16,64,128]{2,1,0:T(8,128)S(1)}, f32[16,64,128]{2,1,0:T(8,128)S(1)}, f32[16,64,128]{2,1,0:T(8,128)S(1)}) custom-call(f32[16,64,128]{2,1,0:T(8,128)} %src.3, f32[16,64,128]{2,1,0:T(8,128)} %guess.3, s32[16,64,128]{2,1,0:T(8,128)} %cls.3, f32[8]{0:T(128)} %table.3), custom_call_target="tpu_custom_call" | custom-call | tf_op jit(solution)/shard_map/load_kernel/pallas_call | solution.py:65
  8.8 0.7 zpack_kernel.1
  9.6 4.8 %collective-permute-start.4 = (f32[48,8,128]{2,1,0:T(8,128)S(1)}, f32[48,8,128]{2,1,0:T(8,128)S(1)}, u32[]{:S(2)}, u32[]{:S(2)}) collective-permute-start(f32[48,8,128]{2,1,0:T(8,128)S(1)} %zpack_kernel.1), channel_id=1, source_target_pairs={{1,2},{2,1},{5,6},{6,5},{9,10},{10,9},{13,14},{14,13},{17,18},{18,... | collective-permute-start | bytes 589832 | tf_op jit(solution)/shard_map/ppermute | solution.py:40
  14.5 3.3 %collective-permute-done.4.z_b = f32[48,8,128]{2,1,0:T(8,128)S(1)} collective-permute-done((f32[48,8,128]{2,1,0:T(8,128)S(1)}, f32[48,8,128]{2,1,0:T(8,128)S(1)}, u32[]{:S(2)}, u32[]{:S(2)}) %collective-permute-start.4) | collective-permute-done | bytes 196640 | tf_op jit(solution)/shard_map/ppermute | solution.py:40
  18.1 2.7 %fine_prep_kernel.1 = (f32[23,96,128]{2,1,0:T(8,128)S(1)}, f32[23,8,128]{2,1,0:T(8,128)S(1)}, f32[21,80,128]{2,1,0:T(8,128)S(1)}, f32[21,8,128]{2,1,0:T(8,128)S(...) custom-call(f32[16,64,128]{2,1,0:T(8,128)S(1)} %get-tuple-element.76, ...), custom_call_target="tpu_custom_call" | custom-call | tf_op jit(solution)/shard_map/fine_prep_kernel/pallas_call | solution.py:65
  21.1 7.2 %fine_down_kernel.1 = (f32[23,96,128]{2,1,0:T(8,128)S(1)}, f32[23,8,128]{2,1,0:T(8,128)S(1)}, f32[21,80,128]{2,1,0:T(8,128)S(1)}, f32[21,8,128]{2,1,0:T(8,128)S(...) custom-call(f32[16,64,128]{2,1,0:T(8,128)S(1)} %get-tuple-element.76, ...), custom_call_target="tpu_custom_call", output_to_operand_aliasing={{0}: (4, {}), {1}: (5, {}), {2}: (6, {}), {3}: (7, {}), {4}... | custom-call | tf_op jit(solution)/shard_map/fine_down_kernel/pallas_call | solution.py:65
  28.3 1.1 %collective-permute-start.8 = (f32[8,32,128]{2,1,0:T(8,128)S(1)}, f32[8,32,128]{2,1,0:T(8,128)S(1)}, u32[]{:S(2)}, u32[]{:S(2)}) collective-permute-start(f32[8,32,128]{2,1,0:T(8,128)S(1)} %get-tuple-element.108.own), channel_id=1, source_target_pairs={{0,16},{16,0},{1,17},{17,1},{2,18},{18,2},{3,19},{19,3},{4,20},{20... | collective-permute-start | bytes 393224 | tf_op jit(solution)/shard_map/ppermute | solution.py:36
  29.3 4.3 %collective-permute-done.8.other = f32[8,32,128]{2,1,0:T(8,128)S(1)} collective-permute-done((f32[8,32,128]{2,1,0:T(8,128)S(1)}, f32[8,32,128]{2,1,0:T(8,128)S(1)}, u32[]{:S(2)}, u32[]{:S(2)}) %collective-permute-start.8) | collective-permute-done | bytes 131104 | tf_op jit(solution)/shard_map/ppermute | solution.py:36
  33.7 0.7 collective-permute-start.10
  34.4 7.3 %collective-permute-start.9 = (f32[16,32,128]{2,1,0:T(8,128)S(1)}, f32[16,32,128]{2,1,0:T(8,128)S(1)}, u32[]{:S(2)}, u32[]{:S(2)}) collective-permute-start(f32[16,32,128]{2,1,0:T(8,128)S(1)} %join_kernel.1.full), channel_id=1, source_target_pairs={{0,4},{4,0},{8,12},{12,8},{1,5},{5,1},{9,13},{13,9},{2,6},{6,2},{1... | collective-permute-start | bytes 786440 | tf_op jit(solution)/shard_map/ppermute | solution.py:36
  41.8 0.7 collective-permute-start.7
  42.5 6.7 %collective-permute-done.6.vr_a = f32[16,8,128]{2,1,0:T(8,128)S(1)} collective-permute-done((f32[16,8,128]{2,1,0:T(8,128)S(1)}, f32[16,8,128]{2,1,0:T(8,128)S(1)}, u32[]{:S(2)}, u32[]{:S(2)}) %collective-permute-start.6) | collective-permute-done | bytes 65568 | tf_op jit(solution)/shard_map/ppermute | solution.py:36
  49.2 0.9 mid_z_kernel.1
  50.0 1.3 %collective-permute-start.14 = (f32[8,96,128]{2,1,0:T(8,128)S(1)}, f32[8,96,128]{2,1,0:T(8,128)S(1)}, u32[]{:S(2)}, u32[]{:S(2)}) collective-permute-start(f32[8,96,128]{2,1,0:T(8,128)S(1)} %get-tuple-element.111), channel_id=1, source_target_pairs={{0,1},{1,0},{2,3},{3,2},{4,5},{5,4},{6,7},{7,6},{8,9},{9,8},{10,11... | collective-permute-start | bytes 1179656 | tf_op jit(solution)/shard_map/ppermute | solution.py:36
  51.3 1.9 %collective-permute-start.15 = (f32[8,96,128]{2,1,0:T(8,128)S(1)}, f32[8,96,128]{2,1,0:T(8,128)S(1)}, u32[]{:S(2)}, u32[]{:S(2)}) collective-permute-start(f32[8,96,128]{2,1,0:T(8,128)S(1)} %get-tuple-element.112), channel_id=1, source_target_pairs={{1,2},{2,1},{5,6},{6,5},{9,10},{10,9},{13,14},{14,13},{17,18},{18,... | collective-permute-start | bytes 1179656 | tf_op jit(solution)/shard_map/ppermute | solution.py:40
  53.3 3.6 %collective-permute-start.12 = (f32[16,8,128]{2,1,0:T(8,128)S(1)}, f32[16,8,128]{2,1,0:T(8,128)S(1)}, u32[]{:S(2)}, u32[]{:S(2)}) collective-permute-start(f32[16,8,128]{2,1,0:T(8,128)S(1)} %get-tuple-element.109), channel_id=1, source_target_pairs={{1,2},{2,1},{5,6},{6,5},{9,10},{10,9},{13,14},{14,13},{17,18},{18,... | collective-permute-start | bytes 196616 | tf_op jit(solution)/shard_map/ppermute | solution.py:40
  57.1 4.3 %collective-permute-done.12.vz_b = f32[16,8,128]{2,1,0:T(8,128)S(1)} collective-permute-done((f32[16,8,128]{2,1,0:T(8,128)S(1)}, f32[16,8,128]{2,1,0:T(8,128)S(1)}, u32[]{:S(2)}, u32[]{:S(2)}) %collective-permute-start.12) | collective-permute-done | bytes 65568 | tf_op jit(solution)/shard_map/ppermute | solution.py:40
  61.4 8.0 %mid_down_kernel.1 = (f32[18,112,128]{2,1,0:T(8,128)S(1)}, f32[18,112,128]{2,1,0:T(8,128)S(1)}, f32[16,96,128]{2,1,0:T(8,128)S(1)}, f32[16,96,128]{2,1,0:T(8,128...) custom-call(f32[16,32,128]{2,1,0:T(8,128)S(1)} %join_kernel.1.full, ...), custom_call_target="tpu_custom_call" | custom-call | tf_op jit(solution)/shard_map/mid_down_kernel/pallas_call | solution.py:65
  69.5 0.9 collective-permute-start.19
  70.4 1.7 %collective-permute-start.18 = (f32[8,128]{1,0:T(8,128)S(1)}, f32[8,128]{1,0:T(8,128)S(1)}, u32[]{:S(2)}, u32[]{:S(2)}) collective-permute-start(f32[8,128]{1,0:T(8,128)S(1)} %get-tuple-element.114), channel_id=1, source_target_pairs={{0,8},{4,12},{8,0},{12,4},{1,9},{5,13},{9,1},{13,5},{2,10},{6,14},... | collective-permute-start | bytes 12296 | tf_op jit(solution)/shard_map/ppermute | solution.py:44
  72.1 0.9 collective-permute-start.17
  73.1 0.7 collective-permute-done.19
  73.8 0.8 collective-permute-done.17
  74.6 2.6 %collective-permute-done.20 = f32[4,8,128]{2,1,0:T(8,128)S(1)} collective-permute-done((f32[4,8,128]{2,1,0:T(8,128)S(1)}, f32[4,8,128]{2,1,0:T(8,128)S(1)}, u32[]{:S(2)}, u32[]{:S(2)}) %collective-permute-start.20) | collective-permute-done | bytes 16416 | tf_op jit(solution)/shard_map/ppermute | solution.py:44
  77.2 1.8 %collective-permute-start.21 = (f32[8,8,128]{2,1,0:T(8,128)S(1)}, f32[8,8,128]{2,1,0:T(8,128)S(1)}, u32[]{:S(2)}, u32[]{:S(2)}) collective-permute-start(f32[8,8,128]{2,1,0:T(8,128)S(1)} %get-tuple-element.150), channel_id=1, source_target_pairs={{0,1},{1,0},{2,3},{3,2},{4,5},{5,4},{6,7},{7,6},{8,9},{9,8},{10,11... | collective-permute-start | bytes 98312 | tf_op jit(solution)/shard_map/ppermute | solution.py:44
  79.2 0.6 collective-permute-done.21
  79.9 6.3 %coarse_kernel.1.v1 = f32[18,112,128]{2,1,0:T(8,128)S(1)} custom-call(f32[16,8,128]{2,1,0:T(8,128)S(1)} %constant_dynamic-update-slice_fusion.5.blocks, f32[18,112,128]{2,1,0:T(8,128)S(1)} %get-tuple-element.115.s_0_, f32[18,112,128]{2,1,0:T(8,128)S(1)} %get-tuple-element.116.s_1_, f32[16,96,128]{2,1,0:T(8,128)S(1)} %get-tuple-element.117.s_2_, ...), custom_call_target="tpu_custom_call" | custom-call | tf_op jit(solution)/shard_map/coarse_kernel/pallas_call | solution.py:65
  86.2 8.2 %fine_up_kernel.1 = (f32[16,64,128]{2,1,0:T(8,128)}, f32[16,64,128]{2,1,0:T(8,128)}) custom-call(f32[16,64,128]{2,1,0:T(8,128)S(1)} %get-tuple-element.105.v0.v_own, f32[16,64,128]{2,1,0:T(8,128)S(1)} %get-tuple-element.77.refs_2_.src, f32[16,8,128]{2,1,0:T(8,128)S(1)} %collective-permute-done.6.vr_a, f32[16,8,128]{2,1,0:T(8,128)S(1)} %collective-permute-done.7.vr_b, ...), custom_call_target="tpu_custom_call" | custom-call | tf_op jit(solution)/shard_map/fine_up_kernel/pallas_call | solution.py:65
  (30 shorter events, 1.4 us)
Async XLA Ops:
  2.6 18.5 %collective-permute-start = (f32[14,64,128]{2,1,0:T(8,128)S(1)}, f32[14,64,128]{2,1,0:T(8,128)S(1)}, u32[]{:S(2)}, u32[]{:S(2)}) collective-permute-start(f32[14,64,128]{2,1,0:T(8,128)S(1)} %get-tuple-element.78), channel_id=1, source_target_pairs={{0,16},{16,0},{1,17},{17,1},{2,18},{18,2},{3,19},{19,3},{4,20},{20... | collective-permute-start | bytes 1376264 | tf_op jit(solution)/shard_map/ppermute | solution.py:36
  4.7 4.1 %collective-permute-start.1 = (f32[16,16,128]{2,1,0:T(8,128)S(1)}, f32[16,16,128]{2,1,0:T(8,128)S(1)}, u32[]{:S(2)}, u32[]{:S(2)}) collective-permute-start(f32[16,16,128]{2,1,0:T(8,128)S(1)} %get-tuple-element.79), channel_id=1, source_target_pairs={{0,4},{4,0},{8,12},{12,8},{1,5},{5,1},{9,13},{13,9},{2,6},{6,2},{1... | collective-permute-start | bytes 393224 | tf_op jit(solution)/shard_map/ppermute | solution.py:36
  6.0 2.8 %collective-permute-start.2 = (f32[16,16,128]{2,1,0:T(8,128)S(1)}, f32[16,16,128]{2,1,0:T(8,128)S(1)}, u32[]{:S(2)}, u32[]{:S(2)}) collective-permute-start(f32[16,16,128]{2,1,0:T(8,128)S(1)} %get-tuple-element.80), channel_id=1, source_target_pairs={{4,8},{8,4},{5,9},{9,5},{6,10},{10,6},{7,11},{11,7},{20,24},{24,20... | collective-permute-start | bytes 393224 | tf_op jit(solution)/shard_map/ppermute | solution.py:40
  9.6 8.2 %collective-permute-start.4 = (f32[48,8,128]{2,1,0:T(8,128)S(1)}, f32[48,8,128]{2,1,0:T(8,128)S(1)}, u32[]{:S(2)}, u32[]{:S(2)}) collective-permute-start(f32[48,8,128]{2,1,0:T(8,128)S(1)} %zpack_kernel.1), channel_id=1, source_target_pairs={{1,2},{2,1},{5,6},{6,5},{9,10},{10,9},{13,14},{14,13},{17,18},{18,... | collective-permute-start | bytes 589832 | tf_op jit(solution)/shard_map/ppermute | solution.py:40
  14.4 3.3 %collective-permute-start.3 = (f32[48,8,128]{2,1,0:T(8,128)S(1)}, f32[48,8,128]{2,1,0:T(8,128)S(1)}, u32[]{:S(2)}, u32[]{:S(2)}) collective-permute-start(f32[48,8,128]{2,1,0:T(8,128)S(1)} %zpack_kernel.1), channel_id=1, source_target_pairs={{0,1},{1,0},{2,3},{3,2},{4,5},{5,4},{6,7},{7,6},{8,9},{9,8},{10,11... | collective-permute-start | bytes 589832 | tf_op jit(solution)/shard_map/ppermute | solution.py:36
  17.8 3.3 %collective-permute-start.5 = (f32[144,128]{1,0:T(8,128)S(1)}, f32[144,128]{1,0:T(8,128)S(1)}, u32[]{:S(2)}, u32[]{:S(2)}) collective-permute-start(f32[144,128]{1,0:T(8,128)S(1)} %xframe_kernel.1), channel_id=1, source_target_pairs={{0,16},{16,0},{1,17},{17,1},{2,18},{18,2},{3,19},{19,3},{4,20},{20... | collective-permute-start | bytes 221192 | tf_op jit(solution)/shard_map/ppermute | solution.py:36
  28.3 5.4 %collective-permute-start.8 = (f32[8,32,128]{2,1,0:T(8,128)S(1)}, f32[8,32,128]{2,1,0:T(8,128)S(1)}, u32[]{:S(2)}, u32[]{:S(2)}) collective-permute-start(f32[8,32,128]{2,1,0:T(8,128)S(1)} %get-tuple-element.108.own), channel_id=1, source_target_pairs={{0,16},{16,0},{1,17},{17,1},{2,18},{18,2},{3,19},{19,3},{4,20},{20... | collective-permute-start | bytes 393224 | tf_op jit(solution)/shard_map/ppermute | solution.py:36
  33.7 15.4 %collective-permute-start.10 = (f32[16,32,128]{2,1,0:T(8,128)S(1)}, f32[16,32,128]{2,1,0:T(8,128)S(1)}, u32[]{:S(2)}, u32[]{:S(2)}) collective-permute-start(f32[16,32,128]{2,1,0:T(8,128)S(1)} %join_kernel.1.full), channel_id=1, source_target_pairs={{4,8},{8,4},{5,9},{9,5},{6,10},{10,6},{7,11},{11,7},{20,24},{24,20... | collective-permute-start | bytes 786440 | tf_op jit(solution)/shard_map/ppermute | solution.py:40
  34.4 14.8 %collective-permute-start.9 = (f32[16,32,128]{2,1,0:T(8,128)S(1)}, f32[16,32,128]{2,1,0:T(8,128)S(1)}, u32[]{:S(2)}, u32[]{:S(2)}) collective-permute-start(f32[16,32,128]{2,1,0:T(8,128)S(1)} %join_kernel.1.full), channel_id=1, source_target_pairs={{0,4},{4,0},{8,12},{12,8},{1,5},{5,1},{9,13},{13,9},{2,6},{6,2},{1... | collective-permute-start | bytes 786440 | tf_op jit(solution)/shard_map/ppermute | solution.py:36
  41.7 7.4 %collective-permute-start.6 = (f32[16,8,128]{2,1,0:T(8,128)S(1)}, f32[16,8,128]{2,1,0:T(8,128)S(1)}, u32[]{:S(2)}, u32[]{:S(2)}) collective-permute-start(f32[16,8,128]{2,1,0:T(8,128)S(1)} %get-tuple-element.106), channel_id=1, source_target_pairs={{0,4},{4,0},{8,12},{12,8},{1,5},{5,1},{9,13},{13,9},{2,6},{6,2},{1... | collective-permute-start | bytes 196616 | tf_op jit(solution)/shard_map/ppermute | solution.py:36
  41.8 7.3 %collective-permute-start.7 = (f32[16,8,128]{2,1,0:T(8,128)S(1)}, f32[16,8,128]{2,1,0:T(8,128)S(1)}, u32[]{:S(2)}, u32[]{:S(2)}) collective-permute-start(f32[16,8,128]{2,1,0:T(8,128)S(1)} %get-tuple-element.107), channel_id=1, source_target_pairs={{4,8},{8,4},{5,9},{9,5},{6,10},{10,6},{7,11},{11,7},{20,24},{24,20... | collective-permute-start | bytes 196616 | tf_op jit(solution)/shard_map/ppermute | solution.py:40
  50.0 11.4 %collective-permute-start.14 = (f32[8,96,128]{2,1,0:T(8,128)S(1)}, f32[8,96,128]{2,1,0:T(8,128)S(1)}, u32[]{:S(2)}, u32[]{:S(2)}) collective-permute-start(f32[8,96,128]{2,1,0:T(8,128)S(1)} %get-tuple-element.111), channel_id=1, source_target_pairs={{0,1},{1,0},{2,3},{3,2},{4,5},{5,4},{6,7},{7,6},{8,9},{9,8},{10,11... | collective-permute-start | bytes 1179656 | tf_op jit(solution)/shard_map/ppermute | solution.py:36
  51.3 10.1 %collective-permute-start.15 = (f32[8,96,128]{2,1,0:T(8,128)S(1)}, f32[8,96,128]{2,1,0:T(8,128)S(1)}, u32[]{:S(2)}, u32[]{:S(2)}) collective-permute-start(f32[8,96,128]{2,1,0:T(8,128)S(1)} %get-tuple-element.112), channel_id=1, source_target_pairs={{1,2},{2,1},{5,6},{6,5},{9,10},{10,9},{13,14},{14,13},{17,18},{18,... | collective-permute-start | bytes 1179656 | tf_op jit(solution)/shard_map/ppermute | solution.py:40
  53.3 8.2 %collective-permute-start.12 = (f32[16,8,128]{2,1,0:T(8,128)S(1)}, f32[16,8,128]{2,1,0:T(8,128)S(1)}, u32[]{:S(2)}, u32[]{:S(2)}) collective-permute-start(f32[16,8,128]{2,1,0:T(8,128)S(1)} %get-tuple-element.109), channel_id=1, source_target_pairs={{1,2},{2,1},{5,6},{6,5},{9,10},{10,9},{13,14},{14,13},{17,18},{18,... | collective-permute-start | bytes 196616 | tf_op jit(solution)/shard_map/ppermute | solution.py:40
  56.9 4.5 %collective-permute-start.11 = (f32[16,8,128]{2,1,0:T(8,128)S(1)}, f32[16,8,128]{2,1,0:T(8,128)S(1)}, u32[]{:S(2)}, u32[]{:S(2)}) collective-permute-start(f32[16,8,128]{2,1,0:T(8,128)S(1)} %get-tuple-element.109), channel_id=1, source_target_pairs={{0,1},{1,0},{2,3},{3,2},{4,5},{5,4},{6,7},{7,6},{8,9},{9,8},{10,11... | collective-permute-start | bytes 196616 | tf_op jit(solution)/shard_map/ppermute | solution.py:36
  57.0 29.2 %collective-permute-start.13 = (f32[5,64,128]{2,1,0:T(8,128)S(1)}, f32[5,64,128]{2,1,0:T(8,128)S(1)}, u32[]{:S(2)}, u32[]{:S(2)}) collective-permute-start(f32[5,64,128]{2,1,0:T(8,128)S(1)} %get-tuple-element.110), channel_id=1, source_target_pairs={{0,16},{16,0},{1,17},{17,1},{2,18},{18,2},{3,19},{19,3},{4,20},{20... | collective-permute-start | bytes 491528 | tf_op jit(solution)/shard_map/ppermute | solution.py:36
  69.5 4.3 %collective-permute-start.19 = (f32[8,128]{1,0:T(8,128)S(1)}, f32[8,128]{1,0:T(8,128)S(1)}, u32[]{:S(2)}, u32[]{:S(2)}) collective-permute-start(f32[8,128]{1,0:T(8,128)S(1)} %get-tuple-element.114), channel_id=1, source_target_pairs={{0,12},{4,8},{8,4},{12,0},{1,13},{5,9},{9,5},{13,1},{2,14},{6,10},... | collective-permute-start | bytes 12296 | tf_op jit(solution)/shard_map/ppermute | solution.py:44
  70.4 3.4 %collective-permute-start.18 = (f32[8,128]{1,0:T(8,128)S(1)}, f32[8,128]{1,0:T(8,128)S(1)}, u32[]{:S(2)}, u32[]{:S(2)}) collective-permute-start(f32[8,128]{1,0:T(8,128)S(1)} %get-tuple-element.114), channel_id=1, source_target_pairs={{0,8},{4,12},{8,0},{12,4},{1,9},{5,13},{9,1},{13,5},{2,10},{6,14},... | collective-permute-start | bytes 12296 | tf_op jit(solution)/shard_map/ppermute | solution.py:44
  72.1 2.5 %collective-permute-start.17 = (f32[8,128]{1,0:T(8,128)S(1)}, f32[8,128]{1,0:T(8,128)S(1)}, u32[]{:S(2)}, u32[]{:S(2)}) collective-permute-start(f32[8,128]{1,0:T(8,128)S(1)} %get-tuple-element.114), channel_id=1, source_target_pairs={{0,4},{4,0},{8,12},{12,8},{1,5},{5,1},{9,13},{13,9},{2,6},{6,2},{1... | collective-permute-start | bytes 12296 | tf_op jit(solution)/shard_map/ppermute | solution.py:44
  74.6 2.6 %collective-permute-start.20 = (f32[4,8,128]{2,1,0:T(8,128)S(1)}, f32[4,8,128]{2,1,0:T(8,128)S(1)}, u32[]{:S(2)}, u32[]{:S(2)}) collective-permute-start(f32[4,8,128]{2,1,0:T(8,128)S(1)} %pad_maximum_fusion), channel_id=1, source_target_pairs={{0,2},{1,3},{2,0},{3,1},{4,6},{5,7},{6,4},{7,5},{8,10},{9,11},{10,... | collective-permute-start | bytes 49160 | tf_op jit(solution)/shard_map/ppermute | solution.py:44
  77.2 2.6 %collective-permute-start.21 = (f32[8,8,128]{2,1,0:T(8,128)S(1)}, f32[8,8,128]{2,1,0:T(8,128)S(1)}, u32[]{:S(2)}, u32[]{:S(2)}) collective-permute-start(f32[8,8,128]{2,1,0:T(8,128)S(1)} %get-tuple-element.150), channel_id=1, source_target_pairs={{0,1},{1,0},{2,3},{3,2},{4,5},{5,4},{6,7},{7,6},{8,9},{9,8},{10,11... | collective-permute-start | bytes 98312 | tf_op jit(solution)/shard_map/ppermute | solution.py:44
  79.0 7.2 %collective-permute-start.16 = (f32[56,128]{1,0:T(8,128)S(1)}, f32[56,128]{1,0:T(8,128)S(1)}, u32[]{:S(2)}, u32[]{:S(2)}) collective-permute-start(f32[56,128]{1,0:T(8,128)S(1)} %get-tuple-element.113), channel_id=1, source_target_pairs={{0,16},{16,0},{1,17},{17,1},{2,18},{18,2},{3,19},{19,3},{4,20},{20... | collective-permute-start | bytes 86024 | tf_op jit(solution)/shard_map/ppermute | solution.py:36

commit v7 on v6

--- a/solution.py
+++ b/solution.py
@@ -16,7 +16,7 @@
 HX = 5
 HL = 6
 GW = 2 * HL
-UNROLL = 4
+UNROLL = 7
 H2 = 12
 F32 = jnp.float32
 

time: 95 us -> 93.3 us (0.982)
  Pallas kernels: 38.1 us -> 36.3 us
    pallas_call x11, Pallas kernels: 38.1 us -> 36.3 us  [call(): pl.pallas_call(body, out_shape=shapes, in_specs=specs, out_specs=[pl.Bloc...]
  transfers between devices with their start and end apart: 22 -> 22, of which waited for: 10 -> 10; matrix products, arithmetic and copies ran while one was open for 0% -> 0% of each run, Pallas kernels for 21% -> 19%
where the time goes in v7:
time: 93.3 us; the launch traced here: 92.6 us
  Pallas kernels  36.3 us (39%)
  starting transfers between devices  31.8 us (34%)
  waiting for transfers between devices  23.6 us (25%)
    pallas_call x11, Pallas kernels, call(): pl.pallas_call(body, out_shape=shapes, in_specs=specs, out_specs=[pl.Bloc...  36.3 us
    ppermute x11, starting transfers between devices, swap_even(): return lax.ppermute(x, axis, pairs_even(lax.axis_size(axis)))  14 us
    ppermute x6, starting transfers between devices, swap_odd(): return lax.ppermute(x, axis, pairs_odd(lax.axis_size(axis)))  12.4 us
    ppermute x11, waiting for transfers between devices, swap_even(): return lax.ppermute(x, axis, pairs_even(lax.axis_size(axis)))  11.3 us
    ppermute x6, waiting for transfers between devices, swap_odd(): return lax.ppermute(x, axis, pairs_odd(lax.axis_size(axis)))  7.59 us
    ppermute x5, starting transfers between devices, swap_xor(): lax.ppermute(x, axis, [(i, i ^ m) for i in range(lax.axis_size(axis))])  5.41 us
    ppermute x5, waiting for transfers between devices, swap_xor(): lax.ppermute(x, axis, [(i, i ^ m) for i in range(lax.axis_size(axis))])  4.72 us
  transfers between devices with their start and end apart: 22, of which 10 were waited for; matrix products, arithmetic and copies ran while one was open for 0% of the time, Pallas kernels for 19%

profile of v7, /device:TPU:1, one launch (start us, length us, event | category | flops | bytes accessed | tf_op | source)
XLA Modules:
  0.0 92.6 jit_solution(12767026028959555579)
XLA Ops:
  0.6 2.0 %face_kernel.1 = (f32[16,16,128]{2,1,0:T(8,128)S(1)}, f32[16,16,128]{2,1,0:T(8,128)S(1)}, f32[14,64,128]{2,1,0:T(8,128)S(1)}) custom-call(f32[16,64,128]{2,1,0:T(8,128)} %src.3, f32[16,64,128]{2,1,0:T(8,128)} %guess.3, s32[16,64,128]{2,1,0:T(8,128)} %cls.3, f32[8]{0:T(128)} %table.3), custom_call_target="tpu_custom_call" | custom-call | tf_op jit(solution)/shard_map/face_kernel/pallas_call | solution.py:65
  2.6 2.1 %collective-permute-start = (f32[14,64,128]{2,1,0:T(8,128)S(1)}, f32[14,64,128]{2,1,0:T(8,128)S(1)}, u32[]{:S(2)}, u32[]{:S(2)}) collective-permute-start(f32[14,64,128]{2,1,0:T(8,128)S(1)} %get-tuple-element.78), channel_id=1, source_target_pairs={{0,16},{16,0},{1,17},{17,1},{2,18},{18,2},{3,19},{19,3},{4,20},{20... | collective-permute-start | bytes 1376264 | tf_op jit(solution)/shard_map/ppermute | solution.py:36
  4.7 1.3 %collective-permute-start.1 = (f32[16,16,128]{2,1,0:T(8,128)S(1)}, f32[16,16,128]{2,1,0:T(8,128)S(1)}, u32[]{:S(2)}, u32[]{:S(2)}) collective-permute-start(f32[16,16,128]{2,1,0:T(8,128)S(1)} %get-tuple-element.79), channel_id=1, source_target_pairs={{0,4},{4,0},{8,12},{12,8},{1,5},{5,1},{9,13},{13,9},{2,6},{6,2},{1... | collective-permute-start | bytes 393224 | tf_op jit(solution)/shard_map/ppermute | solution.py:36
  6.0 0.7 collective-permute-start.2
  6.7 2.1 %load_kernel.1 = (f32[16,64,128]{2,1,0:T(8,128)S(1)}, f32[16,64,128]{2,1,0:T(8,128)S(1)}, f32[16,64,128]{2,1,0:T(8,128)S(1)}) custom-call(f32[16,64,128]{2,1,0:T(8,128)} %src.3, f32[16,64,128]{2,1,0:T(8,128)} %guess.3, s32[16,64,128]{2,1,0:T(8,128)} %cls.3, f32[8]{0:T(128)} %table.3), custom_call_target="tpu_custom_call" | custom-call | tf_op jit(solution)/shard_map/load_kernel/pallas_call | solution.py:65
  8.8 0.7 zpack_kernel.1
  9.6 4.8 %collective-permute-start.4 = (f32[48,8,128]{2,1,0:T(8,128)S(1)}, f32[48,8,128]{2,1,0:T(8,128)S(1)}, u32[]{:S(2)}, u32[]{:S(2)}) collective-permute-start(f32[48,8,128]{2,1,0:T(8,128)S(1)} %zpack_kernel.1), channel_id=1, source_target_pairs={{1,2},{2,1},{5,6},{6,5},{9,10},{10,9},{13,14},{14,13},{17,18},{18,... | collective-permute-start | bytes 589832 | tf_op jit(solution)/shard_map/ppermute | solution.py:40
  14.5 3.3 %collective-permute-done.4.z_b = f32[48,8,128]{2,1,0:T(8,128)S(1)} collective-permute-done((f32[48,8,128]{2,1,0:T(8,128)S(1)}, f32[48,8,128]{2,1,0:T(8,128)S(1)}, u32[]{:S(2)}, u32[]{:S(2)}) %collective-permute-start.4) | collective-permute-done | bytes 196640 | tf_op jit(solution)/shard_map/ppermute | solution.py:40
  18.1 2.7 %fine_prep_kernel.1 = (f32[23,96,128]{2,1,0:T(8,128)S(1)}, f32[23,8,128]{2,1,0:T(8,128)S(1)}, f32[21,80,128]{2,1,0:T(8,128)S(1)}, f32[21,8,128]{2,1,0:T(8,128)S(...) custom-call(f32[16,64,128]{2,1,0:T(8,128)S(1)} %get-tuple-element.76, ...), custom_call_target="tpu_custom_call" | custom-call | tf_op jit(solution)/shard_map/fine_prep_kernel/pallas_call | solution.py:65
  21.1 7.2 %fine_down_kernel.1 = (f32[23,96,128]{2,1,0:T(8,128)S(1)}, f32[23,8,128]{2,1,0:T(8,128)S(1)}, f32[21,80,128]{2,1,0:T(8,128)S(1)}, f32[21,8,128]{2,1,0:T(8,128)S(...) custom-call(f32[16,64,128]{2,1,0:T(8,128)S(1)} %get-tuple-element.76, ...), custom_call_target="tpu_custom_call", output_to_operand_aliasing={{0}: (4, {}), {1}: (5, {}), {2}: (6, {}), {3}: (7, {}), {4}... | custom-call | tf_op jit(solution)/shard_map/fine_down_kernel/pallas_call | solution.py:65
  28.3 1.1 %collective-permute-start.8 = (f32[8,32,128]{2,1,0:T(8,128)S(1)}, f32[8,32,128]{2,1,0:T(8,128)S(1)}, u32[]{:S(2)}, u32[]{:S(2)}) collective-permute-start(f32[8,32,128]{2,1,0:T(8,128)S(1)} %get-tuple-element.108.own), channel_id=1, source_target_pairs={{0,16},{16,0},{1,17},{17,1},{2,18},{18,2},{3,19},{19,3},{4,20},{20... | collective-permute-start | bytes 393224 | tf_op jit(solution)/shard_map/ppermute | solution.py:36
  29.3 4.3 %collective-permute-done.8.other = f32[8,32,128]{2,1,0:T(8,128)S(1)} collective-permute-done((f32[8,32,128]{2,1,0:T(8,128)S(1)}, f32[8,32,128]{2,1,0:T(8,128)S(1)}, u32[]{:S(2)}, u32[]{:S(2)}) %collective-permute-start.8) | collective-permute-done | bytes 131104 | tf_op jit(solution)/shard_map/ppermute | solution.py:36
  33.7 0.7 collective-permute-start.10
  34.4 7.3 %collective-permute-start.9 = (f32[16,32,128]{2,1,0:T(8,128)S(1)}, f32[16,32,128]{2,1,0:T(8,128)S(1)}, u32[]{:S(2)}, u32[]{:S(2)}) collective-permute-start(f32[16,32,128]{2,1,0:T(8,128)S(1)} %join_kernel.1.full), channel_id=1, source_target_pairs={{0,4},{4,0},{8,12},{12,8},{1,5},{5,1},{9,13},{13,9},{2,6},{6,2},{1... | collective-permute-start | bytes 786440 | tf_op jit(solution)/shard_map/ppermute | solution.py:36
  41.8 0.7 collective-permute-start.7
  42.5 6.7 %collective-permute-done.6.vr_a = f32[16,8,128]{2,1,0:T(8,128)S(1)} collective-permute-done((f32[16,8,128]{2,1,0:T(8,128)S(1)}, f32[16,8,128]{2,1,0:T(8,128)S(1)}, u32[]{:S(2)}, u32[]{:S(2)}) %collective-permute-start.6) | collective-permute-done | bytes 65568 | tf_op jit(solution)/shard_map/ppermute | solution.py:36
  49.2 0.9 mid_z_kernel.1
  50.0 1.3 %collective-permute-start.14 = (f32[8,96,128]{2,1,0:T(8,128)S(1)}, f32[8,96,128]{2,1,0:T(8,128)S(1)}, u32[]{:S(2)}, u32[]{:S(2)}) collective-permute-start(f32[8,96,128]{2,1,0:T(8,128)S(1)} %get-tuple-element.111), channel_id=1, source_target_pairs={{0,1},{1,0},{2,3},{3,2},{4,5},{5,4},{6,7},{7,6},{8,9},{9,8},{10,11... | collective-permute-start | bytes 1179656 | tf_op jit(solution)/shard_map/ppermute | solution.py:36
  51.3 1.9 %collective-permute-start.15 = (f32[8,96,128]{2,1,0:T(8,128)S(1)}, f32[8,96,128]{2,1,0:T(8,128)S(1)}, u32[]{:S(2)}, u32[]{:S(2)}) collective-permute-start(f32[8,96,128]{2,1,0:T(8,128)S(1)} %get-tuple-element.112), channel_id=1, source_target_pairs={{1,2},{2,1},{5,6},{6,5},{9,10},{10,9},{13,14},{14,13},{17,18},{18,... | collective-permute-start | bytes 1179656 | tf_op jit(solution)/shard_map/ppermute | solution.py:40
  53.3 3.6 %collective-permute-start.12 = (f32[16,8,128]{2,1,0:T(8,128)S(1)}, f32[16,8,128]{2,1,0:T(8,128)S(1)}, u32[]{:S(2)}, u32[]{:S(2)}) collective-permute-start(f32[16,8,128]{2,1,0:T(8,128)S(1)} %get-tuple-element.109), channel_id=1, source_target_pairs={{1,2},{2,1},{5,6},{6,5},{9,10},{10,9},{13,14},{14,13},{17,18},{18,... | collective-permute-start | bytes 196616 | tf_op jit(solution)/shard_map/ppermute | solution.py:40
  57.1 4.3 %collective-permute-done.12.vz_b = f32[16,8,128]{2,1,0:T(8,128)S(1)} collective-permute-done((f32[16,8,128]{2,1,0:T(8,128)S(1)}, f32[16,8,128]{2,1,0:T(8,128)S(1)}, u32[]{:S(2)}, u32[]{:S(2)}) %collective-permute-start.12) | collective-permute-done | bytes 65568 | tf_op jit(solution)/shard_map/ppermute | solution.py:40
  61.4 7.2 %mid_down_kernel.1 = (f32[18,112,128]{2,1,0:T(8,128)S(1)}, f32[18,112,128]{2,1,0:T(8,128)S(1)}, f32[16,96,128]{2,1,0:T(8,128)S(1)}, f32[16,96,128]{2,1,0:T(8,128...) custom-call(f32[16,32,128]{2,1,0:T(8,128)S(1)} %join_kernel.1.full, ...), custom_call_target="tpu_custom_call" | custom-call | tf_op jit(solution)/shard_map/mid_down_kernel/pallas_call | solution.py:65
  68.6 1.0 %collective-permute-start.19 = (f32[8,128]{1,0:T(8,128)S(1)}, f32[8,128]{1,0:T(8,128)S(1)}, u32[]{:S(2)}, u32[]{:S(2)}) collective-permute-start(f32[8,128]{1,0:T(8,128)S(1)} %get-tuple-element.114), channel_id=1, source_target_pairs={{0,12},{4,8},{8,4},{12,0},{1,13},{5,9},{9,5},{13,1},{2,14},{6,10},... | collective-permute-start | bytes 12296 | tf_op jit(solution)/shard_map/ppermute | solution.py:44
  69.6 1.7 %collective-permute-start.18 = (f32[8,128]{1,0:T(8,128)S(1)}, f32[8,128]{1,0:T(8,128)S(1)}, u32[]{:S(2)}, u32[]{:S(2)}) collective-permute-start(f32[8,128]{1,0:T(8,128)S(1)} %get-tuple-element.114), channel_id=1, source_target_pairs={{0,8},{4,12},{8,0},{12,4},{1,9},{5,13},{9,1},{13,5},{2,10},{6,14},... | collective-permute-start | bytes 12296 | tf_op jit(solution)/shard_map/ppermute | solution.py:44
  71.3 0.9 collective-permute-start.17
  72.2 0.7 collective-permute-done.19
  73.0 0.8 collective-permute-done.17
  73.8 2.6 %collective-permute-done.20 = f32[4,8,128]{2,1,0:T(8,128)S(1)} collective-permute-done((f32[4,8,128]{2,1,0:T(8,128)S(1)}, f32[4,8,128]{2,1,0:T(8,128)S(1)}, u32[]{:S(2)}, u32[]{:S(2)}) %collective-permute-start.20) | collective-permute-done | bytes 16416 | tf_op jit(solution)/shard_map/ppermute | solution.py:44
  76.4 1.8 %collective-permute-start.21 = (f32[8,8,128]{2,1,0:T(8,128)S(1)}, f32[8,8,128]{2,1,0:T(8,128)S(1)}, u32[]{:S(2)}, u32[]{:S(2)}) collective-permute-start(f32[8,8,128]{2,1,0:T(8,128)S(1)} %get-tuple-element.150), channel_id=1, source_target_pairs={{0,1},{1,0},{2,3},{3,2},{4,5},{5,4},{6,7},{7,6},{8,9},{9,8},{10,11... | collective-permute-start | bytes 98312 | tf_op jit(solution)/shard_map/ppermute | solution.py:44
  78.4 0.6 collective-permute-done.21
  79.0 5.3 %coarse_kernel.1.v1 = f32[18,112,128]{2,1,0:T(8,128)S(1)} custom-call(f32[16,8,128]{2,1,0:T(8,128)S(1)} %constant_dynamic-update-slice_fusion.5.blocks, f32[18,112,128]{2,1,0:T(8,128)S(1)} %get-tuple-element.115.s_0_, f32[18,112,128]{2,1,0:T(8,128)S(1)} %get-tuple-element.116.s_1_, f32[16,96,128]{2,1,0:T(8,128)S(1)} %get-tuple-element.117.s_2_, ...), custom_call_target="tpu_custom_call" | custom-call | tf_op jit(solution)/shard_map/coarse_kernel/pallas_call | solution.py:65
  84.4 8.2 %fine_up_kernel.1 = (f32[16,64,128]{2,1,0:T(8,128)}, f32[16,64,128]{2,1,0:T(8,128)}) custom-call(f32[16,64,128]{2,1,0:T(8,128)S(1)} %get-tuple-element.105.v0.v_own, f32[16,64,128]{2,1,0:T(8,128)S(1)} %get-tuple-element.77.refs_2_.src, f32[16,8,128]{2,1,0:T(8,128)S(1)} %collective-permute-done.6.vr_a, f32[16,8,128]{2,1,0:T(8,128)S(1)} %collective-permute-done.7.vr_b, ...), custom_call_target="tpu_custom_call" | custom-call | tf_op jit(solution)/shard_map/fine_up_kernel/pallas_call | solution.py:65
  (30 shorter events, 1.4 us)
Async XLA Ops:
  2.6 18.5 %collective-permute-start = (f32[14,64,128]{2,1,0:T(8,128)S(1)}, f32[14,64,128]{2,1,0:T(8,128)S(1)}, u32[]{:S(2)}, u32[]{:S(2)}) collective-permute-start(f32[14,64,128]{2,1,0:T(8,128)S(1)} %get-tuple-element.78), channel_id=1, source_target_pairs={{0,16},{16,0},{1,17},{17,1},{2,18},{18,2},{3,19},{19,3},{4,20},{20... | collective-permute-start | bytes 1376264 | tf_op jit(solution)/shard_map/ppermute | solution.py:36
  4.7 4.1 %collective-permute-start.1 = (f32[16,16,128]{2,1,0:T(8,128)S(1)}, f32[16,16,128]{2,1,0:T(8,128)S(1)}, u32[]{:S(2)}, u32[]{:S(2)}) collective-permute-start(f32[16,16,128]{2,1,0:T(8,128)S(1)} %get-tuple-element.79), channel_id=1, source_target_pairs={{0,4},{4,0},{8,12},{12,8},{1,5},{5,1},{9,13},{13,9},{2,6},{6,2},{1... | collective-permute-start | bytes 393224 | tf_op jit(solution)/shard_map/ppermute | solution.py:36
  6.0 2.8 %collective-permute-start.2 = (f32[16,16,128]{2,1,0:T(8,128)S(1)}, f32[16,16,128]{2,1,0:T(8,128)S(1)}, u32[]{:S(2)}, u32[]{:S(2)}) collective-permute-start(f32[16,16,128]{2,1,0:T(8,128)S(1)} %get-tuple-element.80), channel_id=1, source_target_pairs={{4,8},{8,4},{5,9},{9,5},{6,10},{10,6},{7,11},{11,7},{20,24},{24,20... | collective-permute-start | bytes 393224 | tf_op jit(solution)/shard_map/ppermute | solution.py:40
  9.6 8.2 %collective-permute-start.4 = (f32[48,8,128]{2,1,0:T(8,128)S(1)}, f32[48,8,128]{2,1,0:T(8,128)S(1)}, u32[]{:S(2)}, u32[]{:S(2)}) collective-permute-start(f32[48,8,128]{2,1,0:T(8,128)S(1)} %zpack_kernel.1), channel_id=1, source_target_pairs={{1,2},{2,1},{5,6},{6,5},{9,10},{10,9},{13,14},{14,13},{17,18},{18,... | collective-permute-start | bytes 589832 | tf_op jit(solution)/shard_map/ppermute | solution.py:40
  14.4 3.3 %collective-permute-start.3 = (f32[48,8,128]{2,1,0:T(8,128)S(1)}, f32[48,8,128]{2,1,0:T(8,128)S(1)}, u32[]{:S(2)}, u32[]{:S(2)}) collective-permute-start(f32[48,8,128]{2,1,0:T(8,128)S(1)} %zpack_kernel.1), channel_id=1, source_target_pairs={{0,1},{1,0},{2,3},{3,2},{4,5},{5,4},{6,7},{7,6},{8,9},{9,8},{10,11... | collective-permute-start | bytes 589832 | tf_op jit(solution)/shard_map/ppermute | solution.py:36
  17.8 3.3 %collective-permute-start.5 = (f32[144,128]{1,0:T(8,128)S(1)}, f32[144,128]{1,0:T(8,128)S(1)}, u32[]{:S(2)}, u32[]{:S(2)}) collective-permute-start(f32[144,128]{1,0:T(8,128)S(1)} %xframe_kernel.1), channel_id=1, source_target_pairs={{0,16},{16,0},{1,17},{17,1},{2,18},{18,2},{3,19},{19,3},{4,20},{20... | collective-permute-start | bytes 221192 | tf_op jit(solution)/shard_map/ppermute | solution.py:36
  28.3 5.4 %collective-permute-start.8 = (f32[8,32,128]{2,1,0:T(8,128)S(1)}, f32[8,32,128]{2,1,0:T(8,128)S(1)}, u32[]{:S(2)}, u32[]{:S(2)}) collective-permute-start(f32[8,32,128]{2,1,0:T(8,128)S(1)} %get-tuple-element.108.own), channel_id=1, source_target_pairs={{0,16},{16,0},{1,17},{17,1},{2,18},{18,2},{3,19},{19,3},{4,20},{20... | collective-permute-start | bytes 393224 | tf_op jit(solution)/shard_map/ppermute | solution.py:36
  33.7 15.4 %collective-permute-start.10 = (f32[16,32,128]{2,1,0:T(8,128)S(1)}, f32[16,32,128]{2,1,0:T(8,128)S(1)}, u32[]{:S(2)}, u32[]{:S(2)}) collective-permute-start(f32[16,32,128]{2,1,0:T(8,128)S(1)} %join_kernel.1.full), channel_id=1, source_target_pairs={{4,8},{8,4},{5,9},{9,5},{6,10},{10,6},{7,11},{11,7},{20,24},{24,20... | collective-permute-start | bytes 786440 | tf_op jit(solution)/shard_map/ppermute | solution.py:40
  34.4 14.8 %collective-permute-start.9 = (f32[16,32,128]{2,1,0:T(8,128)S(1)}, f32[16,32,128]{2,1,0:T(8,128)S(1)}, u32[]{:S(2)}, u32[]{:S(2)}) collective-permute-start(f32[16,32,128]{2,1,0:T(8,128)S(1)} %join_kernel.1.full), channel_id=1, source_target_pairs={{0,4},{4,0},{8,12},{12,8},{1,5},{5,1},{9,13},{13,9},{2,6},{6,2},{1... | collective-permute-start | bytes 786440 | tf_op jit(solution)/shard_map/ppermute | solution.py:36
  41.7 7.4 %collective-permute-start.6 = (f32[16,8,128]{2,1,0:T(8,128)S(1)}, f32[16,8,128]{2,1,0:T(8,128)S(1)}, u32[]{:S(2)}, u32[]{:S(2)}) collective-permute-start(f32[16,8,128]{2,1,0:T(8,128)S(1)} %get-tuple-element.106), channel_id=1, source_target_pairs={{0,4},{4,0},{8,12},{12,8},{1,5},{5,1},{9,13},{13,9},{2,6},{6,2},{1... | collective-permute-start | bytes 196616 | tf_op jit(solution)/shard_map/ppermute | solution.py:36
  41.8 7.3 %collective-permute-start.7 = (f32[16,8,128]{2,1,0:T(8,128)S(1)}, f32[16,8,128]{2,1,0:T(8,128)S(1)}, u32[]{:S(2)}, u32[]{:S(2)}) collective-permute-start(f32[16,8,128]{2,1,0:T(8,128)S(1)} %get-tuple-element.107), channel_id=1, source_target_pairs={{4,8},{8,4},{5,9},{9,5},{6,10},{10,6},{7,11},{11,7},{20,24},{24,20... | collective-permute-start | bytes 196616 | tf_op jit(solution)/shard_map/ppermute | solution.py:40
  50.0 11.4 %collective-permute-start.14 = (f32[8,96,128]{2,1,0:T(8,128)S(1)}, f32[8,96,128]{2,1,0:T(8,128)S(1)}, u32[]{:S(2)}, u32[]{:S(2)}) collective-permute-start(f32[8,96,128]{2,1,0:T(8,128)S(1)} %get-tuple-element.111), channel_id=1, source_target_pairs={{0,1},{1,0},{2,3},{3,2},{4,5},{5,4},{6,7},{7,6},{8,9},{9,8},{10,11... | collective-permute-start | bytes 1179656 | tf_op jit(solution)/shard_map/ppermute | solution.py:36
  51.3 10.1 %collective-permute-start.15 = (f32[8,96,128]{2,1,0:T(8,128)S(1)}, f32[8,96,128]{2,1,0:T(8,128)S(1)}, u32[]{:S(2)}, u32[]{:S(2)}) collective-permute-start(f32[8,96,128]{2,1,0:T(8,128)S(1)} %get-tuple-element.112), channel_id=1, source_target_pairs={{1,2},{2,1},{5,6},{6,5},{9,10},{10,9},{13,14},{14,13},{17,18},{18,... | collective-permute-start | bytes 1179656 | tf_op jit(solution)/shard_map/ppermute | solution.py:40
  53.3 8.2 %collective-permute-start.12 = (f32[16,8,128]{2,1,0:T(8,128)S(1)}, f32[16,8,128]{2,1,0:T(8,128)S(1)}, u32[]{:S(2)}, u32[]{:S(2)}) collective-permute-start(f32[16,8,128]{2,1,0:T(8,128)S(1)} %get-tuple-element.109), channel_id=1, source_target_pairs={{1,2},{2,1},{5,6},{6,5},{9,10},{10,9},{13,14},{14,13},{17,18},{18,... | collective-permute-start | bytes 196616 | tf_op jit(solution)/shard_map/ppermute | solution.py:40
  56.9 4.5 %collective-permute-start.11 = (f32[16,8,128]{2,1,0:T(8,128)S(1)}, f32[16,8,128]{2,1,0:T(8,128)S(1)}, u32[]{:S(2)}, u32[]{:S(2)}) collective-permute-start(f32[16,8,128]{2,1,0:T(8,128)S(1)} %get-tuple-element.109), channel_id=1, source_target_pairs={{0,1},{1,0},{2,3},{3,2},{4,5},{5,4},{6,7},{7,6},{8,9},{9,8},{10,11... | collective-permute-start | bytes 196616 | tf_op jit(solution)/shard_map/ppermute | solution.py:36
  57.0 27.4 %collective-permute-start.13 = (f32[5,64,128]{2,1,0:T(8,128)S(1)}, f32[5,64,128]{2,1,0:T(8,128)S(1)}, u32[]{:S(2)}, u32[]{:S(2)}) collective-permute-start(f32[5,64,128]{2,1,0:T(8,128)S(1)} %get-tuple-element.110), channel_id=1, source_target_pairs={{0,16},{16,0},{1,17},{17,1},{2,18},{18,2},{3,19},{19,3},{4,20},{20... | collective-permute-start | bytes 491528 | tf_op jit(solution)/shard_map/ppermute | solution.py:36
  68.6 4.3 %collective-permute-start.19 = (f32[8,128]{1,0:T(8,128)S(1)}, f32[8,128]{1,0:T(8,128)S(1)}, u32[]{:S(2)}, u32[]{:S(2)}) collective-permute-start(f32[8,128]{1,0:T(8,128)S(1)} %get-tuple-element.114), channel_id=1, source_target_pairs={{0,12},{4,8},{8,4},{12,0},{1,13},{5,9},{9,5},{13,1},{2,14},{6,10},... | collective-permute-start | bytes 12296 | tf_op jit(solution)/shard_map/ppermute | solution.py:44
  69.6 3.4 %collective-permute-start.18 = (f32[8,128]{1,0:T(8,128)S(1)}, f32[8,128]{1,0:T(8,128)S(1)}, u32[]{:S(2)}, u32[]{:S(2)}) collective-permute-start(f32[8,128]{1,0:T(8,128)S(1)} %get-tuple-element.114), channel_id=1, source_target_pairs={{0,8},{4,12},{8,0},{12,4},{1,9},{5,13},{9,1},{13,5},{2,10},{6,14},... | collective-permute-start | bytes 12296 | tf_op jit(solution)/shard_map/ppermute | solution.py:44
  71.3 2.5 %collective-permute-start.17 = (f32[8,128]{1,0:T(8,128)S(1)}, f32[8,128]{1,0:T(8,128)S(1)}, u32[]{:S(2)}, u32[]{:S(2)}) collective-permute-start(f32[8,128]{1,0:T(8,128)S(1)} %get-tuple-element.114), channel_id=1, source_target_pairs={{0,4},{4,0},{8,12},{12,8},{1,5},{5,1},{9,13},{13,9},{2,6},{6,2},{1... | collective-permute-start | bytes 12296 | tf_op jit(solution)/shard_map/ppermute | solution.py:44
  73.8 2.6 %collective-permute-start.20 = (f32[4,8,128]{2,1,0:T(8,128)S(1)}, f32[4,8,128]{2,1,0:T(8,128)S(1)}, u32[]{:S(2)}, u32[]{:S(2)}) collective-permute-start(f32[4,8,128]{2,1,0:T(8,128)S(1)} %pad_maximum_fusion), channel_id=1, source_target_pairs={{0,2},{1,3},{2,0},{3,1},{4,6},{5,7},{6,4},{7,5},{8,10},{9,11},{10,... | collective-permute-start | bytes 49160 | tf_op jit(solution)/shard_map/ppermute | solution.py:44
  76.4 2.7 %collective-permute-start.21 = (f32[8,8,128]{2,1,0:T(8,128)S(1)}, f32[8,8,128]{2,1,0:T(8,128)S(1)}, u32[]{:S(2)}, u32[]{:S(2)}) collective-permute-start(f32[8,8,128]{2,1,0:T(8,128)S(1)} %get-tuple-element.150), channel_id=1, source_target_pairs={{0,1},{1,0},{2,3},{3,2},{4,5},{5,4},{6,7},{7,6},{8,9},{9,8},{10,11... | collective-permute-start | bytes 98312 | tf_op jit(solution)/shard_map/ppermute | solution.py:44
  78.2 6.2 %collective-permute-start.16 = (f32[56,128]{1,0:T(8,128)S(1)}, f32[56,128]{1,0:T(8,128)S(1)}, u32[]{:S(2)}, u32[]{:S(2)}) collective-permute-start(f32[56,128]{1,0:T(8,128)S(1)} %get-tuple-element.113), channel_id=1, source_target_pairs={{0,16},{16,0},{1,17},{17,1},{2,18},{18,2},{3,19},{19,3},{4,20},{20... | collective-permute-start | bytes 86024 | tf_op jit(solution)/shard_map/ppermute | solution.py:36

commit v8 on v7

--- a/solution.py
+++ b/solution.py
@@ -346,7 +346,7 @@
                 if d is not None:
                     d[t][x - 1, rw] = total * (0.5 * scale / W)
 
-    fine_loop(1, nx, plane, 2)
+    fine_loop(1, nx, plane, 3)
 
 
 def weighted(a, vals, nb, t, x, rw):

time: 93.3 us -> 92.7 us (level)
  no operation moved by 1% of the time
where the time goes in v8:
time: 92.7 us; the launch traced here: 92.1 us
  Pallas kernels  35.8 us (39%)
  starting transfers between devices  31.8 us (34%)
  waiting for transfers between devices  23.6 us (25%)
    pallas_call x11, Pallas kernels, call(): pl.pallas_call(body, out_shape=shapes, in_specs=specs, out_specs=[pl.Bloc...  35.8 us
    ppermute x11, starting transfers between devices, swap_even(): return lax.ppermute(x, axis, pairs_even(lax.axis_size(axis)))  14 us
    ppermute x6, starting transfers between devices, swap_odd(): return lax.ppermute(x, axis, pairs_odd(lax.axis_size(axis)))  12.4 us
    ppermute x11, waiting for transfers between devices, swap_even(): return lax.ppermute(x, axis, pairs_even(lax.axis_size(axis)))  11.3 us
    ppermute x6, waiting for transfers between devices, swap_odd(): return lax.ppermute(x, axis, pairs_odd(lax.axis_size(axis)))  7.59 us
    ppermute x5, starting transfers between devices, swap_xor(): lax.ppermute(x, axis, [(i, i ^ m) for i in range(lax.axis_size(axis))])  5.41 us
    ppermute x5, waiting for transfers between devices, swap_xor(): lax.ppermute(x, axis, [(i, i ^ m) for i in range(lax.axis_size(axis))])  4.72 us
  transfers between devices with their start and end apart: 22, of which 10 were waited for; matrix products, arithmetic and copies ran while one was open for 0% of the time, Pallas kernels for 19%

profile of v8, /device:TPU:1, one launch (start us, length us, event | category | flops | bytes accessed | tf_op | source)
XLA Modules:
  0.0 92.1 jit_solution(17920272444791192042)
XLA Ops:
  0.6 2.0 %face_kernel.1 = (f32[16,16,128]{2,1,0:T(8,128)S(1)}, f32[16,16,128]{2,1,0:T(8,128)S(1)}, f32[14,64,128]{2,1,0:T(8,128)S(1)}) custom-call(f32[16,64,128]{2,1,0:T(8,128)} %src.3, f32[16,64,128]{2,1,0:T(8,128)} %guess.3, s32[16,64,128]{2,1,0:T(8,128)} %cls.3, f32[8]{0:T(128)} %table.3), custom_call_target="tpu_custom_call" | custom-call | tf_op jit(solution)/shard_map/face_kernel/pallas_call | solution.py:65
  2.6 2.1 %collective-permute-start = (f32[14,64,128]{2,1,0:T(8,128)S(1)}, f32[14,64,128]{2,1,0:T(8,128)S(1)}, u32[]{:S(2)}, u32[]{:S(2)}) collective-permute-start(f32[14,64,128]{2,1,0:T(8,128)S(1)} %get-tuple-element.78), channel_id=1, source_target_pairs={{0,16},{16,0},{1,17},{17,1},{2,18},{18,2},{3,19},{19,3},{4,20},{20... | collective-permute-start | bytes 1376264 | tf_op jit(solution)/shard_map/ppermute | solution.py:36
  4.7 1.3 %collective-permute-start.1 = (f32[16,16,128]{2,1,0:T(8,128)S(1)}, f32[16,16,128]{2,1,0:T(8,128)S(1)}, u32[]{:S(2)}, u32[]{:S(2)}) collective-permute-start(f32[16,16,128]{2,1,0:T(8,128)S(1)} %get-tuple-element.79), channel_id=1, source_target_pairs={{0,4},{4,0},{8,12},{12,8},{1,5},{5,1},{9,13},{13,9},{2,6},{6,2},{1... | collective-permute-start | bytes 393224 | tf_op jit(solution)/shard_map/ppermute | solution.py:36
  6.0 0.7 collective-permute-start.2
  6.7 2.1 %load_kernel.1 = (f32[16,64,128]{2,1,0:T(8,128)S(1)}, f32[16,64,128]{2,1,0:T(8,128)S(1)}, f32[16,64,128]{2,1,0:T(8,128)S(1)}) custom-call(f32[16,64,128]{2,1,0:T(8,128)} %src.3, f32[16,64,128]{2,1,0:T(8,128)} %guess.3, s32[16,64,128]{2,1,0:T(8,128)} %cls.3, f32[8]{0:T(128)} %table.3), custom_call_target="tpu_custom_call" | custom-call | tf_op jit(solution)/shard_map/load_kernel/pallas_call | solution.py:65
  8.8 0.7 zpack_kernel.1
  9.6 4.8 %collective-permute-start.4 = (f32[48,8,128]{2,1,0:T(8,128)S(1)}, f32[48,8,128]{2,1,0:T(8,128)S(1)}, u32[]{:S(2)}, u32[]{:S(2)}) collective-permute-start(f32[48,8,128]{2,1,0:T(8,128)S(1)} %zpack_kernel.1), channel_id=1, source_target_pairs={{1,2},{2,1},{5,6},{6,5},{9,10},{10,9},{13,14},{14,13},{17,18},{18,... | collective-permute-start | bytes 589832 | tf_op jit(solution)/shard_map/ppermute | solution.py:40
  14.5 3.3 %collective-permute-done.4.z_b = f32[48,8,128]{2,1,0:T(8,128)S(1)} collective-permute-done((f32[48,8,128]{2,1,0:T(8,128)S(1)}, f32[48,8,128]{2,1,0:T(8,128)S(1)}, u32[]{:S(2)}, u32[]{:S(2)}) %collective-permute-start.4) | collective-permute-done | bytes 196640 | tf_op jit(solution)/shard_map/ppermute | solution.py:40
  18.1 2.7 %fine_prep_kernel.1 = (f32[23,96,128]{2,1,0:T(8,128)S(1)}, f32[23,8,128]{2,1,0:T(8,128)S(1)}, f32[21,80,128]{2,1,0:T(8,128)S(1)}, f32[21,8,128]{2,1,0:T(8,128)S(...) custom-call(f32[16,64,128]{2,1,0:T(8,128)S(1)} %get-tuple-element.76, ...), custom_call_target="tpu_custom_call" | custom-call | tf_op jit(solution)/shard_map/fine_prep_kernel/pallas_call | solution.py:65
  21.1 7.2 %fine_down_kernel.1 = (f32[23,96,128]{2,1,0:T(8,128)S(1)}, f32[23,8,128]{2,1,0:T(8,128)S(1)}, f32[21,80,128]{2,1,0:T(8,128)S(1)}, f32[21,8,128]{2,1,0:T(8,128)S(...) custom-call(f32[16,64,128]{2,1,0:T(8,128)S(1)} %get-tuple-element.76, ...), custom_call_target="tpu_custom_call", output_to_operand_aliasing={{0}: (4, {}), {1}: (5, {}), {2}: (6, {}), {3}: (7, {}), {4}... | custom-call | tf_op jit(solution)/shard_map/fine_down_kernel/pallas_call | solution.py:65
  28.3 1.1 %collective-permute-start.8 = (f32[8,32,128]{2,1,0:T(8,128)S(1)}, f32[8,32,128]{2,1,0:T(8,128)S(1)}, u32[]{:S(2)}, u32[]{:S(2)}) collective-permute-start(f32[8,32,128]{2,1,0:T(8,128)S(1)} %get-tuple-element.108.own), channel_id=1, source_target_pairs={{0,16},{16,0},{1,17},{17,1},{2,18},{18,2},{3,19},{19,3},{4,20},{20... | collective-permute-start | bytes 393224 | tf_op jit(solution)/shard_map/ppermute | solution.py:36
  29.3 4.3 %collective-permute-done.8.other = f32[8,32,128]{2,1,0:T(8,128)S(1)} collective-permute-done((f32[8,32,128]{2,1,0:T(8,128)S(1)}, f32[8,32,128]{2,1,0:T(8,128)S(1)}, u32[]{:S(2)}, u32[]{:S(2)}) %collective-permute-start.8) | collective-permute-done | bytes 131104 | tf_op jit(solution)/shard_map/ppermute | solution.py:36
  33.7 0.7 collective-permute-start.10
  34.4 7.3 %collective-permute-start.9 = (f32[16,32,128]{2,1,0:T(8,128)S(1)}, f32[16,32,128]{2,1,0:T(8,128)S(1)}, u32[]{:S(2)}, u32[]{:S(2)}) collective-permute-start(f32[16,32,128]{2,1,0:T(8,128)S(1)} %join_kernel.1.full), channel_id=1, source_target_pairs={{0,4},{4,0},{8,12},{12,8},{1,5},{5,1},{9,13},{13,9},{2,6},{6,2},{1... | collective-permute-start | bytes 786440 | tf_op jit(solution)/shard_map/ppermute | solution.py:36
  41.8 0.7 collective-permute-start.7
  42.5 6.7 %collective-permute-done.6.vr_a = f32[16,8,128]{2,1,0:T(8,128)S(1)} collective-permute-done((f32[16,8,128]{2,1,0:T(8,128)S(1)}, f32[16,8,128]{2,1,0:T(8,128)S(1)}, u32[]{:S(2)}, u32[]{:S(2)}) %collective-permute-start.6) | collective-permute-done | bytes 65568 | tf_op jit(solution)/shard_map/ppermute | solution.py:36
  49.2 0.9 mid_z_kernel.1
  50.0 1.3 %collective-permute-start.14 = (f32[8,96,128]{2,1,0:T(8,128)S(1)}, f32[8,96,128]{2,1,0:T(8,128)S(1)}, u32[]{:S(2)}, u32[]{:S(2)}) collective-permute-start(f32[8,96,128]{2,1,0:T(8,128)S(1)} %get-tuple-element.111), channel_id=1, source_target_pairs={{0,1},{1,0},{2,3},{3,2},{4,5},{5,4},{6,7},{7,6},{8,9},{9,8},{10,11... | collective-permute-start | bytes 1179656 | tf_op jit(solution)/shard_map/ppermute | solution.py:36
  51.3 1.9 %collective-permute-start.15 = (f32[8,96,128]{2,1,0:T(8,128)S(1)}, f32[8,96,128]{2,1,0:T(8,128)S(1)}, u32[]{:S(2)}, u32[]{:S(2)}) collective-permute-start(f32[8,96,128]{2,1,0:T(8,128)S(1)} %get-tuple-element.112), channel_id=1, source_target_pairs={{1,2},{2,1},{5,6},{6,5},{9,10},{10,9},{13,14},{14,13},{17,18},{18,... | collective-permute-start | bytes 1179656 | tf_op jit(solution)/shard_map/ppermute | solution.py:40
  53.3 3.6 %collective-permute-start.12 = (f32[16,8,128]{2,1,0:T(8,128)S(1)}, f32[16,8,128]{2,1,0:T(8,128)S(1)}, u32[]{:S(2)}, u32[]{:S(2)}) collective-permute-start(f32[16,8,128]{2,1,0:T(8,128)S(1)} %get-tuple-element.109), channel_id=1, source_target_pairs={{1,2},{2,1},{5,6},{6,5},{9,10},{10,9},{13,14},{14,13},{17,18},{18,... | collective-permute-start | bytes 196616 | tf_op jit(solution)/shard_map/ppermute | solution.py:40
  57.1 4.3 %collective-permute-done.12.vz_b = f32[16,8,128]{2,1,0:T(8,128)S(1)} collective-permute-done((f32[16,8,128]{2,1,0:T(8,128)S(1)}, f32[16,8,128]{2,1,0:T(8,128)S(1)}, u32[]{:S(2)}, u32[]{:S(2)}) %collective-permute-start.12) | collective-permute-done | bytes 65568 | tf_op jit(solution)/shard_map/ppermute | solution.py:40
  61.4 6.7 %mid_down_kernel.1 = (f32[18,112,128]{2,1,0:T(8,128)S(1)}, f32[18,112,128]{2,1,0:T(8,128)S(1)}, f32[16,96,128]{2,1,0:T(8,128)S(1)}, f32[16,96,128]{2,1,0:T(8,128...) custom-call(f32[16,32,128]{2,1,0:T(8,128)S(1)} %join_kernel.1.full, ...), custom_call_target="tpu_custom_call" | custom-call | tf_op jit(solution)/shard_map/mid_down_kernel/pallas_call | solution.py:65
  68.2 1.0 %collective-permute-start.19 = (f32[8,128]{1,0:T(8,128)S(1)}, f32[8,128]{1,0:T(8,128)S(1)}, u32[]{:S(2)}, u32[]{:S(2)}) collective-permute-start(f32[8,128]{1,0:T(8,128)S(1)} %get-tuple-element.114), channel_id=1, source_target_pairs={{0,12},{4,8},{8,4},{12,0},{1,13},{5,9},{9,5},{13,1},{2,14},{6,10},... | collective-permute-start | bytes 12296 | tf_op jit(solution)/shard_map/ppermute | solution.py:44
  69.2 1.7 %collective-permute-start.18 = (f32[8,128]{1,0:T(8,128)S(1)}, f32[8,128]{1,0:T(8,128)S(1)}, u32[]{:S(2)}, u32[]{:S(2)}) collective-permute-start(f32[8,128]{1,0:T(8,128)S(1)} %get-tuple-element.114), channel_id=1, source_target_pairs={{0,8},{4,12},{8,0},{12,4},{1,9},{5,13},{9,1},{13,5},{2,10},{6,14},... | collective-permute-start | bytes 12296 | tf_op jit(solution)/shard_map/ppermute | solution.py:44
  70.9 0.9 collective-permute-start.17
  71.8 0.7 collective-permute-done.19
  72.6 0.8 collective-permute-done.17
  73.4 2.6 %collective-permute-done.20 = f32[4,8,128]{2,1,0:T(8,128)S(1)} collective-permute-done((f32[4,8,128]{2,1,0:T(8,128)S(1)}, f32[4,8,128]{2,1,0:T(8,128)S(1)}, u32[]{:S(2)}, u32[]{:S(2)}) %collective-permute-start.20) | collective-permute-done | bytes 16416 | tf_op jit(solution)/shard_map/ppermute | solution.py:44
  76.0 1.8 %collective-permute-start.21 = (f32[8,8,128]{2,1,0:T(8,128)S(1)}, f32[8,8,128]{2,1,0:T(8,128)S(1)}, u32[]{:S(2)}, u32[]{:S(2)}) collective-permute-start(f32[8,8,128]{2,1,0:T(8,128)S(1)} %get-tuple-element.150), channel_id=1, source_target_pairs={{0,1},{1,0},{2,3},{3,2},{4,5},{5,4},{6,7},{7,6},{8,9},{9,8},{10,11... | collective-permute-start | bytes 98312 | tf_op jit(solution)/shard_map/ppermute | solution.py:44
  78.0 0.6 collective-permute-done.21
  78.6 5.2 %coarse_kernel.1.v1 = f32[18,112,128]{2,1,0:T(8,128)S(1)} custom-call(f32[16,8,128]{2,1,0:T(8,128)S(1)} %constant_dynamic-update-slice_fusion.5.blocks, f32[18,112,128]{2,1,0:T(8,128)S(1)} %get-tuple-element.115.s_0_, f32[18,112,128]{2,1,0:T(8,128)S(1)} %get-tuple-element.116.s_1_, f32[16,96,128]{2,1,0:T(8,128)S(1)} %get-tuple-element.117.s_2_, ...), custom_call_target="tpu_custom_call" | custom-call | tf_op jit(solution)/shard_map/coarse_kernel/pallas_call | solution.py:65
  83.8 8.2 %fine_up_kernel.1 = (f32[16,64,128]{2,1,0:T(8,128)}, f32[16,64,128]{2,1,0:T(8,128)}) custom-call(f32[16,64,128]{2,1,0:T(8,128)S(1)} %get-tuple-element.105.v0.v_own, f32[16,64,128]{2,1,0:T(8,128)S(1)} %get-tuple-element.77.refs_2_.src, f32[16,8,128]{2,1,0:T(8,128)S(1)} %collective-permute-done.6.vr_a, f32[16,8,128]{2,1,0:T(8,128)S(1)} %collective-permute-done.7.vr_b, ...), custom_call_target="tpu_custom_call" | custom-call | tf_op jit(solution)/shard_map/fine_up_kernel/pallas_call | solution.py:65
  (30 shorter events, 1.4 us)
Async XLA Ops:
  2.6 18.5 %collective-permute-start = (f32[14,64,128]{2,1,0:T(8,128)S(1)}, f32[14,64,128]{2,1,0:T(8,128)S(1)}, u32[]{:S(2)}, u32[]{:S(2)}) collective-permute-start(f32[14,64,128]{2,1,0:T(8,128)S(1)} %get-tuple-element.78), channel_id=1, source_target_pairs={{0,16},{16,0},{1,17},{17,1},{2,18},{18,2},{3,19},{19,3},{4,20},{20... | collective-permute-start | bytes 1376264 | tf_op jit(solution)/shard_map/ppermute | solution.py:36
  4.7 4.1 %collective-permute-start.1 = (f32[16,16,128]{2,1,0:T(8,128)S(1)}, f32[16,16,128]{2,1,0:T(8,128)S(1)}, u32[]{:S(2)}, u32[]{:S(2)}) collective-permute-start(f32[16,16,128]{2,1,0:T(8,128)S(1)} %get-tuple-element.79), channel_id=1, source_target_pairs={{0,4},{4,0},{8,12},{12,8},{1,5},{5,1},{9,13},{13,9},{2,6},{6,2},{1... | collective-permute-start | bytes 393224 | tf_op jit(solution)/shard_map/ppermute | solution.py:36
  6.0 2.8 %collective-permute-start.2 = (f32[16,16,128]{2,1,0:T(8,128)S(1)}, f32[16,16,128]{2,1,0:T(8,128)S(1)}, u32[]{:S(2)}, u32[]{:S(2)}) collective-permute-start(f32[16,16,128]{2,1,0:T(8,128)S(1)} %get-tuple-element.80), channel_id=1, source_target_pairs={{4,8},{8,4},{5,9},{9,5},{6,10},{10,6},{7,11},{11,7},{20,24},{24,20... | collective-permute-start | bytes 393224 | tf_op jit(solution)/shard_map/ppermute | solution.py:40
  9.6 8.2 %collective-permute-start.4 = (f32[48,8,128]{2,1,0:T(8,128)S(1)}, f32[48,8,128]{2,1,0:T(8,128)S(1)}, u32[]{:S(2)}, u32[]{:S(2)}) collective-permute-start(f32[48,8,128]{2,1,0:T(8,128)S(1)} %zpack_kernel.1), channel_id=1, source_target_pairs={{1,2},{2,1},{5,6},{6,5},{9,10},{10,9},{13,14},{14,13},{17,18},{18,... | collective-permute-start | bytes 589832 | tf_op jit(solution)/shard_map/ppermute | solution.py:40
  14.4 3.3 %collective-permute-start.3 = (f32[48,8,128]{2,1,0:T(8,128)S(1)}, f32[48,8,128]{2,1,0:T(8,128)S(1)}, u32[]{:S(2)}, u32[]{:S(2)}) collective-permute-start(f32[48,8,128]{2,1,0:T(8,128)S(1)} %zpack_kernel.1), channel_id=1, source_target_pairs={{0,1},{1,0},{2,3},{3,2},{4,5},{5,4},{6,7},{7,6},{8,9},{9,8},{10,11... | collective-permute-start | bytes 589832 | tf_op jit(solution)/shard_map/ppermute | solution.py:36
  17.8 3.3 %collective-permute-start.5 = (f32[144,128]{1,0:T(8,128)S(1)}, f32[144,128]{1,0:T(8,128)S(1)}, u32[]{:S(2)}, u32[]{:S(2)}) collective-permute-start(f32[144,128]{1,0:T(8,128)S(1)} %xframe_kernel.1), channel_id=1, source_target_pairs={{0,16},{16,0},{1,17},{17,1},{2,18},{18,2},{3,19},{19,3},{4,20},{20... | collective-permute-start | bytes 221192 | tf_op jit(solution)/shard_map/ppermute | solution.py:36
  28.3 5.4 %collective-permute-start.8 = (f32[8,32,128]{2,1,0:T(8,128)S(1)}, f32[8,32,128]{2,1,0:T(8,128)S(1)}, u32[]{:S(2)}, u32[]{:S(2)}) collective-permute-start(f32[8,32,128]{2,1,0:T(8,128)S(1)} %get-tuple-element.108.own), channel_id=1, source_target_pairs={{0,16},{16,0},{1,17},{17,1},{2,18},{18,2},{3,19},{19,3},{4,20},{20... | collective-permute-start | bytes 393224 | tf_op jit(solution)/shard_map/ppermute | solution.py:36
  33.7 15.4 %collective-permute-start.10 = (f32[16,32,128]{2,1,0:T(8,128)S(1)}, f32[16,32,128]{2,1,0:T(8,128)S(1)}, u32[]{:S(2)}, u32[]{:S(2)}) collective-permute-start(f32[16,32,128]{2,1,0:T(8,128)S(1)} %join_kernel.1.full), channel_id=1, source_target_pairs={{4,8},{8,4},{5,9},{9,5},{6,10},{10,6},{7,11},{11,7},{20,24},{24,20... | collective-permute-start | bytes 786440 | tf_op jit(solution)/shard_map/ppermute | solution.py:40
  34.4 14.8 %collective-permute-start.9 = (f32[16,32,128]{2,1,0:T(8,128)S(1)}, f32[16,32,128]{2,1,0:T(8,128)S(1)}, u32[]{:S(2)}, u32[]{:S(2)}) collective-permute-start(f32[16,32,128]{2,1,0:T(8,128)S(1)} %join_kernel.1.full), channel_id=1, source_target_pairs={{0,4},{4,0},{8,12},{12,8},{1,5},{5,1},{9,13},{13,9},{2,6},{6,2},{1... | collective-permute-start | bytes 786440 | tf_op jit(solution)/shard_map/ppermute | solution.py:36
  41.7 7.4 %collective-permute-start.6 = (f32[16,8,128]{2,1,0:T(8,128)S(1)}, f32[16,8,128]{2,1,0:T(8,128)S(1)}, u32[]{:S(2)}, u32[]{:S(2)}) collective-permute-start(f32[16,8,128]{2,1,0:T(8,128)S(1)} %get-tuple-element.106), channel_id=1, source_target_pairs={{0,4},{4,0},{8,12},{12,8},{1,5},{5,1},{9,13},{13,9},{2,6},{6,2},{1... | collective-permute-start | bytes 196616 | tf_op jit(solution)/shard_map/ppermute | solution.py:36
  41.8 7.3 %collective-permute-start.7 = (f32[16,8,128]{2,1,0:T(8,128)S(1)}, f32[16,8,128]{2,1,0:T(8,128)S(1)}, u32[]{:S(2)}, u32[]{:S(2)}) collective-permute-start(f32[16,8,128]{2,1,0:T(8,128)S(1)} %get-tuple-element.107), channel_id=1, source_target_pairs={{4,8},{8,4},{5,9},{9,5},{6,10},{10,6},{7,11},{11,7},{20,24},{24,20... | collective-permute-start | bytes 196616 | tf_op jit(solution)/shard_map/ppermute | solution.py:40
  50.0 11.4 %collective-permute-start.14 = (f32[8,96,128]{2,1,0:T(8,128)S(1)}, f32[8,96,128]{2,1,0:T(8,128)S(1)}, u32[]{:S(2)}, u32[]{:S(2)}) collective-permute-start(f32[8,96,128]{2,1,0:T(8,128)S(1)} %get-tuple-element.111), channel_id=1, source_target_pairs={{0,1},{1,0},{2,3},{3,2},{4,5},{5,4},{6,7},{7,6},{8,9},{9,8},{10,11... | collective-permute-start | bytes 1179656 | tf_op jit(solution)/shard_map/ppermute | solution.py:36
  51.3 10.1 %collective-permute-start.15 = (f32[8,96,128]{2,1,0:T(8,128)S(1)}, f32[8,96,128]{2,1,0:T(8,128)S(1)}, u32[]{:S(2)}, u32[]{:S(2)}) collective-permute-start(f32[8,96,128]{2,1,0:T(8,128)S(1)} %get-tuple-element.112), channel_id=1, source_target_pairs={{1,2},{2,1},{5,6},{6,5},{9,10},{10,9},{13,14},{14,13},{17,18},{18,... | collective-permute-start | bytes 1179656 | tf_op jit(solution)/shard_map/ppermute | solution.py:40
  53.3 8.2 %collective-permute-start.12 = (f32[16,8,128]{2,1,0:T(8,128)S(1)}, f32[16,8,128]{2,1,0:T(8,128)S(1)}, u32[]{:S(2)}, u32[]{:S(2)}) collective-permute-start(f32[16,8,128]{2,1,0:T(8,128)S(1)} %get-tuple-element.109), channel_id=1, source_target_pairs={{1,2},{2,1},{5,6},{6,5},{9,10},{10,9},{13,14},{14,13},{17,18},{18,... | collective-permute-start | bytes 196616 | tf_op jit(solution)/shard_map/ppermute | solution.py:40
  56.9 4.5 %collective-permute-start.11 = (f32[16,8,128]{2,1,0:T(8,128)S(1)}, f32[16,8,128]{2,1,0:T(8,128)S(1)}, u32[]{:S(2)}, u32[]{:S(2)}) collective-permute-start(f32[16,8,128]{2,1,0:T(8,128)S(1)} %get-tuple-element.109), channel_id=1, source_target_pairs={{0,1},{1,0},{2,3},{3,2},{4,5},{5,4},{6,7},{7,6},{8,9},{9,8},{10,11... | collective-permute-start | bytes 196616 | tf_op jit(solution)/shard_map/ppermute | solution.py:36
  57.0 26.8 %collective-permute-start.13 = (f32[5,64,128]{2,1,0:T(8,128)S(1)}, f32[5,64,128]{2,1,0:T(8,128)S(1)}, u32[]{:S(2)}, u32[]{:S(2)}) collective-permute-start(f32[5,64,128]{2,1,0:T(8,128)S(1)} %get-tuple-element.110), channel_id=1, source_target_pairs={{0,16},{16,0},{1,17},{17,1},{2,18},{18,2},{3,19},{19,3},{4,20},{20... | collective-permute-start | bytes 491528 | tf_op jit(solution)/shard_map/ppermute | solution.py:36
  68.2 4.3 %collective-permute-start.19 = (f32[8,128]{1,0:T(8,128)S(1)}, f32[8,128]{1,0:T(8,128)S(1)}, u32[]{:S(2)}, u32[]{:S(2)}) collective-permute-start(f32[8,128]{1,0:T(8,128)S(1)} %get-tuple-element.114), channel_id=1, source_target_pairs={{0,12},{4,8},{8,4},{12,0},{1,13},{5,9},{9,5},{13,1},{2,14},{6,10},... | collective-permute-start | bytes 12296 | tf_op jit(solution)/shard_map/ppermute | solution.py:44
  69.2 3.4 %collective-permute-start.18 = (f32[8,128]{1,0:T(8,128)S(1)}, f32[8,128]{1,0:T(8,128)S(1)}, u32[]{:S(2)}, u32[]{:S(2)}) collective-permute-start(f32[8,128]{1,0:T(8,128)S(1)} %get-tuple-element.114), channel_id=1, source_target_pairs={{0,8},{4,12},{8,0},{12,4},{1,9},{5,13},{9,1},{13,5},{2,10},{6,14},... | collective-permute-start | bytes 12296 | tf_op jit(solution)/shard_map/ppermute | solution.py:44
  70.9 2.5 %collective-permute-start.17 = (f32[8,128]{1,0:T(8,128)S(1)}, f32[8,128]{1,0:T(8,128)S(1)}, u32[]{:S(2)}, u32[]{:S(2)}) collective-permute-start(f32[8,128]{1,0:T(8,128)S(1)} %get-tuple-element.114), channel_id=1, source_target_pairs={{0,4},{4,0},{8,12},{12,8},{1,5},{5,1},{9,13},{13,9},{2,6},{6,2},{1... | collective-permute-start | bytes 12296 | tf_op jit(solution)/shard_map/ppermute | solution.py:44
  73.4 2.6 %collective-permute-start.20 = (f32[4,8,128]{2,1,0:T(8,128)S(1)}, f32[4,8,128]{2,1,0:T(8,128)S(1)}, u32[]{:S(2)}, u32[]{:S(2)}) collective-permute-start(f32[4,8,128]{2,1,0:T(8,128)S(1)} %pad_maximum_fusion), channel_id=1, source_target_pairs={{0,2},{1,3},{2,0},{3,1},{4,6},{5,7},{6,4},{7,5},{8,10},{9,11},{10,... | collective-permute-start | bytes 49160 | tf_op jit(solution)/shard_map/ppermute | solution.py:44
  76.0 2.7 %collective-permute-start.21 = (f32[8,8,128]{2,1,0:T(8,128)S(1)}, f32[8,8,128]{2,1,0:T(8,128)S(1)}, u32[]{:S(2)}, u32[]{:S(2)}) collective-permute-start(f32[8,8,128]{2,1,0:T(8,128)S(1)} %get-tuple-element.150), channel_id=1, source_target_pairs={{0,1},{1,0},{2,3},{3,2},{4,5},{5,4},{6,7},{7,6},{8,9},{9,8},{10,11... | collective-permute-start | bytes 98312 | tf_op jit(solution)/shard_map/ppermute | solution.py:44
  77.7 6.1 %collective-permute-start.16 = (f32[56,128]{1,0:T(8,128)S(1)}, f32[56,128]{1,0:T(8,128)S(1)}, u32[]{:S(2)}, u32[]{:S(2)}) collective-permute-start(f32[56,128]{1,0:T(8,128)S(1)} %get-tuple-element.113), channel_id=1, source_target_pairs={{0,16},{16,0},{1,17},{17,1},{2,18},{18,2},{3,19},{19,3},{4,20},{20... | collective-permute-start | bytes 86024 | tf_op jit(solution)/shard_map/ppermute | solution.py:36
